TPU v7x, 512 devices: a whole 4x4x16 slice. The times are simulated.
512 devices in a mesh: tm: 8 (over x, z_hi), space: 64 (over y, z_lo, core).
Axes of the slice: x: 4, y: 4, z: 16 (z_hi: 2, z_lo: 8; z = z_hi * 8 + z_lo), core: 2. Of those that a mesh axis runs over, the one named last changes fastest.
Arguments:
- initial: float32 [128, 64, 128], P('space'), may hold values from -1.5 to 1.5
- coeff: float32 [128, 64, 128], P('space'), may hold values from 0.5 to 4
- guess: float32 [8, 128, 64, 128], P('tm', 'space'), may hold values from -1.5 to 1.5
Outputs:
- fine_nodes: float32 [8, 2, 128, 64, 128], P('tm', None, 'space')
- coarse_end: float32 [8, 64, 32, 64], P('tm', 'space')
All inputs are finite; a program needn't handle non-finite values.
Results may differ from a plain program's by a relative error of at most 0.0001.
Values sent between devices are 32-bit elements; how exact they have to be, the bound alone decides.
No kernel may reach another device: no remote copies, remote signals or barrier semaphores. Data moves between devices by JAX's collectives and lax.ppermute only.
A program may use at most 128 MiB of HBM per device.

v0:
```python
import jax
import jax.numpy as jnp
from jax import lax
from jax.sharding import PartitionSpec as P

ITERS = 2


STEP = 0.06
QUAD = ((0.0, 0.0, 0.0), (5.0 / 24.0, 1.0 / 3.0, -1.0 / 24.0), (1.0 / 6.0, 2.0 / 3.0, 1.0 / 6.0))


def padded_2(cells, sides, width):
    for axis, dim in sides:
        count = lax.axis_size(axis)
        head = lax.slice_in_dim(cells, 0, width, axis=dim)
        tail = lax.slice_in_dim(cells, cells.shape[dim] - width, cells.shape[dim], axis=dim)
        cells = jnp.concatenate(
            [
                lax.ppermute(tail, axis, [(i, (i + 1) % count) for i in range(count)]),
                cells,
                lax.ppermute(head, axis, [((i + 1) % count, i) for i in range(count)]),
            ],
            axis=dim,
        )
    return cells


def from_behind(value, axis, by):
    length = lax.axis_size(axis)
    pairs = [(i, i + by) for i in range(length) if 0 <= i + by < length]
    return lax.ppermute(value, axis, pairs)


def plane_sum(centre):
    return (
        jnp.roll(centre, 1, -2)
        + jnp.roll(centre, -1, -2)
        + jnp.roll(centre, 1, -1)
        + jnp.roll(centre, -1, -1)
    )


def neighbours(padded, stacked):
    return padded[:, 2:] + padded[:, :-2] + plane_sum(stacked) - 6.0 * stacked


def fine_rhs(stacked, coeff):
    padded = padded_2(stacked, (("space", 1),), 1)
    return neighbours(padded, stacked) + coeff * (stacked - stacked * stacked * stacked)


def coarse_rhs(stacked, coarse_coeff):
    padded = padded_2(stacked, (("space", 1),), 1)
    return neighbours(padded, stacked) / 4.0 + coarse_coeff * (
        stacked - stacked * stacked * stacked
    )


def restrict(field):
    leading = field.shape[:-3]
    extent = field.shape[-3:]
    blocks = field.reshape(leading + (extent[0] // 2, 2, extent[1] // 2, 2, extent[2] // 2, 2))
    return blocks.mean(axis=(-5, -3, -1))


def prolong(field):
    leading = field.shape[:-3]
    extent = field.shape[-3:]
    grown = jnp.broadcast_to(
        field[..., :, None, :, None, :, None], leading + (extent[0], 2, extent[1], 2, extent[2], 2)
    )
    return grown.reshape(leading + (2 * extent[0], 2 * extent[1], 2 * extent[2]))


def integral(rates, row):
    return STEP * (QUAD[row][0] * rates[0] + QUAD[row][1] * rates[1] + QUAD[row][2] * rates[2])


def on_device(initial, coeff, guess):
    section_index = lax.axis_index("tm")
    sections = lax.axis_size("tm")
    leading_section = section_index == 0
    fine_state = jnp.stack([guess[0], guess[0], guess[0]])
    coarse_coeff = restrict(coeff)
    coarse_initial = restrict(initial)
    finish = coarse_initial
    for iteration in range(ITERS):
        last_nodes = fine_state[2]
        fine_rates = fine_rhs(fine_state, coeff)
        coarse_nodes = restrict(fine_state)
        coarse_rates = coarse_rhs(coarse_nodes, coarse_coeff)
        carry_one = (
            STEP * (QUAD[1][1] * coarse_rates[1] + QUAD[1][2] * coarse_rates[2])
            + restrict(integral(fine_rates, 1))
            - integral(coarse_rates, 1)
        )
        carry_two = (
            STEP * (QUAD[2][1] * coarse_rates[1] + QUAD[2][2] * coarse_rates[2])
            + restrict(integral(fine_rates, 2))
            - integral(coarse_rates, 2)
        )
        begin_coarse = jnp.where(leading_section, coarse_initial, coarse_nodes[0])
        for segment_index in range(sections):
            if segment_index > 0:
                passed = from_behind(finish, "tm", 1)
                begin_coarse = jnp.where(leading_section, coarse_initial, passed)
            slopes = coarse_rhs(begin_coarse[None], coarse_coeff)[0]
            middle = begin_coarse + STEP * QUAD[1][0] * slopes + carry_one
            finish = begin_coarse + STEP * QUAD[2][0] * slopes + carry_two
        coarse_new = jnp.stack([begin_coarse, middle, finish])
        fine_state = fine_state + prolong(coarse_new - coarse_nodes)
        received = from_behind(last_nodes, "tm", 1)
        start_fine = jnp.where(leading_section, initial, received)
        fine_rates = fine_rhs(fine_state, coeff)
        fine_state = jnp.stack(
            [start_fine, start_fine + integral(fine_rates, 1), start_fine + integral(fine_rates, 2)]
        )
    return (fine_state[1:][None], finish[None])


def solution(mesh):
    return jax.shard_map(
        on_device,
        mesh=mesh,
        in_specs=(P("space", None, None), P("space", None, None), P("tm", "space", None, None)),
        out_specs=(P("tm", None, "space", None, None), P("tm", "space", None, None)),
        check_vma=False,
    )
```

profile of v0, /device:TPU:1, one launch (start us, length us, event | category | flops | bytes accessed | tf_op | source)
XLA Modules:
  0.0 640.8 jit_solution(10805431325167113936)
XLA Ops:
  0.6 6.3 stack.77
  7.0 3.0 copy.26
  10.0 8.8 %collective-permute-start.3 = (f32[3,1,32,64]{3,2,0,1:T(8,128)S(1)}, f32[3,1,32,64]{3,2,0,1:T(8,128)}, u32[]{:S(2)}, u32[]{:S(2)}) collective-permute-start(f32[3,1,32,64]{3,2,0,1:T(8,128)S(1)} %get-tuple-element.79), channel_id=1, source_target_pairs={{1,0},{2,1},{3,2},{4,3},{5,4},{6,5},{7,6},{8,7},{9,8},{10,9},{11,1... | collective-permute-start | bytes 73736 | tf_op jit(solution)/shard_map/ppermute | solution.py:22
  23.2 9.7 %collective-permute-start.1 = (f32[1,1,32,64]{3,2,1,0:T(8,128)S(1)}, f32[1,1,32,64]{3,2,1,0:T(8,128)}, u32[]{:S(2)}, u32[]{:S(2)}) collective-permute-start(f32[1,1,32,64]{3,2,1,0:T(8,128)S(1)} %bitcast_select_fusion.1), channel_id=1, source_target_pairs={{1,0},{2,1},{3,2},{4,3},{5,4},{6,5},{7,6},{8,7},{9,8},{10,9},{11,1... | collective-permute-start | bytes 24584 | tf_op jit(solution)/shard_map/ppermute | solution.py:22
  34.9 12.4 %collective-permute-start.5 = (f32[3,1,64,128]{3,2,1,0:T(8,128)S(1)}, f32[3,1,64,128]{3,2,1,0:T(8,128)S(1)}, u32[]{:S(2)}, u32[]{:S(2)}) collective-permute-start(f32[3,1,64,128]{3,2,1,0:T(8,128)S(1)} %stack.79), channel_id=1, source_target_pairs={{1,0},{2,1},{3,2},{4,3},{5,4},{6,5},{7,6},{8,7},{9,8},{10,9},{11,1... | collective-permute-start | bytes 294920 | tf_op jit(solution)/shard_map/ppermute | solution.py:22
  55.0 10.2 %collective-permute-done.6 = f32[3,1,64,128]{3,2,1,0:T(8,128)S(1)} collective-permute-done((f32[3,1,64,128]{3,2,1,0:T(8,128)S(1)}, f32[3,1,64,128]{3,2,1,0:T(8,128)S(1)}, u32[]{:S(2)}, u32[]{:S(2)}) %collective-permute-start.6) | collective-permute-done | bytes 98336 | tf_op jit(solution)/shard_map/ppermute | solution.py:20
  70.4 7.9 %collective-permute-start.7 = (f32[1,32,64]{2,1,0:T(8,128)S(1)}, f32[1,32,64]{2,1,0:T(8,128)S(1)}, u32[]{:S(2)}, u32[]{:S(2)}) collective-permute-start(f32[1,32,64]{2,1,0:T(8,128)S(1)} %get-tuple-element.16), channel_id=1, source_target_pairs={{0,64},{64,128},{128,192},{192,256},{256,320},{320,384},{384,448},... | collective-permute-start | bytes 24584 | tf_op jit(solution)/shard_map/ppermute | solution.py:32
  79.3 14.9 %collective-permute-start.8 = (f32[1,1,32,64]{3,2,1,0:T(8,128)S(1)}, f32[1,1,32,64]{3,2,1,0:T(8,128)S(1)}, u32[]{:S(2)}, u32[]{:S(2)}) collective-permute-start(f32[1,1,32,64]{3,2,1,0:T(8,128)S(1)} %fusion.232), channel_id=1, source_target_pairs={{1,0},{2,1},{3,2},{4,3},{5,4},{6,5},{7,6},{8,7},{9,8},{10,9},{11,1... | collective-permute-start | bytes 24584 | tf_op jit(solution)/shard_map/ppermute | solution.py:22
  97.4 12.6 %collective-permute-start.10 = (f32[1,32,64]{2,1,0:T(8,128)S(1)}, f32[1,32,64]{2,1,0:T(8,128)S(1)}, u32[]{:S(2)}, u32[]{:S(2)}) collective-permute-start(f32[1,32,64]{2,1,0:T(8,128)S(1)} %fusion.55), channel_id=1, source_target_pairs={{0,64},{64,128},{128,192},{192,256},{256,320},{320,384},{384,448},... | collective-permute-start | bytes 24584 | tf_op jit(solution)/shard_map/ppermute | solution.py:32
  111.1 13.5 %collective-permute-start.11 = (f32[1,1,32,64]{3,2,1,0:T(8,128)S(1)}, f32[1,1,32,64]{3,2,1,0:T(8,128)S(1)}, u32[]{:S(2)}, u32[]{:S(2)}) collective-permute-start(f32[1,1,32,64]{3,2,1,0:T(8,128)S(1)} %fusion.233), channel_id=1, source_target_pairs={{1,0},{2,1},{3,2},{4,3},{5,4},{6,5},{7,6},{8,7},{9,8},{10,9},{11,1... | collective-permute-start | bytes 24584 | tf_op jit(solution)/shard_map/ppermute | solution.py:22
  127.7 12.6 %collective-permute-start.13 = (f32[1,32,64]{2,1,0:T(8,128)S(1)}, f32[1,32,64]{2,1,0:T(8,128)S(1)}, u32[]{:S(2)}, u32[]{:S(2)}) collective-permute-start(f32[1,32,64]{2,1,0:T(8,128)S(1)} %fusion.61), channel_id=1, source_target_pairs={{0,64},{64,128},{128,192},{192,256},{256,320},{320,384},{384,448},... | collective-permute-start | bytes 24584 | tf_op jit(solution)/shard_map/ppermute | solution.py:32
  141.3 13.5 %collective-permute-start.14 = (f32[1,1,32,64]{3,2,1,0:T(8,128)S(1)}, f32[1,1,32,64]{3,2,1,0:T(8,128)S(1)}, u32[]{:S(2)}, u32[]{:S(2)}) collective-permute-start(f32[1,1,32,64]{3,2,1,0:T(8,128)S(1)} %fusion.234), channel_id=1, source_target_pairs={{1,0},{2,1},{3,2},{4,3},{5,4},{6,5},{7,6},{8,7},{9,8},{10,9},{11,1... | collective-permute-start | bytes 24584 | tf_op jit(solution)/shard_map/ppermute | solution.py:22
  158.0 12.6 %collective-permute-start.16 = (f32[1,32,64]{2,1,0:T(8,128)S(1)}, f32[1,32,64]{2,1,0:T(8,128)S(1)}, u32[]{:S(2)}, u32[]{:S(2)}) collective-permute-start(f32[1,32,64]{2,1,0:T(8,128)S(1)} %fusion.67), channel_id=1, source_target_pairs={{0,64},{64,128},{128,192},{192,256},{256,320},{320,384},{384,448},... | collective-permute-start | bytes 24584 | tf_op jit(solution)/shard_map/ppermute | solution.py:32
  171.6 13.5 %collective-permute-start.17 = (f32[1,1,32,64]{3,2,1,0:T(8,128)S(1)}, f32[1,1,32,64]{3,2,1,0:T(8,128)S(1)}, u32[]{:S(2)}, u32[]{:S(2)}) collective-permute-start(f32[1,1,32,64]{3,2,1,0:T(8,128)S(1)} %fusion.235), channel_id=1, source_target_pairs={{1,0},{2,1},{3,2},{4,3},{5,4},{6,5},{7,6},{8,7},{9,8},{10,9},{11,1... | collective-permute-start | bytes 24584 | tf_op jit(solution)/shard_map/ppermute | solution.py:22
  188.3 12.6 %collective-permute-start.19 = (f32[1,32,64]{2,1,0:T(8,128)S(1)}, f32[1,32,64]{2,1,0:T(8,128)S(1)}, u32[]{:S(2)}, u32[]{:S(2)}) collective-permute-start(f32[1,32,64]{2,1,0:T(8,128)S(1)} %fusion.73), channel_id=1, source_target_pairs={{0,64},{64,128},{128,192},{192,256},{256,320},{320,384},{384,448},... | collective-permute-start | bytes 24584 | tf_op jit(solution)/shard_map/ppermute | solution.py:32
  201.9 13.5 %collective-permute-start.20 = (f32[1,1,32,64]{3,2,1,0:T(8,128)S(1)}, f32[1,1,32,64]{3,2,1,0:T(8,128)S(1)}, u32[]{:S(2)}, u32[]{:S(2)}) collective-permute-start(f32[1,1,32,64]{3,2,1,0:T(8,128)S(1)} %fusion.236), channel_id=1, source_target_pairs={{1,0},{2,1},{3,2},{4,3},{5,4},{6,5},{7,6},{8,7},{9,8},{10,9},{11,1... | collective-permute-start | bytes 24584 | tf_op jit(solution)/shard_map/ppermute | solution.py:22
  218.5 12.6 %collective-permute-start.22 = (f32[1,32,64]{2,1,0:T(8,128)S(1)}, f32[1,32,64]{2,1,0:T(8,128)S(1)}, u32[]{:S(2)}, u32[]{:S(2)}) collective-permute-start(f32[1,32,64]{2,1,0:T(8,128)S(1)} %fusion.79), channel_id=1, source_target_pairs={{0,64},{64,128},{128,192},{192,256},{256,320},{320,384},{384,448},... | collective-permute-start | bytes 24584 | tf_op jit(solution)/shard_map/ppermute | solution.py:32
  232.2 13.5 %collective-permute-start.23 = (f32[1,1,32,64]{3,2,1,0:T(8,128)S(1)}, f32[1,1,32,64]{3,2,1,0:T(8,128)S(1)}, u32[]{:S(2)}, u32[]{:S(2)}) collective-permute-start(f32[1,1,32,64]{3,2,1,0:T(8,128)S(1)} %fusion.237), channel_id=1, source_target_pairs={{1,0},{2,1},{3,2},{4,3},{5,4},{6,5},{7,6},{8,7},{9,8},{10,9},{11,1... | collective-permute-start | bytes 24584 | tf_op jit(solution)/shard_map/ppermute | solution.py:22
  248.8 12.6 %collective-permute-start.25 = (f32[1,32,64]{2,1,0:T(8,128)S(1)}, f32[1,32,64]{2,1,0:T(8,128)S(1)}, u32[]{:S(2)}, u32[]{:S(2)}) collective-permute-start(f32[1,32,64]{2,1,0:T(8,128)S(1)} %fusion.85), channel_id=1, source_target_pairs={{0,64},{64,128},{128,192},{192,256},{256,320},{320,384},{384,448},... | collective-permute-start | bytes 24584 | tf_op jit(solution)/shard_map/ppermute | solution.py:32
  261.5 12.7 %collective-permute-start = (f32[2,64,128]{2,1,0:T(8,128)S(1)}, f32[2,64,128]{2,1,0:T(8,128)S(1)}, u32[]{:S(2)}, u32[]{:S(2)}) collective-permute-start(f32[2,64,128]{2,1,0:T(8,128)S(1)} %bitcast.405), channel_id=1, source_target_pairs={{0,64},{64,128},{128,192},{192,256},{256,320},{320,384},{384,448},... | collective-permute-start | bytes 196616 | tf_op jit(solution)/shard_map/ppermute | solution.py:32
  276.7 13.4 %collective-permute-start.26 = (f32[1,1,32,64]{3,2,1,0:T(8,128)S(1)}, f32[1,1,32,64]{3,2,1,0:T(8,128)S(1)}, u32[]{:S(2)}, u32[]{:S(2)}) collective-permute-start(f32[1,1,32,64]{3,2,1,0:T(8,128)S(1)} %bitcast.420), channel_id=1, source_target_pairs={{1,0},{2,1},{3,2},{4,3},{5,4},{6,5},{7,6},{8,7},{9,8},{10,9},{11,1... | collective-permute-start | bytes 24584 | tf_op jit(solution)/shard_map/ppermute | solution.py:22
  293.3 3.1 broadcast_in_dim.44
  296.4 5.6 broadcast_in_dim.45
  302.3 12.6 %collective-permute-start.28 = (f32[3,1,64,128]{3,2,1,0:T(8,128)S(1)}, f32[3,1,64,128]{3,2,1,0:T(8,128)S(1)}, u32[]{:S(2)}, u32[]{:S(2)}) collective-permute-start(f32[3,1,64,128]{3,2,1,0:T(8,128)S(1)} %get-tuple-element.48), channel_id=1, source_target_pairs={{1,0},{2,1},{3,2},{4,3},{5,4},{6,5},{7,6},{8,7},{9,8},{10,9},{11,1... | collective-permute-start | bytes 294920 | tf_op jit(solution)/shard_map/ppermute | solution.py:22
  319.1 5.6 stack.98
  324.7 5.6 stack.96
  330.2 5.6 stack.97
  345.0 13.0 %collective-permute-start.33 = (f32[3,1,32,64]{3,2,0,1:T(8,128)S(1)}, f32[3,1,32,64]{3,2,0,1:T(8,128)S(1)}, u32[]{:S(2)}, u32[]{:S(2)}) collective-permute-start(f32[3,1,32,64]{3,2,0,1:T(8,128)S(1)} %get-tuple-element.69), channel_id=1, source_target_pairs={{1,0},{2,1},{3,2},{4,3},{5,4},{6,5},{7,6},{8,7},{9,8},{10,9},{11,1... | collective-permute-start | bytes 73736 | tf_op jit(solution)/shard_map/ppermute | solution.py:22
  362.5 3.2 collective-permute-start.32
  365.7 10.6 %collective-permute-start.35 = (f32[3,1,64,128]{3,2,1,0:T(8,128)S(1)}, f32[3,1,64,128]{3,2,1,0:T(8,128)S(1)}, u32[]{:S(2)}, u32[]{:S(2)}) collective-permute-start(f32[3,1,64,128]{3,2,1,0:T(8,128)S(1)} %get-tuple-element.38), channel_id=1, source_target_pairs={{1,0},{2,1},{3,2},{4,3},{5,4},{6,5},{7,6},{8,7},{9,8},{10,9},{11,1... | collective-permute-start | bytes 294920 | tf_op jit(solution)/shard_map/ppermute | solution.py:22
  378.4 11.1 %collective-permute-done.36 = f32[3,1,64,128]{3,2,1,0:T(8,128)S(1)} collective-permute-done((f32[3,1,64,128]{3,2,1,0:T(8,128)S(1)}, f32[3,1,64,128]{3,2,1,0:T(8,128)S(1)}, u32[]{:S(2)}, u32[]{:S(2)}) %collective-permute-start.36) | collective-permute-done | bytes 98336 | tf_op jit(solution)/shard_map/ppermute | solution.py:20
  395.5 14.8 %collective-permute-start.38 = (f32[1,1,32,64]{3,2,1,0:T(8,128)S(1)}, f32[1,1,32,64]{3,2,1,0:T(8,128)S(1)}, u32[]{:S(2)}, u32[]{:S(2)}) collective-permute-start(f32[1,1,32,64]{3,2,1,0:T(8,128)S(1)} %fusion.238), channel_id=1, source_target_pairs={{1,0},{2,1},{3,2},{4,3},{5,4},{6,5},{7,6},{8,7},{9,8},{10,9},{11,1... | collective-permute-start | bytes 24584 | tf_op jit(solution)/shard_map/ppermute | solution.py:22
  413.5 12.6 %collective-permute-start.40 = (f32[1,32,64]{2,1,0:T(8,128)S(1)}, f32[1,32,64]{2,1,0:T(8,128)S(1)}, u32[]{:S(2)}, u32[]{:S(2)}) collective-permute-start(f32[1,32,64]{2,1,0:T(8,128)S(1)} %fusion.99), channel_id=1, source_target_pairs={{0,64},{64,128},{128,192},{192,256},{256,320},{320,384},{384,448},... | collective-permute-start | bytes 24584 | tf_op jit(solution)/shard_map/ppermute | solution.py:32
  427.1 13.5 %collective-permute-start.41 = (f32[1,1,32,64]{3,2,1,0:T(8,128)S(1)}, f32[1,1,32,64]{3,2,1,0:T(8,128)S(1)}, u32[]{:S(2)}, u32[]{:S(2)}) collective-permute-start(f32[1,1,32,64]{3,2,1,0:T(8,128)S(1)} %fusion.239), channel_id=1, source_target_pairs={{1,0},{2,1},{3,2},{4,3},{5,4},{6,5},{7,6},{8,7},{9,8},{10,9},{11,1... | collective-permute-start | bytes 24584 | tf_op jit(solution)/shard_map/ppermute | solution.py:22
  443.8 13.3 %collective-permute-start.43 = (f32[1,32,64]{2,1,0:T(8,128)S(1)}, f32[1,32,64]{2,1,0:T(8,128)S(1)}, u32[]{:S(2)}, u32[]{:S(2)}) collective-permute-start(f32[1,32,64]{2,1,0:T(8,128)S(1)} %fusion.105), channel_id=1, source_target_pairs={{0,64},{64,128},{128,192},{192,256},{256,320},{320,384},{384,448},... | collective-permute-start | bytes 24584 | tf_op jit(solution)/shard_map/ppermute | solution.py:32
  458.0 13.5 %collective-permute-start.44 = (f32[1,1,32,64]{3,2,1,0:T(8,128)S(1)}, f32[1,1,32,64]{3,2,1,0:T(8,128)S(1)}, u32[]{:S(2)}, u32[]{:S(2)}) collective-permute-start(f32[1,1,32,64]{3,2,1,0:T(8,128)S(1)} %fusion.240), channel_id=1, source_target_pairs={{1,0},{2,1},{3,2},{4,3},{5,4},{6,5},{7,6},{8,7},{9,8},{10,9},{11,1... | collective-permute-start | bytes 24584 | tf_op jit(solution)/shard_map/ppermute | solution.py:22
  474.7 13.5 %collective-permute-start.46 = (f32[1,32,64]{2,1,0:T(8,128)S(1)}, f32[1,32,64]{2,1,0:T(8,128)S(1)}, u32[]{:S(2)}, u32[]{:S(2)}) collective-permute-start(f32[1,32,64]{2,1,0:T(8,128)S(1)} %fusion.111), channel_id=1, source_target_pairs={{0,64},{64,128},{128,192},{192,256},{256,320},{320,384},{384,448},... | collective-permute-start | bytes 24584 | tf_op jit(solution)/shard_map/ppermute | solution.py:32
  489.2 13.5 %collective-permute-start.47 = (f32[1,1,32,64]{3,2,1,0:T(8,128)S(1)}, f32[1,1,32,64]{3,2,1,0:T(8,128)S(1)}, u32[]{:S(2)}, u32[]{:S(2)}) collective-permute-start(f32[1,1,32,64]{3,2,1,0:T(8,128)S(1)} %fusion.241), channel_id=1, source_target_pairs={{1,0},{2,1},{3,2},{4,3},{5,4},{6,5},{7,6},{8,7},{9,8},{10,9},{11,1... | collective-permute-start | bytes 24584 | tf_op jit(solution)/shard_map/ppermute | solution.py:22
  505.9 13.6 %collective-permute-start.49 = (f32[1,32,64]{2,1,0:T(8,128)S(1)}, f32[1,32,64]{2,1,0:T(8,128)S(1)}, u32[]{:S(2)}, u32[]{:S(2)}) collective-permute-start(f32[1,32,64]{2,1,0:T(8,128)S(1)} %fusion.117), channel_id=1, source_target_pairs={{0,64},{64,128},{128,192},{192,256},{256,320},{320,384},{384,448},... | collective-permute-start | bytes 24584 | tf_op jit(solution)/shard_map/ppermute | solution.py:32
  520.5 13.6 %collective-permute-start.50 = (f32[1,1,32,64]{3,2,1,0:T(8,128)S(1)}, f32[1,1,32,64]{3,2,1,0:T(8,128)S(1)}, u32[]{:S(2)}, u32[]{:S(2)}) collective-permute-start(f32[1,1,32,64]{3,2,1,0:T(8,128)S(1)} %fusion.242), channel_id=1, source_target_pairs={{1,0},{2,1},{3,2},{4,3},{5,4},{6,5},{7,6},{8,7},{9,8},{10,9},{11,1... | collective-permute-start | bytes 24584 | tf_op jit(solution)/shard_map/ppermute | solution.py:22
  537.3 13.4 %collective-permute-start.52 = (f32[1,32,64]{2,1,0:T(8,128)S(1)}, f32[1,32,64]{2,1,0:T(8,128)S(1)}, u32[]{:S(2)}, u32[]{:S(2)}) collective-permute-start(f32[1,32,64]{2,1,0:T(8,128)S(1)} %fusion.123), channel_id=1, source_target_pairs={{0,64},{64,128},{128,192},{192,256},{256,320},{320,384},{384,448},... | collective-permute-start | bytes 24584 | tf_op jit(solution)/shard_map/ppermute | solution.py:32
  551.7 13.5 %collective-permute-start.53 = (f32[1,1,32,64]{3,2,1,0:T(8,128)S(1)}, f32[1,1,32,64]{3,2,1,0:T(8,128)S(1)}, u32[]{:S(2)}, u32[]{:S(2)}) collective-permute-start(f32[1,1,32,64]{3,2,1,0:T(8,128)S(1)} %fusion.243), channel_id=1, source_target_pairs={{1,0},{2,1},{3,2},{4,3},{5,4},{6,5},{7,6},{8,7},{9,8},{10,9},{11,1... | collective-permute-start | bytes 24584 | tf_op jit(solution)/shard_map/ppermute | solution.py:22
  568.3 13.5 %collective-permute-start.55 = (f32[1,32,64]{2,1,0:T(8,128)S(1)}, f32[1,32,64]{2,1,0:T(8,128)S(1)}, u32[]{:S(2)}, u32[]{:S(2)}) collective-permute-start(f32[1,32,64]{2,1,0:T(8,128)S(1)} %fusion.129), channel_id=1, source_target_pairs={{0,64},{64,128},{128,192},{192,256},{256,320},{320,384},{384,448},... | collective-permute-start | bytes 24584 | tf_op jit(solution)/shard_map/ppermute | solution.py:32
  581.8 13.8 %collective-permute-start.30 = (f32[2,64,128]{2,1,0:T(8,128)S(1)}, f32[2,64,128]{2,1,0:T(8,128)S(1)}, u32[]{:S(2)}, u32[]{:S(2)}) collective-permute-start(f32[2,64,128]{2,1,0:T(8,128)S(1)} %bitcast_add_fusion.3), channel_id=1, source_target_pairs={{0,64},{64,128},{128,192},{192,256},{256,320},{320,384},{384,448},... | collective-permute-start | bytes 196616 | tf_op jit(solution)/shard_map/ppermute | solution.py:32
  598.2 13.2 %collective-permute-start.56 = (f32[1,1,32,64]{3,2,1,0:T(8,128)S(1)}, f32[1,1,32,64]{3,2,1,0:T(8,128)S(1)}, u32[]{:S(2)}, u32[]{:S(2)}) collective-permute-start(f32[1,1,32,64]{3,2,1,0:T(8,128)S(1)} %bitcast.414), channel_id=1, source_target_pairs={{1,0},{2,1},{3,2},{4,3},{5,4},{6,5},{7,6},{8,7},{9,8},{10,9},{11,1... | collective-permute-start | bytes 24584 | tf_op jit(solution)/shard_map/ppermute | solution.py:22
  614.6 3.2 broadcast_in_dim.101
  617.8 5.6 broadcast_in_dim.102
  623.7 12.6 %collective-permute-start.58 = (f32[3,1,64,128]{3,2,1,0:T(8,128)S(1)}, f32[3,1,64,128]{3,2,1,0:T(8,128)S(1)}, u32[]{:S(2)}, u32[]{:S(2)}) collective-permute-start(f32[3,1,64,128]{3,2,1,0:T(8,128)S(1)} %get-tuple-element.28), channel_id=1, source_target_pairs={{1,0},{2,1},{3,2},{4,3},{5,4},{6,5},{7,6},{8,7},{9,8},{10,9},{11,1... | collective-permute-start | bytes 294920 | tf_op jit(solution)/shard_map/ppermute | solution.py:22
  (271 shorter events, 110.1 us)
Async XLA Ops:
  10.0 42.1 %collective-permute-start.3 = (f32[3,1,32,64]{3,2,0,1:T(8,128)S(1)}, f32[3,1,32,64]{3,2,0,1:T(8,128)}, u32[]{:S(2)}, u32[]{:S(2)}) collective-permute-start(f32[3,1,32,64]{3,2,0,1:T(8,128)S(1)} %get-tuple-element.79), channel_id=1, source_target_pairs={{1,0},{2,1},{3,2},{4,3},{5,4},{6,5},{7,6},{8,7},{9,8},{10,9},{11,1... | collective-permute-start | bytes 73736 | tf_op jit(solution)/shard_map/ppermute | solution.py:22
  18.8 35.2 %collective-permute-start.4 = (f32[3,1,32,64]{3,2,0,1:T(8,128)S(1)}, f32[3,1,32,64]{3,2,0,1:T(8,128)}, u32[]{:S(2)}, u32[]{:S(2)}) collective-permute-start(f32[3,1,32,64]{3,2,0,1:T(8,128)S(1)} %get-tuple-element.79), channel_id=1, source_target_pairs={{0,1},{1,2},{2,3},{3,4},{4,5},{5,6},{6,7},{7,8},{8,9},{9,10},{10,1... | collective-permute-start | bytes 73736 | tf_op jit(solution)/shard_map/ppermute | solution.py:20
  23.2 46.3 %collective-permute-start.1 = (f32[1,1,32,64]{3,2,1,0:T(8,128)S(1)}, f32[1,1,32,64]{3,2,1,0:T(8,128)}, u32[]{:S(2)}, u32[]{:S(2)}) collective-permute-start(f32[1,1,32,64]{3,2,1,0:T(8,128)S(1)} %bitcast_select_fusion.1), channel_id=1, source_target_pairs={{1,0},{2,1},{3,2},{4,3},{5,4},{6,5},{7,6},{8,7},{9,8},{10,9},{11,1... | collective-permute-start | bytes 24584 | tf_op jit(solution)/shard_map/ppermute | solution.py:22
  32.9 36.6 %collective-permute-start.2 = (f32[1,1,32,64]{3,2,1,0:T(8,128)S(1)}, f32[1,1,32,64]{3,2,1,0:T(8,128)}, u32[]{:S(2)}, u32[]{:S(2)}) collective-permute-start(f32[1,1,32,64]{3,2,1,0:T(8,128)S(1)} %bitcast_select_fusion.1), channel_id=1, source_target_pairs={{0,1},{1,2},{2,3},{3,4},{4,5},{5,6},{6,7},{7,8},{8,9},{9,10},{10,1... | collective-permute-start | bytes 24584 | tf_op jit(solution)/shard_map/ppermute | solution.py:20
  34.9 20.1 %collective-permute-start.5 = (f32[3,1,64,128]{3,2,1,0:T(8,128)S(1)}, f32[3,1,64,128]{3,2,1,0:T(8,128)S(1)}, u32[]{:S(2)}, u32[]{:S(2)}) collective-permute-start(f32[3,1,64,128]{3,2,1,0:T(8,128)S(1)} %stack.79), channel_id=1, source_target_pairs={{1,0},{2,1},{3,2},{4,3},{5,4},{6,5},{7,6},{8,7},{9,8},{10,9},{11,1... | collective-permute-start | bytes 294920 | tf_op jit(solution)/shard_map/ppermute | solution.py:22
  52.1 13.1 %collective-permute-start.6 = (f32[3,1,64,128]{3,2,1,0:T(8,128)S(1)}, f32[3,1,64,128]{3,2,1,0:T(8,128)S(1)}, u32[]{:S(2)}, u32[]{:S(2)}) collective-permute-start(f32[3,1,64,128]{3,2,1,0:T(8,128)S(1)} %stack.80), channel_id=1, source_target_pairs={{0,1},{1,2},{2,3},{3,4},{4,5},{5,6},{6,7},{7,8},{8,9},{9,10},{10,1... | collective-permute-start | bytes 294920 | tf_op jit(solution)/shard_map/ppermute | solution.py:20
  70.4 8.8 %collective-permute-start.7 = (f32[1,32,64]{2,1,0:T(8,128)S(1)}, f32[1,32,64]{2,1,0:T(8,128)S(1)}, u32[]{:S(2)}, u32[]{:S(2)}) collective-permute-start(f32[1,32,64]{2,1,0:T(8,128)S(1)} %get-tuple-element.16), channel_id=1, source_target_pairs={{0,64},{64,128},{128,192},{192,256},{256,320},{320,384},{384,448},... | collective-permute-start | bytes 24584 | tf_op jit(solution)/shard_map/ppermute | solution.py:32
  79.3 16.8 %collective-permute-start.8 = (f32[1,1,32,64]{3,2,1,0:T(8,128)S(1)}, f32[1,1,32,64]{3,2,1,0:T(8,128)S(1)}, u32[]{:S(2)}, u32[]{:S(2)}) collective-permute-start(f32[1,1,32,64]{3,2,1,0:T(8,128)S(1)} %fusion.232), channel_id=1, source_target_pairs={{1,0},{2,1},{3,2},{4,3},{5,4},{6,5},{7,6},{8,7},{9,8},{10,9},{11,1... | collective-permute-start | bytes 24584 | tf_op jit(solution)/shard_map/ppermute | solution.py:22
  94.2 3.1 collective-permute-start.9
  97.4 13.5 %collective-permute-start.10 = (f32[1,32,64]{2,1,0:T(8,128)S(1)}, f32[1,32,64]{2,1,0:T(8,128)S(1)}, u32[]{:S(2)}, u32[]{:S(2)}) collective-permute-start(f32[1,32,64]{2,1,0:T(8,128)S(1)} %fusion.55), channel_id=1, source_target_pairs={{0,64},{64,128},{128,192},{192,256},{256,320},{320,384},{384,448},... | collective-permute-start | bytes 24584 | tf_op jit(solution)/shard_map/ppermute | solution.py:32
  111.1 15.4 %collective-permute-start.11 = (f32[1,1,32,64]{3,2,1,0:T(8,128)S(1)}, f32[1,1,32,64]{3,2,1,0:T(8,128)S(1)}, u32[]{:S(2)}, u32[]{:S(2)}) collective-permute-start(f32[1,1,32,64]{3,2,1,0:T(8,128)S(1)} %fusion.233), channel_id=1, source_target_pairs={{1,0},{2,1},{3,2},{4,3},{5,4},{6,5},{7,6},{8,7},{9,8},{10,9},{11,1... | collective-permute-start | bytes 24584 | tf_op jit(solution)/shard_map/ppermute | solution.py:22
  124.5 3.1 collective-permute-start.12
  127.7 13.5 %collective-permute-start.13 = (f32[1,32,64]{2,1,0:T(8,128)S(1)}, f32[1,32,64]{2,1,0:T(8,128)S(1)}, u32[]{:S(2)}, u32[]{:S(2)}) collective-permute-start(f32[1,32,64]{2,1,0:T(8,128)S(1)} %fusion.61), channel_id=1, source_target_pairs={{0,64},{64,128},{128,192},{192,256},{256,320},{320,384},{384,448},... | collective-permute-start | bytes 24584 | tf_op jit(solution)/shard_map/ppermute | solution.py:32
  141.3 15.4 %collective-permute-start.14 = (f32[1,1,32,64]{3,2,1,0:T(8,128)S(1)}, f32[1,1,32,64]{3,2,1,0:T(8,128)S(1)}, u32[]{:S(2)}, u32[]{:S(2)}) collective-permute-start(f32[1,1,32,64]{3,2,1,0:T(8,128)S(1)} %fusion.234), channel_id=1, source_target_pairs={{1,0},{2,1},{3,2},{4,3},{5,4},{6,5},{7,6},{8,7},{9,8},{10,9},{11,1... | collective-permute-start | bytes 24584 | tf_op jit(solution)/shard_map/ppermute | solution.py:22
  154.8 3.1 collective-permute-start.15
  158.0 13.5 %collective-permute-start.16 = (f32[1,32,64]{2,1,0:T(8,128)S(1)}, f32[1,32,64]{2,1,0:T(8,128)S(1)}, u32[]{:S(2)}, u32[]{:S(2)}) collective-permute-start(f32[1,32,64]{2,1,0:T(8,128)S(1)} %fusion.67), channel_id=1, source_target_pairs={{0,64},{64,128},{128,192},{192,256},{256,320},{320,384},{384,448},... | collective-permute-start | bytes 24584 | tf_op jit(solution)/shard_map/ppermute | solution.py:32
  171.6 15.4 %collective-permute-start.17 = (f32[1,1,32,64]{3,2,1,0:T(8,128)S(1)}, f32[1,1,32,64]{3,2,1,0:T(8,128)S(1)}, u32[]{:S(2)}, u32[]{:S(2)}) collective-permute-start(f32[1,1,32,64]{3,2,1,0:T(8,128)S(1)} %fusion.235), channel_id=1, source_target_pairs={{1,0},{2,1},{3,2},{4,3},{5,4},{6,5},{7,6},{8,7},{9,8},{10,9},{11,1... | collective-permute-start | bytes 24584 | tf_op jit(solution)/shard_map/ppermute | solution.py:22
  188.3 13.5 %collective-permute-start.19 = (f32[1,32,64]{2,1,0:T(8,128)S(1)}, f32[1,32,64]{2,1,0:T(8,128)S(1)}, u32[]{:S(2)}, u32[]{:S(2)}) collective-permute-start(f32[1,32,64]{2,1,0:T(8,128)S(1)} %fusion.73), channel_id=1, source_target_pairs={{0,64},{64,128},{128,192},{192,256},{256,320},{320,384},{384,448},... | collective-permute-start | bytes 24584 | tf_op jit(solution)/shard_map/ppermute | solution.py:32
  201.9 15.4 %collective-permute-start.20 = (f32[1,1,32,64]{3,2,1,0:T(8,128)S(1)}, f32[1,1,32,64]{3,2,1,0:T(8,128)S(1)}, u32[]{:S(2)}, u32[]{:S(2)}) collective-permute-start(f32[1,1,32,64]{3,2,1,0:T(8,128)S(1)} %fusion.236), channel_id=1, source_target_pairs={{1,0},{2,1},{3,2},{4,3},{5,4},{6,5},{7,6},{8,7},{9,8},{10,9},{11,1... | collective-permute-start | bytes 24584 | tf_op jit(solution)/shard_map/ppermute | solution.py:22
  218.5 13.5 %collective-permute-start.22 = (f32[1,32,64]{2,1,0:T(8,128)S(1)}, f32[1,32,64]{2,1,0:T(8,128)S(1)}, u32[]{:S(2)}, u32[]{:S(2)}) collective-permute-start(f32[1,32,64]{2,1,0:T(8,128)S(1)} %fusion.79), channel_id=1, source_target_pairs={{0,64},{64,128},{128,192},{192,256},{256,320},{320,384},{384,448},... | collective-permute-start | bytes 24584 | tf_op jit(solution)/shard_map/ppermute | solution.py:32
  232.2 15.4 %collective-permute-start.23 = (f32[1,1,32,64]{3,2,1,0:T(8,128)S(1)}, f32[1,1,32,64]{3,2,1,0:T(8,128)S(1)}, u32[]{:S(2)}, u32[]{:S(2)}) collective-permute-start(f32[1,1,32,64]{3,2,1,0:T(8,128)S(1)} %fusion.237), channel_id=1, source_target_pairs={{1,0},{2,1},{3,2},{4,3},{5,4},{6,5},{7,6},{8,7},{9,8},{10,9},{11,1... | collective-permute-start | bytes 24584 | tf_op jit(solution)/shard_map/ppermute | solution.py:22
  248.8 27.7 %collective-permute-start.25 = (f32[1,32,64]{2,1,0:T(8,128)S(1)}, f32[1,32,64]{2,1,0:T(8,128)S(1)}, u32[]{:S(2)}, u32[]{:S(2)}) collective-permute-start(f32[1,32,64]{2,1,0:T(8,128)S(1)} %fusion.85), channel_id=1, source_target_pairs={{0,64},{64,128},{128,192},{192,256},{256,320},{320,384},{384,448},... | collective-permute-start | bytes 24584 | tf_op jit(solution)/shard_map/ppermute | solution.py:32
  261.5 57.2 %collective-permute-start = (f32[2,64,128]{2,1,0:T(8,128)S(1)}, f32[2,64,128]{2,1,0:T(8,128)S(1)}, u32[]{:S(2)}, u32[]{:S(2)}) collective-permute-start(f32[2,64,128]{2,1,0:T(8,128)S(1)} %bitcast.405), channel_id=1, source_target_pairs={{0,64},{64,128},{128,192},{192,256},{256,320},{320,384},{384,448},... | collective-permute-start | bytes 196616 | tf_op jit(solution)/shard_map/ppermute | solution.py:32
  276.7 15.5 %collective-permute-start.26 = (f32[1,1,32,64]{3,2,1,0:T(8,128)S(1)}, f32[1,1,32,64]{3,2,1,0:T(8,128)S(1)}, u32[]{:S(2)}, u32[]{:S(2)}) collective-permute-start(f32[1,1,32,64]{3,2,1,0:T(8,128)S(1)} %bitcast.420), channel_id=1, source_target_pairs={{1,0},{2,1},{3,2},{4,3},{5,4},{6,5},{7,6},{8,7},{9,8},{10,9},{11,1... | collective-permute-start | bytes 24584 | tf_op jit(solution)/shard_map/ppermute | solution.py:22
  302.3 14.6 %collective-permute-start.28 = (f32[3,1,64,128]{3,2,1,0:T(8,128)S(1)}, f32[3,1,64,128]{3,2,1,0:T(8,128)S(1)}, u32[]{:S(2)}, u32[]{:S(2)}) collective-permute-start(f32[3,1,64,128]{3,2,1,0:T(8,128)S(1)} %get-tuple-element.48), channel_id=1, source_target_pairs={{1,0},{2,1},{3,2},{4,3},{5,4},{6,5},{7,6},{8,7},{9,8},{10,9},{11,1... | collective-permute-start | bytes 294920 | tf_op jit(solution)/shard_map/ppermute | solution.py:22
  314.9 3.5 collective-permute-start.29
  345.0 31.4 %collective-permute-start.33 = (f32[3,1,32,64]{3,2,0,1:T(8,128)S(1)}, f32[3,1,32,64]{3,2,0,1:T(8,128)S(1)}, u32[]{:S(2)}, u32[]{:S(2)}) collective-permute-start(f32[3,1,32,64]{3,2,0,1:T(8,128)S(1)} %get-tuple-element.69), channel_id=1, source_target_pairs={{1,0},{2,1},{3,2},{4,3},{5,4},{6,5},{7,6},{8,7},{9,8},{10,9},{11,1... | collective-permute-start | bytes 73736 | tf_op jit(solution)/shard_map/ppermute | solution.py:22
  358.0 20.3 %collective-permute-start.34 = (f32[3,1,32,64]{3,2,0,1:T(8,128)S(1)}, f32[3,1,32,64]{3,2,0,1:T(8,128)S(1)}, u32[]{:S(2)}, u32[]{:S(2)}) collective-permute-start(f32[3,1,32,64]{3,2,0,1:T(8,128)S(1)} %get-tuple-element.69), channel_id=1, source_target_pairs={{0,1},{1,2},{2,3},{3,4},{4,5},{5,6},{6,7},{7,8},{8,9},{9,10},{10,1... | collective-permute-start | bytes 73736 | tf_op jit(solution)/shard_map/ppermute | solution.py:20
  360.1 32.1 %collective-permute-start.31 = (f32[1,1,32,64]{3,2,1,0:T(8,128)S(1)}, f32[1,1,32,64]{3,2,1,0:T(8,128)S(1)}, u32[]{:S(2)}, u32[]{:S(2)}) collective-permute-start(f32[1,1,32,64]{3,2,1,0:T(8,128)S(1)} %bitcast_select_fusion), channel_id=1, source_target_pairs={{1,0},{2,1},{3,2},{4,3},{5,4},{6,5},{7,6},{8,7},{9,8},{10,9},{11,1... | collective-permute-start | bytes 24584 | tf_op jit(solution)/shard_map/ppermute | solution.py:22
  362.5 29.7 %collective-permute-start.32 = (f32[1,1,32,64]{3,2,1,0:T(8,128)S(1)}, f32[1,1,32,64]{3,2,1,0:T(8,128)S(1)}, u32[]{:S(2)}, u32[]{:S(2)}) collective-permute-start(f32[1,1,32,64]{3,2,1,0:T(8,128)S(1)} %bitcast_select_fusion), channel_id=1, source_target_pairs={{0,1},{1,2},{2,3},{3,4},{4,5},{5,6},{6,7},{7,8},{8,9},{9,10},{10,1... | collective-permute-start | bytes 24584 | tf_op jit(solution)/shard_map/ppermute | solution.py:20
  365.7 12.7 %collective-permute-start.35 = (f32[3,1,64,128]{3,2,1,0:T(8,128)S(1)}, f32[3,1,64,128]{3,2,1,0:T(8,128)S(1)}, u32[]{:S(2)}, u32[]{:S(2)}) collective-permute-start(f32[3,1,64,128]{3,2,1,0:T(8,128)S(1)} %get-tuple-element.38), channel_id=1, source_target_pairs={{1,0},{2,1},{3,2},{4,3},{5,4},{6,5},{7,6},{8,7},{9,8},{10,9},{11,1... | collective-permute-start | bytes 294920 | tf_op jit(solution)/shard_map/ppermute | solution.py:22
  376.3 13.1 %collective-permute-start.36 = (f32[3,1,64,128]{3,2,1,0:T(8,128)S(1)}, f32[3,1,64,128]{3,2,1,0:T(8,128)S(1)}, u32[]{:S(2)}, u32[]{:S(2)}) collective-permute-start(f32[3,1,64,128]{3,2,1,0:T(8,128)S(1)} %get-tuple-element.39), channel_id=1, source_target_pairs={{0,1},{1,2},{2,3},{3,4},{4,5},{5,6},{6,7},{7,8},{8,9},{9,10},{10,1... | collective-permute-start | bytes 294920 | tf_op jit(solution)/shard_map/ppermute | solution.py:20
  395.5 16.8 %collective-permute-start.38 = (f32[1,1,32,64]{3,2,1,0:T(8,128)S(1)}, f32[1,1,32,64]{3,2,1,0:T(8,128)S(1)}, u32[]{:S(2)}, u32[]{:S(2)}) collective-permute-start(f32[1,1,32,64]{3,2,1,0:T(8,128)S(1)} %fusion.238), channel_id=1, source_target_pairs={{1,0},{2,1},{3,2},{4,3},{5,4},{6,5},{7,6},{8,7},{9,8},{10,9},{11,1... | collective-permute-start | bytes 24584 | tf_op jit(solution)/shard_map/ppermute | solution.py:22
  413.5 13.5 %collective-permute-start.40 = (f32[1,32,64]{2,1,0:T(8,128)S(1)}, f32[1,32,64]{2,1,0:T(8,128)S(1)}, u32[]{:S(2)}, u32[]{:S(2)}) collective-permute-start(f32[1,32,64]{2,1,0:T(8,128)S(1)} %fusion.99), channel_id=1, source_target_pairs={{0,64},{64,128},{128,192},{192,256},{256,320},{320,384},{384,448},... | collective-permute-start | bytes 24584 | tf_op jit(solution)/shard_map/ppermute | solution.py:32
  427.1 15.4 %collective-permute-start.41 = (f32[1,1,32,64]{3,2,1,0:T(8,128)S(1)}, f32[1,1,32,64]{3,2,1,0:T(8,128)S(1)}, u32[]{:S(2)}, u32[]{:S(2)}) collective-permute-start(f32[1,1,32,64]{3,2,1,0:T(8,128)S(1)} %fusion.239), channel_id=1, source_target_pairs={{1,0},{2,1},{3,2},{4,3},{5,4},{6,5},{7,6},{8,7},{9,8},{10,9},{11,1... | collective-permute-start | bytes 24584 | tf_op jit(solution)/shard_map/ppermute | solution.py:22
  443.8 14.1 %collective-permute-start.43 = (f32[1,32,64]{2,1,0:T(8,128)S(1)}, f32[1,32,64]{2,1,0:T(8,128)S(1)}, u32[]{:S(2)}, u32[]{:S(2)}) collective-permute-start(f32[1,32,64]{2,1,0:T(8,128)S(1)} %fusion.105), channel_id=1, source_target_pairs={{0,64},{64,128},{128,192},{192,256},{256,320},{320,384},{384,448},... | collective-permute-start | bytes 24584 | tf_op jit(solution)/shard_map/ppermute | solution.py:32
  458.0 15.5 %collective-permute-start.44 = (f32[1,1,32,64]{3,2,1,0:T(8,128)S(1)}, f32[1,1,32,64]{3,2,1,0:T(8,128)S(1)}, u32[]{:S(2)}, u32[]{:S(2)}) collective-permute-start(f32[1,1,32,64]{3,2,1,0:T(8,128)S(1)} %fusion.240), channel_id=1, source_target_pairs={{1,0},{2,1},{3,2},{4,3},{5,4},{6,5},{7,6},{8,7},{9,8},{10,9},{11,1... | collective-permute-start | bytes 24584 | tf_op jit(solution)/shard_map/ppermute | solution.py:22
  474.7 14.4 %collective-permute-start.46 = (f32[1,32,64]{2,1,0:T(8,128)S(1)}, f32[1,32,64]{2,1,0:T(8,128)S(1)}, u32[]{:S(2)}, u32[]{:S(2)}) collective-permute-start(f32[1,32,64]{2,1,0:T(8,128)S(1)} %fusion.111), channel_id=1, source_target_pairs={{0,64},{64,128},{128,192},{192,256},{256,320},{320,384},{384,448},... | collective-permute-start | bytes 24584 | tf_op jit(solution)/shard_map/ppermute | solution.py:32
  489.2 15.4 %collective-permute-start.47 = (f32[1,1,32,64]{3,2,1,0:T(8,128)S(1)}, f32[1,1,32,64]{3,2,1,0:T(8,128)S(1)}, u32[]{:S(2)}, u32[]{:S(2)}) collective-permute-start(f32[1,1,32,64]{3,2,1,0:T(8,128)S(1)} %fusion.241), channel_id=1, source_target_pairs={{1,0},{2,1},{3,2},{4,3},{5,4},{6,5},{7,6},{8,7},{9,8},{10,9},{11,1... | collective-permute-start | bytes 24584 | tf_op jit(solution)/shard_map/ppermute | solution.py:22
  505.9 14.5 %collective-permute-start.49 = (f32[1,32,64]{2,1,0:T(8,128)S(1)}, f32[1,32,64]{2,1,0:T(8,128)S(1)}, u32[]{:S(2)}, u32[]{:S(2)}) collective-permute-start(f32[1,32,64]{2,1,0:T(8,128)S(1)} %fusion.117), channel_id=1, source_target_pairs={{0,64},{64,128},{128,192},{192,256},{256,320},{320,384},{384,448},... | collective-permute-start | bytes 24584 | tf_op jit(solution)/shard_map/ppermute | solution.py:32
  520.5 15.6 %collective-permute-start.50 = (f32[1,1,32,64]{3,2,1,0:T(8,128)S(1)}, f32[1,1,32,64]{3,2,1,0:T(8,128)S(1)}, u32[]{:S(2)}, u32[]{:S(2)}) collective-permute-start(f32[1,1,32,64]{3,2,1,0:T(8,128)S(1)} %fusion.242), channel_id=1, source_target_pairs={{1,0},{2,1},{3,2},{4,3},{5,4},{6,5},{7,6},{8,7},{9,8},{10,9},{11,1... | collective-permute-start | bytes 24584 | tf_op jit(solution)/shard_map/ppermute | solution.py:22
  537.3 14.2 %collective-permute-start.52 = (f32[1,32,64]{2,1,0:T(8,128)S(1)}, f32[1,32,64]{2,1,0:T(8,128)S(1)}, u32[]{:S(2)}, u32[]{:S(2)}) collective-permute-start(f32[1,32,64]{2,1,0:T(8,128)S(1)} %fusion.123), channel_id=1, source_target_pairs={{0,64},{64,128},{128,192},{192,256},{256,320},{320,384},{384,448},... | collective-permute-start | bytes 24584 | tf_op jit(solution)/shard_map/ppermute | solution.py:32
  551.7 15.4 %collective-permute-start.53 = (f32[1,1,32,64]{3,2,1,0:T(8,128)S(1)}, f32[1,1,32,64]{3,2,1,0:T(8,128)S(1)}, u32[]{:S(2)}, u32[]{:S(2)}) collective-permute-start(f32[1,1,32,64]{3,2,1,0:T(8,128)S(1)} %fusion.243), channel_id=1, source_target_pairs={{1,0},{2,1},{3,2},{4,3},{5,4},{6,5},{7,6},{8,7},{9,8},{10,9},{11,1... | collective-permute-start | bytes 24584 | tf_op jit(solution)/shard_map/ppermute | solution.py:22
  568.3 29.8 %collective-permute-start.55 = (f32[1,32,64]{2,1,0:T(8,128)S(1)}, f32[1,32,64]{2,1,0:T(8,128)S(1)}, u32[]{:S(2)}, u32[]{:S(2)}) collective-permute-start(f32[1,32,64]{2,1,0:T(8,128)S(1)} %fusion.129), channel_id=1, source_target_pairs={{0,64},{64,128},{128,192},{192,256},{256,320},{320,384},{384,448},... | collective-permute-start | bytes 24584 | tf_op jit(solution)/shard_map/ppermute | solution.py:32
  581.8 58.3 %collective-permute-start.30 = (f32[2,64,128]{2,1,0:T(8,128)S(1)}, f32[2,64,128]{2,1,0:T(8,128)S(1)}, u32[]{:S(2)}, u32[]{:S(2)}) collective-permute-start(f32[2,64,128]{2,1,0:T(8,128)S(1)} %bitcast_add_fusion.3), channel_id=1, source_target_pairs={{0,64},{64,128},{128,192},{192,256},{256,320},{320,384},{384,448},... | collective-permute-start | bytes 196616 | tf_op jit(solution)/shard_map/ppermute | solution.py:32
  598.2 15.1 %collective-permute-start.56 = (f32[1,1,32,64]{3,2,1,0:T(8,128)S(1)}, f32[1,1,32,64]{3,2,1,0:T(8,128)S(1)}, u32[]{:S(2)}, u32[]{:S(2)}) collective-permute-start(f32[1,1,32,64]{3,2,1,0:T(8,128)S(1)} %bitcast.414), channel_id=1, source_target_pairs={{1,0},{2,1},{3,2},{4,3},{5,4},{6,5},{7,6},{8,7},{9,8},{10,9},{11,1... | collective-permute-start | bytes 24584 | tf_op jit(solution)/shard_map/ppermute | solution.py:22
  623.7 14.6 %collective-permute-start.58 = (f32[3,1,64,128]{3,2,1,0:T(8,128)S(1)}, f32[3,1,64,128]{3,2,1,0:T(8,128)S(1)}, u32[]{:S(2)}, u32[]{:S(2)}) collective-permute-start(f32[3,1,64,128]{3,2,1,0:T(8,128)S(1)} %get-tuple-element.28), channel_id=1, source_target_pairs={{1,0},{2,1},{3,2},{4,3},{5,4},{6,5},{7,6},{8,7},{9,8},{10,9},{11,1... | collective-permute-start | bytes 294920 | tf_op jit(solution)/shard_map/ppermute | solution.py:22
  636.4 3.5 collective-permute-start.59
  (19 other events, 176.9 us)
where the time goes:
time: 653 us; the launch traced here: 641 us
  starting transfers between devices  509 us (78%)
  local copies, waits for them, and re-layouts  72.1 us (11%)
  waiting for transfers between devices  50.4 us (8%)
  other arithmetic  7.23 us (1%)
    ppermute x22, starting transfers between devices, padded_2(): lax.ppermute(head, axis, [((i + 1) % count, i) for i in range(count)])  273 us
    ppermute x16, starting transfers between devices, from_behind(): return lax.ppermute(value, axis, pairs)  192 us
    ppermute x22, starting transfers between devices, padded_2(): lax.ppermute(tail, axis, [(i, (i + 1) % count) for i in range(count)])  43.7 us
    ppermute x22, waiting for transfers between devices, padded_2(): lax.ppermute(tail, axis, [(i, (i + 1) % count) for i in range(count)])  40.1 us
    another operation x6, local copies, waits for them, and re-layouts, on_device(): jnp.stack([start_fine, start_fine + integral(fine_rates, 1), start_fine +...  25.6 us
    broadcast_in_dim x4, local copies, waits for them, and re-layouts, prolong(): jnp.broadcast_to(field[..., :, None, :, None, :, None], leading + (extent...  17.4 us
  transfers between devices with their start and end apart: 60, of which 30 were waited for; matrix products, arithmetic and copies ran while one was open for 6% of the time, Pallas kernels for 0%

commit v1 on v0

v1 whole, which is shorter than its diff:
```python
import jax
import jax.numpy as jnp
from jax import lax
from jax.experimental import pallas as pl
from jax.experimental.pallas import tpu as pltpu
from jax.sharding import Mesh, PartitionSpec as P

STEP = 0.06
QUAD = ((0.0, 0.0, 0.0), (5.0 / 24.0, 1.0 / 3.0, -1.0 / 24.0), (1.0 / 6.0, 2.0 / 3.0, 1.0 / 6.0))
ROWSUM = tuple(sum(row) for row in QUAD)
START = tuple(STEP * (row[1] * QUAD[1][0] + row[2] * QUAD[2][0]) for row in QUAD)
SECTIONS = 8
BLOCK = 8
F32 = jnp.float32

COEF, NEAR1, NEAR2 = 10, 11, 12
ITEMS = (
    ((0, 8), (1, 7), (COEF, 7), (2, 6), (3, 5), (4, 4), (5, 3), (6, 2), (NEAR1, 1), (NEAR2, 1)),
    ((0, 8), (1, 7), (2, 6), (3, 5), (4, 4), (5, 3), (6, 2), (NEAR1, 1), (NEAR2, 1)),
)


def count(items, distance):
    return sum(1 for _, reach in items if reach >= distance)


def slots(items):
    return max(count(items, d) + count(items, BLOCK - d) for d in range(1, BLOCK))


def turn(x, by, axis):
    return pltpu.roll(x, by % x.shape[axis], axis)


def around(x):
    return turn(x, 1, 0) + turn(x, -1, 0) + turn(x, 1, 1) + turn(x, -1, 1)


def cubic(u):
    return u - u * u * u


def dot(a, b):
    return jnp.dot(a, b, precision=lax.Precision.HIGHEST, preferred_element_type=F32)


def pair_lanes():
    z = lax.broadcasted_iota(jnp.int32, (128, 128), 0)
    c = lax.broadcasted_iota(jnp.int32, (128, 128), 1)
    return jnp.where((z >> 1) == (c & 63), 1.0, 0.0).astype(F32)


def spread_lanes():
    c = lax.broadcasted_iota(jnp.int32, (128, 128), 0)
    z = lax.broadcasted_iota(jnp.int32, (128, 128), 1)
    return jnp.where((z >> 1) == c, 1.0, 0.0).astype(F32)


def squash(planes, scratch):
    for i, plane in enumerate(planes):
        scratch[64 * i : 64 * i + 64, :] = plane
    both = scratch[pl.ds(0, 32 * len(planes), 2), :] + scratch[pl.ds(1, 32 * len(planes), 2), :]
    sums = dot(both, pair_lanes())
    return [sums[32 * i : 32 * i + 32] for i in range(len(planes))]


def spread(planes, scratch):
    wide = dot(jnp.concatenate(planes, axis=0), spread_lanes())
    scratch[pl.ds(0, 32 * len(planes), 2), :] = wide
    scratch[pl.ds(1, 32 * len(planes), 2), :] = wide
    return [scratch[64 * i : 64 * i + 64, :] for i in range(len(planes))]


def left(shape):
    return lax.broadcasted_iota(jnp.int32, shape, 1) < 64


def pack(x):
    return jnp.where(left((16, 128)), x[:16], x[16:])


def unpack(t):
    other = turn(t, 64, 1)
    here = left((16, 128))
    return jnp.concatenate([jnp.where(here, t, other), jnp.where(here, other, t)], axis=0)


def coarse_slope(below, centre, above, coef):
    return 0.25 * (around(centre) + below + above - 6.0 * centre) + coef * cubic(centre)


def mix(row, nodes):
    return QUAD[row][0] * nodes[0] + QUAD[row][1] * nodes[1] + QUAD[row][2] * nodes[2]


def own_part(sums, rates, scratch):
    planes = []
    for m in (0, 1):
        total = None
        for x in (0, 1):
            part = around(sums[m][x]) - 6.0 * sums[m][x] + sums[m][1 - x] + rates[m][x]
            total = part if total is None else total + part
        planes.append(total)
    return squash(planes, scratch)


def first_kernel(initial, coeff, guess, up, down, keep, scratch):
    u = [guess[0], guess[1]]
    c = [coeff[0], coeff[1]]
    rate = [c[x] * cubic(u[x]) for x in (0, 1)]
    total = None
    for x in (0, 1):
        part = around(u[x]) - 6.0 * u[x] + u[1 - x] + rate[x]
        total = part if total is None else total + part
    own, value, coef, start = squash([total, u[0] + u[1], c[0] + c[1], initial[0] + initial[1]], scratch)
    value, coef, start = 0.125 * value, 0.125 * coef, 0.125 * start
    for out, plane in ((up, u[1]), (down, u[0])):
        out[0:64, :] = plane
        out[64:80, :] = pack(value)
        out[80:96, :] = pack(start)
    keep[0] = own
    keep[1] = value
    keep[2] = coef
    keep[3] = start


def hand_over(spot, own, values, value0, value0_sides, coef, start, start_slope, out, gathered):
    slope = coarse_slope(value0_sides[0], value0, value0_sides[1], coef)
    k = [(STEP / 8.0) * own[m] - (STEP * QUAD[m + 1][0]) * slope for m in (0, 1)]
    first = (jnp.full((32, 128), spot[0], jnp.int32) == 0)
    out[0:16, :] = pack(k[1] + jnp.where(first, start + STEP * QUAD[2][0] * start_slope, 0.0))
    for m in (0, 1):
        near = QUAD[m + 1][1] * k[0] + QUAD[m + 1][2] * k[1] - values[m]
        near = near + jnp.where(first, ROWSUM[m + 1] * start + START[m + 1] * start_slope, 0.0)
        out[16 * (m + 1) : 16 * (m + 2), :] = pack(near)
    gathered[0] = k[0]
    gathered[1] = k[1]


def complete_first(spot, below, above, kept, out, keep, scratch):
    own, value, coef, start = (kept[i] for i in range(4))
    low, high = squash([below[0:64, :], above[0:64, :]], scratch)
    whole = own + low + high
    sides = [unpack(below[64:80, :]), unpack(above[64:80, :])]
    start_sides = [unpack(below[80:96, :]), unpack(above[80:96, :])]
    start_slope = coarse_slope(start_sides[0], start, start_sides[1], coef)
    hand_over(
        spot, [ROWSUM[1] * whole, ROWSUM[2] * whole], [ROWSUM[1] * value, ROWSUM[2] * value],
        value, sides, coef, start, start_slope, out, keep,
    )
    out[48:64, :] = pack(coef)
    keep[2] = start
    keep[3] = start_slope
    keep[4] = start_sides[0]
    keep[5] = start_sides[1]


def complete_second(spot, below, above, kept, started, kept_first, out, keep, scratch):
    low1, low2, high1, high2 = squash(
        [below[0:64, :], below[64:128, :], above[0:64, :], above[64:128, :]], scratch
    )
    own = [kept[0] + low1 + high1, kept[1] + low2 + high2]
    values = [mix(m, [kept[2], kept[3], kept[4]]) for m in (1, 2)]
    sides = [unpack(below[128:144, :]), unpack(above[128:144, :])]
    hand_over(spot, own, values, kept[2], sides, kept_first[2], started[2], started[3], out, keep)


def pack_kernel(items):
    total = slots(items)

    def body(spot, owned, behind, ahead, sections, out):
        place = spot[1]

        def plane(side, item):
            if item < SECTIONS:
                return sections[item, 16 * side : 16 * side + 16, :]
            row = {NEAR1: 16, NEAR2: 32, COEF: 48}[item]
            return (owned, behind, ahead)[side][row : row + 16, :]

        def fill(to, distance, side):
            slot = 0
            for origin, least in ((0, distance), (side, BLOCK - distance)):
                for item, reach in items:
                    if reach >= least:
                        out[to, 16 * slot : 16 * slot + 16, :] = plane(origin, item)
                        slot += 1

        for d in range(1, BLOCK):

            @pl.when(place + d < BLOCK)
            def _():
                fill(place + d, d, 2)

            @pl.when(place + d >= BLOCK)
            def _():
                fill(place + d - BLOCK, BLOCK - d, 1)

    return body, total


def sweep(spot, items, owned, behind, ahead, sections, windows, coefs, started, line, history):
    place = spot[1]
    rank = {item: i for i, (item, _) in enumerate(items)}
    reach_of = dict(items)

    def fetch(item, w):
        if w in (0, -BLOCK, BLOCK):
            side = {0: 0, -BLOCK: 1, BLOCK: 2}[w]
            if item < SECTIONS:
                return unpack(sections[item, 16 * side : 16 * side + 16, :])
            row = {NEAR1: 16, NEAR2: 32, COEF: 48}[item]
            return unpack((owned, behind, ahead)[side][row : row + 16, :])
        at = place + w
        outside = jnp.logical_or(at < 0, at >= BLOCK)
        slot = rank[item] + jnp.where(outside, count(items, BLOCK - abs(w)), 0)
        return unpack(windows[at & (BLOCK - 1), pl.ds(pl.multiple_of(16 * slot, 16), 16), :])

    if COEF in rank:
        for w in range(-7, 8):
            coefs[w + 7] = fetch(COEF, w)
    history[0] = jnp.zeros((32, 128), F32)
    history[1] = started[4]
    history[2] = started[2]
    history[3] = started[5]
    history[4] = jnp.zeros((32, 128), F32)
    for w in range(-8, 9):
        value = fetch(0, w)
        line[0, w + 8] = value
        if abs(w) <= 2:
            history[5 + w + 2] = value
    for k in range(1, SECTIONS - 1):
        old, new = (k - 1) % 2, k % 2
        for w in range(-reach_of[k], reach_of[k] + 1):
            centre = line[old, w + 8]
            slope = coarse_slope(line[old, w + 7], centre, line[old, w + 9], coefs[w + 7])
            value = centre + (STEP * QUAD[2][0]) * slope + fetch(k, w)
            line[new, w + 8] = value
            if abs(w) <= 2:
                history[5 * (k + 1) + w + 2] = value
    return fetch


def correct(spot, fetch, coefs, started, history, kept, values, nodes, below, above, coeff, begin, scratch):
    section = spot[0]
    s = [history[5 * section + i] for i in range(5)]
    slope = [coarse_slope(s[i], s[i + 1], s[i + 2], coefs[6 + i]) for i in range(3)]
    later = jnp.full((32, 128), section, jnp.int32) > 0
    edges = []
    for w, i in ((-1, 0), (1, 2)):
        for m, near in ((1, NEAR1), (2, NEAR2)):
            edges.append(fetch(near, w) + jnp.where(later, ROWSUM[m] * s[i + 1] + START[m] * slope[i], 0.0))
    coarse = [s[2]] + [s[2] + (STEP * QUAD[m][0]) * slope[1] + kept[m - 1] for m in (1, 2)]
    wide = spread([coarse[j] - values[j] for j in range(3)] + edges, scratch)
    fixed = [[nodes[j][x] + wide[j] for x in (0, 1)] for j in range(3)]
    rates = [[cubic(fixed[j][x]) for x in (0, 1)] for j in range(3)]
    fresh = []
    for m in (1, 2):
        sums = [mix(m, [fixed[j][x] for j in range(3)]) for x in (0, 1)]
        ends = [below[m - 1] + wide[2 + m], above[m - 1] + wide[4 + m]]
        fresh.append([])
        for x in (0, 1):
            change = around(sums[x]) - 6.0 * sums[x] + sums[1 - x] + ends[x]
            change = change + coeff[x] * mix(m, [rates[j][x] for j in range(3)])
            fresh[-1].append(begin[x] + STEP * change)
    return coarse[2], fresh


def starting(spot, initial, received):
    first = jnp.full((64, 128), spot[0], jnp.int32) == 0
    return [jnp.where(first, initial[x], received[x]) for x in (0, 1)]


def finish_first(
    spot, owned, behind, ahead, sections, windows, started, kept, below, above, initial, coeff, guess, received,
    fresh_out, begin_out, up, down, keep, coefs, line, history, scratch,
):
    fetch = sweep(spot, ITEMS[0], owned, behind, ahead, sections, windows, coefs, started, line, history)
    begin = starting(spot, initial, received)
    u = [guess[0], guess[1]]
    c = [coeff[0], coeff[1]]
    low = [ROWSUM[m] * below[0:64, :] for m in (1, 2)]
    high = [ROWSUM[m] * above[0:64, :] for m in (1, 2)]
    value = kept[1]
    _, fresh = correct(
        spot, fetch, coefs, started, history, (started[0], started[1]), [value] * 3, [u] * 3, low, high, c, begin, scratch
    )
    nodes = [begin] + fresh
    rates = [[cubic(nodes[j][x]) for x in (0, 1)] for j in range(3)]
    planes = []
    for m in (1, 2):
        sums = [mix(m, [nodes[j][x] for j in range(3)]) for x in (0, 1)]
        down[64 * (m - 1) : 64 * m, :] = sums[0]
        up[64 * (m - 1) : 64 * m, :] = sums[1]
        both = sums[0] + sums[1]
        part = around(both) - 5.0 * both
        for x in (0, 1):
            part = part + c[x] * mix(m, [rates[j][x] for j in range(3)])
        planes.append(part)
    for j in range(3):
        planes.append(nodes[j][0] + nodes[j][1])
    for x in (0, 1):
        begin_out[x] = begin[x]
        for m in (0, 1):
            fresh_out[m, x] = fresh[m][x]
    small = squash(planes, scratch)
    keep[0] = small[0]
    keep[1] = small[1]
    for j in range(3):
        keep[2 + j] = 0.125 * small[2 + j]
    up[128:144, :] = pack(keep[2])
    down[128:144, :] = pack(keep[2])


def finish_second(
    spot, owned, behind, ahead, sections, windows, started, kept, kept_k, below, above, initial, coeff, begin_in, fresh_in,
    received, coefs, fresh_out, coarse_out, line, history, scratch,
):
    fetch = sweep(spot, ITEMS[1], owned, behind, ahead, sections, windows, coefs, started, line, history)
    begin = starting(spot, initial, received)
    nodes = [[begin_in[0], begin_in[1]]] + [[fresh_in[m, 0], fresh_in[m, 1]] for m in (0, 1)]
    low = [below[64 * m : 64 * m + 64, :] for m in (0, 1)]
    high = [above[64 * m : 64 * m + 64, :] for m in (0, 1)]
    end, fresh = correct(
        spot, fetch, coefs, started, history, (kept_k[0], kept_k[1]), [kept[2], kept[3], kept[4]], nodes, low, high,
        [coeff[0], coeff[1]], begin, scratch,
    )
    for m in (0, 1):
        for x in (0, 1):
            fresh_out[m, x] = fresh[m][x]
    coarse_out[...] = end[:, :64]


def run(body, args, outs, scratch=(), name=None):
    scalars = args[0].dtype == jnp.int32
    specs = [pl.BlockSpec(memory_space=pltpu.SMEM)] if scalars else []
    specs += [pl.BlockSpec(memory_space=pltpu.VMEM)] * (len(args) - len(specs))
    return pl.pallas_call(
        body,
        out_shape=[jax.ShapeDtypeStruct(shape, F32) for shape in outs],
        in_specs=specs,
        out_specs=[pl.BlockSpec(memory_space=pltpu.VMEM)] * len(outs),
        scratch_shapes=[pltpu.VMEM(shape, F32) for shape in scratch],
        name=name,
    )(*args)


class Links:
    call = staticmethod(run)

    @staticmethod
    def spot():
        return jnp.stack([lax.axis_index("tm"), lax.axis_index("place")]).astype(jnp.int32)

    @staticmethod
    def shift(x, by):
        n = lax.axis_size("block") * lax.axis_size("place")
        return lax.ppermute(x, ("block", "place"), [(i, (i + by) % n) for i in range(n)])

    @staticmethod
    def onward(x):
        n = lax.axis_size("tm")
        return lax.ppermute(x, "tm", [(i, i + 1) for i in range(n - 1)])

    @staticmethod
    def sections(x):
        return lax.all_to_all(jnp.broadcast_to(x, (SECTIONS,) + x.shape), "tm", 0, 0)

    @staticmethod
    def block(x):
        return lax.all_to_all(x, "place", 0, 0)

    @staticmethod
    def stack(*planes):
        return jnp.concatenate([p[:16] for p in planes], axis=0)


def iterate(links, initial, coeff, guess):
    spot = links.spot()
    coarse = (32, 128)
    work = [(2, 17) + coarse, (40,) + coarse]

    up, down, kept = links.call(
        first_kernel, (initial, coeff, guess), [(96, 128), (96, 128), (4,) + coarse], [(256, 128)], name="first"
    )
    below, above = links.shift(up, 1), links.shift(down, -1)
    received = links.onward(guess)
    owned, started = links.call(
        complete_first, (spot, below, above, kept), [(64, 128), (6,) + coarse], [(128, 128)], name="complete_first"
    )

    def windows(owned, items):
        behind, ahead = links.shift(owned, BLOCK), links.shift(owned, -BLOCK)
        sections = links.sections(links.stack(owned, behind, ahead))
        body, total = pack_kernel(items)
        (packets,) = links.call(
            body, (spot, owned, behind, ahead, sections), [(BLOCK, 16 * total, 128)], name="hand_out"
        )
        return behind, ahead, sections, links.block(packets)

    behind, ahead, sections, around_us = windows(owned, ITEMS[0])
    fresh, begin, up, down, kept2, coefs = links.call(
        finish_first,
        (spot, owned, behind, ahead, sections, around_us, started, kept, below, above, initial, coeff, guess, received),
        [(2, 2, 64, 128), (2, 64, 128), (144, 128), (144, 128), (5,) + coarse, (15,) + coarse],
        work + [(448, 128)],
        name="finish_first",
    )
    below, above = links.shift(up, 1), links.shift(down, -1)
    received = links.onward(fresh[1])
    owned, kept_k = links.call(
        complete_second, (spot, below, above, kept2, started, kept), [(48, 128), (2,) + coarse], [(256, 128)],
        name="complete_second",
    )
    behind, ahead, sections, around_us = windows(owned, ITEMS[1])
    fine, coarse_end = links.call(
        finish_second,
        (spot, owned, behind, ahead, sections, around_us, started, kept2, kept_k, below, above, initial, coeff, begin, fresh,
         received, coefs),
        [(2, 2, 64, 128), (32, 64)],
        work + [(448, 128)],
        name="finish_second",
    )
    return fine, coarse_end


def on_device(initial, coeff, guess):
    fine, coarse_end = iterate(Links, initial, coeff, guess[0])
    return fine[None], coarse_end[None, None]


def solution(mesh):
    split = Mesh(
        mesh.devices.reshape(mesh.shape["tm"], mesh.shape["space"] // BLOCK, BLOCK), ("tm", "block", "place")
    )
    space = ("block", "place")
    return jax.shard_map(
        on_device,
        mesh=split,
        in_specs=(P(space, None, None), P(space, None, None), P("tm", space, None, None)),
        out_specs=(P("tm", None, space, None, None), P("tm", space, None, None)),
        check_vma=False,
    )
```

time: 653 us -> 205 us (0.31); the launches traced: 641 us -> 204 us
  starting transfers between devices: 509 us -> 82.5 us
  local copies, waits for them, and re-layouts: 72.1 us -> 5.7 us
  blocking collectives: 0 us -> 44.8 us
  Pallas kernels: 0 us -> 17 us
  other arithmetic: 7.23 us -> 0.6 us
    ppermute x60 -> x10, starting transfers between devices: 509 us -> 46.5 us  [the longest x8 38.6 us: shift(): lax.ppermute(x, ('block', 'place'), [(i, (i + by) % n) for i in range(n)])]
    all_to_all x0 -> x2, blocking collectives: none -> 44.8 us  [sections(): lax.all_to_all(jnp.broadcast_to(x, (SECTIONS,) + x.shape), 'tm', 0, 0)]
    another operation x19 -> x0, local copies, waits for them, and re-layouts: 36.5 us -> none  [the longest x6 25.6 us: on_device(): jnp.stack([start_fine, start_fine + integral(fine_rates, 1), start_fine +...]
    all_to_all x0 -> x2, starting transfers between devices: none -> 36 us  [block(): return lax.all_to_all(x, 'place', 0, 0)]
    broadcast_in_dim x4 -> x2, local copies, waits for them, and re-layouts: 17.4 us -> 0.03 us  [sections(): jnp.broadcast_to(x, (SECTIONS,) + x.shape)]
    pallas_call x0 -> x7, Pallas kernels: none -> 17 us  [run(): pl.pallas_call(body, out_shape=[jax.ShapeDtypeStruct(shape, F32) for shap...]
    all_to_all x0 -> x2, waiting for transfers between devices: none -> 13.9 us  [block(): return lax.all_to_all(x, 'place', 0, 0)]
    reduce_sum x6 -> x0, local copies, waits for them, and re-layouts: 12.5 us -> none  [restrict(): return blocks.mean(axis=(-5, -3, -1))]
  transfers between devices with their start and end apart: 60 -> 12, of which waited for: 30 -> 8; matrix products, arithmetic and copies ran while one was open for 6% -> 1% of each run, Pallas kernels for 0% -> 0%
where the time goes in v1:
time: 205 us; the launch traced here: 204 us
  starting transfers between devices  82.5 us (40%)
  waiting for transfers between devices  52.4 us (26%)
  blocking collectives  44.8 us (22%)
  Pallas kernels  17 us (8%)
  local copies, waits for them, and re-layouts  5.7 us (3%)
    all_to_all x2, blocking collectives, sections(): lax.all_to_all(jnp.broadcast_to(x, (SECTIONS,) + x.shape), 'tm', 0, 0)  44.8 us
    ppermute x8, starting transfers between devices, shift(): lax.ppermute(x, ('block', 'place'), [(i, (i + by) % n) for i in range(n)])  38.6 us
    all_to_all x2, starting transfers between devices, block(): return lax.all_to_all(x, 'place', 0, 0)  36 us
    ppermute x2, waiting for transfers between devices, onward(): return lax.ppermute(x, 'tm', [(i, i + 1) for i in range(n - 1)])  29.6 us
    pallas_call x7, Pallas kernels, run(): pl.pallas_call(body, out_shape=[jax.ShapeDtypeStruct(shape, F32) for shap...  17 us
    all_to_all x2, waiting for transfers between devices, block(): return lax.all_to_all(x, 'place', 0, 0)  13.9 us
    ppermute x8, waiting for transfers between devices, shift(): lax.ppermute(x, ('block', 'place'), [(i, (i + by) % n) for i in range(n)])  8.8 us
    ppermute x2, starting transfers between devices, onward(): return lax.ppermute(x, 'tm', [(i, i + 1) for i in range(n - 1)])  7.85 us
  transfers between devices with their start and end apart: 12, of which 8 were waited for; matrix products, arithmetic and copies ran while one was open for 1% of the time, Pallas kernels for 0%

profile of v1, /device:TPU:1, one launch (start us, length us, event | category | flops | bytes accessed | tf_op | source)
XLA Modules:
  0.0 203.7 jit_solution(14378413514624756853)
XLA Ops:
  0.6 1.9 first.1
  2.5 4.9 %collective-permute-start = (f32[96,128]{1,0:T(8,128)}, f32[96,128]{1,0:T(8,128)S(1)}, u32[]{:S(2)}, u32[]{:S(2)}) collective-permute-start(f32[96,128]{1,0:T(8,128)} %get-tuple-element.17), channel_id=1, source_target_pairs={{0,1},{1,2},{2,3},{3,4},{4,5},{5,6},{6,7},{7,8},{8,9},{9,10},{10,1... | collective-permute-start | bytes 147464 | tf_op jit(solution)/shard_map/ppermute | solution.py:357
  7.4 5.8 %collective-permute-start.1 = (f32[96,128]{1,0:T(8,128)}, f32[96,128]{1,0:T(8,128)S(1)}, u32[]{:S(2)}, u32[]{:S(2)}) collective-permute-start(f32[96,128]{1,0:T(8,128)} %get-tuple-element.18), channel_id=1, source_target_pairs={{0,63},{1,0},{2,1},{3,2},{4,3},{5,4},{6,5},{7,6},{8,7},{9,8},{10,9... | collective-permute-start | bytes 147464 | tf_op jit(solution)/shard_map/ppermute | solution.py:357
  13.2 0.6 pad_add_fusion.spot
  13.8 0.0 collective-permute-done.below
  13.8 0.5 collective-permute-done.1.above
  14.3 0.1 copy-done.6
  14.4 0.5 copy-done.7
  14.9 1.8 complete_first.1
  16.6 7.6 %collective-permute-start.2 = (f32[64,128]{1,0:T(8,128)}, f32[64,128]{1,0:T(8,128)S(1)}, u32[]{:S(2)}, u32[]{:S(2)}) collective-permute-start(f32[64,128]{1,0:T(8,128)} %get-tuple-element.20.owned), channel_id=1, source_target_pairs={{0,8},{1,9},{2,10},{3,11},{4,12},{5,13},{6,14},{7,15},{8,16},{9,17... | collective-permute-start | bytes 98312 | tf_op jit(solution)/shard_map/ppermute | solution.py:357
  24.2 4.4 %collective-permute-start.3 = (f32[64,128]{1,0:T(8,128)}, f32[64,128]{1,0:T(8,128)S(1)}, u32[]{:S(2)}, u32[]{:S(2)}) collective-permute-start(f32[64,128]{1,0:T(8,128)} %get-tuple-element.20.owned), channel_id=1, source_target_pairs={{0,56},{1,57},{2,58},{3,59},{4,60},{5,61},{6,62},{7,63},{8,0},{9,1... | collective-permute-start | bytes 98312 | tf_op jit(solution)/shard_map/ppermute | solution.py:357
  28.6 0.7 slice.21
  29.3 0.0 collective-permute-done.2.behind
  29.3 4.0 %collective-permute-done.3.ahead = f32[64,128]{1,0:T(8,128)S(1)} collective-permute-done((f32[64,128]{1,0:T(8,128)}, f32[64,128]{1,0:T(8,128)S(1)}, u32[]{:S(2)}, u32[]{:S(2)}) %collective-permute-start.3) | collective-permute-done | bytes 32800 | tf_op jit(solution)/shard_map/ppermute | solution.py:357
  33.3 0.0 copy-done.8
  33.3 0.6 copy-done.9
  33.9 25.9 %all_to_all.20.sections = f32[8,48,128]{2,1,0:T(8,128)} all-to-all(f32[8,48,128]{2,1,0:T(8,128)S(1)} %broadcast_in_dim.12), channel_id=1, replica_groups=mesh['tm'=8,'block'=8,'place'=8] {'tm'}, dimensions={0} | all-to-all | bytes 393216 | tf_op jit(solution)/shard_map/all_to_all | solution.py:366
  59.9 2.0 hand_out.2
  61.9 16.6 %all-to-all-start.1 = ((f32[8,208,128]{2,1,0:T(8,128)}), f32[8,208,128]{2,1,0:T(8,128)S(1)}, u32[]{:S(2)}, u32[]{:S(2)}) async-start(f32[8,208,128]{2,1,0:T(8,128)} %hand_out.2), calls=%async_computation.1 | async-start | bytes 1703936 | tf_op jit(solution)/shard_map/all_to_all | solution.py:370
  78.5 0.0 copy-done.5
  78.5 4.9 %collective-permute-start.4 = (f32[2,64,128]{2,1,0:T(8,128)S(1)}, f32[2,64,128]{2,1,0:T(8,128)S(1)}, u32[]{:S(2)}, u32[]{:S(2)}) collective-permute-start(f32[2,64,128]{2,1,0:T(8,128)S(1)} %bitcast.9), channel_id=1, source_target_pairs={{0,64},{64,128},{128,192},{192,256},{256,320},{320,384},{384,448},... | collective-permute-start | bytes 196616 | tf_op jit(solution)/shard_map/ppermute | solution.py:362
  83.4 15.0 %collective-permute-done.4.received = f32[2,64,128]{2,1,0:T(8,128)S(1)} collective-permute-done((f32[2,64,128]{2,1,0:T(8,128)S(1)}, f32[2,64,128]{2,1,0:T(8,128)S(1)}, u32[]{:S(2)}, u32[]{:S(2)}) %collective-permute-start.4) | collective-permute-done | bytes 65568 | tf_op jit(solution)/shard_map/ppermute | solution.py:362
  98.4 7.2 %all-to-all-done.1.windows = f32[8,208,128]{2,1,0:T(8,128)S(1)} async-done(((f32[8,208,128]{2,1,0:T(8,128)}), f32[8,208,128]{2,1,0:T(8,128)S(1)}, u32[]{:S(2)}, u32[]{:S(2)}) %all-to-all-start.1) | async-done | bytes 852000 | tf_op jit(solution)/shard_map/all_to_all | solution.py:370
  105.6 0.0 copy-done.13
  105.6 0.9 copy-done
  106.6 3.9 %finish_first.1 = (f32[2,2,64,128]{3,2,1,0:T(8,128)}, f32[2,64,128]{2,1,0:T(8,128)}, f32[144,128]{1,0:T(8,128)}, f32[144,128]{1,0:T(8,128)}, f32[5,32,128]{2,1,0:T(8,128)}, /*index=5*/f32[15,32,128]{2,1,0:T(8,128)}) custom-call(s32[2]{0:T(128)} %pad_add_fusion.spot, f32[64,128]{1,0:T(8,128)} %get-tuple-element.20.owned, f32[64,128]{1,0:T(8,128)} %copy-done.8, ...), custom_call_target="tpu_custom_call" | custom-call | tf_op jit(solution)/shard_map/finish_first/pallas_call | solution.py:337
  110.4 1.9 collective-permute-start.5
  112.3 2.8 %collective-permute-start.6 = (f32[144,128]{1,0:T(8,128)}, f32[144,128]{1,0:T(8,128)S(1)}, u32[]{:S(2)}, u32[]{:S(2)}) collective-permute-start(f32[144,128]{1,0:T(8,128)} %get-tuple-element.23), channel_id=1, source_target_pairs={{0,63},{1,0},{2,1},{3,2},{4,3},{5,4},{6,5},{7,6},{8,7},{9,8},{10,9... | collective-permute-start | bytes 221192 | tf_op jit(solution)/shard_map/ppermute | solution.py:357
  115.1 0.0 collective-permute-done.5.below
  115.2 3.1 %collective-permute-done.6.above = f32[144,128]{1,0:T(8,128)S(1)} collective-permute-done((f32[144,128]{1,0:T(8,128)}, f32[144,128]{1,0:T(8,128)S(1)}, u32[]{:S(2)}, u32[]{:S(2)}) %collective-permute-start.6) | collective-permute-done | bytes 73760 | tf_op jit(solution)/shard_map/ppermute | solution.py:357
  118.2 0.0 copy-done.2
  118.2 0.6 copy-done.3
  118.9 1.8 complete_second.1
  120.7 4.3 %collective-permute-start.7 = (f32[48,128]{1,0:T(8,128)}, f32[48,128]{1,0:T(8,128)S(1)}, u32[]{:S(2)}, u32[]{:S(2)}) collective-permute-start(f32[48,128]{1,0:T(8,128)} %get-tuple-element.25.owned), channel_id=1, source_target_pairs={{0,8},{1,9},{2,10},{3,11},{4,12},{5,13},{6,14},{7,15},{8,16},{9,17... | collective-permute-start | bytes 73736 | tf_op jit(solution)/shard_map/ppermute | solution.py:357
  125.0 7.0 %collective-permute-start.8 = (f32[48,128]{1,0:T(8,128)}, f32[48,128]{1,0:T(8,128)S(1)}, u32[]{:S(2)}, u32[]{:S(2)}) collective-permute-start(f32[48,128]{1,0:T(8,128)} %get-tuple-element.25.owned), channel_id=1, source_target_pairs={{0,56},{1,57},{2,58},{3,59},{4,60},{5,61},{6,62},{7,63},{8,0},{9,1... | collective-permute-start | bytes 73736 | tf_op jit(solution)/shard_map/ppermute | solution.py:357
  132.0 0.7 slice.24
  132.7 0.0 collective-permute-done.7.behind
  132.7 1.3 collective-permute-done.8.ahead
  134.0 0.6 copy-done.11
  134.6 18.9 %all_to_all.21.sections = f32[8,48,128]{2,1,0:T(8,128)} all-to-all(f32[8,48,128]{2,1,0:T(8,128)S(1)} %broadcast_in_dim.13), channel_id=1, replica_groups=mesh['tm'=8,'block'=8,'place'=8] {'tm'}, dimensions={0} | all-to-all | bytes 393216 | tf_op jit(solution)/shard_map/all_to_all | solution.py:366
  153.5 2.0 hand_out.3
  155.5 19.4 %all-to-all-start.3 = ((f32[8,176,128]{2,1,0:T(8,128)}), f32[8,176,128]{2,1,0:T(8,128)S(1)}, u32[]{:S(2)}, u32[]{:S(2)}) async-start(f32[8,176,128]{2,1,0:T(8,128)} %hand_out.3), calls=%async_computation.3 | async-start | bytes 1441792 | tf_op jit(solution)/shard_map/all_to_all | solution.py:370
  174.9 0.0 copy-done.4
  174.9 2.9 %collective-permute-start.9 = (f32[2,64,128]{2,1,0:T(8,128)S(1)}, f32[2,64,128]{2,1,0:T(8,128)S(1)}, u32[]{:S(2)}, u32[]{:S(2)}) collective-permute-start(f32[2,64,128]{2,1,0:T(8,128)S(1)} %slice_bitcast_fusion), channel_id=1, source_target_pairs={{0,64},{64,128},{128,192},{192,256},{256,320},{320,384},{384,448},... | collective-permute-start | bytes 196616 | tf_op jit(solution)/shard_map/ppermute | solution.py:362
  177.8 14.7 %collective-permute-done.9.received = f32[2,64,128]{2,1,0:T(8,128)S(1)} collective-permute-done((f32[2,64,128]{2,1,0:T(8,128)S(1)}, f32[2,64,128]{2,1,0:T(8,128)S(1)}, u32[]{:S(2)}, u32[]{:S(2)}) %collective-permute-start.9) | collective-permute-done | bytes 65568 | tf_op jit(solution)/shard_map/ppermute | solution.py:362
  192.5 6.7 %all-to-all-done.3.windows = f32[8,176,128]{2,1,0:T(8,128)S(1)} async-done(((f32[8,176,128]{2,1,0:T(8,128)}), f32[8,176,128]{2,1,0:T(8,128)S(1)}, u32[]{:S(2)}, u32[]{:S(2)}) %all-to-all-start.3) | async-done | bytes 720928 | tf_op jit(solution)/shard_map/all_to_all | solution.py:370
  199.2 0.9 copy-done.1
  200.1 3.6 %finish_second.1 = (f32[2,2,64,128]{3,2,1,0:T(8,128)}, f32[32,64]{1,0:T(8,128)}) custom-call(s32[2]{0:T(128)} %pad_add_fusion.spot, f32[48,128]{1,0:T(8,128)} %get-tuple-element.25.owned, f32[48,128]{1,0:T(8,128)} %copy-done.10, f32[48,128]{1,0:T(8,128)} %copy-done.11, f32[8,48,128]{2,1,0:T(8,128)} %all_to_all.21.sections, f32[8,176,128]{2,1,0:T(8,128)} %copy-done.1, ...), custom_call_target="tpu_custom_call" | custom-call | tf_op jit(solution)/shard_map/finish_second/pallas_call | solution.py:337
  (25 shorter events, 0.1 us)
Async XLA Ops:
  2.5 11.3 %collective-permute-start = (f32[96,128]{1,0:T(8,128)}, f32[96,128]{1,0:T(8,128)S(1)}, u32[]{:S(2)}, u32[]{:S(2)}) collective-permute-start(f32[96,128]{1,0:T(8,128)} %get-tuple-element.17), channel_id=1, source_target_pairs={{0,1},{1,2},{2,3},{3,4},{4,5},{5,6},{6,7},{7,8},{8,9},{9,10},{10,1... | collective-permute-start | bytes 147464 | tf_op jit(solution)/shard_map/ppermute | solution.py:357
  7.4 6.8 %collective-permute-start.1 = (f32[96,128]{1,0:T(8,128)}, f32[96,128]{1,0:T(8,128)S(1)}, u32[]{:S(2)}, u32[]{:S(2)}) collective-permute-start(f32[96,128]{1,0:T(8,128)} %get-tuple-element.18), channel_id=1, source_target_pairs={{0,63},{1,0},{2,1},{3,2},{4,3},{5,4},{6,5},{7,6},{8,7},{9,8},{10,9... | collective-permute-start | bytes 147464 | tf_op jit(solution)/shard_map/ppermute | solution.py:357
  13.8 0.6 copy-start.6
  14.3 0.6 copy-start.7
  16.6 12.7 %collective-permute-start.2 = (f32[64,128]{1,0:T(8,128)}, f32[64,128]{1,0:T(8,128)S(1)}, u32[]{:S(2)}, u32[]{:S(2)}) collective-permute-start(f32[64,128]{1,0:T(8,128)} %get-tuple-element.20.owned), channel_id=1, source_target_pairs={{0,8},{1,9},{2,10},{3,11},{4,12},{5,13},{6,14},{7,15},{8,16},{9,17... | collective-permute-start | bytes 98312 | tf_op jit(solution)/shard_map/ppermute | solution.py:357
  24.2 9.1 %collective-permute-start.3 = (f32[64,128]{1,0:T(8,128)}, f32[64,128]{1,0:T(8,128)S(1)}, u32[]{:S(2)}, u32[]{:S(2)}) collective-permute-start(f32[64,128]{1,0:T(8,128)} %get-tuple-element.20.owned), channel_id=1, source_target_pairs={{0,56},{1,57},{2,58},{3,59},{4,60},{5,61},{6,62},{7,63},{8,0},{9,1... | collective-permute-start | bytes 98312 | tf_op jit(solution)/shard_map/ppermute | solution.py:357
  29.3 4.0 %copy-start.8 = (f32[64,128]{1,0:T(8,128)}, f32[64,128]{1,0:T(8,128)S(1)}, u32[]{:S(2)}) copy-start(f32[64,128]{1,0:T(8,128)S(1)} %collective-permute-done.2.behind) | copy-start | bytes 98308
  33.3 0.6 copy-start.9
  61.9 16.6 %copy-start.5 = (f32[1,2,64,128]{3,2,1,0:T(8,128)S(1)}, f32[1,2,64,128]{3,2,1,0:T(8,128)}, u32[]{:S(2)}) copy-start(f32[1,2,64,128]{3,2,1,0:T(8,128)} %param.5) | copy-start | bytes 196612
  61.9 43.7 %all-to-all-start.1 = ((f32[8,208,128]{2,1,0:T(8,128)}), f32[8,208,128]{2,1,0:T(8,128)S(1)}, u32[]{:S(2)}, u32[]{:S(2)}) async-start(f32[8,208,128]{2,1,0:T(8,128)} %hand_out.2), calls=%async_computation.1 | async-start | bytes 1703936 | tf_op jit(solution)/shard_map/all_to_all | solution.py:370
  78.5 19.9 %collective-permute-start.4 = (f32[2,64,128]{2,1,0:T(8,128)S(1)}, f32[2,64,128]{2,1,0:T(8,128)S(1)}, u32[]{:S(2)}, u32[]{:S(2)}) collective-permute-start(f32[2,64,128]{2,1,0:T(8,128)S(1)} %bitcast.9), channel_id=1, source_target_pairs={{0,64},{64,128},{128,192},{192,256},{256,320},{320,384},{384,448},... | collective-permute-start | bytes 196616 | tf_op jit(solution)/shard_map/ppermute | solution.py:362
  98.4 7.3 %copy-start.13 = (f32[2,64,128]{2,1,0:T(8,128)}, f32[2,64,128]{2,1,0:T(8,128)S(1)}, u32[]{:S(2)}) copy-start(f32[2,64,128]{2,1,0:T(8,128)S(1)} %collective-permute-done.4.received) | copy-start | bytes 196612
  105.6 0.9 copy-start
  110.4 4.7 %collective-permute-start.5 = (f32[144,128]{1,0:T(8,128)}, f32[144,128]{1,0:T(8,128)S(1)}, u32[]{:S(2)}, u32[]{:S(2)}) collective-permute-start(f32[144,128]{1,0:T(8,128)} %get-tuple-element.22), channel_id=1, source_target_pairs={{0,1},{1,2},{2,3},{3,4},{4,5},{5,6},{6,7},{7,8},{8,9},{9,10},{10,1... | collective-permute-start | bytes 221192 | tf_op jit(solution)/shard_map/ppermute | solution.py:357
  112.3 5.9 %collective-permute-start.6 = (f32[144,128]{1,0:T(8,128)}, f32[144,128]{1,0:T(8,128)S(1)}, u32[]{:S(2)}, u32[]{:S(2)}) collective-permute-start(f32[144,128]{1,0:T(8,128)} %get-tuple-element.23), channel_id=1, source_target_pairs={{0,63},{1,0},{2,1},{3,2},{4,3},{5,4},{6,5},{7,6},{8,7},{9,8},{10,9... | collective-permute-start | bytes 221192 | tf_op jit(solution)/shard_map/ppermute | solution.py:357
  115.1 3.1 %copy-start.2 = (f32[144,128]{1,0:T(8,128)}, f32[144,128]{1,0:T(8,128)S(1)}, u32[]{:S(2)}) copy-start(f32[144,128]{1,0:T(8,128)S(1)} %collective-permute-done.5.below) | copy-start | bytes 221188
  118.2 0.6 copy-start.3
  120.7 12.0 %collective-permute-start.7 = (f32[48,128]{1,0:T(8,128)}, f32[48,128]{1,0:T(8,128)S(1)}, u32[]{:S(2)}, u32[]{:S(2)}) collective-permute-start(f32[48,128]{1,0:T(8,128)} %get-tuple-element.25.owned), channel_id=1, source_target_pairs={{0,8},{1,9},{2,10},{3,11},{4,12},{5,13},{6,14},{7,15},{8,16},{9,17... | collective-permute-start | bytes 73736 | tf_op jit(solution)/shard_map/ppermute | solution.py:357
  125.0 9.0 %collective-permute-start.8 = (f32[48,128]{1,0:T(8,128)}, f32[48,128]{1,0:T(8,128)S(1)}, u32[]{:S(2)}, u32[]{:S(2)}) collective-permute-start(f32[48,128]{1,0:T(8,128)} %get-tuple-element.25.owned), channel_id=1, source_target_pairs={{0,56},{1,57},{2,58},{3,59},{4,60},{5,61},{6,62},{7,63},{8,0},{9,1... | collective-permute-start | bytes 73736 | tf_op jit(solution)/shard_map/ppermute | solution.py:357
  132.7 1.3 copy-start.10
  134.0 0.6 copy-start.11
  155.5 19.4 %copy-start.4 = (f32[2,2,64,128]{3,2,1,0:T(8,128)S(1)}, f32[2,2,64,128]{3,2,1,0:T(8,128)}, u32[]{:S(2)}) copy-start(f32[2,2,64,128]{3,2,1,0:T(8,128)} %get-tuple-element.28.fresh_in) | copy-start | bytes 393220
  155.5 43.7 %all-to-all-start.3 = ((f32[8,176,128]{2,1,0:T(8,128)}), f32[8,176,128]{2,1,0:T(8,128)S(1)}, u32[]{:S(2)}, u32[]{:S(2)}) async-start(f32[8,176,128]{2,1,0:T(8,128)} %hand_out.3), calls=%async_computation.3 | async-start | bytes 1441792 | tf_op jit(solution)/shard_map/all_to_all | solution.py:370
  174.9 17.6 %collective-permute-start.9 = (f32[2,64,128]{2,1,0:T(8,128)S(1)}, f32[2,64,128]{2,1,0:T(8,128)S(1)}, u32[]{:S(2)}, u32[]{:S(2)}) collective-permute-start(f32[2,64,128]{2,1,0:T(8,128)S(1)} %slice_bitcast_fusion), channel_id=1, source_target_pairs={{0,64},{64,128},{128,192},{192,256},{256,320},{320,384},{384,448},... | collective-permute-start | bytes 196616 | tf_op jit(solution)/shard_map/ppermute | solution.py:362
  192.5 6.7 %copy-start.12 = (f32[2,64,128]{2,1,0:T(8,128)}, f32[2,64,128]{2,1,0:T(8,128)S(1)}, u32[]{:S(2)}) copy-start(f32[2,64,128]{2,1,0:T(8,128)S(1)} %collective-permute-done.9.received) | copy-start | bytes 196612
  199.2 0.9 copy-start.1

commit v2 on v1

--- a/solution.py
+++ b/solution.py
@@ -91,17 +91,6 @@
 
 def mix(row, nodes):
     return QUAD[row][0] * nodes[0] + QUAD[row][1] * nodes[1] + QUAD[row][2] * nodes[2]
-
-
-def own_part(sums, rates, scratch):
-    planes = []
-    for m in (0, 1):
-        total = None
-        for x in (0, 1):
-            part = around(sums[m][x]) - 6.0 * sums[m][x] + sums[m][1 - x] + rates[m][x]
-            total = part if total is None else total + part
-        planes.append(total)
-    return squash(planes, scratch)
 
 
 def first_kernel(initial, coeff, guess, up, down, keep, scratch):
@@ -370,6 +359,10 @@
         return lax.all_to_all(x, "place", 0, 0)
 
     @staticmethod
+    def together(*values):
+        return lax.optimization_barrier(values)
+
+    @staticmethod
     def stack(*planes):
         return jnp.concatenate([p[:16] for p in planes], axis=0)
 
@@ -383,7 +376,7 @@
         first_kernel, (initial, coeff, guess), [(96, 128), (96, 128), (4,) + coarse], [(256, 128)], name="first"
     )
     below, above = links.shift(up, 1), links.shift(down, -1)
-    received = links.onward(guess)
+    below, above, received = links.together(below, above, links.onward(guess))
     owned, started = links.call(
         complete_first, (spot, below, above, kept), [(64, 128), (6,) + coarse], [(128, 128)], name="complete_first"
     )
@@ -406,7 +399,7 @@
         name="finish_first",
     )
     below, above = links.shift(up, 1), links.shift(down, -1)
-    received = links.onward(fresh[1])
+    below, above, received = links.together(below, above, links.onward(fresh[1]))
     owned, kept_k = links.call(
         complete_second, (spot, below, above, kept2, started, kept), [(48, 128), (2,) + coarse], [(256, 128)],
         name="complete_second",

time: 205 us -> 207 us (level)
  blocking collectives: 44.8 us -> 120 us
  waiting for transfers between devices: 52.4 us -> 15.3 us
  starting transfers between devices: 82.5 us -> 47 us
    all_to_all x0 -> x2, blocking collectives: none -> 70.5 us  [block(): return lax.all_to_all(x, 'place', 0, 0)]
    all_to_all x2 -> x0, starting transfers between devices: 36 us -> none  [block(): return lax.all_to_all(x, 'place', 0, 0)]
    ppermute x2, waiting for transfers between devices: 29.6 us -> 1.31 us  [onward(): return lax.ppermute(x, 'tm', [(i, i + 1) for i in range(n - 1)])]
    all_to_all x2 -> x0, waiting for transfers between devices: 13.9 us -> none  [block(): return lax.all_to_all(x, 'place', 0, 0)]
    ppermute x2, starting transfers between devices: 7.85 us -> 18.7 us  [onward(): return lax.ppermute(x, 'tm', [(i, i + 1) for i in range(n - 1)])]
    ppermute x8, starting transfers between devices: 38.6 us -> 28.3 us  [shift(): lax.ppermute(x, ('block', 'place'), [(i, (i + by) % n) for i in range(n)])]
    ppermute x8, waiting for transfers between devices: 8.8 us -> 14 us  [shift(): lax.ppermute(x, ('block', 'place'), [(i, (i + by) % n) for i in range(n)])]
    all_to_all x2, blocking collectives: 44.8 us -> 49.7 us  [sections(): lax.all_to_all(jnp.broadcast_to(x, (SECTIONS,) + x.shape), 'tm', 0, 0)]
  transfers between devices with their start and end apart: 12 -> 10, of which waited for: 8 -> 5; matrix products, arithmetic and copies ran while one was open for 1% -> 1% of each run, Pallas kernels for 0% -> 1%
where the time goes in v2:
time: 207 us; the launch traced here: 206 us
  blocking collectives  120 us (58%)
  starting transfers between devices  47 us (23%)
  Pallas kernels  17 us (8%)
  waiting for transfers between devices  15.3 us (7%)
  local copies, waits for them, and re-layouts  4.72 us (2%)
    all_to_all x2, blocking collectives, block(): return lax.all_to_all(x, 'place', 0, 0)  70.5 us
    all_to_all x2, blocking collectives, sections(): lax.all_to_all(jnp.broadcast_to(x, (SECTIONS,) + x.shape), 'tm', 0, 0)  49.7 us
    ppermute x8, starting transfers between devices, shift(): lax.ppermute(x, ('block', 'place'), [(i, (i + by) % n) for i in range(n)])  28.3 us
    ppermute x2, starting transfers between devices, onward(): return lax.ppermute(x, 'tm', [(i, i + 1) for i in range(n - 1)])  18.7 us
    pallas_call x7, Pallas kernels, run(): pl.pallas_call(body, out_shape=[jax.ShapeDtypeStruct(shape, F32) for shap...  17 us
    ppermute x8, waiting for transfers between devices, shift(): lax.ppermute(x, ('block', 'place'), [(i, (i + by) % n) for i in range(n)])  14 us
  transfers between devices with their start and end apart: 10, of which 5 were waited for; matrix products, arithmetic and copies ran while one was open for 1% of the time, Pallas kernels for 1%

profile of v2, /device:TPU:1, one launch (start us, length us, event | category | flops | bytes accessed | tf_op | source)
XLA Modules:
  0.0 205.6 jit_solution(11287866017398667732)
XLA Ops:
  0.6 16.3 %collective-permute-start.2 = (f32[2,64,128]{2,1,0:T(8,128)}, f32[2,64,128]{2,1,0:T(8,128)S(1)}, u32[]{:S(2)}, u32[]{:S(2)}) collective-permute-start(f32[2,64,128]{2,1,0:T(8,128)} %bitcast.7), channel_id=1, source_target_pairs={{0,64},{64,128},{128,192},{192,256},{256,320},{320,384},{384,448},... | collective-permute-start | bytes 196616 | tf_op jit(solution)/shard_map/ppermute | solution.py:351
  16.9 1.9 first.1
  18.8 3.5 %collective-permute-start = (f32[96,128]{1,0:T(8,128)}, f32[96,128]{1,0:T(8,128)S(1)}, u32[]{:S(2)}, u32[]{:S(2)}) collective-permute-start(f32[96,128]{1,0:T(8,128)} %get-tuple-element.23), channel_id=1, source_target_pairs={{0,1},{1,2},{2,3},{3,4},{4,5},{5,6},{6,7},{7,8},{8,9},{9,10},{10,1... | collective-permute-start | bytes 147464 | tf_op jit(solution)/shard_map/ppermute | solution.py:346
  22.3 1.9 collective-permute-start.1
  24.2 0.6 pad_add_fusion.spot
  24.8 0.0 collective-permute-done.below
  24.8 0.0 copy-start.2
  24.8 3.1 %collective-permute-done.1.above = f32[96,128]{1,0:T(8,128)S(1)} collective-permute-done((f32[96,128]{1,0:T(8,128)}, f32[96,128]{1,0:T(8,128)S(1)}, u32[]{:S(2)}, u32[]{:S(2)}) %collective-permute-start.1) | collective-permute-done | bytes 49184 | tf_op jit(solution)/shard_map/ppermute | solution.py:346
  27.9 0.0 copy-start.3
  27.9 0.0 collective-permute-done.2.received
  27.9 0.0 copy-start.8
  27.9 0.0 copy-done.2
  27.9 0.6 copy-done.3
  28.5 1.8 complete_first.1
  30.2 0.0 copy-done.8
  30.2 6.5 %collective-permute-start.4 = (f32[64,128]{1,0:T(8,128)}, f32[64,128]{1,0:T(8,128)S(1)}, u32[]{:S(2)}, u32[]{:S(2)}) collective-permute-start(f32[64,128]{1,0:T(8,128)} %get-tuple-element.28.owned), channel_id=1, source_target_pairs={{0,56},{1,57},{2,58},{3,59},{4,60},{5,61},{6,62},{7,63},{8,0},{9,1... | collective-permute-start | bytes 98312 | tf_op jit(solution)/shard_map/ppermute | solution.py:346
  36.7 2.7 %collective-permute-start.3 = (f32[64,128]{1,0:T(8,128)}, f32[64,128]{1,0:T(8,128)S(1)}, u32[]{:S(2)}, u32[]{:S(2)}) collective-permute-start(f32[64,128]{1,0:T(8,128)} %get-tuple-element.28.owned), channel_id=1, source_target_pairs={{0,8},{1,9},{2,10},{3,11},{4,12},{5,13},{6,14},{7,15},{8,16},{9,17... | collective-permute-start | bytes 98312 | tf_op jit(solution)/shard_map/ppermute | solution.py:346
  39.4 0.7 slice.21
  40.1 0.0 collective-permute-done.4.ahead
  40.2 7.4 %collective-permute-done.3.behind = f32[64,128]{1,0:T(8,128)S(1)} collective-permute-done((f32[64,128]{1,0:T(8,128)}, f32[64,128]{1,0:T(8,128)S(1)}, u32[]{:S(2)}, u32[]{:S(2)}) %collective-permute-start.3) | collective-permute-done | bytes 32800 | tf_op jit(solution)/shard_map/ppermute | solution.py:346
  47.6 0.0 copy-done.4
  47.6 0.6 copy-done.5
  48.2 21.3 %all_to_all.20.sections = f32[8,48,128]{2,1,0:T(8,128)} all-to-all(f32[8,48,128]{2,1,0:T(8,128)S(1)} %broadcast_in_dim.12), channel_id=1, replica_groups=mesh['tm'=8,'block'=8,'place'=8] {'tm'}, dimensions={0} | all-to-all | bytes 393216 | tf_op jit(solution)/shard_map/all_to_all | solution.py:355
  69.5 2.1 %hand_out.2 = f32[8,208,128]{2,1,0:T(8,128)} custom-call(s32[2]{0:T(128)} %pad_add_fusion.spot, f32[64,128]{1,0:T(8,128)} %get-tuple-element.28.owned, f32[64,128]{1,0:T(8,128)} %copy-done.5, f32[64,128]{1,0:T(8,128)} %copy-done.4, f32[8,48,128]{2,1,0:T(8,128)} %all_to_all.20.sections), custom_call_target="tpu_custom_call" | custom-call | tf_op jit(solution)/shard_map/hand_out/pallas_call | solution.py:326
  71.5 34.5 %all_to_all.21.windows = f32[8,208,128]{2,1,0:T(8,128)} all-to-all(f32[8,208,128]{2,1,0:T(8,128)} %hand_out.2), channel_id=1, replica_groups=mesh['tm'=8,'block'=8,'place'=8] {'place'}, dimensions={0} | all-to-all | bytes 1703936 | tf_op jit(solution)/shard_map/all_to_all | solution.py:359
  106.0 3.9 %finish_first.1 = (f32[2,2,64,128]{3,2,1,0:T(8,128)}, f32[2,64,128]{2,1,0:T(8,128)}, f32[144,128]{1,0:T(8,128)}, f32[144,128]{1,0:T(8,128)}, f32[5,32,128]{2,1,0:T(8,128)}, /*index=5*/f32[15,32,128]{2,1,0:T(8,128)}) custom-call(s32[2]{0:T(128)} %pad_add_fusion.spot, f32[64,128]{1,0:T(8,128)} %get-tuple-element.28.owned, f32[64,128]{1,0:T(8,128)} %copy-done.5, ...), custom_call_target="tpu_custom_call" | custom-call | tf_op jit(solution)/shard_map/finish_first/pallas_call | solution.py:326
  109.9 2.6 %collective-permute-start.5 = (f32[144,128]{1,0:T(8,128)}, f32[144,128]{1,0:T(8,128)S(1)}, u32[]{:S(2)}, u32[]{:S(2)}) collective-permute-start(f32[144,128]{1,0:T(8,128)} %get-tuple-element.31), channel_id=1, source_target_pairs={{0,1},{1,2},{2,3},{3,4},{4,5},{5,6},{6,7},{7,8},{8,9},{9,10},{10,1... | collective-permute-start | bytes 221192 | tf_op jit(solution)/shard_map/ppermute | solution.py:346
  112.5 1.9 collective-permute-start.6
  114.5 0.8 slice_bitcast_fusion
  115.3 2.4 %collective-permute-start.7 = (f32[2,64,128]{2,1,0:T(8,128)S(1)}, f32[2,64,128]{2,1,0:T(8,128)S(1)}, u32[]{:S(2)}, u32[]{:S(2)}) collective-permute-start(f32[2,64,128]{2,1,0:T(8,128)S(1)} %slice_bitcast_fusion), channel_id=1, source_target_pairs={{0,64},{64,128},{128,192},{192,256},{256,320},{320,384},{384,448},... | collective-permute-start | bytes 196616 | tf_op jit(solution)/shard_map/ppermute | solution.py:351
  117.8 1.3 collective-permute-done.7.received
  119.1 0.0 collective-permute-done.5.below
  119.1 0.3 collective-permute-done.6.above
  119.4 0.3 copy-done
  119.7 0.3 copy-done.1
  120.0 1.8 complete_second.1
  121.9 0.0 copy-done.9
  121.9 1.9 collective-permute-start.9
  123.8 7.3 %collective-permute-start.8 = (f32[48,128]{1,0:T(8,128)}, f32[48,128]{1,0:T(8,128)S(1)}, u32[]{:S(2)}, u32[]{:S(2)}) collective-permute-start(f32[48,128]{1,0:T(8,128)} %get-tuple-element.37.owned), channel_id=1, source_target_pairs={{0,8},{1,9},{2,10},{3,11},{4,12},{5,13},{6,14},{7,15},{8,16},{9,17... | collective-permute-start | bytes 73736 | tf_op jit(solution)/shard_map/ppermute | solution.py:346
  131.1 0.7 slice.25
  131.8 0.0 collective-permute-done.9.ahead
  131.8 3.1 %collective-permute-done.8.behind = f32[48,128]{1,0:T(8,128)S(1)} collective-permute-done((f32[48,128]{1,0:T(8,128)}, f32[48,128]{1,0:T(8,128)S(1)}, u32[]{:S(2)}, u32[]{:S(2)}) %collective-permute-start.8) | collective-permute-done | bytes 24608 | tf_op jit(solution)/shard_map/ppermute | solution.py:346
  134.9 0.0 copy-done.6
  134.9 0.6 copy-done.7
  135.5 28.5 %all_to_all.22.sections = f32[8,48,128]{2,1,0:T(8,128)} all-to-all(f32[8,48,128]{2,1,0:T(8,128)S(1)} %broadcast_in_dim.13), channel_id=1, replica_groups=mesh['tm'=8,'block'=8,'place'=8] {'tm'}, dimensions={0} | all-to-all | bytes 393216 | tf_op jit(solution)/shard_map/all_to_all | solution.py:355
  164.0 2.0 hand_out.3
  166.0 36.0 %all_to_all.23.windows = f32[8,176,128]{2,1,0:T(8,128)} all-to-all(f32[8,176,128]{2,1,0:T(8,128)} %hand_out.3), channel_id=1, replica_groups=mesh['tm'=8,'block'=8,'place'=8] {'place'}, dimensions={0} | all-to-all | bytes 1441792 | tf_op jit(solution)/shard_map/all_to_all | solution.py:359
  202.0 3.6 %finish_second.1 = (f32[2,2,64,128]{3,2,1,0:T(8,128)}, f32[32,64]{1,0:T(8,128)}) custom-call(s32[2]{0:T(128)} %pad_add_fusion.spot, f32[48,128]{1,0:T(8,128)} %get-tuple-element.37.owned, f32[48,128]{1,0:T(8,128)} %copy-done.7, f32[48,128]{1,0:T(8,128)} %copy-done.6, f32[8,48,128]{2,1,0:T(8,128)} %all_to_all.22.sections, f32[8,176,128]{2,1,0:T(8,128)} %all_to_all.23.windows, ...), custom_call_target="tpu_custom_call" | custom-call | tf_op jit(solution)/shard_map/finish_second/pallas_call | solution.py:326
  (15 shorter events, 0.1 us)
Async XLA Ops:
  0.6 27.2 %collective-permute-start.2 = (f32[2,64,128]{2,1,0:T(8,128)}, f32[2,64,128]{2,1,0:T(8,128)S(1)}, u32[]{:S(2)}, u32[]{:S(2)}) collective-permute-start(f32[2,64,128]{2,1,0:T(8,128)} %bitcast.7), channel_id=1, source_target_pairs={{0,64},{64,128},{128,192},{192,256},{256,320},{320,384},{384,448},... | collective-permute-start | bytes 196616 | tf_op jit(solution)/shard_map/ppermute | solution.py:351
  18.8 6.0 %collective-permute-start = (f32[96,128]{1,0:T(8,128)}, f32[96,128]{1,0:T(8,128)S(1)}, u32[]{:S(2)}, u32[]{:S(2)}) collective-permute-start(f32[96,128]{1,0:T(8,128)} %get-tuple-element.23), channel_id=1, source_target_pairs={{0,1},{1,2},{2,3},{3,4},{4,5},{5,6},{6,7},{7,8},{8,9},{9,10},{10,1... | collective-permute-start | bytes 147464 | tf_op jit(solution)/shard_map/ppermute | solution.py:346
  22.3 5.6 %collective-permute-start.1 = (f32[96,128]{1,0:T(8,128)}, f32[96,128]{1,0:T(8,128)S(1)}, u32[]{:S(2)}, u32[]{:S(2)}) collective-permute-start(f32[96,128]{1,0:T(8,128)} %get-tuple-element.24), channel_id=1, source_target_pairs={{0,63},{1,0},{2,1},{3,2},{4,3},{5,4},{6,5},{7,6},{8,7},{9,8},{10,9... | collective-permute-start | bytes 147464 | tf_op jit(solution)/shard_map/ppermute | solution.py:346
  24.8 3.1 %copy-start.2 = (f32[96,128]{1,0:T(8,128)}, f32[96,128]{1,0:T(8,128)S(1)}, u32[]{:S(2)}) copy-start(f32[96,128]{1,0:T(8,128)S(1)} %collective-permute-done.below) | copy-start | bytes 147460
  27.9 0.6 copy-start.3
  27.9 2.4 %copy-start.8 = (f32[2,64,128]{2,1,0:T(8,128)}, f32[2,64,128]{2,1,0:T(8,128)S(1)}, u32[]{:S(2)}) copy-start(f32[2,64,128]{2,1,0:T(8,128)S(1)} %collective-permute-done.2.received) | copy-start | bytes 196612
  30.2 9.9 %collective-permute-start.4 = (f32[64,128]{1,0:T(8,128)}, f32[64,128]{1,0:T(8,128)S(1)}, u32[]{:S(2)}, u32[]{:S(2)}) collective-permute-start(f32[64,128]{1,0:T(8,128)} %get-tuple-element.28.owned), channel_id=1, source_target_pairs={{0,56},{1,57},{2,58},{3,59},{4,60},{5,61},{6,62},{7,63},{8,0},{9,1... | collective-permute-start | bytes 98312 | tf_op jit(solution)/shard_map/ppermute | solution.py:346
  36.7 10.9 %collective-permute-start.3 = (f32[64,128]{1,0:T(8,128)}, f32[64,128]{1,0:T(8,128)S(1)}, u32[]{:S(2)}, u32[]{:S(2)}) collective-permute-start(f32[64,128]{1,0:T(8,128)} %get-tuple-element.28.owned), channel_id=1, source_target_pairs={{0,8},{1,9},{2,10},{3,11},{4,12},{5,13},{6,14},{7,15},{8,16},{9,17... | collective-permute-start | bytes 98312 | tf_op jit(solution)/shard_map/ppermute | solution.py:346
  40.2 7.5 %copy-start.4 = (f32[64,128]{1,0:T(8,128)}, f32[64,128]{1,0:T(8,128)S(1)}, u32[]{:S(2)}) copy-start(f32[64,128]{1,0:T(8,128)S(1)} %collective-permute-done.4.ahead) | copy-start | bytes 98308
  47.6 0.6 copy-start.5
  109.9 9.2 %collective-permute-start.5 = (f32[144,128]{1,0:T(8,128)}, f32[144,128]{1,0:T(8,128)S(1)}, u32[]{:S(2)}, u32[]{:S(2)}) collective-permute-start(f32[144,128]{1,0:T(8,128)} %get-tuple-element.31), channel_id=1, source_target_pairs={{0,1},{1,2},{2,3},{3,4},{4,5},{5,6},{6,7},{7,8},{8,9},{9,10},{10,1... | collective-permute-start | bytes 221192 | tf_op jit(solution)/shard_map/ppermute | solution.py:346
  112.5 6.9 %collective-permute-start.6 = (f32[144,128]{1,0:T(8,128)}, f32[144,128]{1,0:T(8,128)S(1)}, u32[]{:S(2)}, u32[]{:S(2)}) collective-permute-start(f32[144,128]{1,0:T(8,128)} %get-tuple-element.32), channel_id=1, source_target_pairs={{0,63},{1,0},{2,1},{3,2},{4,3},{5,4},{6,5},{7,6},{8,7},{9,8},{10,9... | collective-permute-start | bytes 221192 | tf_op jit(solution)/shard_map/ppermute | solution.py:346
  115.3 3.8 %collective-permute-start.7 = (f32[2,64,128]{2,1,0:T(8,128)S(1)}, f32[2,64,128]{2,1,0:T(8,128)S(1)}, u32[]{:S(2)}, u32[]{:S(2)}) collective-permute-start(f32[2,64,128]{2,1,0:T(8,128)S(1)} %slice_bitcast_fusion), channel_id=1, source_target_pairs={{0,64},{64,128},{128,192},{192,256},{256,320},{320,384},{384,448},... | collective-permute-start | bytes 196616 | tf_op jit(solution)/shard_map/ppermute | solution.py:351
  119.1 2.8 %copy-start.9 = (f32[2,64,128]{2,1,0:T(8,128)}, f32[2,64,128]{2,1,0:T(8,128)S(1)}, u32[]{:S(2)}) copy-start(f32[2,64,128]{2,1,0:T(8,128)S(1)} %collective-permute-done.7.received) | copy-start | bytes 196612
  119.1 0.6 copy-start
  119.4 0.6 copy-start.1
  121.9 9.9 %collective-permute-start.9 = (f32[48,128]{1,0:T(8,128)}, f32[48,128]{1,0:T(8,128)S(1)}, u32[]{:S(2)}, u32[]{:S(2)}) collective-permute-start(f32[48,128]{1,0:T(8,128)} %get-tuple-element.37.owned), channel_id=1, source_target_pairs={{0,56},{1,57},{2,58},{3,59},{4,60},{5,61},{6,62},{7,63},{8,0},{9,1... | collective-permute-start | bytes 73736 | tf_op jit(solution)/shard_map/ppermute | solution.py:346
  123.8 11.1 %collective-permute-start.8 = (f32[48,128]{1,0:T(8,128)}, f32[48,128]{1,0:T(8,128)S(1)}, u32[]{:S(2)}, u32[]{:S(2)}) collective-permute-start(f32[48,128]{1,0:T(8,128)} %get-tuple-element.37.owned), channel_id=1, source_target_pairs={{0,8},{1,9},{2,10},{3,11},{4,12},{5,13},{6,14},{7,15},{8,16},{9,17... | collective-permute-start | bytes 73736 | tf_op jit(solution)/shard_map/ppermute | solution.py:346
  131.8 3.1 %copy-start.6 = (f32[48,128]{1,0:T(8,128)}, f32[48,128]{1,0:T(8,128)S(1)}, u32[]{:S(2)}) copy-start(f32[48,128]{1,0:T(8,128)S(1)} %collective-permute-done.9.ahead) | copy-start | bytes 73732
  134.9 0.6 copy-start.7

commit v3 on v2

--- a/solution.py
+++ b/solution.py
@@ -11,6 +11,7 @@
 START = tuple(STEP * (row[1] * QUAD[1][0] + row[2] * QUAD[2][0]) for row in QUAD)
 SECTIONS = 8
 BLOCK = 8
+CHIPS = BLOCK // 2
 F32 = jnp.float32
 
 COEF, NEAR1, NEAR2 = 10, 11, 12
@@ -24,8 +25,16 @@
     return sum(1 for _, reach in items if reach >= distance)
 
 
+def shares(core, ahead):
+    if ahead == 0:
+        return (0, 1), (2 - core, BLOCK - 1)
+    if ahead > 0:
+        return (0, 2 * ahead - core), (2, BLOCK - 1 - 2 * ahead + core)
+    return (0, -2 * ahead + core - 1), (1, BLOCK + 2 * ahead - core)
+
+
 def slots(items):
-    return max(count(items, d) + count(items, BLOCK - d) for d in range(1, BLOCK))
+    return max(sum(count(items, least) for _, least in shares(core, a)) for core in (0, 1) for a in range(-3, 4))
 
 
 def turn(x, by, axis):
@@ -93,31 +102,57 @@
     return QUAD[row][0] * nodes[0] + QUAD[row][1] * nodes[1] + QUAD[row][2] * nodes[2]
 
 
-def first_kernel(initial, coeff, guess, up, down, keep, scratch):
+def packets(spot, up, down, inner, outer):
+    low = spot[2] == 0
+
+    @pl.when(low)
+    def _():
+        for row, part_up, part_down in zip_rows(up, down):
+            inner[row : row + part_up.shape[0], :] = part_up
+            outer[row : row + part_up.shape[0], :] = part_down
+
+    @pl.when(jnp.logical_not(low))
+    def _():
+        for row, part_up, part_down in zip_rows(up, down):
+            inner[row : row + part_up.shape[0], :] = part_down
+            outer[row : row + part_up.shape[0], :] = part_up
+
+
+def zip_rows(up, down):
+    row = 0
+    for part_up, part_down in zip(up, down):
+        yield row, part_up, part_down
+        row += part_up.shape[0]
+
+
+def sides(spot, inner, outer):
+    low = jnp.full(inner.shape, spot[2], jnp.int32) == 0
+    a, b = inner[...], outer[...]
+    return jnp.where(low, b, a), jnp.where(low, a, b)
+
+
+def first_kernel(spot, initial, coeff, guess, inner, outer, keep, scratch):
     u = [guess[0], guess[1]]
     c = [coeff[0], coeff[1]]
-    rate = [c[x] * cubic(u[x]) for x in (0, 1)]
-    total = None
-    for x in (0, 1):
-        part = around(u[x]) - 6.0 * u[x] + u[1 - x] + rate[x]
-        total = part if total is None else total + part
-    own, value, coef, start = squash([total, u[0] + u[1], c[0] + c[1], initial[0] + initial[1]], scratch)
+    both = u[0] + u[1]
+    total = around(both) - 5.0 * both + c[0] * cubic(u[0]) + c[1] * cubic(u[1])
+    own, value, coef, start = squash([total, both, c[0] + c[1], initial[0] + initial[1]], scratch)
     value, coef, start = 0.125 * value, 0.125 * coef, 0.125 * start
-    for out, plane in ((up, u[1]), (down, u[0])):
-        out[0:64, :] = plane
-        out[64:80, :] = pack(value)
-        out[80:96, :] = pack(start)
+    small = [pack(value), pack(start)]
+    packets(spot, [u[1]] + small, [u[0]] + small, inner, outer)
     keep[0] = own
     keep[1] = value
     keep[2] = coef
     keep[3] = start
 
 
-def hand_over(spot, own, values, value0, value0_sides, coef, start, start_slope, out, gathered):
+def hand_over(spot, own, values, value0, value0_sides, coef, start, start_slope, out, mine, gathered):
     slope = coarse_slope(value0_sides[0], value0, value0_sides[1], coef)
     k = [(STEP / 8.0) * own[m] - (STEP * QUAD[m + 1][0]) * slope for m in (0, 1)]
     first = (jnp.full((32, 128), spot[0], jnp.int32) == 0)
-    out[0:16, :] = pack(k[1] + jnp.where(first, start + STEP * QUAD[2][0] * start_slope, 0.0))
+    ours = pack(k[1] + jnp.where(first, start + STEP * QUAD[2][0] * start_slope, 0.0))
+    out[0:16, :] = ours
+    mine[...] = ours
     for m in (0, 1):
         near = QUAD[m + 1][1] * k[0] + QUAD[m + 1][2] * k[1] - values[m]
         near = near + jnp.where(first, ROWSUM[m + 1] * start + START[m + 1] * start_slope, 0.0)
@@ -126,16 +161,17 @@
     gathered[1] = k[1]
 
 
-def complete_first(spot, below, above, kept, out, keep, scratch):
+def complete_first(spot, inner, outer, kept, out, mine, keep, scratch):
+    below, above = sides(spot, inner, outer)
     own, value, coef, start = (kept[i] for i in range(4))
     low, high = squash([below[0:64, :], above[0:64, :]], scratch)
     whole = own + low + high
-    sides = [unpack(below[64:80, :]), unpack(above[64:80, :])]
+    value_sides = [unpack(below[64:80, :]), unpack(above[64:80, :])]
     start_sides = [unpack(below[80:96, :]), unpack(above[80:96, :])]
     start_slope = coarse_slope(start_sides[0], start, start_sides[1], coef)
     hand_over(
         spot, [ROWSUM[1] * whole, ROWSUM[2] * whole], [ROWSUM[1] * value, ROWSUM[2] * value],
-        value, sides, coef, start, start_slope, out, keep,
+        value, value_sides, coef, start, start_slope, out, mine, keep,
     )
     out[48:64, :] = pack(coef)
     keep[2] = start
@@ -144,21 +180,22 @@
     keep[5] = start_sides[1]
 
 
-def complete_second(spot, below, above, kept, started, kept_first, out, keep, scratch):
+def complete_second(spot, inner, outer, kept, started, kept_first, out, mine, keep, scratch):
+    below, above = sides(spot, inner, outer)
     low1, low2, high1, high2 = squash(
         [below[0:64, :], below[64:128, :], above[0:64, :], above[64:128, :]], scratch
     )
     own = [kept[0] + low1 + high1, kept[1] + low2 + high2]
     values = [mix(m, [kept[2], kept[3], kept[4]]) for m in (1, 2)]
-    sides = [unpack(below[128:144, :]), unpack(above[128:144, :])]
-    hand_over(spot, own, values, kept[2], sides, kept_first[2], started[2], started[3], out, keep)
+    value_sides = [unpack(below[128:144, :]), unpack(above[128:144, :])]
+    hand_over(spot, own, values, kept[2], value_sides, kept_first[2], started[2], started[3], out, mine, keep)
 
 
 def pack_kernel(items):
     total = slots(items)
 
     def body(spot, owned, behind, ahead, sections, out):
-        place = spot[1]
+        chip, core = spot[1], spot[2]
 
         def plane(side, item):
             if item < SECTIONS:
@@ -166,29 +203,28 @@
             row = {NEAR1: 16, NEAR2: 32, COEF: 48}[item]
             return (owned, behind, ahead)[side][row : row + 16, :]
 
-        def fill(to, distance, side):
+        def fill(own_core, away):
             slot = 0
-            for origin, least in ((0, distance), (side, BLOCK - distance)):
+            for side, least in shares(own_core, away):
                 for item, reach in items:
                     if reach >= least:
-                        out[to, 16 * slot : 16 * slot + 16, :] = plane(origin, item)
+                        out[chip + away, 16 * slot : 16 * slot + 16, :] = plane(side, item)
                         slot += 1
 
-        for d in range(1, BLOCK):
-
-            @pl.when(place + d < BLOCK)
-            def _():
-                fill(place + d, d, 2)
-
-            @pl.when(place + d >= BLOCK)
-            def _():
-                fill(place + d - BLOCK, BLOCK - d, 1)
+        for own_core in (0, 1):
+            for away in range(1 - CHIPS, CHIPS):
+                there = jnp.logical_and(chip + away >= 0, chip + away < CHIPS)
+
+                @pl.when(jnp.logical_and(core == own_core, there))
+                def _():
+                    fill(own_core, away)
 
     return body, total
 
 
-def sweep(spot, items, owned, behind, ahead, sections, windows, coefs, started, line, history):
-    place = spot[1]
+def sweep(spot, items, owned, behind, ahead, sections, windows, swapped, coefs, started, line, history):
+    core = spot[2]
+    place = 2 * spot[1] + core
     rank = {item: i for i, (item, _) in enumerate(items)}
     reach_of = dict(items)
 
@@ -200,9 +236,14 @@
             row = {NEAR1: 16, NEAR2: 32, COEF: 48}[item]
             return unpack((owned, behind, ahead)[side][row : row + 16, :])
         at = place + w
-        outside = jnp.logical_or(at < 0, at >= BLOCK)
-        slot = rank[item] + jnp.where(outside, count(items, BLOCK - abs(w)), 0)
-        return unpack(windows[at & (BLOCK - 1), pl.ds(pl.multiple_of(16 * slot, 16), 16), :])
+        if w > 0:
+            outside, least = at >= BLOCK, [max(1, BLOCK - w - i) for i in (0, 1)]
+        else:
+            outside, least = at < 0, [max(1, BLOCK - 1 + w + i) for i in (0, 1)]
+        before = jnp.where(core == 0, count(items, least[0]), count(items, least[1]))
+        slot = rank[item] + jnp.where(outside, before, 0)
+        source = windows if w % 2 == 0 else swapped
+        return unpack(source[(at & (BLOCK - 1)) >> 1, pl.ds(pl.multiple_of(16 * slot, 16), 16), :])
 
     if COEF in rank:
         for w in range(-7, 8):
@@ -260,10 +301,11 @@
 
 
 def finish_first(
-    spot, owned, behind, ahead, sections, windows, started, kept, below, above, initial, coeff, guess, received,
-    fresh_out, begin_out, up, down, keep, coefs, line, history, scratch,
+    spot, owned, behind, ahead, sections, windows, swapped, started, kept, inner, outer, initial, coeff, guess, received,
+    fresh_out, begin_out, inner_out, outer_out, keep, coefs, line, history, scratch,
 ):
-    fetch = sweep(spot, ITEMS[0], owned, behind, ahead, sections, windows, coefs, started, line, history)
+    below, above = sides(spot, inner, outer)
+    fetch = sweep(spot, ITEMS[0], owned, behind, ahead, sections, windows, swapped, coefs, started, line, history)
     begin = starting(spot, initial, received)
     u = [guess[0], guess[1]]
     c = [coeff[0], coeff[1]]
@@ -275,11 +317,11 @@
     )
     nodes = [begin] + fresh
     rates = [[cubic(nodes[j][x]) for x in (0, 1)] for j in range(3)]
-    planes = []
+    planes, up, down = [], [], []
     for m in (1, 2):
         sums = [mix(m, [nodes[j][x] for j in range(3)]) for x in (0, 1)]
-        down[64 * (m - 1) : 64 * m, :] = sums[0]
-        up[64 * (m - 1) : 64 * m, :] = sums[1]
+        down.append(sums[0])
+        up.append(sums[1])
         both = sums[0] + sums[1]
         part = around(both) - 5.0 * both
         for x in (0, 1):
@@ -296,15 +338,16 @@
     keep[1] = small[1]
     for j in range(3):
         keep[2 + j] = 0.125 * small[2 + j]
-    up[128:144, :] = pack(keep[2])
-    down[128:144, :] = pack(keep[2])
+    small = [pack(0.125 * small[2])]
+    packets(spot, up + small, down + small, inner_out, outer_out)
 
 
 def finish_second(
-    spot, owned, behind, ahead, sections, windows, started, kept, kept_k, below, above, initial, coeff, begin_in, fresh_in,
-    received, coefs, fresh_out, coarse_out, line, history, scratch,
+    spot, owned, behind, ahead, sections, windows, swapped, started, kept, kept_k, inner, outer, initial, coeff, begin_in,
+    fresh_in, received, coefs, fresh_out, coarse_out, line, history, scratch,
 ):
-    fetch = sweep(spot, ITEMS[1], owned, behind, ahead, sections, windows, coefs, started, line, history)
+    below, above = sides(spot, inner, outer)
+    fetch = sweep(spot, ITEMS[1], owned, behind, ahead, sections, windows, swapped, coefs, started, line, history)
     begin = starting(spot, initial, received)
     nodes = [[begin_in[0], begin_in[1]]] + [[fresh_in[m, 0], fresh_in[m, 1]] for m in (0, 1)]
     low = [below[64 * m : 64 * m + 64, :] for m in (0, 1)]
@@ -338,12 +381,21 @@
 
     @staticmethod
     def spot():
-        return jnp.stack([lax.axis_index("tm"), lax.axis_index("place")]).astype(jnp.int32)
+        return jnp.stack([lax.axis_index(a) for a in ("tm", "chip", "core")]).astype(jnp.int32)
 
     @staticmethod
     def shift(x, by):
-        n = lax.axis_size("block") * lax.axis_size("place")
-        return lax.ppermute(x, ("block", "place"), [(i, (i + by) % n) for i in range(n)])
+        n = lax.axis_size("block") * BLOCK
+        return lax.ppermute(x, ("block", "chip", "core"), [(i, (i + by) % n) for i in range(n)])
+
+    @staticmethod
+    def swap_inner(x):
+        return lax.ppermute(x, "core", [(0, 1), (1, 0)])
+
+    @staticmethod
+    def swap_outer(x):
+        n = lax.axis_size("block") * BLOCK
+        return lax.ppermute(x, ("block", "chip", "core"), [(i, (i + 2 * (i % 2) - 1) % n) for i in range(n)])
 
     @staticmethod
     def onward(x):
@@ -356,7 +408,7 @@
 
     @staticmethod
     def block(x):
-        return lax.all_to_all(x, "place", 0, 0)
+        return lax.all_to_all(x, "chip", 0, 0)
 
     @staticmethod
     def together(*values):
@@ -372,42 +424,39 @@
     coarse = (32, 128)
     work = [(2, 17) + coarse, (40,) + coarse]
 
-    up, down, kept = links.call(
-        first_kernel, (initial, coeff, guess), [(96, 128), (96, 128), (4,) + coarse], [(256, 128)], name="first"
-    )
-    below, above = links.shift(up, 1), links.shift(down, -1)
-    below, above, received = links.together(below, above, links.onward(guess))
-    owned, started = links.call(
-        complete_first, (spot, below, above, kept), [(64, 128), (6,) + coarse], [(128, 128)], name="complete_first"
-    )
-
-    def windows(owned, items):
+    def windows(owned, mine, items):
         behind, ahead = links.shift(owned, BLOCK), links.shift(owned, -BLOCK)
-        sections = links.sections(links.stack(owned, behind, ahead))
+        sections = links.sections(links.stack(mine, behind, ahead))
         body, total = pack_kernel(items)
-        (packets,) = links.call(
-            body, (spot, owned, behind, ahead, sections), [(BLOCK, 16 * total, 128)], name="hand_out"
+        (parcels,) = links.call(
+            body, (spot, owned, behind, ahead, sections), [(CHIPS, 16 * total, 128)], name="hand_out"
         )
-        return behind, ahead, sections, links.block(packets)
-
-    behind, ahead, sections, around_us = windows(owned, ITEMS[0])
-    fresh, begin, up, down, kept2, coefs = links.call(
+        parcels = links.block(parcels)
+        return owned, behind, ahead, sections, parcels, links.swap_inner(parcels)
+
+    inner, outer, kept = links.call(
+        first_kernel, (spot, initial, coeff, guess), [(96, 128), (96, 128), (4,) + coarse], [(256, 128)], name="first"
+    )
+    inner, outer, received = links.together(links.swap_inner(inner), links.swap_outer(outer), links.onward(guess))
+    owned, mine, started = links.call(
+        complete_first, (spot, inner, outer, kept), [(64, 128), (16, 128), (6,) + coarse], [(128, 128)],
+        name="complete_first",
+    )
+    fresh, begin, inner, outer, kept2, coefs = links.call(
         finish_first,
-        (spot, owned, behind, ahead, sections, around_us, started, kept, below, above, initial, coeff, guess, received),
+        (spot, *windows(owned, mine, ITEMS[0]), started, kept, inner, outer, initial, coeff, guess, received),
         [(2, 2, 64, 128), (2, 64, 128), (144, 128), (144, 128), (5,) + coarse, (15,) + coarse],
         work + [(448, 128)],
         name="finish_first",
     )
-    below, above = links.shift(up, 1), links.shift(down, -1)
-    below, above, received = links.together(below, above, links.onward(fresh[1]))
-    owned, kept_k = links.call(
-        complete_second, (spot, below, above, kept2, started, kept), [(48, 128), (2,) + coarse], [(256, 128)],
+    inner, outer, received = links.together(links.swap_inner(inner), links.swap_outer(outer), links.onward(fresh[1]))
+    owned, mine, kept_k = links.call(
+        complete_second, (spot, inner, outer, kept2, started, kept), [(48, 128), (16, 128), (2,) + coarse], [(256, 128)],
         name="complete_second",
     )
-    behind, ahead, sections, around_us = windows(owned, ITEMS[1])
     fine, coarse_end = links.call(
         finish_second,
-        (spot, owned, behind, ahead, sections, around_us, started, kept2, kept_k, below, above, initial, coeff, begin, fresh,
+        (spot, *windows(owned, mine, ITEMS[1]), started, kept2, kept_k, inner, outer, initial, coeff, begin, fresh,
          received, coefs),
         [(2, 2, 64, 128), (32, 64)],
         work + [(448, 128)],
@@ -423,9 +472,9 @@
 
 def solution(mesh):
     split = Mesh(
-        mesh.devices.reshape(mesh.shape["tm"], mesh.shape["space"] // BLOCK, BLOCK), ("tm", "block", "place")
-    )
-    space = ("block", "place")
+        mesh.devices.reshape(mesh.shape["tm"], mesh.shape["space"] // BLOCK, CHIPS, 2), ("tm", "block", "chip", "core")
+    )
+    space = ("block", "chip", "core")
     return jax.shard_map(
         on_device,
         mesh=split,

time: 207 us -> 194 us (0.937)
  blocking collectives: 120 us -> 93 us
  waiting for transfers between devices: 15.3 us -> 23.6 us
  starting transfers between devices: 47 us -> 53.1 us
    all_to_all x2, blocking collectives: 70.5 us -> 43.6 us  [block(): return lax.all_to_all(x, 'chip', 0, 0)]
    ppermute x8 -> x10, waiting for transfers between devices: 14 us -> 22 us  [the longest x4 15.8 us: shift(): lax.ppermute(x, ('block', 'chip', 'core'), [(i, (i + by) % n) for i in ra...]
    ppermute x8 -> x10, starting transfers between devices: 28.3 us -> 33.2 us  [the longest x4 18.4 us: shift(): lax.ppermute(x, ('block', 'chip', 'core'), [(i, (i + by) % n) for i in ra...]
  transfers between devices with their start and end apart: 10 -> 12, of which waited for: 5 -> 6; matrix products, arithmetic and copies ran while one was open for 1% -> 1% of each run, Pallas kernels for 1% -> 1%
where the time goes in v3:
time: 194 us; the launch traced here: 193 us
  blocking collectives  93 us (48%)
  starting transfers between devices  53.1 us (27%)
  waiting for transfers between devices  23.6 us (12%)
  Pallas kernels  16.7 us (9%)
  local copies, waits for them, and re-layouts  4.89 us (3%)
    all_to_all x2, blocking collectives, sections(): lax.all_to_all(jnp.broadcast_to(x, (SECTIONS,) + x.shape), 'tm', 0, 0)  49.4 us
    all_to_all x2, blocking collectives, block(): return lax.all_to_all(x, 'chip', 0, 0)  43.6 us
    ppermute x2, starting transfers between devices, onward(): return lax.ppermute(x, 'tm', [(i, i + 1) for i in range(n - 1)])  19.9 us
    ppermute x4, starting transfers between devices, shift(): lax.ppermute(x, ('block', 'chip', 'core'), [(i, (i + by) % n) for i in ra...  18.4 us
    pallas_call x7, Pallas kernels, run(): pl.pallas_call(body, out_shape=[jax.ShapeDtypeStruct(shape, F32) for shap...  16.7 us
    ppermute x4, waiting for transfers between devices, shift(): lax.ppermute(x, ('block', 'chip', 'core'), [(i, (i + by) % n) for i in ra...  15.8 us
    ppermute x4, starting transfers between devices, swap_inner(): return lax.ppermute(x, 'core', [(0, 1), (1, 0)])  10.1 us
    ppermute x2, starting transfers between devices, swap_outer(): lax.ppermute(x, ('block', 'chip', 'core'), [(i, (i + 2 * (i % 2) - 1) % n...  4.83 us
  transfers between devices with their start and end apart: 12, of which 6 were waited for; matrix products, arithmetic and copies ran while one was open for 1% of the time, Pallas kernels for 1%

profile of v3, /device:TPU:1, one launch (start us, length us, event | category | flops | bytes accessed | tf_op | source)
XLA Modules:
  0.0 192.9 jit_solution(243481248033570468)
XLA Ops:
  0.6 16.3 %collective-permute-start.2 = (f32[2,64,128]{2,1,0:T(8,128)}, f32[2,64,128]{2,1,0:T(8,128)S(1)}, u32[]{:S(2)}, u32[]{:S(2)}) collective-permute-start(f32[2,64,128]{2,1,0:T(8,128)} %bitcast.8), channel_id=1, source_target_pairs={{0,64},{64,128},{128,192},{192,256},{256,320},{320,384},{384,448},... | collective-permute-start | bytes 196616 | tf_op jit(solution)/shard_map/ppermute | solution.py:403
  16.9 0.7 pad_add_fusion.spot
  17.6 1.8 first.1
  19.4 2.8 %collective-permute-start = (f32[96,128]{1,0:T(8,128)}, f32[96,128]{1,0:T(8,128)S(1)}, u32[]{:S(2)}, u32[]{:S(2)}) collective-permute-start(f32[96,128]{1,0:T(8,128)} %get-tuple-element.25), channel_id=1, source_target_pairs={{0,1},{1,0},{2,3},{3,2},{4,5},{5,4},{6,7},{7,6},{8,9},{9,8},{10,11... | collective-permute-start | bytes 147464 | tf_op jit(solution)/shard_map/ppermute | solution.py:393
  22.3 2.5 %collective-permute-start.1 = (f32[96,128]{1,0:T(8,128)}, f32[96,128]{1,0:T(8,128)S(1)}, u32[]{:S(2)}, u32[]{:S(2)}) collective-permute-start(f32[96,128]{1,0:T(8,128)} %get-tuple-element.26), channel_id=1, source_target_pairs={{0,63},{1,2},{2,1},{3,4},{4,3},{5,6},{6,5},{7,8},{8,7},{9,10},{10,... | collective-permute-start | bytes 147464 | tf_op jit(solution)/shard_map/ppermute | solution.py:398
  24.8 0.0 collective-permute-done.inner
  24.9 3.0 %collective-permute-done.1.outer = f32[96,128]{1,0:T(8,128)S(1)} collective-permute-done((f32[96,128]{1,0:T(8,128)}, f32[96,128]{1,0:T(8,128)S(1)}, u32[]{:S(2)}, u32[]{:S(2)}) %collective-permute-start.1) | collective-permute-done | bytes 49184 | tf_op jit(solution)/shard_map/ppermute | solution.py:398
  27.9 0.0 collective-permute-done.2.received
  27.9 0.6 copy-done.7
  28.5 1.7 complete_first.1
  30.3 6.7 %collective-permute-start.4 = (f32[64,128]{1,0:T(8,128)}, f32[64,128]{1,0:T(8,128)S(1)}, u32[]{:S(2)}, u32[]{:S(2)}) collective-permute-start(f32[64,128]{1,0:T(8,128)} %get-tuple-element.30.owned), channel_id=1, source_target_pairs={{0,56},{1,57},{2,58},{3,59},{4,60},{5,61},{6,62},{7,63},{8,0},{9,1... | collective-permute-start | bytes 98312 | tf_op jit(solution)/shard_map/ppermute | solution.py:389
  37.0 2.4 %collective-permute-start.3 = (f32[64,128]{1,0:T(8,128)}, f32[64,128]{1,0:T(8,128)S(1)}, u32[]{:S(2)}, u32[]{:S(2)}) collective-permute-start(f32[64,128]{1,0:T(8,128)} %get-tuple-element.30.owned), channel_id=1, source_target_pairs={{0,8},{1,9},{2,10},{3,11},{4,12},{5,13},{6,14},{7,15},{8,16},{9,17... | collective-permute-start | bytes 98312 | tf_op jit(solution)/shard_map/ppermute | solution.py:389
  39.5 0.0 collective-permute-done.4.ahead
  39.5 0.0 copy-start.15
  39.5 10.2 %collective-permute-done.3.behind = f32[64,128]{1,0:T(8,128)S(1)} collective-permute-done((f32[64,128]{1,0:T(8,128)}, f32[64,128]{1,0:T(8,128)S(1)}, u32[]{:S(2)}, u32[]{:S(2)}) %collective-permute-start.3) | collective-permute-done | bytes 32800 | tf_op jit(solution)/shard_map/ppermute | solution.py:389
  49.8 0.0 copy-done.8
  49.8 0.6 copy-done.9
  50.4 18.8 %all_to_all.20.sections = f32[8,48,128]{2,1,0:T(8,128)} all-to-all(f32[8,48,128]{2,1,0:T(8,128)S(1)} %broadcast_in_dim.12), channel_id=1, replica_groups=mesh['tm'=8,'block'=8,'chip'=4,'core'=2] {'tm'}, dimensions={0} | all-to-all | bytes 393216 | tf_op jit(solution)/shard_map/all_to_all | solution.py:407
  69.2 1.9 hand_out.2
  71.1 24.0 %all_to_all.21.windows = f32[4,224,128]{2,1,0:T(8,128)S(1)} all-to-all(f32[4,224,128]{2,1,0:T(8,128)} %hand_out.2), channel_id=1, replica_groups=mesh['tm'=8,'block'=8,'chip'=4,'core'=2] {'chip'}, dimensions={0} | all-to-all | bytes 917504 | tf_op jit(solution)/shard_map/all_to_all | solution.py:411
  95.1 1.9 collective-permute-start.5
  97.0 1.8 collective-permute-done.5.swapped
  98.8 0.8 copy-done.2
  99.6 4.0 %finish_first.1 = (f32[2,2,64,128]{3,2,1,0:T(8,128)}, f32[2,64,128]{2,1,0:T(8,128)}, f32[144,128]{1,0:T(8,128)}, f32[144,128]{1,0:T(8,128)}, f32[5,32,128]{2,1,0:T(8,128)}, /*index=5*/f32[15,32,128]{2,1,0:T(8,128)}) custom-call(s32[3]{0:T(128)} %pad_add_fusion.spot, f32[64,128]{1,0:T(8,128)} %get-tuple-element.30.owned, f32[64,128]{1,0:T(8,128)} %copy-done.9, ...), custom_call_target="tpu_custom_call" | custom-call | tf_op jit(solution)/shard_map/finish_first/pallas_call | solution.py:369
  103.5 2.0 %collective-permute-start.6 = (f32[144,128]{1,0:T(8,128)}, f32[144,128]{1,0:T(8,128)S(1)}, u32[]{:S(2)}, u32[]{:S(2)}) collective-permute-start(f32[144,128]{1,0:T(8,128)} %get-tuple-element.34), channel_id=1, source_target_pairs={{0,1},{1,0},{2,3},{3,2},{4,5},{5,4},{6,7},{7,6},{8,9},{9,8},{10,11... | collective-permute-start | bytes 221192 | tf_op jit(solution)/shard_map/ppermute | solution.py:393
  105.6 2.3 %collective-permute-start.7 = (f32[144,128]{1,0:T(8,128)}, f32[144,128]{1,0:T(8,128)S(1)}, u32[]{:S(2)}, u32[]{:S(2)}) collective-permute-start(f32[144,128]{1,0:T(8,128)} %get-tuple-element.35), channel_id=1, source_target_pairs={{0,63},{1,2},{2,1},{3,4},{4,3},{5,6},{6,5},{7,8},{8,7},{9,10},{10,... | collective-permute-start | bytes 221192 | tf_op jit(solution)/shard_map/ppermute | solution.py:398
  107.8 0.8 slice_bitcast_fusion
  108.7 3.6 %collective-permute-start.8 = (f32[2,64,128]{2,1,0:T(8,128)S(1)}, f32[2,64,128]{2,1,0:T(8,128)S(1)}, u32[]{:S(2)}, u32[]{:S(2)}) collective-permute-start(f32[2,64,128]{2,1,0:T(8,128)S(1)} %slice_bitcast_fusion), channel_id=1, source_target_pairs={{0,64},{64,128},{128,192},{192,256},{256,320},{320,384},{384,448},... | collective-permute-start | bytes 196616 | tf_op jit(solution)/shard_map/ppermute | solution.py:403
  112.3 1.6 collective-permute-done.8.received
  113.9 0.0 collective-permute-done.6.inner
  113.9 0.0 collective-permute-done.7.outer
  113.9 0.6 copy-done.4
  114.6 0.0 copy-done.5
  114.6 1.9 complete_second.1
  116.5 3.6 %collective-permute-start.10 = (f32[48,128]{1,0:T(8,128)}, f32[48,128]{1,0:T(8,128)S(1)}, u32[]{:S(2)}, u32[]{:S(2)}) collective-permute-start(f32[48,128]{1,0:T(8,128)} %get-tuple-element.40.owned), channel_id=1, source_target_pairs={{0,56},{1,57},{2,58},{3,59},{4,60},{5,61},{6,62},{7,63},{8,0},{9,1... | collective-permute-start | bytes 73736 | tf_op jit(solution)/shard_map/ppermute | solution.py:389
  120.1 5.6 %collective-permute-start.9 = (f32[48,128]{1,0:T(8,128)}, f32[48,128]{1,0:T(8,128)S(1)}, u32[]{:S(2)}, u32[]{:S(2)}) collective-permute-start(f32[48,128]{1,0:T(8,128)} %get-tuple-element.40.owned), channel_id=1, source_target_pairs={{0,8},{1,9},{2,10},{3,11},{4,12},{5,13},{6,14},{7,15},{8,16},{9,17... | collective-permute-start | bytes 73736 | tf_op jit(solution)/shard_map/ppermute | solution.py:389
  125.7 0.0 collective-permute-done.10.ahead
  125.7 0.0 copy-start.10
  125.7 0.0 copy-start.14
  125.7 5.6 %collective-permute-done.9.behind = f32[48,128]{1,0:T(8,128)S(1)} collective-permute-done((f32[48,128]{1,0:T(8,128)}, f32[48,128]{1,0:T(8,128)S(1)}, u32[]{:S(2)}, u32[]{:S(2)}) %collective-permute-start.9) | collective-permute-done | bytes 24608 | tf_op jit(solution)/shard_map/ppermute | solution.py:389
  131.3 0.6 copy-done.11
  131.9 30.6 %all_to_all.22.sections = f32[8,48,128]{2,1,0:T(8,128)} all-to-all(f32[8,48,128]{2,1,0:T(8,128)S(1)} %broadcast_in_dim.13), channel_id=1, replica_groups=mesh['tm'=8,'block'=8,'chip'=4,'core'=2] {'tm'}, dimensions={0} | all-to-all | bytes 393216 | tf_op jit(solution)/shard_map/all_to_all | solution.py:407
  162.5 1.9 hand_out.3
  164.4 19.6 %all_to_all.23.windows = f32[4,192,128]{2,1,0:T(8,128)S(1)} all-to-all(f32[4,192,128]{2,1,0:T(8,128)} %hand_out.3), channel_id=1, replica_groups=mesh['tm'=8,'block'=8,'chip'=4,'core'=2] {'chip'}, dimensions={0} | all-to-all | bytes 786432 | tf_op jit(solution)/shard_map/all_to_all | solution.py:411
  183.9 3.3 %collective-permute-start.11 = (f32[4,192,128]{2,1,0:T(8,128)S(1)}, f32[4,192,128]{2,1,0:T(8,128)S(1)}, u32[]{:S(2)}, u32[]{:S(2)}) collective-permute-start(f32[4,192,128]{2,1,0:T(8,128)S(1)} %all_to_all.23.windows), channel_id=1, source_target_pairs={{0,1},{1,0},{2,3},{3,2},{4,5},{5,4},{6,7},{7,6},{8,9},{9,8},{10,11... | collective-permute-start | bytes 1179656 | tf_op jit(solution)/shard_map/ppermute | solution.py:393
  187.2 1.3 collective-permute-done.11.swapped
  188.6 0.8 copy-done.3
  189.3 3.6 %finish_second.1 = (f32[2,2,64,128]{3,2,1,0:T(8,128)}, f32[32,64]{1,0:T(8,128)}) custom-call(s32[3]{0:T(128)} %pad_add_fusion.spot, f32[48,128]{1,0:T(8,128)} %get-tuple-element.40.owned, f32[48,128]{1,0:T(8,128)} %copy-done.11, f32[48,128]{1,0:T(8,128)} %copy-done.10, f32[8,48,128]{2,1,0:T(8,128)} %all_to_all.22.sections, f32[4,192,128]{2,1,0:T(8,128)} %copy-done.1, ...), custom_call_target="tpu_custom_call" | custom-call | tf_op jit(solution)/shard_map/finish_second/pallas_call | solution.py:369
  (29 shorter events, 0.1 us)
Async XLA Ops:
  0.6 27.3 %collective-permute-start.2 = (f32[2,64,128]{2,1,0:T(8,128)}, f32[2,64,128]{2,1,0:T(8,128)S(1)}, u32[]{:S(2)}, u32[]{:S(2)}) collective-permute-start(f32[2,64,128]{2,1,0:T(8,128)} %bitcast.8), channel_id=1, source_target_pairs={{0,64},{64,128},{128,192},{192,256},{256,320},{320,384},{384,448},... | collective-permute-start | bytes 196616 | tf_op jit(solution)/shard_map/ppermute | solution.py:403
  19.4 5.4 %collective-permute-start = (f32[96,128]{1,0:T(8,128)}, f32[96,128]{1,0:T(8,128)S(1)}, u32[]{:S(2)}, u32[]{:S(2)}) collective-permute-start(f32[96,128]{1,0:T(8,128)} %get-tuple-element.25), channel_id=1, source_target_pairs={{0,1},{1,0},{2,3},{3,2},{4,5},{5,4},{6,7},{7,6},{8,9},{9,8},{10,11... | collective-permute-start | bytes 147464 | tf_op jit(solution)/shard_map/ppermute | solution.py:393
  22.3 5.6 %collective-permute-start.1 = (f32[96,128]{1,0:T(8,128)}, f32[96,128]{1,0:T(8,128)S(1)}, u32[]{:S(2)}, u32[]{:S(2)}) collective-permute-start(f32[96,128]{1,0:T(8,128)} %get-tuple-element.26), channel_id=1, source_target_pairs={{0,63},{1,2},{2,1},{3,4},{4,3},{5,6},{6,5},{7,8},{8,7},{9,10},{10,... | collective-permute-start | bytes 147464 | tf_op jit(solution)/shard_map/ppermute | solution.py:398
  24.8 3.1 %copy-start.6 = (f32[96,128]{1,0:T(8,128)}, f32[96,128]{1,0:T(8,128)S(1)}, u32[]{:S(2)}) copy-start(f32[96,128]{1,0:T(8,128)S(1)} %collective-permute-done.inner) | copy-start | bytes 147460
  27.9 0.6 copy-start.7
  27.9 2.4 %copy-start.12 = (f32[2,64,128]{2,1,0:T(8,128)}, f32[2,64,128]{2,1,0:T(8,128)S(1)}, u32[]{:S(2)}) copy-start(f32[2,64,128]{2,1,0:T(8,128)S(1)} %collective-permute-done.2.received) | copy-start | bytes 196612
  30.3 9.2 %collective-permute-start.4 = (f32[64,128]{1,0:T(8,128)}, f32[64,128]{1,0:T(8,128)S(1)}, u32[]{:S(2)}, u32[]{:S(2)}) collective-permute-start(f32[64,128]{1,0:T(8,128)} %get-tuple-element.30.owned), channel_id=1, source_target_pairs={{0,56},{1,57},{2,58},{3,59},{4,60},{5,61},{6,62},{7,63},{8,0},{9,1... | collective-permute-start | bytes 98312 | tf_op jit(solution)/shard_map/ppermute | solution.py:389
  37.0 12.7 %collective-permute-start.3 = (f32[64,128]{1,0:T(8,128)}, f32[64,128]{1,0:T(8,128)S(1)}, u32[]{:S(2)}, u32[]{:S(2)}) collective-permute-start(f32[64,128]{1,0:T(8,128)} %get-tuple-element.30.owned), channel_id=1, source_target_pairs={{0,8},{1,9},{2,10},{3,11},{4,12},{5,13},{6,14},{7,15},{8,16},{9,17... | collective-permute-start | bytes 98312 | tf_op jit(solution)/shard_map/ppermute | solution.py:389
  39.5 10.3 %copy-start.8 = (f32[64,128]{1,0:T(8,128)}, f32[64,128]{1,0:T(8,128)S(1)}, u32[]{:S(2)}) copy-start(f32[64,128]{1,0:T(8,128)S(1)} %collective-permute-done.4.ahead) | copy-start | bytes 98308
  39.5 10.3 %copy-start.15 = (f32[16,128]{1,0:T(8,128)S(1)}, f32[16,128]{1,0:T(8,128)}, u32[]{:S(2)}) copy-start(f32[16,128]{1,0:T(8,128)} %get-tuple-element.31) | copy-start | bytes 24580
  49.8 0.6 copy-start.9
  95.1 3.7 %copy-start = (f32[4,224,128]{2,1,0:T(8,128)}, f32[4,224,128]{2,1,0:T(8,128)S(1)}, u32[]{:S(2)}) copy-start(f32[4,224,128]{2,1,0:T(8,128)S(1)} %all_to_all.21.windows) | copy-start | bytes 1376260
  95.1 3.7 %collective-permute-start.5 = (f32[4,224,128]{2,1,0:T(8,128)S(1)}, f32[4,224,128]{2,1,0:T(8,128)S(1)}, u32[]{:S(2)}, u32[]{:S(2)}) collective-permute-start(f32[4,224,128]{2,1,0:T(8,128)S(1)} %all_to_all.21.windows), channel_id=1, source_target_pairs={{0,1},{1,0},{2,3},{3,2},{4,5},{5,4},{6,7},{7,6},{8,9},{9,8},{10,11... | collective-permute-start | bytes 1376264 | tf_op jit(solution)/shard_map/ppermute | solution.py:393
  98.8 0.8 copy-start.2
  103.5 10.4 %collective-permute-start.6 = (f32[144,128]{1,0:T(8,128)}, f32[144,128]{1,0:T(8,128)S(1)}, u32[]{:S(2)}, u32[]{:S(2)}) collective-permute-start(f32[144,128]{1,0:T(8,128)} %get-tuple-element.34), channel_id=1, source_target_pairs={{0,1},{1,0},{2,3},{3,2},{4,5},{5,4},{6,7},{7,6},{8,9},{9,8},{10,11... | collective-permute-start | bytes 221192 | tf_op jit(solution)/shard_map/ppermute | solution.py:393
  105.6 8.4 %collective-permute-start.7 = (f32[144,128]{1,0:T(8,128)}, f32[144,128]{1,0:T(8,128)S(1)}, u32[]{:S(2)}, u32[]{:S(2)}) collective-permute-start(f32[144,128]{1,0:T(8,128)} %get-tuple-element.35), channel_id=1, source_target_pairs={{0,63},{1,2},{2,1},{3,4},{4,3},{5,6},{6,5},{7,8},{8,7},{9,10},{10,... | collective-permute-start | bytes 221192 | tf_op jit(solution)/shard_map/ppermute | solution.py:398
  108.7 5.2 %collective-permute-start.8 = (f32[2,64,128]{2,1,0:T(8,128)S(1)}, f32[2,64,128]{2,1,0:T(8,128)S(1)}, u32[]{:S(2)}, u32[]{:S(2)}) collective-permute-start(f32[2,64,128]{2,1,0:T(8,128)S(1)} %slice_bitcast_fusion), channel_id=1, source_target_pairs={{0,64},{64,128},{128,192},{192,256},{256,320},{320,384},{384,448},... | collective-permute-start | bytes 196616 | tf_op jit(solution)/shard_map/ppermute | solution.py:403
  113.9 2.5 %copy-start.13 = (f32[2,64,128]{2,1,0:T(8,128)}, f32[2,64,128]{2,1,0:T(8,128)S(1)}, u32[]{:S(2)}) copy-start(f32[2,64,128]{2,1,0:T(8,128)S(1)} %collective-permute-done.8.received) | copy-start | bytes 196612
  113.9 0.6 copy-start.4
  113.9 0.7 copy-start.5
  116.5 9.2 %collective-permute-start.10 = (f32[48,128]{1,0:T(8,128)}, f32[48,128]{1,0:T(8,128)S(1)}, u32[]{:S(2)}, u32[]{:S(2)}) collective-permute-start(f32[48,128]{1,0:T(8,128)} %get-tuple-element.40.owned), channel_id=1, source_target_pairs={{0,56},{1,57},{2,58},{3,59},{4,60},{5,61},{6,62},{7,63},{8,0},{9,1... | collective-permute-start | bytes 73736 | tf_op jit(solution)/shard_map/ppermute | solution.py:389
  120.1 11.2 %collective-permute-start.9 = (f32[48,128]{1,0:T(8,128)}, f32[48,128]{1,0:T(8,128)S(1)}, u32[]{:S(2)}, u32[]{:S(2)}) collective-permute-start(f32[48,128]{1,0:T(8,128)} %get-tuple-element.40.owned), channel_id=1, source_target_pairs={{0,8},{1,9},{2,10},{3,11},{4,12},{5,13},{6,14},{7,15},{8,16},{9,17... | collective-permute-start | bytes 73736 | tf_op jit(solution)/shard_map/ppermute | solution.py:389
  125.7 5.6 %copy-start.10 = (f32[48,128]{1,0:T(8,128)}, f32[48,128]{1,0:T(8,128)S(1)}, u32[]{:S(2)}) copy-start(f32[48,128]{1,0:T(8,128)S(1)} %collective-permute-done.10.ahead) | copy-start | bytes 73732
  125.7 5.6 %copy-start.14 = (f32[16,128]{1,0:T(8,128)S(1)}, f32[16,128]{1,0:T(8,128)}, u32[]{:S(2)}) copy-start(f32[16,128]{1,0:T(8,128)} %get-tuple-element.41) | copy-start | bytes 24580
  131.3 0.6 copy-start.11
  183.9 4.6 %copy-start.1 = (f32[4,192,128]{2,1,0:T(8,128)}, f32[4,192,128]{2,1,0:T(8,128)S(1)}, u32[]{:S(2)}) copy-start(f32[4,192,128]{2,1,0:T(8,128)S(1)} %all_to_all.23.windows) | copy-start | bytes 1179652
  183.9 4.6 %collective-permute-start.11 = (f32[4,192,128]{2,1,0:T(8,128)S(1)}, f32[4,192,128]{2,1,0:T(8,128)S(1)}, u32[]{:S(2)}, u32[]{:S(2)}) collective-permute-start(f32[4,192,128]{2,1,0:T(8,128)S(1)} %all_to_all.23.windows), channel_id=1, source_target_pairs={{0,1},{1,0},{2,3},{3,2},{4,5},{5,4},{6,7},{7,6},{8,9},{9,8},{10,11... | collective-permute-start | bytes 1179656 | tf_op jit(solution)/shard_map/ppermute | solution.py:393
  188.5 0.8 copy-start.3

commit v4 on v3

--- a/solution.py
+++ b/solution.py
@@ -362,18 +362,18 @@
     coarse_out[...] = end[:, :64]
 
 
-def run(body, args, outs, scratch=(), name=None):
+def run(body, args, outs, scratch=(), name=None, last=False):
     scalars = args[0].dtype == jnp.int32
     specs = [pl.BlockSpec(memory_space=pltpu.SMEM)] if scalars else []
     specs += [pl.BlockSpec(memory_space=pltpu.VMEM)] * (len(args) - len(specs))
     return pl.pallas_call(
         body,
-        out_shape=[jax.ShapeDtypeStruct(shape, F32) for shape in outs],
+        out_shape=[jax.ShapeDtypeStruct(shape, F32) if last else pltpu.VMEM(shape, F32) for shape in outs],
         in_specs=specs,
         out_specs=[pl.BlockSpec(memory_space=pltpu.VMEM)] * len(outs),
         scratch_shapes=[pltpu.VMEM(shape, F32) for shape in scratch],
         name=name,
-    )(*args)
+    )(*(a if a.dtype == jnp.int32 else pltpu.with_memory_space_constraint(a, pltpu.VMEM) for a in args))
 
 
 class Links:
@@ -461,6 +461,7 @@
         [(2, 2, 64, 128), (32, 64)],
         work + [(448, 128)],
         name="finish_second",
+        last=True,
     )
     return fine, coarse_end
 

time: 194 us -> 183 us (0.943)
  Pallas kernels: 16.7 us -> 9.4 us
  local copies, waits for them, and re-layouts: 4.89 us -> 2.59 us
    pallas_call x7, Pallas kernels: 16.7 us -> 9.4 us  [run(): pl.pallas_call(body, out_shape=[jax.ShapeDtypeStruct(shape, F32) if last...]
    unnamed x32 -> x16, local copies, waits for them, and re-layouts: 4.01 us -> 2.54 us
  transfers between devices with their start and end apart: 12 -> 12, of which waited for: 6 -> 6; matrix products, arithmetic and copies ran while one was open for 1% -> 0% of each run, Pallas kernels for 1% -> 1%
where the time goes in v4:
time: 183 us; the launch traced here: 182 us
  blocking collectives  91.9 us (50%)
  starting transfers between devices  54.1 us (30%)
  waiting for transfers between devices  22.2 us (12%)
  Pallas kernels  9.4 us (5%)
  local copies, waits for them, and re-layouts  2.59 us (1%)
    all_to_all x2, blocking collectives, sections(): lax.all_to_all(jnp.broadcast_to(x, (SECTIONS,) + x.shape), 'tm', 0, 0)  49.6 us
    all_to_all x2, blocking collectives, block(): return lax.all_to_all(x, 'chip', 0, 0)  42.4 us
    ppermute x2, starting transfers between devices, onward(): return lax.ppermute(x, 'tm', [(i, i + 1) for i in range(n - 1)])  20 us
    ppermute x4, starting transfers between devices, shift(): lax.ppermute(x, ('block', 'chip', 'core'), [(i, (i + by) % n) for i in ra...  18.4 us
    ppermute x4, waiting for transfers between devices, shift(): lax.ppermute(x, ('block', 'chip', 'core'), [(i, (i + by) % n) for i in ra...  14.7 us
    ppermute x4, starting transfers between devices, swap_inner(): return lax.ppermute(x, 'core', [(0, 1), (1, 0)])  10.8 us
    pallas_call x7, Pallas kernels, run(): pl.pallas_call(body, out_shape=[jax.ShapeDtypeStruct(shape, F32) if last...  9.4 us
    ppermute x2, starting transfers between devices, swap_outer(): lax.ppermute(x, ('block', 'chip', 'core'), [(i, (i + 2 * (i % 2) - 1) % n...  4.85 us
  transfers between devices with their start and end apart: 12, of which 6 were waited for; matrix products, arithmetic and copies ran while one was open for 0% of the time, Pallas kernels for 1%

profile of v4, /device:TPU:1, one launch (start us, length us, event | category | flops | bytes accessed | tf_op | source)
XLA Modules:
  0.0 181.7 jit_solution(4052441464198619868)
XLA Ops:
  0.6 16.3 %collective-permute-start.2 = (f32[2,64,128]{2,1,0:T(8,128)}, f32[2,64,128]{2,1,0:T(8,128)S(1)}, u32[]{:S(2)}, u32[]{:S(2)}) collective-permute-start(f32[2,64,128]{2,1,0:T(8,128)} %bitcast.8), channel_id=1, source_target_pairs={{0,64},{64,128},{128,192},{192,256},{256,320},{320,384},{384,448},... | collective-permute-start | bytes 196616 | tf_op jit(solution)/shard_map/ppermute | solution.py:403
  16.9 0.6 pad_add_fusion.spot
  17.5 0.8 copy-done
  18.4 0.8 copy-done.2
  19.2 0.8 copy-done.4
  20.0 0.9 first.1
  21.0 2.9 %collective-permute-start = (f32[96,128]{1,0:T(8,128)S(1)}, f32[96,128]{1,0:T(8,128)S(1)}, u32[]{:S(2)}, u32[]{:S(2)}) collective-permute-start(f32[96,128]{1,0:T(8,128)S(1)} %get-tuple-element.25), channel_id=1, source_target_pairs={{0,1},{1,0},{2,3},{3,2},{4,5},{5,4},{6,7},{7,6},{8,9},{9,8},{10,11... | collective-permute-start | bytes 147464 | tf_op jit(solution)/shard_map/ppermute | solution.py:393
  23.9 2.5 %collective-permute-start.1 = (f32[96,128]{1,0:T(8,128)S(1)}, f32[96,128]{1,0:T(8,128)S(1)}, u32[]{:S(2)}, u32[]{:S(2)}) collective-permute-start(f32[96,128]{1,0:T(8,128)S(1)} %get-tuple-element.26), channel_id=1, source_target_pairs={{0,63},{1,2},{2,1},{3,4},{4,3},{5,6},{6,5},{7,8},{8,7},{9,10},{10,... | collective-permute-start | bytes 147464 | tf_op jit(solution)/shard_map/ppermute | solution.py:398
  26.4 0.0 collective-permute-done.inner
  26.4 2.8 %collective-permute-done.1.outer = f32[96,128]{1,0:T(8,128)S(1)} collective-permute-done((f32[96,128]{1,0:T(8,128)S(1)}, f32[96,128]{1,0:T(8,128)S(1)}, u32[]{:S(2)}, u32[]{:S(2)}) %collective-permute-start.1) | collective-permute-done | bytes 49184 | tf_op jit(solution)/shard_map/ppermute | solution.py:398
  29.3 0.0 collective-permute-done.2.received
  29.3 0.9 complete_first.1
  30.2 6.8 %collective-permute-start.4 = (f32[64,128]{1,0:T(8,128)S(1)}, f32[64,128]{1,0:T(8,128)S(1)}, u32[]{:S(2)}, u32[]{:S(2)}) collective-permute-start(f32[64,128]{1,0:T(8,128)S(1)} %get-tuple-element.30.owned), channel_id=1, source_target_pairs={{0,56},{1,57},{2,58},{3,59},{4,60},{5,61},{6,62},{7,63},{8,0},{9,1... | collective-permute-start | bytes 98312 | tf_op jit(solution)/shard_map/ppermute | solution.py:389
  36.9 2.4 %collective-permute-start.3 = (f32[64,128]{1,0:T(8,128)S(1)}, f32[64,128]{1,0:T(8,128)S(1)}, u32[]{:S(2)}, u32[]{:S(2)}) collective-permute-start(f32[64,128]{1,0:T(8,128)S(1)} %get-tuple-element.30.owned), channel_id=1, source_target_pairs={{0,8},{1,9},{2,10},{3,11},{4,12},{5,13},{6,14},{7,15},{8,16},{9,17... | collective-permute-start | bytes 98312 | tf_op jit(solution)/shard_map/ppermute | solution.py:389
  39.4 0.0 collective-permute-done.4.ahead
  39.4 10.4 %collective-permute-done.3.behind = f32[64,128]{1,0:T(8,128)S(1)} collective-permute-done((f32[64,128]{1,0:T(8,128)S(1)}, f32[64,128]{1,0:T(8,128)S(1)}, u32[]{:S(2)}, u32[]{:S(2)}) %collective-permute-start.3) | collective-permute-done | bytes 32800 | tf_op jit(solution)/shard_map/ppermute | solution.py:389
  49.8 18.4 %all_to_all.20.sections = f32[8,48,128]{2,1,0:T(8,128)S(1)} all-to-all(f32[8,48,128]{2,1,0:T(8,128)S(1)} %broadcast_in_dim.12), channel_id=1, replica_groups=mesh['tm'=8,'block'=8,'chip'=4,'core'=2] {'tm'}, dimensions={0} | all-to-all | bytes 393216 | tf_op jit(solution)/shard_map/all_to_all | solution.py:407
  68.2 0.8 hand_out.2
  69.0 0.0 copy-start.1
  69.0 0.0 copy-start.3
  69.0 0.0 copy-start.5
  69.0 23.1 %all_to_all.21.windows = f32[4,224,128]{2,1,0:T(8,128)S(1)} all-to-all(f32[4,224,128]{2,1,0:T(8,128)S(1)} %hand_out.2), channel_id=1, replica_groups=mesh['tm'=8,'block'=8,'chip'=4,'core'=2] {'chip'}, dimensions={0} | all-to-all | bytes 917504 | tf_op jit(solution)/shard_map/all_to_all | solution.py:411
  92.1 1.9 %collective-permute-start.5 = (f32[4,224,128]{2,1,0:T(8,128)S(1)}, f32[4,224,128]{2,1,0:T(8,128)S(1)}, u32[]{:S(2)}, u32[]{:S(2)}) collective-permute-start(f32[4,224,128]{2,1,0:T(8,128)S(1)} %all_to_all.21.windows), channel_id=1, source_target_pairs={{0,1},{1,0},{2,3},{3,2},{4,5},{5,4},{6,7},{7,6},{8,9},{9,8},{10,11... | collective-permute-start | bytes 1376264 | tf_op jit(solution)/shard_map/ppermute | solution.py:393
  94.0 1.8 collective-permute-done.5.swapped
  95.8 0.0 copy-done.1
  95.8 0.0 copy-done.3
  95.8 0.0 copy-done.5
  95.8 2.5 %finish_first.1 = (f32[2,2,64,128]{3,2,1,0:T(8,128)S(1)}, f32[2,64,128]{2,1,0:T(8,128)S(1)}, f32[144,128]{1,0:T(8,128)S(1)}, f32[144,128]{1,0:T(8,128)S(1)}, f32...) custom-call(s32[3]{0:T(128)} %pad_add_fusion.spot, f32[64,128]{1,0:T(8,128)S(1)} %get-tuple-element.30.owned, ...), custom_call_target="tpu_custom_call" | custom-call | tf_op jit(solution)/shard_map/finish_first/pallas_call | solution.py:369
  98.3 0.0 copy-start.6
  98.3 2.0 %collective-permute-start.6 = (f32[144,128]{1,0:T(8,128)S(1)}, f32[144,128]{1,0:T(8,128)S(1)}, u32[]{:S(2)}, u32[]{:S(2)}) collective-permute-start(f32[144,128]{1,0:T(8,128)S(1)} %get-tuple-element.34), channel_id=1, source_target_pairs={{0,1},{1,0},{2,3},{3,2},{4,5},{5,4},{6,7},{7,6},{8,9},{9,8},{10,11... | collective-permute-start | bytes 221192 | tf_op jit(solution)/shard_map/ppermute | solution.py:393
  100.3 2.3 %collective-permute-start.7 = (f32[144,128]{1,0:T(8,128)S(1)}, f32[144,128]{1,0:T(8,128)S(1)}, u32[]{:S(2)}, u32[]{:S(2)}) collective-permute-start(f32[144,128]{1,0:T(8,128)S(1)} %get-tuple-element.35), channel_id=1, source_target_pairs={{0,63},{1,2},{2,1},{3,4},{4,3},{5,6},{6,5},{7,8},{8,7},{9,10},{10,... | collective-permute-start | bytes 221192 | tf_op jit(solution)/shard_map/ppermute | solution.py:398
  102.6 3.8 %collective-permute-start.8 = (f32[2,64,128]{2,1,0:T(8,128)S(1)}, f32[2,64,128]{2,1,0:T(8,128)S(1)}, u32[]{:S(2)}, u32[]{:S(2)}) collective-permute-start(f32[2,64,128]{2,1,0:T(8,128)S(1)} %slice_bitcast_fusion), channel_id=1, source_target_pairs={{0,64},{64,128},{128,192},{192,256},{256,320},{320,384},{384,448},... | collective-permute-start | bytes 196616 | tf_op jit(solution)/shard_map/ppermute | solution.py:403
  106.4 1.5 collective-permute-done.8.received
  107.9 0.0 collective-permute-done.6.inner
  107.9 0.0 collective-permute-done.7.outer
  107.9 0.9 complete_second.1
  108.8 0.0 copy-done.6
  108.8 2.6 %collective-permute-start.10 = (f32[48,128]{1,0:T(8,128)S(1)}, f32[48,128]{1,0:T(8,128)S(1)}, u32[]{:S(2)}, u32[]{:S(2)}) collective-permute-start(f32[48,128]{1,0:T(8,128)S(1)} %get-tuple-element.40.owned), channel_id=1, source_target_pairs={{0,56},{1,57},{2,58},{3,59},{4,60},{5,61},{6,62},{7,63},{8,0},{9,1... | collective-permute-start | bytes 73736 | tf_op jit(solution)/shard_map/ppermute | solution.py:389
  111.5 6.5 %collective-permute-start.9 = (f32[48,128]{1,0:T(8,128)S(1)}, f32[48,128]{1,0:T(8,128)S(1)}, u32[]{:S(2)}, u32[]{:S(2)}) collective-permute-start(f32[48,128]{1,0:T(8,128)S(1)} %get-tuple-element.40.owned), channel_id=1, source_target_pairs={{0,8},{1,9},{2,10},{3,11},{4,12},{5,13},{6,14},{7,15},{8,16},{9,17... | collective-permute-start | bytes 73736 | tf_op jit(solution)/shard_map/ppermute | solution.py:389
  118.0 0.0 collective-permute-done.10.ahead
  118.0 4.3 %collective-permute-done.9.behind = f32[48,128]{1,0:T(8,128)S(1)} collective-permute-done((f32[48,128]{1,0:T(8,128)S(1)}, f32[48,128]{1,0:T(8,128)S(1)}, u32[]{:S(2)}, u32[]{:S(2)}) %collective-permute-start.9) | collective-permute-done | bytes 24608 | tf_op jit(solution)/shard_map/ppermute | solution.py:389
  122.4 31.2 %all_to_all.22.sections = f32[8,48,128]{2,1,0:T(8,128)S(1)} all-to-all(f32[8,48,128]{2,1,0:T(8,128)S(1)} %broadcast_in_dim.13), channel_id=1, replica_groups=mesh['tm'=8,'block'=8,'chip'=4,'core'=2] {'tm'}, dimensions={0} | all-to-all | bytes 393216 | tf_op jit(solution)/shard_map/all_to_all | solution.py:407
  153.6 0.8 hand_out.3
  154.3 0.0 copy-start.7
  154.4 19.3 %all_to_all.23.windows = f32[4,192,128]{2,1,0:T(8,128)S(1)} all-to-all(f32[4,192,128]{2,1,0:T(8,128)S(1)} %hand_out.3), channel_id=1, replica_groups=mesh['tm'=8,'block'=8,'chip'=4,'core'=2] {'chip'}, dimensions={0} | all-to-all | bytes 786432 | tf_op jit(solution)/shard_map/all_to_all | solution.py:411
  173.6 4.1 %collective-permute-start.11 = (f32[4,192,128]{2,1,0:T(8,128)S(1)}, f32[4,192,128]{2,1,0:T(8,128)S(1)}, u32[]{:S(2)}, u32[]{:S(2)}) collective-permute-start(f32[4,192,128]{2,1,0:T(8,128)S(1)} %all_to_all.23.windows), channel_id=1, source_target_pairs={{0,1},{1,0},{2,3},{3,2},{4,5},{5,4},{6,7},{7,6},{8,9},{9,8},{10,11... | collective-permute-start | bytes 1179656 | tf_op jit(solution)/shard_map/ppermute | solution.py:393
  177.7 1.3 collective-permute-done.11.swapped
  179.0 2.7 %finish_second.1 = (f32[2,2,64,128]{3,2,1,0:T(8,128)}, f32[32,64]{1,0:T(8,128)}) custom-call(s32[3]{0:T(128)} %pad_add_fusion.spot, f32[48,128]{1,0:T(8,128)S(1)} %get-tuple-element.40.owned, f32[48,128]{1,0:T(8,128)S(1)} %collective-permute-done.9.behind, f32[48,128]{1,0:T(8,128)S(1)} %collective-permute-done.10.ahead, ...), custom_call_target="tpu_custom_call" | custom-call | tf_op jit(solution)/shard_map/finish_second/pallas_call | solution.py:369
  (13 shorter events, 0.1 us)
Async XLA Ops:
  0.6 28.6 %collective-permute-start.2 = (f32[2,64,128]{2,1,0:T(8,128)}, f32[2,64,128]{2,1,0:T(8,128)S(1)}, u32[]{:S(2)}, u32[]{:S(2)}) collective-permute-start(f32[2,64,128]{2,1,0:T(8,128)} %bitcast.8), channel_id=1, source_target_pairs={{0,64},{64,128},{128,192},{192,256},{256,320},{320,384},{384,448},... | collective-permute-start | bytes 196616 | tf_op jit(solution)/shard_map/ppermute | solution.py:403
  17.5 0.8 copy-start
  18.4 0.8 copy-start.2
  19.2 0.8 copy-start.4
  21.0 5.4 %collective-permute-start = (f32[96,128]{1,0:T(8,128)S(1)}, f32[96,128]{1,0:T(8,128)S(1)}, u32[]{:S(2)}, u32[]{:S(2)}) collective-permute-start(f32[96,128]{1,0:T(8,128)S(1)} %get-tuple-element.25), channel_id=1, source_target_pairs={{0,1},{1,0},{2,3},{3,2},{4,5},{5,4},{6,7},{7,6},{8,9},{9,8},{10,11... | collective-permute-start | bytes 147464 | tf_op jit(solution)/shard_map/ppermute | solution.py:393
  23.9 5.4 %collective-permute-start.1 = (f32[96,128]{1,0:T(8,128)S(1)}, f32[96,128]{1,0:T(8,128)S(1)}, u32[]{:S(2)}, u32[]{:S(2)}) collective-permute-start(f32[96,128]{1,0:T(8,128)S(1)} %get-tuple-element.26), channel_id=1, source_target_pairs={{0,63},{1,2},{2,1},{3,4},{4,3},{5,6},{6,5},{7,8},{8,7},{9,10},{10,... | collective-permute-start | bytes 147464 | tf_op jit(solution)/shard_map/ppermute | solution.py:398
  30.2 9.2 %collective-permute-start.4 = (f32[64,128]{1,0:T(8,128)S(1)}, f32[64,128]{1,0:T(8,128)S(1)}, u32[]{:S(2)}, u32[]{:S(2)}) collective-permute-start(f32[64,128]{1,0:T(8,128)S(1)} %get-tuple-element.30.owned), channel_id=1, source_target_pairs={{0,56},{1,57},{2,58},{3,59},{4,60},{5,61},{6,62},{7,63},{8,0},{9,1... | collective-permute-start | bytes 98312 | tf_op jit(solution)/shard_map/ppermute | solution.py:389
  36.9 12.9 %collective-permute-start.3 = (f32[64,128]{1,0:T(8,128)S(1)}, f32[64,128]{1,0:T(8,128)S(1)}, u32[]{:S(2)}, u32[]{:S(2)}) collective-permute-start(f32[64,128]{1,0:T(8,128)S(1)} %get-tuple-element.30.owned), channel_id=1, source_target_pairs={{0,8},{1,9},{2,10},{3,11},{4,12},{5,13},{6,14},{7,15},{8,16},{9,17... | collective-permute-start | bytes 98312 | tf_op jit(solution)/shard_map/ppermute | solution.py:389
  69.0 26.8 %copy-start.1 = (f32[2,64,128]{2,1,0:T(8,128)S(1)}, f32[2,64,128]{2,1,0:T(8,128)}, u32[]{:S(2)}) copy-start(f32[2,64,128]{2,1,0:T(8,128)} %initial.5) | copy-start | bytes 196612
  69.0 26.8 %copy-start.3 = (f32[2,64,128]{2,1,0:T(8,128)S(1)}, f32[2,64,128]{2,1,0:T(8,128)}, u32[]{:S(2)}) copy-start(f32[2,64,128]{2,1,0:T(8,128)} %coeff.5) | copy-start | bytes 196612
  69.0 26.8 %copy-start.5 = (f32[1,2,64,128]{3,2,1,0:T(8,128)S(1)}, f32[1,2,64,128]{3,2,1,0:T(8,128)}, u32[]{:S(2)}) copy-start(f32[1,2,64,128]{3,2,1,0:T(8,128)} %param.5) | copy-start | bytes 196612
  92.1 3.7 %collective-permute-start.5 = (f32[4,224,128]{2,1,0:T(8,128)S(1)}, f32[4,224,128]{2,1,0:T(8,128)S(1)}, u32[]{:S(2)}, u32[]{:S(2)}) collective-permute-start(f32[4,224,128]{2,1,0:T(8,128)S(1)} %all_to_all.21.windows), channel_id=1, source_target_pairs={{0,1},{1,0},{2,3},{3,2},{4,5},{5,4},{6,7},{7,6},{8,9},{9,8},{10,11... | collective-permute-start | bytes 1376264 | tf_op jit(solution)/shard_map/ppermute | solution.py:393
  98.3 10.5 %copy-start.6 = (f32[15,32,128]{2,1,0:T(8,128)}, f32[15,32,128]{2,1,0:T(8,128)S(1)}, u32[]{:S(2)}) copy-start(f32[15,32,128]{2,1,0:T(8,128)S(1)} %get-tuple-element.45.coefs) | copy-start | bytes 737284
  98.3 9.6 %collective-permute-start.6 = (f32[144,128]{1,0:T(8,128)S(1)}, f32[144,128]{1,0:T(8,128)S(1)}, u32[]{:S(2)}, u32[]{:S(2)}) collective-permute-start(f32[144,128]{1,0:T(8,128)S(1)} %get-tuple-element.34), channel_id=1, source_target_pairs={{0,1},{1,0},{2,3},{3,2},{4,5},{5,4},{6,7},{7,6},{8,9},{9,8},{10,11... | collective-permute-start | bytes 221192 | tf_op jit(solution)/shard_map/ppermute | solution.py:393
  100.3 7.6 %collective-permute-start.7 = (f32[144,128]{1,0:T(8,128)S(1)}, f32[144,128]{1,0:T(8,128)S(1)}, u32[]{:S(2)}, u32[]{:S(2)}) collective-permute-start(f32[144,128]{1,0:T(8,128)S(1)} %get-tuple-element.35), channel_id=1, source_target_pairs={{0,63},{1,2},{2,1},{3,4},{4,3},{5,6},{6,5},{7,8},{8,7},{9,10},{10,... | collective-permute-start | bytes 221192 | tf_op jit(solution)/shard_map/ppermute | solution.py:398
  102.6 5.3 %collective-permute-start.8 = (f32[2,64,128]{2,1,0:T(8,128)S(1)}, f32[2,64,128]{2,1,0:T(8,128)S(1)}, u32[]{:S(2)}, u32[]{:S(2)}) collective-permute-start(f32[2,64,128]{2,1,0:T(8,128)S(1)} %slice_bitcast_fusion), channel_id=1, source_target_pairs={{0,64},{64,128},{128,192},{192,256},{256,320},{320,384},{384,448},... | collective-permute-start | bytes 196616 | tf_op jit(solution)/shard_map/ppermute | solution.py:403
  108.8 9.2 %collective-permute-start.10 = (f32[48,128]{1,0:T(8,128)S(1)}, f32[48,128]{1,0:T(8,128)S(1)}, u32[]{:S(2)}, u32[]{:S(2)}) collective-permute-start(f32[48,128]{1,0:T(8,128)S(1)} %get-tuple-element.40.owned), channel_id=1, source_target_pairs={{0,56},{1,57},{2,58},{3,59},{4,60},{5,61},{6,62},{7,63},{8,0},{9,1... | collective-permute-start | bytes 73736 | tf_op jit(solution)/shard_map/ppermute | solution.py:389
  111.5 10.9 %collective-permute-start.9 = (f32[48,128]{1,0:T(8,128)S(1)}, f32[48,128]{1,0:T(8,128)S(1)}, u32[]{:S(2)}, u32[]{:S(2)}) collective-permute-start(f32[48,128]{1,0:T(8,128)S(1)} %get-tuple-element.40.owned), channel_id=1, source_target_pairs={{0,8},{1,9},{2,10},{3,11},{4,12},{5,13},{6,14},{7,15},{8,16},{9,17... | collective-permute-start | bytes 73736 | tf_op jit(solution)/shard_map/ppermute | solution.py:389
  154.3 24.7 %copy-start.7 = (f32[15,32,128]{2,1,0:T(8,128)S(1)}, f32[15,32,128]{2,1,0:T(8,128)}, u32[]{:S(2)}) copy-start(f32[15,32,128]{2,1,0:T(8,128)} %copy-done.6) | copy-start | bytes 737284
  173.6 5.4 %collective-permute-start.11 = (f32[4,192,128]{2,1,0:T(8,128)S(1)}, f32[4,192,128]{2,1,0:T(8,128)S(1)}, u32[]{:S(2)}, u32[]{:S(2)}) collective-permute-start(f32[4,192,128]{2,1,0:T(8,128)S(1)} %all_to_all.23.windows), channel_id=1, source_target_pairs={{0,1},{1,0},{2,3},{3,2},{4,5},{5,4},{6,7},{7,6},{8,9},{9,8},{10,11... | collective-permute-start | bytes 1179656 | tf_op jit(solution)/shard_map/ppermute | solution.py:393

commit v5 on v4

--- a/solution.py
+++ b/solution.py
@@ -191,24 +191,33 @@
     hand_over(spot, own, values, kept[2], value_sides, kept_first[2], started[2], started[3], out, mine, keep)
 
 
+def plane(spot, owned, beside, beyond, sections, side, item):
+    odd = spot[3]
+    if item < SECTIONS:
+        if side == 0:
+            return sections[item, 0:16, :]
+        at = jnp.where(odd == 1, side, 3 - side)
+        return sections[item, pl.ds(pl.multiple_of(16 * at, 16), 16), :]
+    row = {NEAR1: 16, NEAR2: 32, COEF: 48}[item]
+    if side == 0:
+        return owned[row : row + 16, :]
+    near, far = beside[row : row + 16, :], beyond[row : row + 16, :]
+    picked = jnp.full((16, 128), odd, jnp.int32) == (1 if side == 1 else 0)
+    return jnp.where(picked, near, far)
+
+
 def pack_kernel(items):
     total = slots(items)
 
-    def body(spot, owned, behind, ahead, sections, out):
+    def body(spot, owned, beside, beyond, sections, out):
         chip, core = spot[1], spot[2]
-
-        def plane(side, item):
-            if item < SECTIONS:
-                return sections[item, 16 * side : 16 * side + 16, :]
-            row = {NEAR1: 16, NEAR2: 32, COEF: 48}[item]
-            return (owned, behind, ahead)[side][row : row + 16, :]
 
         def fill(own_core, away):
             slot = 0
             for side, least in shares(own_core, away):
                 for item, reach in items:
                     if reach >= least:
-                        out[chip + away, 16 * slot : 16 * slot + 16, :] = plane(side, item)
+                        out[chip + away, 16 * slot : 16 * slot + 16, :] = plane(spot, owned, beside, beyond, sections, side, item)
                         slot += 1
 
         for own_core in (0, 1):
@@ -222,7 +231,7 @@
     return body, total
 
 
-def sweep(spot, items, owned, behind, ahead, sections, windows, swapped, coefs, started, line, history):
+def sweep(spot, items, owned, beside, beyond, sections, windows, swapped, coefs, started, line, history):
     core = spot[2]
     place = 2 * spot[1] + core
     rank = {item: i for i, (item, _) in enumerate(items)}
@@ -231,10 +240,7 @@
     def fetch(item, w):
         if w in (0, -BLOCK, BLOCK):
             side = {0: 0, -BLOCK: 1, BLOCK: 2}[w]
-            if item < SECTIONS:
-                return unpack(sections[item, 16 * side : 16 * side + 16, :])
-            row = {NEAR1: 16, NEAR2: 32, COEF: 48}[item]
-            return unpack((owned, behind, ahead)[side][row : row + 16, :])
+            return unpack(plane(spot, owned, beside, beyond, sections, side, item))
         at = place + w
         if w > 0:
             outside, least = at >= BLOCK, [max(1, BLOCK - w - i) for i in (0, 1)]
@@ -301,11 +307,11 @@
 
 
 def finish_first(
-    spot, owned, behind, ahead, sections, windows, swapped, started, kept, inner, outer, initial, coeff, guess, received,
+    spot, owned, beside, beyond, sections, windows, swapped, started, kept, inner, outer, initial, coeff, guess, received,
     fresh_out, begin_out, inner_out, outer_out, keep, coefs, line, history, scratch,
 ):
     below, above = sides(spot, inner, outer)
-    fetch = sweep(spot, ITEMS[0], owned, behind, ahead, sections, windows, swapped, coefs, started, line, history)
+    fetch = sweep(spot, ITEMS[0], owned, beside, beyond, sections, windows, swapped, coefs, started, line, history)
     begin = starting(spot, initial, received)
     u = [guess[0], guess[1]]
     c = [coeff[0], coeff[1]]
@@ -343,11 +349,11 @@
 
 
 def finish_second(
-    spot, owned, behind, ahead, sections, windows, swapped, started, kept, kept_k, inner, outer, initial, coeff, begin_in,
+    spot, owned, beside, beyond, sections, windows, swapped, started, kept, kept_k, inner, outer, initial, coeff, begin_in,
     fresh_in, received, coefs, fresh_out, coarse_out, line, history, scratch,
 ):
     below, above = sides(spot, inner, outer)
-    fetch = sweep(spot, ITEMS[1], owned, behind, ahead, sections, windows, swapped, coefs, started, line, history)
+    fetch = sweep(spot, ITEMS[1], owned, beside, beyond, sections, windows, swapped, coefs, started, line, history)
     begin = starting(spot, initial, received)
     nodes = [[begin_in[0], begin_in[1]]] + [[fresh_in[m, 0], fresh_in[m, 1]] for m in (0, 1)]
     low = [below[64 * m : 64 * m + 64, :] for m in (0, 1)]
@@ -362,31 +368,29 @@
     coarse_out[...] = end[:, :64]
 
 
-def run(body, args, outs, scratch=(), name=None, last=False):
-    scalars = args[0].dtype == jnp.int32
-    specs = [pl.BlockSpec(memory_space=pltpu.SMEM)] if scalars else []
-    specs += [pl.BlockSpec(memory_space=pltpu.VMEM)] * (len(args) - len(specs))
+def run(body, args, outs, scratch=(), name=None, first=False, last=False):
+    def placed(*refs):
+        spot = [lax.axis_index(a) for a in ("tm", "chip", "core", "block")]
+        body(spot[:3] + [spot[3] & 1], *refs)
+
     return pl.pallas_call(
-        body,
+        placed,
         out_shape=[jax.ShapeDtypeStruct(shape, F32) if last else pltpu.VMEM(shape, F32) for shape in outs],
-        in_specs=specs,
+        in_specs=[pl.BlockSpec(memory_space=pltpu.VMEM)] * len(args),
         out_specs=[pl.BlockSpec(memory_space=pltpu.VMEM)] * len(outs),
         scratch_shapes=[pltpu.VMEM(shape, F32) for shape in scratch],
         name=name,
-    )(*(a if a.dtype == jnp.int32 else pltpu.with_memory_space_constraint(a, pltpu.VMEM) for a in args))
+    )(*(a if first else pltpu.with_memory_space_constraint(a, pltpu.VMEM) for a in args))
 
 
 class Links:
     call = staticmethod(run)
 
     @staticmethod
-    def spot():
-        return jnp.stack([lax.axis_index(a) for a in ("tm", "chip", "core")]).astype(jnp.int32)
-
-    @staticmethod
-    def shift(x, by):
-        n = lax.axis_size("block") * BLOCK
-        return lax.ppermute(x, ("block", "chip", "core"), [(i, (i + by) % n) for i in range(n)])
+    def swap_block(x, row):
+        n = lax.axis_size("block")
+        pairs = [(i, i ^ 1 if row else (i + 2 * (i % 2) - 1) % n) for i in range(n)]
+        return lax.ppermute(x, "block", pairs)
 
     @staticmethod
     def swap_inner(x):
@@ -420,43 +424,43 @@
 
 
 def iterate(links, initial, coeff, guess):
-    spot = links.spot()
     coarse = (32, 128)
     work = [(2, 17) + coarse, (40,) + coarse]
 
     def windows(owned, mine, items):
-        behind, ahead = links.shift(owned, BLOCK), links.shift(owned, -BLOCK)
-        sections = links.sections(links.stack(mine, behind, ahead))
+        beside, beyond = links.swap_block(owned, True), links.swap_block(owned, False)
+        sections = links.sections(links.stack(mine, beside, beyond))
         body, total = pack_kernel(items)
         (parcels,) = links.call(
-            body, (spot, owned, behind, ahead, sections), [(CHIPS, 16 * total, 128)], name="hand_out"
+            body, (owned, beside, beyond, sections), [(CHIPS, 16 * total, 128)], name="hand_out"
         )
         parcels = links.block(parcels)
-        return owned, behind, ahead, sections, parcels, links.swap_inner(parcels)
+        return owned, beside, beyond, sections, parcels, links.swap_inner(parcels)
 
     inner, outer, kept = links.call(
-        first_kernel, (spot, initial, coeff, guess), [(96, 128), (96, 128), (4,) + coarse], [(256, 128)], name="first"
+        first_kernel, (initial, coeff, guess), [(96, 128), (96, 128), (4,) + coarse], [(256, 128)], name="first",
+        first=True,
     )
     inner, outer, received = links.together(links.swap_inner(inner), links.swap_outer(outer), links.onward(guess))
     owned, mine, started = links.call(
-        complete_first, (spot, inner, outer, kept), [(64, 128), (16, 128), (6,) + coarse], [(128, 128)],
+        complete_first, (inner, outer, kept), [(64, 128), (16, 128), (6,) + coarse], [(128, 128)],
         name="complete_first",
     )
     fresh, begin, inner, outer, kept2, coefs = links.call(
         finish_first,
-        (spot, *windows(owned, mine, ITEMS[0]), started, kept, inner, outer, initial, coeff, guess, received),
+        (*windows(owned, mine, ITEMS[0]), started, kept, inner, outer, initial, coeff, guess, received),
         [(2, 2, 64, 128), (2, 64, 128), (144, 128), (144, 128), (5,) + coarse, (15,) + coarse],
         work + [(448, 128)],
         name="finish_first",
     )
     inner, outer, received = links.together(links.swap_inner(inner), links.swap_outer(outer), links.onward(fresh[1]))
     owned, mine, kept_k = links.call(
-        complete_second, (spot, inner, outer, kept2, started, kept), [(48, 128), (16, 128), (2,) + coarse], [(256, 128)],
+        complete_second, (inner, outer, kept2, started, kept), [(48, 128), (16, 128), (2,) + coarse], [(256, 128)],
         name="complete_second",
     )
     fine, coarse_end = links.call(
         finish_second,
-        (spot, *windows(owned, mine, ITEMS[1]), started, kept2, kept_k, inner, outer, initial, coeff, begin, fresh,
+        (*windows(owned, mine, ITEMS[1]), started, kept2, kept_k, inner, outer, initial, coeff, begin, fresh,
          received, coefs),
         [(2, 2, 64, 128), (32, 64)],
         work + [(448, 128)],

time: 183 us -> 174 us (0.951)
  waiting for transfers between devices: 22.2 us -> 17 us
  blocking collectives: 91.9 us -> 96.3 us
  Pallas kernels: 9.4 us -> 5.55 us
  local copies, waits for them, and re-layouts: 2.59 us -> 0.07 us
    ppermute x4, waiting for transfers between devices: 14.7 us -> 9.72 us  [swap_block(): return lax.ppermute(x, 'block', pairs)]
    pallas_call x7, Pallas kernels: 9.4 us -> 5.55 us  [run(): pl.pallas_call(placed, out_shape=[jax.ShapeDtypeStruct(shape, F32) if las...]
    all_to_all x2, blocking collectives: 42.4 us -> 46.2 us  [block(): return lax.all_to_all(x, 'chip', 0, 0)]
    unnamed x16 -> x10, local copies, waits for them, and re-layouts: 2.54 us -> 0.03 us
  transfers between devices with their start and end apart: 12 -> 12, of which waited for: 6 -> 8; matrix products, arithmetic and copies ran while one was open for 0% -> 0% of each run, Pallas kernels for 1% -> 1%
where the time goes in v5:
time: 174 us
  blocking collectives  96.3 us (55%)
  starting transfers between devices  53.9 us (31%)
  waiting for transfers between devices  17 us (10%)
  Pallas kernels  5.55 us (3%)
    all_to_all x2, blocking collectives, sections(): lax.all_to_all(jnp.broadcast_to(x, (SECTIONS,) + x.shape), 'tm', 0, 0)  50.1 us
    all_to_all x2, blocking collectives, block(): return lax.all_to_all(x, 'chip', 0, 0)  46.2 us
    ppermute x2, starting transfers between devices, onward(): return lax.ppermute(x, 'tm', [(i, i + 1) for i in range(n - 1)])  19.6 us
    ppermute x4, starting transfers between devices, swap_block(): return lax.ppermute(x, 'block', pairs)  19.3 us
    ppermute x4, starting transfers between devices, swap_inner(): return lax.ppermute(x, 'core', [(0, 1), (1, 0)])  10.1 us
    ppermute x4, waiting for transfers between devices, swap_block(): return lax.ppermute(x, 'block', pairs)  9.72 us
    pallas_call x7, Pallas kernels, run(): pl.pallas_call(placed, out_shape=[jax.ShapeDtypeStruct(shape, F32) if las...  5.55 us
    ppermute x2, starting transfers between devices, swap_outer(): lax.ppermute(x, ('block', 'chip', 'core'), [(i, (i + 2 * (i % 2) - 1) % n...  4.83 us
  transfers between devices with their start and end apart: 12, of which 8 were waited for; matrix products, arithmetic and copies ran while one was open for 0% of the time, Pallas kernels for 1%

profile of v5, /device:TPU:1, one launch (start us, length us, event | category | flops | bytes accessed | tf_op | source)
XLA Modules:
  0.0 173.7 jit_solution(4631727157102859511)
XLA Ops:
  0.6 16.3 %collective-permute-start.2 = (f32[2,64,128]{2,1,0:T(8,128)}, f32[2,64,128]{2,1,0:T(8,128)S(1)}, u32[]{:S(2)}, u32[]{:S(2)}) collective-permute-start(f32[2,64,128]{2,1,0:T(8,128)} %bitcast.5), channel_id=1, source_target_pairs={{0,64},{64,128},{128,192},{192,256},{256,320},{320,384},{384,448},... | collective-permute-start | bytes 196616 | tf_op jit(solution)/shard_map/ppermute | solution.py:407
  16.9 1.2 first.1
  18.1 2.9 %collective-permute-start = (f32[96,128]{1,0:T(8,128)S(1)}, f32[96,128]{1,0:T(8,128)S(1)}, u32[]{:S(2)}, u32[]{:S(2)}) collective-permute-start(f32[96,128]{1,0:T(8,128)S(1)} %get-tuple-element.25), channel_id=1, source_target_pairs={{0,1},{1,0},{2,3},{3,2},{4,5},{5,4},{6,7},{7,6},{8,9},{9,8},{10,11... | collective-permute-start | bytes 147464 | tf_op jit(solution)/shard_map/ppermute | solution.py:397
  21.0 2.5 %collective-permute-start.1 = (f32[96,128]{1,0:T(8,128)S(1)}, f32[96,128]{1,0:T(8,128)S(1)}, u32[]{:S(2)}, u32[]{:S(2)}) collective-permute-start(f32[96,128]{1,0:T(8,128)S(1)} %get-tuple-element.26), channel_id=1, source_target_pairs={{0,63},{1,2},{2,1},{3,4},{4,3},{5,6},{6,5},{7,8},{8,7},{9,10},{10,... | collective-permute-start | bytes 147464 | tf_op jit(solution)/shard_map/ppermute | solution.py:402
  23.5 0.0 collective-permute-done.refs_0_.refs_8_
  23.5 2.8 %collective-permute-done.1.refs_1_.refs_9_ = f32[96,128]{1,0:T(8,128)S(1)} collective-permute-done((f32[96,128]{1,0:T(8,128)S(1)}, f32[96,128]{1,0:T(8,128)S(1)}, u32[]{:S(2)}, u32[]{:S(2)}) %collective-permute-start.1) | collective-permute-done | bytes 49184 | tf_op jit(solution)/shard_map/ppermute | solution.py:402
  26.4 0.0 collective-permute-done.2.refs_13_
  26.4 0.2 complete_first.1
  26.6 6.8 %collective-permute-start.4 = (f32[64,128]{1,0:T(8,128)S(1)}, f32[64,128]{1,0:T(8,128)S(1)}, u32[]{:S(2)}, u32[]{:S(2)}) collective-permute-start(f32[64,128]{1,0:T(8,128)S(1)} %get-tuple-element.30.refs_0_), channel_id=1, source_target_pairs={{0,56},{8,16},{16,8},{24,32},{32,24},{40,48},{48,40},{56,0},{1,57}... | collective-permute-start | bytes 98312 | tf_op jit(solution)/shard_map/ppermute | solution.py:393
  33.4 3.4 %collective-permute-start.3 = (f32[64,128]{1,0:T(8,128)S(1)}, f32[64,128]{1,0:T(8,128)S(1)}, u32[]{:S(2)}, u32[]{:S(2)}) collective-permute-start(f32[64,128]{1,0:T(8,128)S(1)} %get-tuple-element.30.refs_0_), channel_id=1, source_target_pairs={{0,8},{8,0},{16,24},{24,16},{32,40},{40,32},{48,56},{56,48},{1,9},... | collective-permute-start | bytes 98312 | tf_op jit(solution)/shard_map/ppermute | solution.py:393
  36.8 0.5 collective-permute-done.4.refs_2_
  37.3 4.7 %collective-permute-done.3.refs_1_ = f32[64,128]{1,0:T(8,128)S(1)} collective-permute-done((f32[64,128]{1,0:T(8,128)S(1)}, f32[64,128]{1,0:T(8,128)S(1)}, u32[]{:S(2)}, u32[]{:S(2)}) %collective-permute-start.3) | collective-permute-done | bytes 32800 | tf_op jit(solution)/shard_map/ppermute | solution.py:393
  42.0 23.1 %all_to_all.20.refs_3_ = f32[8,48,128]{2,1,0:T(8,128)S(1)} all-to-all(f32[8,48,128]{2,1,0:T(8,128)S(1)} %broadcast_in_dim.12), channel_id=1, replica_groups=mesh['tm'=8,'block'=8,'chip'=4,'core'=2] {'tm'}, dimensions={0} | all-to-all | bytes 393216 | tf_op jit(solution)/shard_map/all_to_all | solution.py:411
  65.1 0.0 copy-start
  65.1 0.0 copy-start.1
  65.1 0.0 copy-start.2
  65.1 21.8 %all_to_all.21.refs_4_ = f32[4,224,128]{2,1,0:T(8,128)S(1)} all-to-all(f32[4,224,128]{2,1,0:T(8,128)S(1)} %hand_out.2), channel_id=1, replica_groups=mesh['tm'=8,'block'=8,'chip'=4,'core'=2] {'chip'}, dimensions={0} | all-to-all | bytes 917504 | tf_op jit(solution)/shard_map/all_to_all | solution.py:415
  87.0 1.9 %collective-permute-start.5 = (f32[4,224,128]{2,1,0:T(8,128)S(1)}, f32[4,224,128]{2,1,0:T(8,128)S(1)}, u32[]{:S(2)}, u32[]{:S(2)}) collective-permute-start(f32[4,224,128]{2,1,0:T(8,128)S(1)} %all_to_all.21.refs_4_), channel_id=1, source_target_pairs={{0,1},{1,0},{2,3},{3,2},{4,5},{5,4},{6,7},{7,6},{8,9},{9,8},{10,11... | collective-permute-start | bytes 1376264 | tf_op jit(solution)/shard_map/ppermute | solution.py:397
  88.9 1.8 %collective-permute-done.5.refs_5_ = f32[4,224,128]{2,1,0:T(8,128)S(1)} collective-permute-done((f32[4,224,128]{2,1,0:T(8,128)S(1)}, f32[4,224,128]{2,1,0:T(8,128)S(1)}, u32[]{:S(2)}, u32[]{:S(2)}) %collective-permute-start.5) | collective-permute-done | bytes 458784 | tf_op jit(solution)/shard_map/ppermute | solution.py:397
  90.7 0.0 copy-done
  90.7 0.0 copy-done.1
  90.7 0.0 copy-done.2
  90.7 1.8 %finish_first.1 = (f32[2,2,64,128]{3,2,1,0:T(8,128)S(1)}, f32[2,64,128]{2,1,0:T(8,128)S(1)}, f32[144,128]{1,0:T(8,128)S(1)}, f32[144,128]{1,0:T(8,128)S(1)}, f32...) custom-call(f32[64,128]{1,0:T(8,128)S(1)} %get-tuple-element.30.refs_0_, ...), custom_call_target="tpu_custom_call" | custom-call | tf_op jit(solution)/shard_map/finish_first/pallas_call | solution.py:376
  92.5 0.0 copy-start.3
  92.5 2.0 %collective-permute-start.6 = (f32[144,128]{1,0:T(8,128)S(1)}, f32[144,128]{1,0:T(8,128)S(1)}, u32[]{:S(2)}, u32[]{:S(2)}) collective-permute-start(f32[144,128]{1,0:T(8,128)S(1)} %get-tuple-element.34), channel_id=1, source_target_pairs={{0,1},{1,0},{2,3},{3,2},{4,5},{5,4},{6,7},{7,6},{8,9},{9,8},{10,11... | collective-permute-start | bytes 221192 | tf_op jit(solution)/shard_map/ppermute | solution.py:397
  94.6 2.3 %collective-permute-start.7 = (f32[144,128]{1,0:T(8,128)S(1)}, f32[144,128]{1,0:T(8,128)S(1)}, u32[]{:S(2)}, u32[]{:S(2)}) collective-permute-start(f32[144,128]{1,0:T(8,128)S(1)} %get-tuple-element.35), channel_id=1, source_target_pairs={{0,63},{1,2},{2,1},{3,4},{4,3},{5,6},{6,5},{7,8},{8,7},{9,10},{10,... | collective-permute-start | bytes 221192 | tf_op jit(solution)/shard_map/ppermute | solution.py:402
  96.9 3.3 %collective-permute-start.8 = (f32[2,64,128]{2,1,0:T(8,128)S(1)}, f32[2,64,128]{2,1,0:T(8,128)S(1)}, u32[]{:S(2)}, u32[]{:S(2)}) collective-permute-start(f32[2,64,128]{2,1,0:T(8,128)S(1)} %slice_bitcast_fusion), channel_id=1, source_target_pairs={{0,64},{64,128},{128,192},{192,256},{256,320},{320,384},{384,448},... | collective-permute-start | bytes 196616 | tf_op jit(solution)/shard_map/ppermute | solution.py:407
  100.2 1.3 collective-permute-done.8.refs_15_
  101.5 0.0 collective-permute-done.6.refs_0_.refs_9_
  101.5 0.0 collective-permute-done.7.refs_1_.refs_10_
  101.5 0.2 complete_second.1
  101.8 0.0 copy-done.3
  101.8 4.4 %collective-permute-start.10 = (f32[48,128]{1,0:T(8,128)S(1)}, f32[48,128]{1,0:T(8,128)S(1)}, u32[]{:S(2)}, u32[]{:S(2)}) collective-permute-start(f32[48,128]{1,0:T(8,128)S(1)} %get-tuple-element.40.refs_0_), channel_id=1, source_target_pairs={{0,56},{8,16},{16,8},{24,32},{32,24},{40,48},{48,40},{56,0},{1,57}... | collective-permute-start | bytes 73736 | tf_op jit(solution)/shard_map/ppermute | solution.py:393
  106.2 4.7 %collective-permute-start.9 = (f32[48,128]{1,0:T(8,128)S(1)}, f32[48,128]{1,0:T(8,128)S(1)}, u32[]{:S(2)}, u32[]{:S(2)}) collective-permute-start(f32[48,128]{1,0:T(8,128)S(1)} %get-tuple-element.40.refs_0_), channel_id=1, source_target_pairs={{0,8},{8,0},{16,24},{24,16},{32,40},{40,32},{48,56},{56,48},{1,9},... | collective-permute-start | bytes 73736 | tf_op jit(solution)/shard_map/ppermute | solution.py:393
  110.9 2.1 %collective-permute-done.10.refs_2_ = f32[48,128]{1,0:T(8,128)S(1)} collective-permute-done((f32[48,128]{1,0:T(8,128)S(1)}, f32[48,128]{1,0:T(8,128)S(1)}, u32[]{:S(2)}, u32[]{:S(2)}) %collective-permute-start.10) | collective-permute-done | bytes 24608 | tf_op jit(solution)/shard_map/ppermute | solution.py:393
  113.0 2.5 %collective-permute-done.9.refs_1_ = f32[48,128]{1,0:T(8,128)S(1)} collective-permute-done((f32[48,128]{1,0:T(8,128)S(1)}, f32[48,128]{1,0:T(8,128)S(1)}, u32[]{:S(2)}, u32[]{:S(2)}) %collective-permute-start.9) | collective-permute-done | bytes 24608 | tf_op jit(solution)/shard_map/ppermute | solution.py:393
  115.6 27.0 %all_to_all.22.refs_3_ = f32[8,48,128]{2,1,0:T(8,128)S(1)} all-to-all(f32[8,48,128]{2,1,0:T(8,128)S(1)} %broadcast_in_dim.13), channel_id=1, replica_groups=mesh['tm'=8,'block'=8,'chip'=4,'core'=2] {'tm'}, dimensions={0} | all-to-all | bytes 393216 | tf_op jit(solution)/shard_map/all_to_all | solution.py:411
  142.6 0.0 copy-start.4
  142.7 24.4 %all_to_all.23.refs_4_ = f32[4,192,128]{2,1,0:T(8,128)S(1)} all-to-all(f32[4,192,128]{2,1,0:T(8,128)S(1)} %hand_out.3), channel_id=1, replica_groups=mesh['tm'=8,'block'=8,'chip'=4,'core'=2] {'chip'}, dimensions={0} | all-to-all | bytes 786432 | tf_op jit(solution)/shard_map/all_to_all | solution.py:415
  167.0 3.3 %collective-permute-start.11 = (f32[4,192,128]{2,1,0:T(8,128)S(1)}, f32[4,192,128]{2,1,0:T(8,128)S(1)}, u32[]{:S(2)}, u32[]{:S(2)}) collective-permute-start(f32[4,192,128]{2,1,0:T(8,128)S(1)} %all_to_all.23.refs_4_), channel_id=1, source_target_pairs={{0,1},{1,0},{2,3},{3,2},{4,5},{5,4},{6,7},{7,6},{8,9},{9,8},{10,11... | collective-permute-start | bytes 1179656 | tf_op jit(solution)/shard_map/ppermute | solution.py:397
  170.3 1.3 collective-permute-done.11.refs_5_
  171.6 0.0 copy-done.4
  171.6 2.0 %finish_second.1 = (f32[2,2,64,128]{3,2,1,0:T(8,128)}, f32[32,64]{1,0:T(8,128)}) custom-call(f32[48,128]{1,0:T(8,128)S(1)} %get-tuple-element.40.refs_0_, f32[48,128]{1,0:T(8,128)S(1)} %collective-permute-done.9.refs_1_, f32[48,128]{1,0:T(8,128)S(1)} %collective-permute-done.10.refs_2_, f32[8,48,128]{2,1,0:T(8,128)S(1)} %all_to_all.22.refs_3_, ...), custom_call_target="tpu_custom_call" | custom-call | tf_op jit(solution)/shard_map/finish_second/pallas_call | solution.py:376
  (11 shorter events, 0.1 us)
Async XLA Ops:
  0.6 25.8 %collective-permute-start.2 = (f32[2,64,128]{2,1,0:T(8,128)}, f32[2,64,128]{2,1,0:T(8,128)S(1)}, u32[]{:S(2)}, u32[]{:S(2)}) collective-permute-start(f32[2,64,128]{2,1,0:T(8,128)} %bitcast.5), channel_id=1, source_target_pairs={{0,64},{64,128},{128,192},{192,256},{256,320},{320,384},{384,448},... | collective-permute-start | bytes 196616 | tf_op jit(solution)/shard_map/ppermute | solution.py:407
  18.1 5.4 %collective-permute-start = (f32[96,128]{1,0:T(8,128)S(1)}, f32[96,128]{1,0:T(8,128)S(1)}, u32[]{:S(2)}, u32[]{:S(2)}) collective-permute-start(f32[96,128]{1,0:T(8,128)S(1)} %get-tuple-element.25), channel_id=1, source_target_pairs={{0,1},{1,0},{2,3},{3,2},{4,5},{5,4},{6,7},{7,6},{8,9},{9,8},{10,11... | collective-permute-start | bytes 147464 | tf_op jit(solution)/shard_map/ppermute | solution.py:397
  21.0 5.4 %collective-permute-start.1 = (f32[96,128]{1,0:T(8,128)S(1)}, f32[96,128]{1,0:T(8,128)S(1)}, u32[]{:S(2)}, u32[]{:S(2)}) collective-permute-start(f32[96,128]{1,0:T(8,128)S(1)} %get-tuple-element.26), channel_id=1, source_target_pairs={{0,63},{1,2},{2,1},{3,4},{4,3},{5,6},{6,5},{7,8},{8,7},{9,10},{10,... | collective-permute-start | bytes 147464 | tf_op jit(solution)/shard_map/ppermute | solution.py:402
  26.6 10.7 %collective-permute-start.4 = (f32[64,128]{1,0:T(8,128)S(1)}, f32[64,128]{1,0:T(8,128)S(1)}, u32[]{:S(2)}, u32[]{:S(2)}) collective-permute-start(f32[64,128]{1,0:T(8,128)S(1)} %get-tuple-element.30.refs_0_), channel_id=1, source_target_pairs={{0,56},{8,16},{16,8},{24,32},{32,24},{40,48},{48,40},{56,0},{1,57}... | collective-permute-start | bytes 98312 | tf_op jit(solution)/shard_map/ppermute | solution.py:393
  33.4 8.6 %collective-permute-start.3 = (f32[64,128]{1,0:T(8,128)S(1)}, f32[64,128]{1,0:T(8,128)S(1)}, u32[]{:S(2)}, u32[]{:S(2)}) collective-permute-start(f32[64,128]{1,0:T(8,128)S(1)} %get-tuple-element.30.refs_0_), channel_id=1, source_target_pairs={{0,8},{8,0},{16,24},{24,16},{32,40},{40,32},{48,56},{56,48},{1,9},... | collective-permute-start | bytes 98312 | tf_op jit(solution)/shard_map/ppermute | solution.py:393
  65.1 25.6 %copy-start = (f32[2,64,128]{2,1,0:T(8,128)S(1)}, f32[2,64,128]{2,1,0:T(8,128)}, u32[]{:S(2)}) copy-start(f32[2,64,128]{2,1,0:T(8,128)} %refs_11_.3) | copy-start | bytes 196612
  65.1 25.6 %copy-start.1 = (f32[2,64,128]{2,1,0:T(8,128)S(1)}, f32[2,64,128]{2,1,0:T(8,128)}, u32[]{:S(2)}) copy-start(f32[2,64,128]{2,1,0:T(8,128)} %refs_12_.1) | copy-start | bytes 196612
  65.1 25.6 %copy-start.2 = (f32[1,2,64,128]{3,2,1,0:T(8,128)S(1)}, f32[1,2,64,128]{3,2,1,0:T(8,128)}, u32[]{:S(2)}) copy-start(f32[1,2,64,128]{3,2,1,0:T(8,128)} %param.5) | copy-start | bytes 196612
  87.0 3.7 %collective-permute-start.5 = (f32[4,224,128]{2,1,0:T(8,128)S(1)}, f32[4,224,128]{2,1,0:T(8,128)S(1)}, u32[]{:S(2)}, u32[]{:S(2)}) collective-permute-start(f32[4,224,128]{2,1,0:T(8,128)S(1)} %all_to_all.21.refs_4_), channel_id=1, source_target_pairs={{0,1},{1,0},{2,3},{3,2},{4,5},{5,4},{6,7},{7,6},{8,9},{9,8},{10,11... | collective-permute-start | bytes 1376264 | tf_op jit(solution)/shard_map/ppermute | solution.py:397
  92.5 9.3 %copy-start.3 = (f32[15,32,128]{2,1,0:T(8,128)}, f32[15,32,128]{2,1,0:T(8,128)S(1)}, u32[]{:S(2)}) copy-start(f32[15,32,128]{2,1,0:T(8,128)S(1)} %get-tuple-element.45.refs_16_) | copy-start | bytes 737284
  92.5 9.0 %collective-permute-start.6 = (f32[144,128]{1,0:T(8,128)S(1)}, f32[144,128]{1,0:T(8,128)S(1)}, u32[]{:S(2)}, u32[]{:S(2)}) collective-permute-start(f32[144,128]{1,0:T(8,128)S(1)} %get-tuple-element.34), channel_id=1, source_target_pairs={{0,1},{1,0},{2,3},{3,2},{4,5},{5,4},{6,7},{7,6},{8,9},{9,8},{10,11... | collective-permute-start | bytes 221192 | tf_op jit(solution)/shard_map/ppermute | solution.py:397
  94.6 7.0 %collective-permute-start.7 = (f32[144,128]{1,0:T(8,128)S(1)}, f32[144,128]{1,0:T(8,128)S(1)}, u32[]{:S(2)}, u32[]{:S(2)}) collective-permute-start(f32[144,128]{1,0:T(8,128)S(1)} %get-tuple-element.35), channel_id=1, source_target_pairs={{0,63},{1,2},{2,1},{3,4},{4,3},{5,6},{6,5},{7,8},{8,7},{9,10},{10,... | collective-permute-start | bytes 221192 | tf_op jit(solution)/shard_map/ppermute | solution.py:402
  96.9 4.7 %collective-permute-start.8 = (f32[2,64,128]{2,1,0:T(8,128)S(1)}, f32[2,64,128]{2,1,0:T(8,128)S(1)}, u32[]{:S(2)}, u32[]{:S(2)}) collective-permute-start(f32[2,64,128]{2,1,0:T(8,128)S(1)} %slice_bitcast_fusion), channel_id=1, source_target_pairs={{0,64},{64,128},{128,192},{192,256},{256,320},{320,384},{384,448},... | collective-permute-start | bytes 196616 | tf_op jit(solution)/shard_map/ppermute | solution.py:407
  101.8 11.2 %collective-permute-start.10 = (f32[48,128]{1,0:T(8,128)S(1)}, f32[48,128]{1,0:T(8,128)S(1)}, u32[]{:S(2)}, u32[]{:S(2)}) collective-permute-start(f32[48,128]{1,0:T(8,128)S(1)} %get-tuple-element.40.refs_0_), channel_id=1, source_target_pairs={{0,56},{8,16},{16,8},{24,32},{32,24},{40,48},{48,40},{56,0},{1,57}... | collective-permute-start | bytes 73736 | tf_op jit(solution)/shard_map/ppermute | solution.py:393
  106.2 9.3 %collective-permute-start.9 = (f32[48,128]{1,0:T(8,128)S(1)}, f32[48,128]{1,0:T(8,128)S(1)}, u32[]{:S(2)}, u32[]{:S(2)}) collective-permute-start(f32[48,128]{1,0:T(8,128)S(1)} %get-tuple-element.40.refs_0_), channel_id=1, source_target_pairs={{0,8},{8,0},{16,24},{24,16},{32,40},{40,32},{48,56},{56,48},{1,9},... | collective-permute-start | bytes 73736 | tf_op jit(solution)/shard_map/ppermute | solution.py:393
  142.6 29.0 %copy-start.4 = (f32[15,32,128]{2,1,0:T(8,128)S(1)}, f32[15,32,128]{2,1,0:T(8,128)}, u32[]{:S(2)}) copy-start(f32[15,32,128]{2,1,0:T(8,128)} %copy-done.3) | copy-start | bytes 737284
  167.0 4.6 %collective-permute-start.11 = (f32[4,192,128]{2,1,0:T(8,128)S(1)}, f32[4,192,128]{2,1,0:T(8,128)S(1)}, u32[]{:S(2)}, u32[]{:S(2)}) collective-permute-start(f32[4,192,128]{2,1,0:T(8,128)S(1)} %all_to_all.23.refs_4_), channel_id=1, source_target_pairs={{0,1},{1,0},{2,3},{3,2},{4,5},{5,4},{6,7},{7,6},{8,9},{9,8},{10,11... | collective-permute-start | bytes 1179656 | tf_op jit(solution)/shard_map/ppermute | solution.py:397

commit v6 on v5

--- a/solution.py
+++ b/solution.py
@@ -14,11 +14,13 @@
 CHIPS = BLOCK // 2
 F32 = jnp.float32
 
-COEF, NEAR1, NEAR2 = 10, 11, 12
+COEF, NEAR1, NEAR2, BEGIN, EDGE = 10, 11, 12, 13, 14
 ITEMS = (
-    ((0, 8), (1, 7), (COEF, 7), (2, 6), (3, 5), (4, 4), (5, 3), (6, 2), (NEAR1, 1), (NEAR2, 1)),
+    ((0, 8), (1, 7), (COEF, 7), (2, 6), (3, 5), (4, 4), (5, 3), (6, 2), (7, 1), (NEAR1, 1), (BEGIN, 1))
+    + tuple((EDGE + i, 1) for i in range(4)),
     ((0, 8), (1, 7), (2, 6), (3, 5), (4, 4), (5, 3), (6, 2), (NEAR1, 1), (NEAR2, 1)),
 )
+ROWS = ({NEAR1: 16, COEF: 32, BEGIN: 48, **{EDGE + i: 64 + 16 * i for i in range(4)}}, {NEAR1: 16, NEAR2: 32})
 
 
 def count(items, distance):
@@ -138,75 +140,68 @@
     total = around(both) - 5.0 * both + c[0] * cubic(u[0]) + c[1] * cubic(u[1])
     own, value, coef, start = squash([total, both, c[0] + c[1], initial[0] + initial[1]], scratch)
     value, coef, start = 0.125 * value, 0.125 * coef, 0.125 * start
-    small = [pack(value), pack(start)]
-    packets(spot, [u[1]] + small, [u[0]] + small, inner, outer)
+    packets(spot, u + [c[1], pack(start)], u + [c[0], pack(start)], inner, outer)
     keep[0] = own
     keep[1] = value
     keep[2] = coef
     keep[3] = start
 
 
-def hand_over(spot, own, values, value0, value0_sides, coef, start, start_slope, out, mine, gathered):
+def own_k(own, value0, value0_sides, coef):
     slope = coarse_slope(value0_sides[0], value0, value0_sides[1], coef)
-    k = [(STEP / 8.0) * own[m] - (STEP * QUAD[m + 1][0]) * slope for m in (0, 1)]
-    first = (jnp.full((32, 128), spot[0], jnp.int32) == 0)
-    ours = pack(k[1] + jnp.where(first, start + STEP * QUAD[2][0] * start_slope, 0.0))
-    out[0:16, :] = ours
-    mine[...] = ours
-    for m in (0, 1):
-        near = QUAD[m + 1][1] * k[0] + QUAD[m + 1][2] * k[1] - values[m]
-        near = near + jnp.where(first, ROWSUM[m + 1] * start + START[m + 1] * start_slope, 0.0)
-        out[16 * (m + 1) : 16 * (m + 2), :] = pack(near)
-    gathered[0] = k[0]
-    gathered[1] = k[1]
-
-
-def complete_first(spot, inner, outer, kept, out, mine, keep, scratch):
+    return [(STEP / 8.0) * own[m] - (STEP * QUAD[m + 1][0]) * slope for m in (0, 1)]
+
+
+def complete_first(
+    spot, inner, outer, kept, initial, received, owned, beside, beyond, mine, keep, begin_out, scratch
+):
     below, above = sides(spot, inner, outer)
+    begin = starting(spot, initial, received)
     own, value, coef, start = (kept[i] for i in range(4))
-    low, high = squash([below[0:64, :], above[0:64, :]], scratch)
+    low, high, value_low, value_high, value_begin = squash(
+        [below[64:128, :], above[0:64, :], below[0:64, :] + below[64:128, :], above[0:64, :] + above[64:128, :],
+         begin[0] + begin[1]],
+        scratch,
+    )
+    value_low, value_high = 0.125 * value_low, 0.125 * value_high
+    start_low, start_high = unpack(below[192:208, :]), unpack(above[192:208, :])
+    start_slope = coarse_slope(start_low, start, start_high, coef)
     whole = own + low + high
-    value_sides = [unpack(below[64:80, :]), unpack(above[64:80, :])]
-    start_sides = [unpack(below[80:96, :]), unpack(above[80:96, :])]
-    start_slope = coarse_slope(start_sides[0], start, start_sides[1], coef)
-    hand_over(
-        spot, [ROWSUM[1] * whole, ROWSUM[2] * whole], [ROWSUM[1] * value, ROWSUM[2] * value],
-        value, value_sides, coef, start, start_slope, out, mine, keep,
-    )
-    out[48:64, :] = pack(coef)
-    keep[2] = start
-    keep[3] = start_slope
-    keep[4] = start_sides[0]
-    keep[5] = start_sides[1]
-
-
-def complete_second(spot, inner, outer, kept, started, kept_first, out, mine, keep, scratch):
-    below, above = sides(spot, inner, outer)
-    low1, low2, high1, high2 = squash(
-        [below[0:64, :], below[64:128, :], above[0:64, :], above[64:128, :]], scratch
-    )
-    own = [kept[0] + low1 + high1, kept[1] + low2 + high2]
-    values = [mix(m, [kept[2], kept[3], kept[4]]) for m in (1, 2)]
-    value_sides = [unpack(below[128:144, :]), unpack(above[128:144, :])]
-    hand_over(spot, own, values, kept[2], value_sides, kept_first[2], started[2], started[3], out, mine, keep)
-
-
-def plane(spot, owned, beside, beyond, sections, side, item):
+    k = own_k([ROWSUM[1] * whole, ROWSUM[2] * whole], value, [value_low, value_high], coef)
+    first = jnp.full((32, 128), spot[0], jnp.int32) == 0
+    given = [pack(k[m - 1] + jnp.where(first, start + (STEP * QUAD[m][0]) * start_slope, 0.0)) for m in (2, 1)]
+    given += [pack(coef), pack(0.125 * value_begin)]
+    mine[...] = given[0]
+    odd = jnp.full((64, 128), spot[3], jnp.int32) == 1
+    for i, part in enumerate(given):
+        for out in (owned, beside, beyond):
+            out[16 * i : 16 * i + 16, :] = part
+    beside[64:128, :] = jnp.where(odd, begin[0], begin[1])
+    beyond[64:128, :] = jnp.where(odd, begin[1], begin[0])
+    for x in (0, 1):
+        owned[64 * (x + 1) : 64 * (x + 2), :] = begin[x]
+        begin_out[x] = begin[x]
+    for i, part in enumerate([k[0], k[1], start, start_slope, start_low, start_high, value_low, value_high]):
+        keep[i] = part
+
+
+def plane(spot, rows, owned, beside, beyond, sections, side, item, up=False):
     odd = spot[3]
     if item < SECTIONS:
         if side == 0:
             return sections[item, 0:16, :]
         at = jnp.where(odd == 1, side, 3 - side)
         return sections[item, pl.ds(pl.multiple_of(16 * at, 16), 16), :]
-    row = {NEAR1: 16, NEAR2: 32, COEF: 48}[item]
+    row = rows[item]
     if side == 0:
+        row += 64 if item >= EDGE and up else 0
         return owned[row : row + 16, :]
     near, far = beside[row : row + 16, :], beyond[row : row + 16, :]
     picked = jnp.full((16, 128), odd, jnp.int32) == (1 if side == 1 else 0)
     return jnp.where(picked, near, far)
 
 
-def pack_kernel(items):
+def pack_kernel(items, rows):
     total = slots(items)
 
     def body(spot, owned, beside, beyond, sections, out):
@@ -214,10 +209,12 @@
 
         def fill(own_core, away):
             slot = 0
+            up = away > 0 or (away == 0 and own_core == 0)
             for side, least in shares(own_core, away):
                 for item, reach in items:
                     if reach >= least:
-                        out[chip + away, 16 * slot : 16 * slot + 16, :] = plane(spot, owned, beside, beyond, sections, side, item)
+                        part = plane(spot, rows, owned, beside, beyond, sections, side, item, up)
+                        out[chip + away, 16 * slot : 16 * slot + 16, :] = part
                         slot += 1
 
         for own_core in (0, 1):
@@ -231,16 +228,16 @@
     return body, total
 
 
-def sweep(spot, items, owned, beside, beyond, sections, windows, swapped, coefs, started, line, history):
+def sweep(spot, items, rows, owned, beside, beyond, sections, windows, swapped, coefs, started, line, history):
     core = spot[2]
     place = 2 * spot[1] + core
     rank = {item: i for i, (item, _) in enumerate(items)}
     reach_of = dict(items)
 
-    def fetch(item, w):
+    def fetch(item, w, whole=False):
         if w in (0, -BLOCK, BLOCK):
             side = {0: 0, -BLOCK: 1, BLOCK: 2}[w]
-            return unpack(plane(spot, owned, beside, beyond, sections, side, item))
+            return unpack(plane(spot, rows, owned, beside, beyond, sections, side, item))
         at = place + w
         if w > 0:
             outside, least = at >= BLOCK, [max(1, BLOCK - w - i) for i in (0, 1)]
@@ -249,7 +246,8 @@
         before = jnp.where(core == 0, count(items, least[0]), count(items, least[1]))
         slot = rank[item] + jnp.where(outside, before, 0)
         source = windows if w % 2 == 0 else swapped
-        return unpack(source[(at & (BLOCK - 1)) >> 1, pl.ds(pl.multiple_of(16 * slot, 16), 16), :])
+        found = source[(at & (BLOCK - 1)) >> 1, pl.ds(pl.multiple_of(16 * slot, 16), 16), :]
+        return found if whole else unpack(found)
 
     if COEF in rank:
         for w in range(-7, 8):
@@ -264,7 +262,9 @@
         line[0, w + 8] = value
         if abs(w) <= 2:
             history[5 + w + 2] = value
-    for k in range(1, SECTIONS - 1):
+    for k in range(1, SECTIONS):
+        if k not in rank:
+            continue
         old, new = (k - 1) % 2, k % 2
         for w in range(-reach_of[k], reach_of[k] + 1):
             centre = line[old, w + 8]
@@ -307,60 +307,84 @@
 
 
 def finish_first(
-    spot, owned, beside, beyond, sections, windows, swapped, started, kept, inner, outer, initial, coeff, guess, received,
-    fresh_out, begin_out, inner_out, outer_out, keep, coefs, line, history, scratch,
+    spot, owned, beside, beyond, sections, windows, swapped, started, kept, inner, outer, coeff, guess, begin,
+    middle_out, end_out, ends, keep, owned_out, mine, coefs, line, history, scratch,
 ):
+    fetch = sweep(
+        spot, ITEMS[0], ROWS[0], owned, beside, beyond, sections, windows, swapped, coefs, started, line, history
+    )
     below, above = sides(spot, inner, outer)
-    fetch = sweep(spot, ITEMS[0], owned, beside, beyond, sections, windows, swapped, coefs, started, line, history)
+    section = spot[0]
+    later = jnp.full((32, 128), section, jnp.int32) > 0
+    s = [history[5 * section + i] for i in range(5)]
+    slope = [coarse_slope(s[i], s[i + 1], s[i + 2], coefs[6 + i]) for i in range(3)]
+    step = [s[i + 1] + (STEP * QUAD[1][0]) * slope[i] for i in range(3)]
+    value = [started[6], kept[1], started[7]]
+    coarse = []
+    for i in range(3):
+        if i == 1:
+            one, two = step[1] + started[0], s[2] + (STEP * QUAD[2][0]) * slope[1] + started[1]
+        else:
+            one = fetch(NEAR1, i - 1) + jnp.where(later, step[i], 0.0)
+            two = history[5 * section + 6 + i]
+        coarse += [s[i + 1] - value[i], one - value[i], two - value[i]]
+    wide = spread(coarse, scratch)
+    u = [below[0:64, :], below[64:128, :], guess[0], guess[1], above[0:64, :], above[64:128, :]]
+    c = [None, below[128:192, :], coeff[0], coeff[1], above[128:192, :], None]
+    b = [None] + [None] * 4 + [None]
+    b[2], b[3] = begin[0], begin[1]
+    for x, w in ((1, -1), (4, 1)):
+        b[x] = jnp.concatenate([fetch(EDGE + i, w, whole=True) for i in range(4)], axis=0)
+    fixed = [[u[x] + wide[3 * (x // 2) + j] for j in range(3)] for x in range(6)]
+    nodes = [None] + [[b[x]] for x in range(1, 5)] + [None]
+    rates = [None] + [[cubic(fixed[x][j]) for j in range(3)] for x in range(1, 5)] + [None]
+    for m in (1, 2):
+        sums = [mix(m, fixed[x]) for x in range(6)]
+        for x in range(1, 5):
+            change = around(sums[x]) - 6.0 * sums[x] + sums[x - 1] + sums[x + 1] + c[x] * mix(m, rates[x])
+            nodes[x].append(b[x] + STEP * change)
+    for x in (0, 1):
+        middle_out[x] = nodes[x + 2][1]
+        end_out[x] = nodes[x + 2][2]
+    rates = [[cubic(nodes[x][j]) for j in range(3)] for x in (2, 3)]
+    planes = []
+    for m in (1, 2):
+        sums = [mix(m, nodes[x]) for x in range(1, 5)]
+        ends[m - 1] = sums[0]
+        ends[m + 1] = sums[3]
+        both = sums[1] + sums[2]
+        planes.append(
+            around(both) - 5.0 * both + sums[0] + sums[3] + c[2] * mix(m, rates[0]) + c[3] * mix(m, rates[1])
+        )
+    for j in range(3):
+        planes.append(nodes[2][j] + nodes[3][j])
+    small = squash(planes, scratch)
+    values = [0.125 * small[2 + j] for j in range(3)]
+    k = own_k(small[:2], values[0], [fetch(BEGIN, -1), fetch(BEGIN, 1)], kept[2])
+    first = jnp.logical_not(later)
+    ours = pack(k[1] + jnp.where(first, started[2] + (STEP * QUAD[2][0]) * started[3], 0.0))
+    owned_out[0:16, :] = ours
+    mine[...] = ours
+    for m in (1, 2):
+        near = QUAD[m][1] * k[0] + QUAD[m][2] * k[1] - mix(m, values)
+        near = near + jnp.where(first, ROWSUM[m] * started[2] + START[m] * started[3], 0.0)
+        owned_out[16 * m : 16 * m + 16, :] = pack(near)
+    for i, part in enumerate(values + k):
+        keep[i] = part
+
+
+def finish_second(
+    spot, owned, beside, beyond, sections, windows, swapped, started, kept, ends, initial, coeff, begin_in, middle_in,
+    end_in, received, coefs, fresh_out, coarse_out, line, history, scratch,
+):
+    fetch = sweep(
+        spot, ITEMS[1], ROWS[1], owned, beside, beyond, sections, windows, swapped, coefs, started, line, history
+    )
     begin = starting(spot, initial, received)
-    u = [guess[0], guess[1]]
-    c = [coeff[0], coeff[1]]
-    low = [ROWSUM[m] * below[0:64, :] for m in (1, 2)]
-    high = [ROWSUM[m] * above[0:64, :] for m in (1, 2)]
-    value = kept[1]
-    _, fresh = correct(
-        spot, fetch, coefs, started, history, (started[0], started[1]), [value] * 3, [u] * 3, low, high, c, begin, scratch
-    )
-    nodes = [begin] + fresh
-    rates = [[cubic(nodes[j][x]) for x in (0, 1)] for j in range(3)]
-    planes, up, down = [], [], []
-    for m in (1, 2):
-        sums = [mix(m, [nodes[j][x] for j in range(3)]) for x in (0, 1)]
-        down.append(sums[0])
-        up.append(sums[1])
-        both = sums[0] + sums[1]
-        part = around(both) - 5.0 * both
-        for x in (0, 1):
-            part = part + c[x] * mix(m, [rates[j][x] for j in range(3)])
-        planes.append(part)
-    for j in range(3):
-        planes.append(nodes[j][0] + nodes[j][1])
-    for x in (0, 1):
-        begin_out[x] = begin[x]
-        for m in (0, 1):
-            fresh_out[m, x] = fresh[m][x]
-    small = squash(planes, scratch)
-    keep[0] = small[0]
-    keep[1] = small[1]
-    for j in range(3):
-        keep[2 + j] = 0.125 * small[2 + j]
-    small = [pack(0.125 * small[2])]
-    packets(spot, up + small, down + small, inner_out, outer_out)
-
-
-def finish_second(
-    spot, owned, beside, beyond, sections, windows, swapped, started, kept, kept_k, inner, outer, initial, coeff, begin_in,
-    fresh_in, received, coefs, fresh_out, coarse_out, line, history, scratch,
-):
-    below, above = sides(spot, inner, outer)
-    fetch = sweep(spot, ITEMS[1], owned, beside, beyond, sections, windows, swapped, coefs, started, line, history)
-    begin = starting(spot, initial, received)
-    nodes = [[begin_in[0], begin_in[1]]] + [[fresh_in[m, 0], fresh_in[m, 1]] for m in (0, 1)]
-    low = [below[64 * m : 64 * m + 64, :] for m in (0, 1)]
-    high = [above[64 * m : 64 * m + 64, :] for m in (0, 1)]
+    nodes = [[part[0], part[1]] for part in (begin_in, middle_in, end_in)]
     end, fresh = correct(
-        spot, fetch, coefs, started, history, (kept_k[0], kept_k[1]), [kept[2], kept[3], kept[4]], nodes, low, high,
-        [coeff[0], coeff[1]], begin, scratch,
+        spot, fetch, coefs, started, history, (kept[3], kept[4]), [kept[0], kept[1], kept[2]], nodes,
+        [ends[0], ends[1]], [ends[2], ends[3]], [coeff[0], coeff[1]], begin, scratch,
     )
     for m in (0, 1):
         for x in (0, 1):
@@ -424,13 +448,12 @@
 
 
 def iterate(links, initial, coeff, guess):
-    coarse = (32, 128)
-    work = [(2, 17) + coarse, (40,) + coarse]
-
-    def windows(owned, mine, items):
-        beside, beyond = links.swap_block(owned, True), links.swap_block(owned, False)
+    coarse, slab = (32, 128), (2, 64, 128)
+    work = [(2, 17) + coarse, (45,) + coarse]
+
+    def windows(owned, beside, beyond, mine, iteration):
         sections = links.sections(links.stack(mine, beside, beyond))
-        body, total = pack_kernel(items)
+        body, total = pack_kernel(ITEMS[iteration], ROWS[iteration])
         (parcels,) = links.call(
             body, (owned, beside, beyond, sections), [(CHIPS, 16 * total, 128)], name="hand_out"
         )
@@ -438,30 +461,28 @@
         return owned, beside, beyond, sections, parcels, links.swap_inner(parcels)
 
     inner, outer, kept = links.call(
-        first_kernel, (initial, coeff, guess), [(96, 128), (96, 128), (4,) + coarse], [(256, 128)], name="first",
+        first_kernel, (initial, coeff, guess), [(208, 128), (208, 128), (4,) + coarse], [(256, 128)], name="first",
         first=True,
     )
     inner, outer, received = links.together(links.swap_inner(inner), links.swap_outer(outer), links.onward(guess))
-    owned, mine, started = links.call(
-        complete_first, (inner, outer, kept), [(64, 128), (16, 128), (6,) + coarse], [(128, 128)],
-        name="complete_first",
-    )
-    fresh, begin, inner, outer, kept2, coefs = links.call(
+    owned, beside, beyond, mine, started, begin = links.call(
+        complete_first, (inner, outer, kept, initial, received),
+        [(192, 128), (128, 128), (128, 128), (16, 128), (8,) + coarse, slab], [(320, 128)], name="complete_first",
+    )
+    beside, beyond = links.swap_block(beside, True), links.swap_block(beyond, False)
+    middle, end, ends, kept, owned, mine, coefs = links.call(
         finish_first,
-        (*windows(owned, mine, ITEMS[0]), started, kept, inner, outer, initial, coeff, guess, received),
-        [(2, 2, 64, 128), (2, 64, 128), (144, 128), (144, 128), (5,) + coarse, (15,) + coarse],
-        work + [(448, 128)],
+        (*windows(owned, beside, beyond, mine, 0), started, kept, inner, outer, coeff, guess, begin),
+        [slab, slab, (4, 64, 128), (5,) + coarse, (48, 128), (16, 128), (15,) + coarse],
+        work + [(576, 128)],
         name="finish_first",
     )
-    inner, outer, received = links.together(links.swap_inner(inner), links.swap_outer(outer), links.onward(fresh[1]))
-    owned, mine, kept_k = links.call(
-        complete_second, (inner, outer, kept2, started, kept), [(48, 128), (16, 128), (2,) + coarse], [(256, 128)],
-        name="complete_second",
+    beside, beyond, received = links.together(
+        links.swap_block(owned, True), links.swap_block(owned, False), links.onward(end)
     )
     fine, coarse_end = links.call(
         finish_second,
-        (*windows(owned, mine, ITEMS[1]), started, kept2, kept_k, inner, outer, initial, coeff, begin, fresh,
-         received, coefs),
+        (*windows(owned, beside, beyond, mine, 1), started, kept, ends, initial, coeff, begin, middle, end, received, coefs),
         [(2, 2, 64, 128), (32, 64)],
         work + [(448, 128)],
         name="finish_second",

time: 174 us -> 170 us (0.977)
  blocking collectives: 96.3 us -> 90.3 us
    all_to_all x2, blocking collectives: 46.2 us -> 33.9 us  [block(): return lax.all_to_all(x, 'chip', 0, 0)]
    ppermute x4 -> x3, starting transfers between devices: 10.1 us -> 18.6 us  [swap_inner(): return lax.ppermute(x, 'core', [(0, 1), (1, 0)])]
    all_to_all x2, blocking collectives: 50.1 us -> 56.5 us  [sections(): lax.all_to_all(jnp.broadcast_to(x, (SECTIONS,) + x.shape), 'tm', 0, 0)]
    ppermute x2, starting transfers between devices: 19.6 us -> 13.3 us  [onward(): return lax.ppermute(x, 'tm', [(i, i + 1) for i in range(n - 1)])]
    ppermute x4, waiting for transfers between devices: 9.72 us -> 12.8 us  [swap_block(): return lax.ppermute(x, 'block', pairs)]
    ppermute x2 -> x1, starting transfers between devices: 4.83 us -> 1.92 us  [swap_outer(): lax.ppermute(x, ('block', 'chip', 'core'), [(i, (i + 2 * (i % 2) - 1) % n...]
    ppermute x2 -> x1, waiting for transfers between devices: 2.85 us -> 0.01 us  [swap_outer(): lax.ppermute(x, ('block', 'chip', 'core'), [(i, (i + 2 * (i % 2) - 1) % n...]
    pallas_call x7 -> x6, Pallas kernels: 5.55 us -> 5.71 us  [run(): pl.pallas_call(placed, out_shape=[jax.ShapeDtypeStruct(shape, F32) if las...]
  transfers between devices with their start and end apart: 12 -> 10, of which waited for: 8 -> 6; matrix products, arithmetic and copies ran while one was open for 0% -> 0% of each run, Pallas kernels for 1% -> 0%
where the time goes in v6:
time: 170 us
  blocking collectives  90.3 us (53%)
  starting transfers between devices  54.7 us (32%)
  waiting for transfers between devices  17.1 us (10%)
  Pallas kernels  5.71 us (3%)
    all_to_all x2, blocking collectives, sections(): lax.all_to_all(jnp.broadcast_to(x, (SECTIONS,) + x.shape), 'tm', 0, 0)  56.5 us
    all_to_all x2, blocking collectives, block(): return lax.all_to_all(x, 'chip', 0, 0)  33.9 us
    ppermute x4, starting transfers between devices, swap_block(): return lax.ppermute(x, 'block', pairs)  20.8 us
    ppermute x3, starting transfers between devices, swap_inner(): return lax.ppermute(x, 'core', [(0, 1), (1, 0)])  18.6 us
    ppermute x2, starting transfers between devices, onward(): return lax.ppermute(x, 'tm', [(i, i + 1) for i in range(n - 1)])  13.3 us
    ppermute x4, waiting for transfers between devices, swap_block(): return lax.ppermute(x, 'block', pairs)  12.8 us
    pallas_call x6, Pallas kernels, run(): pl.pallas_call(placed, out_shape=[jax.ShapeDtypeStruct(shape, F32) if las...  5.71 us
  transfers between devices with their start and end apart: 10, of which 6 were waited for; matrix products, arithmetic and copies ran while one was open for 0% of the time, Pallas kernels for 0%

profile of v6, /device:TPU:1, one launch (start us, length us, event | category | flops | bytes accessed | tf_op | source)
XLA Modules:
  0.0 169.7 jit_solution(16786614464049476629)
XLA Ops:
  0.6 0.0 copy-start.6
  0.6 0.0 copy-start
  0.7 1.2 first.1
  1.9 0.0 copy-start.11
  1.9 8.8 %collective-permute-start = (f32[208,128]{1,0:T(8,128)S(1)}, f32[208,128]{1,0:T(8,128)S(1)}, u32[]{:S(2)}, u32[]{:S(2)}) collective-permute-start(f32[208,128]{1,0:T(8,128)S(1)} %get-tuple-element.26), channel_id=1, source_target_pairs={{0,1},{1,0},{2,3},{3,2},{4,5},{5,4},{6,7},{7,6},{8,9},{9,8},{10,11... | collective-permute-start | bytes 319496 | tf_op jit(solution)/shard_map/ppermute | solution.py:421
  10.7 1.9 %collective-permute-start.1 = (f32[208,128]{1,0:T(8,128)S(1)}, f32[208,128]{1,0:T(8,128)S(1)}, u32[]{:S(2)}, u32[]{:S(2)}) collective-permute-start(f32[208,128]{1,0:T(8,128)S(1)} %get-tuple-element.27), channel_id=1, source_target_pairs={{0,63},{1,2},{2,1},{3,4},{4,3},{5,6},{6,5},{7,8},{8,7},{9,10},{10,... | collective-permute-start | bytes 319496 | tf_op jit(solution)/shard_map/ppermute | solution.py:426
  12.6 0.0 copy-done.6
  12.6 10.7 %collective-permute-start.2 = (f32[2,64,128]{2,1,0:T(8,128)S(1)}, f32[2,64,128]{2,1,0:T(8,128)S(1)}, u32[]{:S(2)}, u32[]{:S(2)}) collective-permute-start(f32[2,64,128]{2,1,0:T(8,128)S(1)} %bitcast.4), channel_id=1, source_target_pairs={{0,64},{64,128},{128,192},{192,256},{256,320},{320,384},{384,448},... | collective-permute-start | bytes 196616 | tf_op jit(solution)/shard_map/ppermute | solution.py:431
  23.3 1.3 collective-permute-done.2.refs_4_
  24.6 0.0 collective-permute-done.refs_0_.refs_8_
  24.6 0.0 collective-permute-done.1.refs_1_.refs_9_
  24.6 0.0 copy-done
  24.6 0.3 complete_first.1
  24.9 0.0 copy-done.11
  24.9 0.0 copy-start.8
  24.9 0.0 copy-start.4
  25.0 4.0 %collective-permute-start.3 = (f32[128,128]{1,0:T(8,128)S(1)}, f32[128,128]{1,0:T(8,128)S(1)}, u32[]{:S(2)}, u32[]{:S(2)}) collective-permute-start(f32[128,128]{1,0:T(8,128)S(1)} %get-tuple-element.33), channel_id=1, source_target_pairs={{0,8},{8,0},{16,24},{24,16},{32,40},{40,32},{48,56},{56,48},{1,9},... | collective-permute-start | bytes 196616 | tf_op jit(solution)/shard_map/ppermute | solution.py:417
  29.0 7.6 %collective-permute-start.4 = (f32[128,128]{1,0:T(8,128)S(1)}, f32[128,128]{1,0:T(8,128)S(1)}, u32[]{:S(2)}, u32[]{:S(2)}) collective-permute-start(f32[128,128]{1,0:T(8,128)S(1)} %get-tuple-element.34), channel_id=1, source_target_pairs={{0,56},{8,16},{16,8},{24,32},{32,24},{40,48},{48,40},{56,0},{1,57}... | collective-permute-start | bytes 196616 | tf_op jit(solution)/shard_map/ppermute | solution.py:417
  36.6 0.0 collective-permute-done.3.refs_1_
  36.6 8.6 %collective-permute-done.4.refs_2_ = f32[128,128]{1,0:T(8,128)S(1)} collective-permute-done((f32[128,128]{1,0:T(8,128)S(1)}, f32[128,128]{1,0:T(8,128)S(1)}, u32[]{:S(2)}, u32[]{:S(2)}) %collective-permute-start.4) | collective-permute-done | bytes 65568 | tf_op jit(solution)/shard_map/ppermute | solution.py:417
  45.3 0.0 copy-done.8
  45.3 30.0 %all_to_all.20.refs_3_ = f32[8,48,128]{2,1,0:T(8,128)S(1)} all-to-all(f32[8,48,128]{2,1,0:T(8,128)S(1)} %broadcast_in_dim.12), channel_id=1, replica_groups=mesh['tm'=8,'block'=8,'chip'=4,'core'=2] {'tm'}, dimensions={0} | all-to-all | bytes 393216 | tf_op jit(solution)/shard_map/all_to_all | solution.py:435
  75.4 0.0 copy-start.2
  75.4 0.0 copy-start.7
  75.4 0.0 copy-start.12
  75.4 17.1 %all_to_all.21.refs_4_ = f32[4,304,128]{2,1,0:T(8,128)S(1)} all-to-all(f32[4,304,128]{2,1,0:T(8,128)S(1)} %hand_out.2), channel_id=1, replica_groups=mesh['tm'=8,'block'=8,'chip'=4,'core'=2] {'chip'}, dimensions={0} | all-to-all | bytes 1245184 | tf_op jit(solution)/shard_map/all_to_all | solution.py:439
  92.5 4.9 %collective-permute-start.5 = (f32[4,304,128]{2,1,0:T(8,128)S(1)}, f32[4,304,128]{2,1,0:T(8,128)S(1)}, u32[]{:S(2)}, u32[]{:S(2)}) collective-permute-start(f32[4,304,128]{2,1,0:T(8,128)S(1)} %all_to_all.21.refs_4_), channel_id=1, source_target_pairs={{0,1},{1,0},{2,3},{3,2},{4,5},{5,4},{6,7},{7,6},{8,9},{9,8},{10,11... | collective-permute-start | bytes 1867784 | tf_op jit(solution)/shard_map/ppermute | solution.py:421
  97.4 1.7 collective-permute-done.5.refs_5_
  99.1 0.0 copy-done.4
  99.1 0.0 copy-done.2
  99.1 0.8 copy-done.9
  99.9 2.1 %finish_first.1 = (f32[2,64,128]{2,1,0:T(8,128)S(1)}, f32[2,64,128]{2,1,0:T(8,128)S(1)}, f32[4,64,128]{2,1,0:T(8,128)S(1)}, f32[5,32,128]{2,1,0:T(8,128)S(1)}, f...) custom-call(f32[192,128]{1,0:T(8,128)S(1)} %get-tuple-element.32.refs_0_, ...), custom_call_target="tpu_custom_call" | custom-call | tf_op jit(solution)/shard_map/finish_first/pallas_call | solution.py:400
  102.0 2.6 %collective-permute-start.8 = (f32[2,64,128]{2,1,0:T(8,128)S(1)}, f32[2,64,128]{2,1,0:T(8,128)S(1)}, u32[]{:S(2)}, u32[]{:S(2)}) collective-permute-start(f32[2,64,128]{2,1,0:T(8,128)S(1)} %get-tuple-element.39.refs_13_), channel_id=1, source_target_pairs={{0,64},{64,128},{128,192},{192,256},{256,320},{320,384},{384,448},... | collective-permute-start | bytes 196616 | tf_op jit(solution)/shard_map/ppermute | solution.py:431
  104.6 4.4 %collective-permute-start.7 = (f32[48,128]{1,0:T(8,128)S(1)}, f32[48,128]{1,0:T(8,128)S(1)}, u32[]{:S(2)}, u32[]{:S(2)}) collective-permute-start(f32[48,128]{1,0:T(8,128)S(1)} %get-tuple-element.38.refs_0_), channel_id=1, source_target_pairs={{0,56},{8,16},{16,8},{24,32},{32,24},{40,48},{48,40},{56,0},{1,57}... | collective-permute-start | bytes 73736 | tf_op jit(solution)/shard_map/ppermute | solution.py:417
  109.0 4.8 %collective-permute-start.6 = (f32[48,128]{1,0:T(8,128)S(1)}, f32[48,128]{1,0:T(8,128)S(1)}, u32[]{:S(2)}, u32[]{:S(2)}) collective-permute-start(f32[48,128]{1,0:T(8,128)S(1)} %get-tuple-element.38.refs_0_), channel_id=1, source_target_pairs={{0,8},{8,0},{16,24},{24,16},{32,40},{40,32},{48,56},{56,48},{1,9},... | collective-permute-start | bytes 73736 | tf_op jit(solution)/shard_map/ppermute | solution.py:417
  113.8 1.7 collective-permute-done.7.refs_2_
  115.5 2.5 %collective-permute-done.6.refs_1_ = f32[48,128]{1,0:T(8,128)S(1)} collective-permute-done((f32[48,128]{1,0:T(8,128)S(1)}, f32[48,128]{1,0:T(8,128)S(1)}, u32[]{:S(2)}, u32[]{:S(2)}) %collective-permute-start.6) | collective-permute-done | bytes 24608 | tf_op jit(solution)/shard_map/ppermute | solution.py:417
  118.0 0.0 collective-permute-done.8.refs_14_
  118.0 26.5 %all_to_all.22.refs_3_ = f32[8,48,128]{2,1,0:T(8,128)S(1)} all-to-all(f32[8,48,128]{2,1,0:T(8,128)S(1)} %broadcast_in_dim.13), channel_id=1, replica_groups=mesh['tm'=8,'block'=8,'chip'=4,'core'=2] {'tm'}, dimensions={0} | all-to-all | bytes 393216 | tf_op jit(solution)/shard_map/all_to_all | solution.py:435
  144.5 0.0 copy-start.1
  144.6 0.0 copy-start.3
  144.6 0.0 copy-start.5
  144.6 16.8 %all_to_all.23.refs_4_ = f32[4,192,128]{2,1,0:T(8,128)S(1)} all-to-all(f32[4,192,128]{2,1,0:T(8,128)S(1)} %hand_out.3), channel_id=1, replica_groups=mesh['tm'=8,'block'=8,'chip'=4,'core'=2] {'chip'}, dimensions={0} | all-to-all | bytes 786432 | tf_op jit(solution)/shard_map/all_to_all | solution.py:439
  161.4 4.9 %collective-permute-start.9 = (f32[4,192,128]{2,1,0:T(8,128)S(1)}, f32[4,192,128]{2,1,0:T(8,128)S(1)}, u32[]{:S(2)}, u32[]{:S(2)}) collective-permute-start(f32[4,192,128]{2,1,0:T(8,128)S(1)} %all_to_all.23.refs_4_), channel_id=1, source_target_pairs={{0,1},{1,0},{2,3},{3,2},{4,5},{5,4},{6,7},{7,6},{8,9},{9,8},{10,11... | collective-permute-start | bytes 1179656 | tf_op jit(solution)/shard_map/ppermute | solution.py:421
  166.3 1.3 collective-permute-done.9.refs_5_
  167.7 0.0 copy-done.3
  167.7 0.0 copy-done.10
  167.7 2.1 %finish_second.1 = (f32[2,2,64,128]{3,2,1,0:T(8,128)}, f32[32,64]{1,0:T(8,128)}) custom-call(f32[48,128]{1,0:T(8,128)S(1)} %get-tuple-element.38.refs_0_, f32[48,128]{1,0:T(8,128)S(1)} %collective-permute-done.6.refs_1_, f32[48,128]{1,0:T(8,128)S(1)} %collective-permute-done.7.refs_2_, f32[8,48,128]{2,1,0:T(8,128)S(1)} %all_to_all.22.refs_3_, ...), custom_call_target="tpu_custom_call" | custom-call | tf_op jit(solution)/shard_map/finish_second/pallas_call | solution.py:400
  (16 shorter events, 0.1 us)
Async XLA Ops:
  0.6 12.0 %copy-start.6 = (f32[1,2,64,128]{3,2,1,0:T(8,128)S(1)}, f32[1,2,64,128]{3,2,1,0:T(8,128)}, u32[]{:S(2)}) copy-start(f32[1,2,64,128]{3,2,1,0:T(8,128)} %param.5) | copy-start | bytes 196612
  0.6 24.0 %copy-start = (f32[2,64,128]{2,1,0:T(8,128)S(1)}, f32[2,64,128]{2,1,0:T(8,128)}, u32[]{:S(2)}) copy-start(f32[2,64,128]{2,1,0:T(8,128)} %refs_9_.1) | copy-start | bytes 196612
  1.9 23.0 %copy-start.11 = (f32[4,32,128]{2,1,0:T(8,128)}, f32[4,32,128]{2,1,0:T(8,128)S(1)}, u32[]{:S(2)}) copy-start(f32[4,32,128]{2,1,0:T(8,128)S(1)} %get-tuple-element.30.refs_2_.refs_7_) | copy-start | bytes 196612
  1.9 22.7 %collective-permute-start = (f32[208,128]{1,0:T(8,128)S(1)}, f32[208,128]{1,0:T(8,128)S(1)}, u32[]{:S(2)}, u32[]{:S(2)}) collective-permute-start(f32[208,128]{1,0:T(8,128)S(1)} %get-tuple-element.26), channel_id=1, source_target_pairs={{0,1},{1,0},{2,3},{3,2},{4,5},{5,4},{6,7},{7,6},{8,9},{9,8},{10,11... | collective-permute-start | bytes 319496 | tf_op jit(solution)/shard_map/ppermute | solution.py:421
  10.7 14.0 %collective-permute-start.1 = (f32[208,128]{1,0:T(8,128)S(1)}, f32[208,128]{1,0:T(8,128)S(1)}, u32[]{:S(2)}, u32[]{:S(2)}) collective-permute-start(f32[208,128]{1,0:T(8,128)S(1)} %get-tuple-element.27), channel_id=1, source_target_pairs={{0,63},{1,2},{2,1},{3,4},{4,3},{5,6},{6,5},{7,8},{8,7},{9,10},{10,... | collective-permute-start | bytes 319496 | tf_op jit(solution)/shard_map/ppermute | solution.py:426
  12.6 12.0 %collective-permute-start.2 = (f32[2,64,128]{2,1,0:T(8,128)S(1)}, f32[2,64,128]{2,1,0:T(8,128)S(1)}, u32[]{:S(2)}, u32[]{:S(2)}) collective-permute-start(f32[2,64,128]{2,1,0:T(8,128)S(1)} %bitcast.4), channel_id=1, source_target_pairs={{0,64},{64,128},{128,192},{192,256},{256,320},{320,384},{384,448},... | collective-permute-start | bytes 196616 | tf_op jit(solution)/shard_map/ppermute | solution.py:431
  24.9 20.4 %copy-start.8 = (f32[2,64,128]{2,1,0:T(8,128)}, f32[2,64,128]{2,1,0:T(8,128)S(1)}, u32[]{:S(2)}) copy-start(f32[2,64,128]{2,1,0:T(8,128)S(1)} %get-tuple-element.37.refs_12_.refs_11_) | copy-start | bytes 196612
  24.9 74.1 %copy-start.4 = (f32[8,32,128]{2,1,0:T(8,128)}, f32[8,32,128]{2,1,0:T(8,128)S(1)}, u32[]{:S(2)}) copy-start(f32[8,32,128]{2,1,0:T(8,128)S(1)} %get-tuple-element.36.refs_6_) | copy-start | bytes 393220
  25.0 11.7 %collective-permute-start.3 = (f32[128,128]{1,0:T(8,128)S(1)}, f32[128,128]{1,0:T(8,128)S(1)}, u32[]{:S(2)}, u32[]{:S(2)}) collective-permute-start(f32[128,128]{1,0:T(8,128)S(1)} %get-tuple-element.33), channel_id=1, source_target_pairs={{0,8},{8,0},{16,24},{24,16},{32,40},{40,32},{48,56},{56,48},{1,9},... | collective-permute-start | bytes 196616 | tf_op jit(solution)/shard_map/ppermute | solution.py:417
  29.0 16.3 %collective-permute-start.4 = (f32[128,128]{1,0:T(8,128)S(1)}, f32[128,128]{1,0:T(8,128)S(1)}, u32[]{:S(2)}, u32[]{:S(2)}) collective-permute-start(f32[128,128]{1,0:T(8,128)S(1)} %get-tuple-element.34), channel_id=1, source_target_pairs={{0,56},{8,16},{16,8},{24,32},{32,24},{40,48},{48,40},{56,0},{1,57}... | collective-permute-start | bytes 196616 | tf_op jit(solution)/shard_map/ppermute | solution.py:417
  75.4 23.7 %copy-start.2 = (f32[2,64,128]{2,1,0:T(8,128)S(1)}, f32[2,64,128]{2,1,0:T(8,128)}, u32[]{:S(2)}) copy-start(f32[2,64,128]{2,1,0:T(8,128)} %refs_10_.3) | copy-start | bytes 196612
  75.4 23.7 %copy-start.7 = (f32[1,2,64,128]{3,2,1,0:T(8,128)S(1)}, f32[1,2,64,128]{3,2,1,0:T(8,128)}, u32[]{:S(2)}) copy-start(f32[1,2,64,128]{3,2,1,0:T(8,128)} %param.5) | copy-start | bytes 196612
  75.4 23.7 %copy-start.12 = (f32[4,32,128]{2,1,0:T(8,128)S(1)}, f32[4,32,128]{2,1,0:T(8,128)}, u32[]{:S(2)}) copy-start(f32[4,32,128]{2,1,0:T(8,128)} %copy-done.11) | copy-start | bytes 196612
  92.5 6.6 %collective-permute-start.5 = (f32[4,304,128]{2,1,0:T(8,128)S(1)}, f32[4,304,128]{2,1,0:T(8,128)S(1)}, u32[]{:S(2)}, u32[]{:S(2)}) collective-permute-start(f32[4,304,128]{2,1,0:T(8,128)S(1)} %all_to_all.21.refs_4_), channel_id=1, source_target_pairs={{0,1},{1,0},{2,3},{3,2},{4,5},{5,4},{6,7},{7,6},{8,9},{9,8},{10,11... | collective-permute-start | bytes 1867784 | tf_op jit(solution)/shard_map/ppermute | solution.py:421
  99.1 0.8 copy-start.9
  102.0 16.0 %collective-permute-start.8 = (f32[2,64,128]{2,1,0:T(8,128)S(1)}, f32[2,64,128]{2,1,0:T(8,128)S(1)}, u32[]{:S(2)}, u32[]{:S(2)}) collective-permute-start(f32[2,64,128]{2,1,0:T(8,128)S(1)} %get-tuple-element.39.refs_13_), channel_id=1, source_target_pairs={{0,64},{64,128},{128,192},{192,256},{256,320},{320,384},{384,448},... | collective-permute-start | bytes 196616 | tf_op jit(solution)/shard_map/ppermute | solution.py:431
  104.6 10.8 %collective-permute-start.7 = (f32[48,128]{1,0:T(8,128)S(1)}, f32[48,128]{1,0:T(8,128)S(1)}, u32[]{:S(2)}, u32[]{:S(2)}) collective-permute-start(f32[48,128]{1,0:T(8,128)S(1)} %get-tuple-element.38.refs_0_), channel_id=1, source_target_pairs={{0,56},{8,16},{16,8},{24,32},{32,24},{40,48},{48,40},{56,0},{1,57}... | collective-permute-start | bytes 73736 | tf_op jit(solution)/shard_map/ppermute | solution.py:417
  109.0 9.0 %collective-permute-start.6 = (f32[48,128]{1,0:T(8,128)S(1)}, f32[48,128]{1,0:T(8,128)S(1)}, u32[]{:S(2)}, u32[]{:S(2)}) collective-permute-start(f32[48,128]{1,0:T(8,128)S(1)} %get-tuple-element.38.refs_0_), channel_id=1, source_target_pairs={{0,8},{8,0},{16,24},{24,16},{32,40},{40,32},{48,56},{56,48},{1,9},... | collective-permute-start | bytes 73736 | tf_op jit(solution)/shard_map/ppermute | solution.py:417
  144.5 23.1 %copy-start.1 = (f32[2,64,128]{2,1,0:T(8,128)S(1)}, f32[2,64,128]{2,1,0:T(8,128)}, u32[]{:S(2)}) copy-start(f32[2,64,128]{2,1,0:T(8,128)} %refs_9_.1) | copy-start | bytes 196612
  144.6 23.1 %copy-start.3 = (f32[2,64,128]{2,1,0:T(8,128)S(1)}, f32[2,64,128]{2,1,0:T(8,128)}, u32[]{:S(2)}) copy-start(f32[2,64,128]{2,1,0:T(8,128)} %refs_10_.3) | copy-start | bytes 196612
  144.6 23.1 %copy-start.5 = (f32[8,32,128]{2,1,0:T(8,128)S(1)}, f32[8,32,128]{2,1,0:T(8,128)}, u32[]{:S(2)}) copy-start(f32[8,32,128]{2,1,0:T(8,128)} %copy-done.4) | copy-start | bytes 393220
  144.6 23.1 %copy-start.10 = (f32[2,64,128]{2,1,0:T(8,128)S(1)}, f32[2,64,128]{2,1,0:T(8,128)}, u32[]{:S(2)}) copy-start(f32[2,64,128]{2,1,0:T(8,128)} %copy-done.8) | copy-start | bytes 196612
  161.4 6.3 %collective-permute-start.9 = (f32[4,192,128]{2,1,0:T(8,128)S(1)}, f32[4,192,128]{2,1,0:T(8,128)S(1)}, u32[]{:S(2)}, u32[]{:S(2)}) collective-permute-start(f32[4,192,128]{2,1,0:T(8,128)S(1)} %all_to_all.23.refs_4_), channel_id=1, source_target_pairs={{0,1},{1,0},{2,3},{3,2},{4,5},{5,4},{6,7},{7,6},{8,9},{9,8},{10,11... | collective-permute-start | bytes 1179656 | tf_op jit(solution)/shard_map/ppermute | solution.py:421

commit v7 on v6

--- a/solution.py
+++ b/solution.py
@@ -14,13 +14,14 @@
 CHIPS = BLOCK // 2
 F32 = jnp.float32
 
-COEF, NEAR1, NEAR2, BEGIN, EDGE = 10, 11, 12, 13, 14
+COEF, NEAR1, NEAR2, BEGIN, INITIAL, EDGE = 10, 11, 12, 13, 14, 15
 ITEMS = (
-    ((0, 8), (1, 7), (COEF, 7), (2, 6), (3, 5), (4, 4), (5, 3), (6, 2), (7, 1), (NEAR1, 1), (BEGIN, 1))
+    ((0, 8), (1, 7), (COEF, 7), (2, 6), (3, 5), (4, 4), (5, 3), (6, 2), (BEGIN, 2), (INITIAL, 2), (7, 1),
+     (NEAR1, 1))
     + tuple((EDGE + i, 1) for i in range(4)),
     ((0, 8), (1, 7), (2, 6), (3, 5), (4, 4), (5, 3), (6, 2), (NEAR1, 1), (NEAR2, 1)),
 )
-ROWS = ({NEAR1: 16, COEF: 32, BEGIN: 48, **{EDGE + i: 64 + 16 * i for i in range(4)}}, {NEAR1: 16, NEAR2: 32})
+ROWS = ({NEAR1: 16, COEF: 32, BEGIN: 48, INITIAL: 64, **{EDGE + i: 80 + 16 * i for i in range(4)}}, {NEAR1: 16, NEAR2: 32})
 
 
 def count(items, distance):
@@ -170,16 +171,16 @@
     k = own_k([ROWSUM[1] * whole, ROWSUM[2] * whole], value, [value_low, value_high], coef)
     first = jnp.full((32, 128), spot[0], jnp.int32) == 0
     given = [pack(k[m - 1] + jnp.where(first, start + (STEP * QUAD[m][0]) * start_slope, 0.0)) for m in (2, 1)]
-    given += [pack(coef), pack(0.125 * value_begin)]
+    given += [pack(coef), pack(0.125 * value_begin), pack(start)]
     mine[...] = given[0]
     odd = jnp.full((64, 128), spot[3], jnp.int32) == 1
     for i, part in enumerate(given):
         for out in (owned, beside, beyond):
             out[16 * i : 16 * i + 16, :] = part
-    beside[64:128, :] = jnp.where(odd, begin[0], begin[1])
-    beyond[64:128, :] = jnp.where(odd, begin[1], begin[0])
+    beside[80:144, :] = jnp.where(odd, begin[0], begin[1])
+    beyond[80:144, :] = jnp.where(odd, begin[1], begin[0])
     for x in (0, 1):
-        owned[64 * (x + 1) : 64 * (x + 2), :] = begin[x]
+        owned[80 + 64 * x : 144 + 64 * x, :] = begin[x]
         begin_out[x] = begin[x]
     for i, part in enumerate([k[0], k[1], start, start_slope, start_low, start_high, value_low, value_high]):
         keep[i] = part
@@ -252,11 +253,12 @@
     if COEF in rank:
         for w in range(-7, 8):
             coefs[w + 7] = fetch(COEF, w)
-    history[0] = jnp.zeros((32, 128), F32)
+    outermost = [fetch(INITIAL, w) if INITIAL in rank else jnp.zeros((32, 128), F32) for w in (-2, 2)]
+    history[0] = outermost[0]
     history[1] = started[4]
     history[2] = started[2]
     history[3] = started[5]
-    history[4] = jnp.zeros((32, 128), F32)
+    history[4] = outermost[1]
     for w in range(-8, 9):
         value = fetch(0, w)
         line[0, w + 8] = value
@@ -306,9 +308,33 @@
     return [jnp.where(first, initial[x], received[x]) for x in (0, 1)]
 
 
+def previous_end(section, fetch, coefs, history, starts, coeff, initial, earlier, scratch):
+    before = jnp.maximum(section - 1, 0)
+    s = [history[5 * before + i] for i in range(5)]
+    value = [fetch(BEGIN, w) for w in range(-2, 3)]
+    shift = []
+    for i in range(3):
+        two = history[5 * section + 1 + i]
+        slope = coarse_slope(s[i], s[i + 1], s[i + 2], coefs[6 + i])
+        slope = slope - coarse_slope(value[i], value[i + 1], value[i + 2], coefs[6 + i])
+        one = 0.5 * (s[i + 1] + two) + (STEP * (QUAD[1][0] - 0.5 * QUAD[2][0])) * slope
+        shift.append([s[i + 1] - value[i + 1], one - value[i + 1], two - value[i + 1]])
+    wide = spread([mix(2, shift[0])] + shift[1] + [mix(2, shift[2])], scratch)
+    fixed = [[starts[x] + wide[1 + j] for j in range(3)] for x in (1, 2)]
+    sums = [ROWSUM[2] * starts[0] + wide[0], mix(2, fixed[0]), mix(2, fixed[1]), ROWSUM[2] * starts[3] + wide[4]]
+    number = jnp.full((64, 128), section, jnp.int32)
+    out = []
+    for x in (0, 1):
+        change = around(sums[x + 1]) - 6.0 * sums[x + 1] + sums[x] + sums[x + 2]
+        change = change + coeff[x] * mix(2, [cubic(part) for part in fixed[x]])
+        end = jnp.where(number == 1, initial[x], earlier[x]) + STEP * change
+        out.append(jnp.where(number == 0, initial[x], end))
+    return out
+
+
 def finish_first(
-    spot, owned, beside, beyond, sections, windows, swapped, started, kept, inner, outer, coeff, guess, begin,
-    middle_out, end_out, ends, keep, owned_out, mine, coefs, line, history, scratch,
+    spot, owned, beside, beyond, sections, windows, swapped, started, kept, inner, outer, initial, coeff, guess, begin,
+    earlier, middle_out, end_out, ends, begin_out, keep, owned_out, mine, coefs, line, history, scratch,
 ):
     fetch = sweep(
         spot, ITEMS[0], ROWS[0], owned, beside, beyond, sections, windows, swapped, coefs, started, line, history
@@ -335,6 +361,9 @@
     b[2], b[3] = begin[0], begin[1]
     for x, w in ((1, -1), (4, 1)):
         b[x] = jnp.concatenate([fetch(EDGE + i, w, whole=True) for i in range(4)], axis=0)
+    begin_next = previous_end(section, fetch, coefs, history, b[1:5], coeff, initial, earlier, scratch)
+    for x in (0, 1):
+        begin_out[x] = begin_next[x]
     fixed = [[u[x] + wide[3 * (x // 2) + j] for j in range(3)] for x in range(6)]
     nodes = [None] + [[b[x]] for x in range(1, 5)] + [None]
     rates = [None] + [[cubic(fixed[x][j]) for j in range(3)] for x in range(1, 5)] + [None]
@@ -374,17 +403,16 @@
 
 
 def finish_second(
-    spot, owned, beside, beyond, sections, windows, swapped, started, kept, ends, initial, coeff, begin_in, middle_in,
-    end_in, received, coefs, fresh_out, coarse_out, line, history, scratch,
+    spot, owned, beside, beyond, sections, windows, swapped, started, kept, ends, coeff, begin_in, middle_in, end_in,
+    begin, coefs, fresh_out, coarse_out, line, history, scratch,
 ):
     fetch = sweep(
         spot, ITEMS[1], ROWS[1], owned, beside, beyond, sections, windows, swapped, coefs, started, line, history
     )
-    begin = starting(spot, initial, received)
     nodes = [[part[0], part[1]] for part in (begin_in, middle_in, end_in)]
     end, fresh = correct(
         spot, fetch, coefs, started, history, (kept[3], kept[4]), [kept[0], kept[1], kept[2]], nodes,
-        [ends[0], ends[1]], [ends[2], ends[3]], [coeff[0], coeff[1]], begin, scratch,
+        [ends[0], ends[1]], [ends[2], ends[3]], [coeff[0], coeff[1]], [begin[0], begin[1]], scratch,
     )
     for m in (0, 1):
         for x in (0, 1):
@@ -403,6 +431,7 @@
         in_specs=[pl.BlockSpec(memory_space=pltpu.VMEM)] * len(args),
         out_specs=[pl.BlockSpec(memory_space=pltpu.VMEM)] * len(outs),
         scratch_shapes=[pltpu.VMEM(shape, F32) for shape in scratch],
+        compiler_params=pltpu.CompilerParams(vmem_limit_bytes=16 << 20),
         name=name,
     )(*(a if first else pltpu.with_memory_space_constraint(a, pltpu.VMEM) for a in args))
 
@@ -426,9 +455,9 @@
         return lax.ppermute(x, ("block", "chip", "core"), [(i, (i + 2 * (i % 2) - 1) % n) for i in range(n)])
 
     @staticmethod
-    def onward(x):
+    def onward(x, by):
         n = lax.axis_size("tm")
-        return lax.ppermute(x, "tm", [(i, i + 1) for i in range(n - 1)])
+        return lax.ppermute(x, "tm", [(i, i + by) for i in range(n - by)])
 
     @staticmethod
     def sections(x):
@@ -464,25 +493,25 @@
         first_kernel, (initial, coeff, guess), [(208, 128), (208, 128), (4,) + coarse], [(256, 128)], name="first",
         first=True,
     )
-    inner, outer, received = links.together(links.swap_inner(inner), links.swap_outer(outer), links.onward(guess))
+    inner, outer, received, earlier = links.together(
+        links.swap_inner(inner), links.swap_outer(outer), links.onward(guess, 1), links.onward(guess, 2)
+    )
     owned, beside, beyond, mine, started, begin = links.call(
         complete_first, (inner, outer, kept, initial, received),
-        [(192, 128), (128, 128), (128, 128), (16, 128), (8,) + coarse, slab], [(320, 128)], name="complete_first",
+        [(208, 128), (144, 128), (144, 128), (16, 128), (8,) + coarse, slab], [(320, 128)], name="complete_first",
     )
     beside, beyond = links.swap_block(beside, True), links.swap_block(beyond, False)
-    middle, end, ends, kept, owned, mine, coefs = links.call(
+    middle, end, ends, begin_next, kept, owned, mine, coefs = links.call(
         finish_first,
-        (*windows(owned, beside, beyond, mine, 0), started, kept, inner, outer, coeff, guess, begin),
-        [slab, slab, (4, 64, 128), (5,) + coarse, (48, 128), (16, 128), (15,) + coarse],
+        (*windows(owned, beside, beyond, mine, 0), started, kept, inner, outer, initial, coeff, guess, begin, earlier),
+        [slab, slab, (4, 64, 128), slab, (5,) + coarse, (48, 128), (16, 128), (15,) + coarse],
         work + [(576, 128)],
         name="finish_first",
     )
-    beside, beyond, received = links.together(
-        links.swap_block(owned, True), links.swap_block(owned, False), links.onward(end)
-    )
+    beside, beyond = links.swap_block(owned, True), links.swap_block(owned, False)
     fine, coarse_end = links.call(
         finish_second,
-        (*windows(owned, beside, beyond, mine, 1), started, kept, ends, initial, coeff, begin, middle, end, received, coefs),
+        (*windows(owned, beside, beyond, mine, 1), started, kept, ends, coeff, begin, middle, end, begin_next, coefs),
         [(2, 2, 64, 128), (32, 64)],
         work + [(448, 128)],
         name="finish_second",

time: 170 us -> 169 us (level)
  the two profiles are of different devices: /device:TPU:1 before, /device:TPU:17 now
where the time goes in v7:
time: 169 us; the launch traced here: 168 us
  blocking collectives  88.6 us (52%)
  starting transfers between devices  50.7 us (30%)
  waiting for transfers between devices  20.7 us (12%)
  Pallas kernels  4.92 us (3%)
  local copies, waits for them, and re-layouts  2.57 us (2%)
    all_to_all x2, blocking collectives, sections(): lax.all_to_all(jnp.broadcast_to(x, (SECTIONS,) + x.shape), 'tm', 0, 0)  51.2 us
    all_to_all x2, blocking collectives, block(): return lax.all_to_all(x, 'chip', 0, 0)  37.4 us
    ppermute x4, starting transfers between devices, swap_block(): return lax.ppermute(x, 'block', pairs)  18.8 us
    ppermute x2, starting transfers between devices, onward(): return lax.ppermute(x, 'tm', [(i, i + by) for i in range(n - by)])  17.7 us
    ppermute x4, waiting for transfers between devices, swap_block(): return lax.ppermute(x, 'block', pairs)  16.4 us
    ppermute x3, starting transfers between devices, swap_inner(): return lax.ppermute(x, 'core', [(0, 1), (1, 0)])  10.8 us
    pallas_call x6, Pallas kernels, run(): pl.pallas_call(placed, out_shape=[jax.ShapeDtypeStruct(shape, F32) if las...  4.92 us
    ppermute x1, starting transfers between devices, swap_outer(): lax.ppermute(x, ('block', 'chip', 'core'), [(i, (i + 2 * (i % 2) - 1) % n...  3.44 us
  transfers between devices with their start and end apart: 10, of which 6 were waited for; matrix products, arithmetic and copies ran while one was open for 0% of the time, Pallas kernels for 0%

profile of v7, /device:TPU:17, one launch (start us, length us, event | category | flops | bytes accessed | tf_op | source)
XLA Modules:
  0.0 168.4 jit_solution(10546194941224995236)
XLA Ops:
  0.6 0.0 copy-start
  0.6 0.8 copy-done
  1.5 0.0 copy-start.2
  1.5 0.8 copy-done.2
  2.3 0.0 copy-start.4
  2.3 0.8 copy-done.4
  3.2 0.3 first.1
  3.5 2.6 %collective-permute-start = (f32[208,128]{1,0:T(8,128)S(1)}, f32[208,128]{1,0:T(8,128)S(1)}, u32[]{:S(2)}, u32[]{:S(2)}) collective-permute-start(f32[208,128]{1,0:T(8,128)S(1)} %get-tuple-element.25), channel_id=1, source_target_pairs={{0,1},{1,0},{2,3},{3,2},{4,5},{5,4},{6,7},{7,6},{8,9},{9,8},{10,11... | collective-permute-start | bytes 319496 | tf_op jit(solution)/shard_map/ppermute | solution.py:450
  6.0 3.4 %collective-permute-start.1 = (f32[208,128]{1,0:T(8,128)S(1)}, f32[208,128]{1,0:T(8,128)S(1)}, u32[]{:S(2)}, u32[]{:S(2)}) collective-permute-start(f32[208,128]{1,0:T(8,128)S(1)} %get-tuple-element.26), channel_id=1, source_target_pairs={{0,63},{1,2},{2,1},{3,4},{4,3},{5,6},{6,5},{7,8},{8,7},{9,10},{10,... | collective-permute-start | bytes 319496 | tf_op jit(solution)/shard_map/ppermute | solution.py:455
  9.5 3.1 %collective-permute-start.3 = (f32[2,64,128]{2,1,0:T(8,128)S(1)}, f32[2,64,128]{2,1,0:T(8,128)S(1)}, u32[]{:S(2)}, u32[]{:S(2)}) collective-permute-start(f32[2,64,128]{2,1,0:T(8,128)S(1)} %bitcast.4), channel_id=1, source_target_pairs={{0,128},{64,192},{128,256},{192,320},{256,384},{320,448},{1,129},{... | collective-permute-start | bytes 196616 | tf_op jit(solution)/shard_map/ppermute | solution.py:460
  12.6 14.5 %collective-permute-start.2 = (f32[2,64,128]{2,1,0:T(8,128)S(1)}, f32[2,64,128]{2,1,0:T(8,128)S(1)}, u32[]{:S(2)}, u32[]{:S(2)}) collective-permute-start(f32[2,64,128]{2,1,0:T(8,128)S(1)} %bitcast.5), channel_id=1, source_target_pairs={{0,64},{64,128},{128,192},{192,256},{256,320},{320,384},{384,448},... | collective-permute-start | bytes 196616 | tf_op jit(solution)/shard_map/ppermute | solution.py:460
  27.2 0.0 collective-permute-done.3.refs_14_
  27.2 1.3 collective-permute-done.2.refs_4_
  28.5 0.0 collective-permute-done.refs_0_.refs_8_
  28.5 0.0 collective-permute-done.1.refs_1_.refs_9_
  28.5 0.3 complete_first.1
  28.8 4.0 %collective-permute-start.4 = (f32[144,128]{1,0:T(8,128)S(1)}, f32[144,128]{1,0:T(8,128)S(1)}, u32[]{:S(2)}, u32[]{:S(2)}) collective-permute-start(f32[144,128]{1,0:T(8,128)S(1)} %get-tuple-element.32), channel_id=1, source_target_pairs={{0,8},{8,0},{16,24},{24,16},{32,40},{40,32},{48,56},{56,48},{1,9},... | collective-permute-start | bytes 221192 | tf_op jit(solution)/shard_map/ppermute | solution.py:446
  32.8 5.1 %collective-permute-start.5 = (f32[144,128]{1,0:T(8,128)S(1)}, f32[144,128]{1,0:T(8,128)S(1)}, u32[]{:S(2)}, u32[]{:S(2)}) collective-permute-start(f32[144,128]{1,0:T(8,128)S(1)} %get-tuple-element.33), channel_id=1, source_target_pairs={{0,56},{8,16},{16,8},{24,32},{32,24},{40,48},{48,40},{56,0},{1,57}... | collective-permute-start | bytes 221192 | tf_op jit(solution)/shard_map/ppermute | solution.py:446
  37.8 1.5 collective-permute-done.4.refs_1_
  39.3 10.0 %collective-permute-done.5.refs_2_ = f32[144,128]{1,0:T(8,128)S(1)} collective-permute-done((f32[144,128]{1,0:T(8,128)S(1)}, f32[144,128]{1,0:T(8,128)S(1)}, u32[]{:S(2)}, u32[]{:S(2)}) %collective-permute-start.5) | collective-permute-done | bytes 73760 | tf_op jit(solution)/shard_map/ppermute | solution.py:446
  49.3 28.9 %all_to_all.20.refs_3_ = f32[8,48,128]{2,1,0:T(8,128)S(1)} all-to-all(f32[8,48,128]{2,1,0:T(8,128)S(1)} %broadcast_in_dim.12), channel_id=1, replica_groups=mesh['tm'=8,'block'=8,'chip'=4,'core'=2] {'tm'}, dimensions={0} | all-to-all | bytes 393216 | tf_op jit(solution)/shard_map/all_to_all | solution.py:464
  78.3 0.0 copy-start.1
  78.4 0.0 copy-start.3
  78.4 18.7 %all_to_all.21.refs_4_ = f32[4,320,128]{2,1,0:T(8,128)S(1)} all-to-all(f32[4,320,128]{2,1,0:T(8,128)S(1)} %hand_out.2), channel_id=1, replica_groups=mesh['tm'=8,'block'=8,'chip'=4,'core'=2] {'chip'}, dimensions={0} | all-to-all | bytes 1310720 | tf_op jit(solution)/shard_map/all_to_all | solution.py:468
  97.0 4.0 %collective-permute-start.6 = (f32[4,320,128]{2,1,0:T(8,128)S(1)}, f32[4,320,128]{2,1,0:T(8,128)S(1)}, u32[]{:S(2)}, u32[]{:S(2)}) collective-permute-start(f32[4,320,128]{2,1,0:T(8,128)S(1)} %all_to_all.21.refs_4_), channel_id=1, source_target_pairs={{0,1},{1,0},{2,3},{3,2},{4,5},{5,4},{6,7},{7,6},{8,9},{9,8},{10,11... | collective-permute-start | bytes 1966088 | tf_op jit(solution)/shard_map/ppermute | solution.py:450
  101.1 1.7 %collective-permute-done.6.refs_5_ = f32[4,320,128]{2,1,0:T(8,128)S(1)} collective-permute-done((f32[4,320,128]{2,1,0:T(8,128)S(1)}, f32[4,320,128]{2,1,0:T(8,128)S(1)}, u32[]{:S(2)}, u32[]{:S(2)}) %collective-permute-start.6) | collective-permute-done | bytes 655392 | tf_op jit(solution)/shard_map/ppermute | solution.py:450
  102.8 0.0 copy-done.1
  102.8 0.0 copy-done.3
  102.8 2.2 %finish_first.1 = (f32[2,64,128]{2,1,0:T(8,128)S(1)}, f32[2,64,128]{2,1,0:T(8,128)S(1)}, f32[4,64,128]{2,1,0:T(8,128)S(1)}, f32[2,64,128]{2,1,0:T(8,128)S(1)}, f...) custom-call(f32[208,128]{1,0:T(8,128)S(1)} %get-tuple-element.31.refs_0_, ...), custom_call_target="tpu_custom_call" | custom-call | tf_op jit(solution)/shard_map/finish_first/pallas_call | solution.py:428
  105.0 6.1 %collective-permute-start.8 = (f32[48,128]{1,0:T(8,128)S(1)}, f32[48,128]{1,0:T(8,128)S(1)}, u32[]{:S(2)}, u32[]{:S(2)}) collective-permute-start(f32[48,128]{1,0:T(8,128)S(1)} %get-tuple-element.38.refs_0_), channel_id=1, source_target_pairs={{0,56},{8,16},{16,8},{24,32},{32,24},{40,48},{48,40},{56,0},{1,57}... | collective-permute-start | bytes 73736 | tf_op jit(solution)/shard_map/ppermute | solution.py:446
  111.1 3.7 %collective-permute-start.7 = (f32[48,128]{1,0:T(8,128)S(1)}, f32[48,128]{1,0:T(8,128)S(1)}, u32[]{:S(2)}, u32[]{:S(2)}) collective-permute-start(f32[48,128]{1,0:T(8,128)S(1)} %get-tuple-element.38.refs_0_), channel_id=1, source_target_pairs={{0,8},{8,0},{16,24},{24,16},{32,40},{40,32},{48,56},{56,48},{1,9},... | collective-permute-start | bytes 73736 | tf_op jit(solution)/shard_map/ppermute | solution.py:446
  114.8 0.0 collective-permute-done.8.refs_2_
  114.8 4.9 %collective-permute-done.7.refs_1_ = f32[48,128]{1,0:T(8,128)S(1)} collective-permute-done((f32[48,128]{1,0:T(8,128)S(1)}, f32[48,128]{1,0:T(8,128)S(1)}, u32[]{:S(2)}, u32[]{:S(2)}) %collective-permute-start.7) | collective-permute-done | bytes 24608 | tf_op jit(solution)/shard_map/ppermute | solution.py:446
  119.8 22.3 %all_to_all.22.refs_3_ = f32[8,48,128]{2,1,0:T(8,128)S(1)} all-to-all(f32[8,48,128]{2,1,0:T(8,128)S(1)} %broadcast_in_dim.13), channel_id=1, replica_groups=mesh['tm'=8,'block'=8,'chip'=4,'core'=2] {'tm'}, dimensions={0} | all-to-all | bytes 393216 | tf_op jit(solution)/shard_map/all_to_all | solution.py:464
  142.1 18.7 %all_to_all.23.refs_4_ = f32[4,192,128]{2,1,0:T(8,128)S(1)} all-to-all(f32[4,192,128]{2,1,0:T(8,128)S(1)} %hand_out.3), channel_id=1, replica_groups=mesh['tm'=8,'block'=8,'chip'=4,'core'=2] {'chip'}, dimensions={0} | all-to-all | bytes 786432 | tf_op jit(solution)/shard_map/all_to_all | solution.py:468
  160.8 4.2 %collective-permute-start.9 = (f32[4,192,128]{2,1,0:T(8,128)S(1)}, f32[4,192,128]{2,1,0:T(8,128)S(1)}, u32[]{:S(2)}, u32[]{:S(2)}) collective-permute-start(f32[4,192,128]{2,1,0:T(8,128)S(1)} %all_to_all.23.refs_4_), channel_id=1, source_target_pairs={{0,1},{1,0},{2,3},{3,2},{4,5},{5,4},{6,7},{7,6},{8,9},{9,8},{10,11... | collective-permute-start | bytes 1179656 | tf_op jit(solution)/shard_map/ppermute | solution.py:450
  165.0 1.3 collective-permute-done.9.refs_5_
  166.3 2.0 %finish_second.1 = (f32[2,2,64,128]{3,2,1,0:T(8,128)}, f32[32,64]{1,0:T(8,128)}) custom-call(f32[48,128]{1,0:T(8,128)S(1)} %get-tuple-element.38.refs_0_, f32[48,128]{1,0:T(8,128)S(1)} %collective-permute-done.7.refs_1_, f32[48,128]{1,0:T(8,128)S(1)} %collective-permute-done.8.refs_2_, f32[8,48,128]{2,1,0:T(8,128)S(1)} %all_to_all.22.refs_3_, ...), custom_call_target="tpu_custom_call" | custom-call | tf_op jit(solution)/shard_map/finish_second/pallas_call | solution.py:428
  (10 shorter events, 0.1 us)
Async XLA Ops:
  0.6 0.8 copy-start
  1.5 0.8 copy-start.2
  2.3 0.8 copy-start.4
  3.5 25.0 %collective-permute-start = (f32[208,128]{1,0:T(8,128)S(1)}, f32[208,128]{1,0:T(8,128)S(1)}, u32[]{:S(2)}, u32[]{:S(2)}) collective-permute-start(f32[208,128]{1,0:T(8,128)S(1)} %get-tuple-element.25), channel_id=1, source_target_pairs={{0,1},{1,0},{2,3},{3,2},{4,5},{5,4},{6,7},{7,6},{8,9},{9,8},{10,11... | collective-permute-start | bytes 319496 | tf_op jit(solution)/shard_map/ppermute | solution.py:450
  6.0 22.4 %collective-permute-start.1 = (f32[208,128]{1,0:T(8,128)S(1)}, f32[208,128]{1,0:T(8,128)S(1)}, u32[]{:S(2)}, u32[]{:S(2)}) collective-permute-start(f32[208,128]{1,0:T(8,128)S(1)} %get-tuple-element.26), channel_id=1, source_target_pairs={{0,63},{1,2},{2,1},{3,4},{4,3},{5,6},{6,5},{7,8},{8,7},{9,10},{10,... | collective-permute-start | bytes 319496 | tf_op jit(solution)/shard_map/ppermute | solution.py:455
  9.5 17.7 %collective-permute-start.3 = (f32[2,64,128]{2,1,0:T(8,128)S(1)}, f32[2,64,128]{2,1,0:T(8,128)S(1)}, u32[]{:S(2)}, u32[]{:S(2)}) collective-permute-start(f32[2,64,128]{2,1,0:T(8,128)S(1)} %bitcast.4), channel_id=1, source_target_pairs={{0,128},{64,192},{128,256},{192,320},{256,384},{320,448},{1,129},{... | collective-permute-start | bytes 196616 | tf_op jit(solution)/shard_map/ppermute | solution.py:460
  12.6 15.9 %collective-permute-start.2 = (f32[2,64,128]{2,1,0:T(8,128)S(1)}, f32[2,64,128]{2,1,0:T(8,128)S(1)}, u32[]{:S(2)}, u32[]{:S(2)}) collective-permute-start(f32[2,64,128]{2,1,0:T(8,128)S(1)} %bitcast.5), channel_id=1, source_target_pairs={{0,64},{64,128},{128,192},{192,256},{256,320},{320,384},{384,448},... | collective-permute-start | bytes 196616 | tf_op jit(solution)/shard_map/ppermute | solution.py:460
  28.8 10.6 %collective-permute-start.4 = (f32[144,128]{1,0:T(8,128)S(1)}, f32[144,128]{1,0:T(8,128)S(1)}, u32[]{:S(2)}, u32[]{:S(2)}) collective-permute-start(f32[144,128]{1,0:T(8,128)S(1)} %get-tuple-element.32), channel_id=1, source_target_pairs={{0,8},{8,0},{16,24},{24,16},{32,40},{40,32},{48,56},{56,48},{1,9},... | collective-permute-start | bytes 221192 | tf_op jit(solution)/shard_map/ppermute | solution.py:446
  32.8 16.5 %collective-permute-start.5 = (f32[144,128]{1,0:T(8,128)S(1)}, f32[144,128]{1,0:T(8,128)S(1)}, u32[]{:S(2)}, u32[]{:S(2)}) collective-permute-start(f32[144,128]{1,0:T(8,128)S(1)} %get-tuple-element.33), channel_id=1, source_target_pairs={{0,56},{8,16},{16,8},{24,32},{32,24},{40,48},{48,40},{56,0},{1,57}... | collective-permute-start | bytes 221192 | tf_op jit(solution)/shard_map/ppermute | solution.py:446
  78.3 24.4 %copy-start.1 = (f32[2,64,128]{2,1,0:T(8,128)S(1)}, f32[2,64,128]{2,1,0:T(8,128)}, u32[]{:S(2)}) copy-start(f32[2,64,128]{2,1,0:T(8,128)} %refs_10_.1) | copy-start | bytes 196612
  78.4 24.4 %copy-start.3 = (f32[2,64,128]{2,1,0:T(8,128)S(1)}, f32[2,64,128]{2,1,0:T(8,128)}, u32[]{:S(2)}) copy-start(f32[2,64,128]{2,1,0:T(8,128)} %refs_9_.1) | copy-start | bytes 196612
  97.0 5.7 %collective-permute-start.6 = (f32[4,320,128]{2,1,0:T(8,128)S(1)}, f32[4,320,128]{2,1,0:T(8,128)S(1)}, u32[]{:S(2)}, u32[]{:S(2)}) collective-permute-start(f32[4,320,128]{2,1,0:T(8,128)S(1)} %all_to_all.21.refs_4_), channel_id=1, source_target_pairs={{0,1},{1,0},{2,3},{3,2},{4,5},{5,4},{6,7},{7,6},{8,9},{9,8},{10,11... | collective-permute-start | bytes 1966088 | tf_op jit(solution)/shard_map/ppermute | solution.py:450
  105.0 9.8 %collective-permute-start.8 = (f32[48,128]{1,0:T(8,128)S(1)}, f32[48,128]{1,0:T(8,128)S(1)}, u32[]{:S(2)}, u32[]{:S(2)}) collective-permute-start(f32[48,128]{1,0:T(8,128)S(1)} %get-tuple-element.38.refs_0_), channel_id=1, source_target_pairs={{0,56},{8,16},{16,8},{24,32},{32,24},{40,48},{48,40},{56,0},{1,57}... | collective-permute-start | bytes 73736 | tf_op jit(solution)/shard_map/ppermute | solution.py:446
  111.1 8.7 %collective-permute-start.7 = (f32[48,128]{1,0:T(8,128)S(1)}, f32[48,128]{1,0:T(8,128)S(1)}, u32[]{:S(2)}, u32[]{:S(2)}) collective-permute-start(f32[48,128]{1,0:T(8,128)S(1)} %get-tuple-element.38.refs_0_), channel_id=1, source_target_pairs={{0,8},{8,0},{16,24},{24,16},{32,40},{40,32},{48,56},{56,48},{1,9},... | collective-permute-start | bytes 73736 | tf_op jit(solution)/shard_map/ppermute | solution.py:446
  160.8 5.5 %collective-permute-start.9 = (f32[4,192,128]{2,1,0:T(8,128)S(1)}, f32[4,192,128]{2,1,0:T(8,128)S(1)}, u32[]{:S(2)}, u32[]{:S(2)}) collective-permute-start(f32[4,192,128]{2,1,0:T(8,128)S(1)} %all_to_all.23.refs_4_), channel_id=1, source_target_pairs={{0,1},{1,0},{2,3},{3,2},{4,5},{5,4},{6,7},{7,6},{8,9},{9,8},{10,11... | collective-permute-start | bytes 1179656 | tf_op jit(solution)/shard_map/ppermute | solution.py:450

commit v8 on v7

--- a/solution.py
+++ b/solution.py
@@ -105,43 +105,41 @@
     return QUAD[row][0] * nodes[0] + QUAD[row][1] * nodes[1] + QUAD[row][2] * nodes[2]
 
 
-def packets(spot, up, down, inner, outer):
-    low = spot[2] == 0
-
-    @pl.when(low)
+def packets(spot, up, down, inner, outers):
+    def put(to_inner, to_outer):
+        whole = jnp.concatenate(to_outer, axis=0)
+        half = whole.shape[0] // 2
+        inner[...] = jnp.concatenate(to_inner, axis=0)
+        outers[0][...] = whole[:half]
+        outers[1][...] = whole[half:]
+
+    @pl.when(spot[2] == 0)
     def _():
-        for row, part_up, part_down in zip_rows(up, down):
-            inner[row : row + part_up.shape[0], :] = part_up
-            outer[row : row + part_up.shape[0], :] = part_down
-
-    @pl.when(jnp.logical_not(low))
+        put(up, down)
+
+    @pl.when(spot[2] != 0)
     def _():
-        for row, part_up, part_down in zip_rows(up, down):
-            inner[row : row + part_up.shape[0], :] = part_down
-            outer[row : row + part_up.shape[0], :] = part_up
-
-
-def zip_rows(up, down):
-    row = 0
-    for part_up, part_down in zip(up, down):
-        yield row, part_up, part_down
-        row += part_up.shape[0]
-
-
-def sides(spot, inner, outer):
+        put(down, up)
+
+
+def sides(spot, inner, outer, outer_rest):
     low = jnp.full(inner.shape, spot[2], jnp.int32) == 0
-    a, b = inner[...], outer[...]
+    a, b = inner[...], jnp.concatenate([outer[...], outer_rest[...]], axis=0)
     return jnp.where(low, b, a), jnp.where(low, a, b)
 
 
-def first_kernel(spot, initial, coeff, guess, inner, outer, keep, scratch):
+def first_kernel(
+    spot, initial, coeff, guess, inner, outer, outer_rest, keep, initial_out, coeff_out, guess_out, scratch
+):
+    for out, given in ((initial_out, initial), (coeff_out, coeff), (guess_out, guess)):
+        out[...] = given[...]
     u = [guess[0], guess[1]]
     c = [coeff[0], coeff[1]]
     both = u[0] + u[1]
     total = around(both) - 5.0 * both + c[0] * cubic(u[0]) + c[1] * cubic(u[1])
     own, value, coef, start = squash([total, both, c[0] + c[1], initial[0] + initial[1]], scratch)
     value, coef, start = 0.125 * value, 0.125 * coef, 0.125 * start
-    packets(spot, u + [c[1], pack(start)], u + [c[0], pack(start)], inner, outer)
+    packets(spot, u + [c[1], pack(start)], u + [c[0], pack(start)], inner, [outer, outer_rest])
     keep[0] = own
     keep[1] = value
     keep[2] = coef
@@ -154,9 +152,9 @@
 
 
 def complete_first(
-    spot, inner, outer, kept, initial, received, owned, beside, beyond, mine, keep, begin_out, scratch
+    spot, inner, outer, outer_rest, kept, initial, received, owned, beside, beyond, mine, keep, begin_out, scratch
 ):
-    below, above = sides(spot, inner, outer)
+    below, above = sides(spot, inner, outer, outer_rest)
     begin = starting(spot, initial, received)
     own, value, coef, start = (kept[i] for i in range(4))
     low, high, value_low, value_high, value_begin = squash(
@@ -333,13 +331,13 @@
 
 
 def finish_first(
-    spot, owned, beside, beyond, sections, windows, swapped, started, kept, inner, outer, initial, coeff, guess, begin,
-    earlier, middle_out, end_out, ends, begin_out, keep, owned_out, mine, coefs, line, history, scratch,
+    spot, owned, beside, beyond, sections, windows, swapped, started, kept, inner, outer, outer_rest, initial, coeff,
+    guess, begin, earlier, middle_out, end_out, ends, begin_out, keep, owned_out, mine, coefs, line, history, scratch,
 ):
     fetch = sweep(
         spot, ITEMS[0], ROWS[0], owned, beside, beyond, sections, windows, swapped, coefs, started, line, history
     )
-    below, above = sides(spot, inner, outer)
+    below, above = sides(spot, inner, outer, outer_rest)
     section = spot[0]
     later = jnp.full((32, 128), section, jnp.int32) > 0
     s = [history[5 * section + i] for i in range(5)]
@@ -431,7 +429,7 @@
         in_specs=[pl.BlockSpec(memory_space=pltpu.VMEM)] * len(args),
         out_specs=[pl.BlockSpec(memory_space=pltpu.VMEM)] * len(outs),
         scratch_shapes=[pltpu.VMEM(shape, F32) for shape in scratch],
-        compiler_params=pltpu.CompilerParams(vmem_limit_bytes=16 << 20),
+        compiler_params=None if first else pltpu.CompilerParams(vmem_limit_bytes=16 << 20),
         name=name,
     )(*(a if first else pltpu.with_memory_space_constraint(a, pltpu.VMEM) for a in args))
 
@@ -489,21 +487,24 @@
         parcels = links.block(parcels)
         return owned, beside, beyond, sections, parcels, links.swap_inner(parcels)
 
-    inner, outer, kept = links.call(
-        first_kernel, (initial, coeff, guess), [(208, 128), (208, 128), (4,) + coarse], [(256, 128)], name="first",
-        first=True,
-    )
-    inner, outer, received, earlier = links.together(
-        links.swap_inner(inner), links.swap_outer(outer), links.onward(guess, 1), links.onward(guess, 2)
+    sent = guess
+    inner, outer, outer_rest, kept, initial, coeff, guess = links.call(
+        first_kernel, (initial, coeff, guess),
+        [(208, 128), (104, 128), (104, 128), (4,) + coarse, slab, slab, slab], [(256, 128)], name="first", first=True,
+    )
+    inner, outer, outer_rest, received, earlier = links.together(
+        links.swap_inner(inner), links.swap_outer(outer), links.swap_outer(outer_rest), links.onward(sent, 1),
+        links.onward(sent, 2),
     )
     owned, beside, beyond, mine, started, begin = links.call(
-        complete_first, (inner, outer, kept, initial, received),
+        complete_first, (inner, outer, outer_rest, kept, initial, received),
         [(208, 128), (144, 128), (144, 128), (16, 128), (8,) + coarse, slab], [(320, 128)], name="complete_first",
     )
     beside, beyond = links.swap_block(beside, True), links.swap_block(beyond, False)
     middle, end, ends, begin_next, kept, owned, mine, coefs = links.call(
         finish_first,
-        (*windows(owned, beside, beyond, mine, 0), started, kept, inner, outer, initial, coeff, guess, begin, earlier),
+        (*windows(owned, beside, beyond, mine, 0), started, kept, inner, outer, outer_rest, initial, coeff, guess, begin,
+         earlier),
         [slab, slab, (4, 64, 128), slab, (5,) + coarse, (48, 128), (16, 128), (15,) + coarse],
         work + [(576, 128)],
         name="finish_first",

time: 169 us -> 166 us (0.982)
  the two profiles are of different devices: /device:TPU:17 before, /device:TPU:1 now
where the time goes in v8:
time: 166 us; the launch traced here: 165 us
  blocking collectives  83.2 us (50%)
  starting transfers between devices  54.1 us (33%)
  waiting for transfers between devices  21.2 us (13%)
  Pallas kernels  5.87 us (4%)
    all_to_all x2, blocking collectives, block(): return lax.all_to_all(x, 'chip', 0, 0)  41.9 us
    all_to_all x2, blocking collectives, sections(): lax.all_to_all(jnp.broadcast_to(x, (SECTIONS,) + x.shape), 'tm', 0, 0)  41.3 us
    ppermute x4, starting transfers between devices, swap_block(): return lax.ppermute(x, 'block', pairs)  18.7 us
    ppermute x3, starting transfers between devices, swap_inner(): return lax.ppermute(x, 'core', [(0, 1), (1, 0)])  16.6 us
    ppermute x4, waiting for transfers between devices, swap_block(): return lax.ppermute(x, 'block', pairs)  15.2 us
    ppermute x2, starting transfers between devices, onward(): return lax.ppermute(x, 'tm', [(i, i + by) for i in range(n - by)])  13.2 us
    pallas_call x6, Pallas kernels, run(): pl.pallas_call(placed, out_shape=[jax.ShapeDtypeStruct(shape, F32) if las...  5.87 us
    ppermute x2, starting transfers between devices, swap_outer(): lax.ppermute(x, ('block', 'chip', 'core'), [(i, (i + 2 * (i % 2) - 1) % n...  5.56 us
  transfers between devices with their start and end apart: 11, of which 8 were waited for; matrix products, arithmetic and copies ran while one was open for 0% of the time, Pallas kernels for 0%

profile of v8, /device:TPU:1, one launch (start us, length us, event | category | flops | bytes accessed | tf_op | source)
XLA Modules:
  0.0 165.3 jit_solution(8151824680715202981)
XLA Ops:
  0.6 0.0 copy-start
  0.6 1.2 first.1
  1.9 8.8 %collective-permute-start = (f32[208,128]{1,0:T(8,128)S(1)}, f32[208,128]{1,0:T(8,128)S(1)}, u32[]{:S(2)}, u32[]{:S(2)}) collective-permute-start(f32[208,128]{1,0:T(8,128)S(1)} %get-tuple-element.30), channel_id=1, source_target_pairs={{0,1},{1,0},{2,3},{3,2},{4,5},{5,4},{6,7},{7,6},{8,9},{9,8},{10,11... | collective-permute-start | bytes 319496 | tf_op jit(solution)/shard_map/ppermute | solution.py:448
  10.7 0.0 copy-done
  10.7 1.3 collective-permute-start.4
  12.0 11.9 %collective-permute-start.3 = (f32[2,64,128]{2,1,0:T(8,128)S(1)}, f32[2,64,128]{2,1,0:T(8,128)S(1)}, u32[]{:S(2)}, u32[]{:S(2)}) collective-permute-start(f32[2,64,128]{2,1,0:T(8,128)S(1)} %bitcast.5), channel_id=1, source_target_pairs={{0,64},{64,128},{128,192},{192,256},{256,320},{320,384},{384,448},... | collective-permute-start | bytes 196616 | tf_op jit(solution)/shard_map/ppermute | solution.py:458
  23.9 3.1 %collective-permute-start.1 = (f32[104,128]{1,0:T(8,128)S(1)}, f32[104,128]{1,0:T(8,128)S(1)}, u32[]{:S(2)}, u32[]{:S(2)}) collective-permute-start(f32[104,128]{1,0:T(8,128)S(1)} %get-tuple-element.31), channel_id=1, source_target_pairs={{0,63},{1,2},{2,1},{3,4},{4,3},{5,6},{6,5},{7,8},{8,7},{9,10},{10,... | collective-permute-start | bytes 159752 | tf_op jit(solution)/shard_map/ppermute | solution.py:453
  27.0 2.5 %collective-permute-start.2 = (f32[104,128]{1,0:T(8,128)S(1)}, f32[104,128]{1,0:T(8,128)S(1)}, u32[]{:S(2)}, u32[]{:S(2)}) collective-permute-start(f32[104,128]{1,0:T(8,128)S(1)} %get-tuple-element.32), channel_id=1, source_target_pairs={{0,63},{1,2},{2,1},{3,4},{4,3},{5,6},{6,5},{7,8},{8,7},{9,10},{10,... | collective-permute-start | bytes 159752 | tf_op jit(solution)/shard_map/ppermute | solution.py:453
  29.5 2.3 %collective-permute-done.1.refs_1_.refs_9_ = f32[104,128]{1,0:T(8,128)S(1)} collective-permute-done((f32[104,128]{1,0:T(8,128)S(1)}, f32[104,128]{1,0:T(8,128)S(1)}, u32[]{:S(2)}, u32[]{:S(2)}) %collective-permute-start.1) | collective-permute-done | bytes 53280 | tf_op jit(solution)/shard_map/ppermute | solution.py:453
  31.8 0.7 collective-permute-done.2.refs_2_.refs_10_
  32.5 0.0 collective-permute-done.4.refs_15_
  32.5 0.0 collective-permute-done.3.refs_5_
  32.5 0.0 collective-permute-done.refs_0_.refs_8_
  32.5 0.3 complete_first.1
  32.7 4.3 %collective-permute-start.5 = (f32[144,128]{1,0:T(8,128)S(1)}, f32[144,128]{1,0:T(8,128)S(1)}, u32[]{:S(2)}, u32[]{:S(2)}) collective-permute-start(f32[144,128]{1,0:T(8,128)S(1)} %get-tuple-element.40), channel_id=1, source_target_pairs={{0,8},{8,0},{16,24},{24,16},{32,40},{40,32},{48,56},{56,48},{1,9},... | collective-permute-start | bytes 221192 | tf_op jit(solution)/shard_map/ppermute | solution.py:444
  37.1 7.3 %collective-permute-start.6 = (f32[144,128]{1,0:T(8,128)S(1)}, f32[144,128]{1,0:T(8,128)S(1)}, u32[]{:S(2)}, u32[]{:S(2)}) collective-permute-start(f32[144,128]{1,0:T(8,128)S(1)} %get-tuple-element.41), channel_id=1, source_target_pairs={{0,56},{8,16},{16,8},{24,32},{32,24},{40,48},{48,40},{56,0},{1,57}... | collective-permute-start | bytes 221192 | tf_op jit(solution)/shard_map/ppermute | solution.py:444
  44.4 1.9 %collective-permute-done.5.refs_1_ = f32[144,128]{1,0:T(8,128)S(1)} collective-permute-done((f32[144,128]{1,0:T(8,128)S(1)}, f32[144,128]{1,0:T(8,128)S(1)}, u32[]{:S(2)}, u32[]{:S(2)}) %collective-permute-start.5) | collective-permute-done | bytes 73760 | tf_op jit(solution)/shard_map/ppermute | solution.py:444
  46.3 7.2 %collective-permute-done.6.refs_2_ = f32[144,128]{1,0:T(8,128)S(1)} collective-permute-done((f32[144,128]{1,0:T(8,128)S(1)}, f32[144,128]{1,0:T(8,128)S(1)}, u32[]{:S(2)}, u32[]{:S(2)}) %collective-permute-start.6) | collective-permute-done | bytes 73760 | tf_op jit(solution)/shard_map/ppermute | solution.py:444
  53.5 23.5 %all_to_all.20.refs_3_ = f32[8,48,128]{2,1,0:T(8,128)S(1)} all-to-all(f32[8,48,128]{2,1,0:T(8,128)S(1)} %broadcast_in_dim.12), channel_id=1, replica_groups=mesh['tm'=8,'block'=8,'chip'=4,'core'=2] {'tm'}, dimensions={0} | all-to-all | bytes 393216 | tf_op jit(solution)/shard_map/all_to_all | solution.py:462
  77.0 22.2 %all_to_all.21.refs_4_ = f32[4,320,128]{2,1,0:T(8,128)S(1)} all-to-all(f32[4,320,128]{2,1,0:T(8,128)S(1)} %hand_out.2), channel_id=1, replica_groups=mesh['tm'=8,'block'=8,'chip'=4,'core'=2] {'chip'}, dimensions={0} | all-to-all | bytes 1310720 | tf_op jit(solution)/shard_map/all_to_all | solution.py:466
  99.3 4.5 %collective-permute-start.7 = (f32[4,320,128]{2,1,0:T(8,128)S(1)}, f32[4,320,128]{2,1,0:T(8,128)S(1)}, u32[]{:S(2)}, u32[]{:S(2)}) collective-permute-start(f32[4,320,128]{2,1,0:T(8,128)S(1)} %all_to_all.21.refs_4_), channel_id=1, source_target_pairs={{0,1},{1,0},{2,3},{3,2},{4,5},{5,4},{6,7},{7,6},{8,9},{9,8},{10,11... | collective-permute-start | bytes 1966088 | tf_op jit(solution)/shard_map/ppermute | solution.py:448
  103.8 1.7 %collective-permute-done.7.refs_5_ = f32[4,320,128]{2,1,0:T(8,128)S(1)} collective-permute-done((f32[4,320,128]{2,1,0:T(8,128)S(1)}, f32[4,320,128]{2,1,0:T(8,128)S(1)}, u32[]{:S(2)}, u32[]{:S(2)}) %collective-permute-start.7) | collective-permute-done | bytes 655392 | tf_op jit(solution)/shard_map/ppermute | solution.py:448
  105.5 2.2 %finish_first.1 = (f32[2,64,128]{2,1,0:T(8,128)S(1)}, f32[2,64,128]{2,1,0:T(8,128)S(1)}, f32[4,64,128]{2,1,0:T(8,128)S(1)}, f32[2,64,128]{2,1,0:T(8,128)S(1)}, f...) custom-call(f32[208,128]{1,0:T(8,128)S(1)} %get-tuple-element.39.refs_0_, ...), custom_call_target="tpu_custom_call" | custom-call | tf_op jit(solution)/shard_map/finish_first/pallas_call | solution.py:426
  107.7 4.6 %collective-permute-start.9 = (f32[48,128]{1,0:T(8,128)S(1)}, f32[48,128]{1,0:T(8,128)S(1)}, u32[]{:S(2)}, u32[]{:S(2)}) collective-permute-start(f32[48,128]{1,0:T(8,128)S(1)} %get-tuple-element.48.refs_0_), channel_id=1, source_target_pairs={{0,56},{8,16},{16,8},{24,32},{32,24},{40,48},{48,40},{56,0},{1,57}... | collective-permute-start | bytes 73736 | tf_op jit(solution)/shard_map/ppermute | solution.py:444
  112.3 2.5 %collective-permute-start.8 = (f32[48,128]{1,0:T(8,128)S(1)}, f32[48,128]{1,0:T(8,128)S(1)}, u32[]{:S(2)}, u32[]{:S(2)}) collective-permute-start(f32[48,128]{1,0:T(8,128)S(1)} %get-tuple-element.48.refs_0_), channel_id=1, source_target_pairs={{0,8},{8,0},{16,24},{24,16},{32,40},{40,32},{48,56},{56,48},{1,9},... | collective-permute-start | bytes 73736 | tf_op jit(solution)/shard_map/ppermute | solution.py:444
  114.8 3.7 %collective-permute-done.9.refs_2_ = f32[48,128]{1,0:T(8,128)S(1)} collective-permute-done((f32[48,128]{1,0:T(8,128)S(1)}, f32[48,128]{1,0:T(8,128)S(1)}, u32[]{:S(2)}, u32[]{:S(2)}) %collective-permute-start.9) | collective-permute-done | bytes 24608 | tf_op jit(solution)/shard_map/ppermute | solution.py:444
  118.5 2.5 %collective-permute-done.8.refs_1_ = f32[48,128]{1,0:T(8,128)S(1)} collective-permute-done((f32[48,128]{1,0:T(8,128)S(1)}, f32[48,128]{1,0:T(8,128)S(1)}, u32[]{:S(2)}, u32[]{:S(2)}) %collective-permute-start.8) | collective-permute-done | bytes 24608 | tf_op jit(solution)/shard_map/ppermute | solution.py:444
  121.0 17.8 %all_to_all.22.refs_3_ = f32[8,48,128]{2,1,0:T(8,128)S(1)} all-to-all(f32[8,48,128]{2,1,0:T(8,128)S(1)} %broadcast_in_dim.13), channel_id=1, replica_groups=mesh['tm'=8,'block'=8,'chip'=4,'core'=2] {'tm'}, dimensions={0} | all-to-all | bytes 393216 | tf_op jit(solution)/shard_map/all_to_all | solution.py:462
  138.9 19.7 %all_to_all.23.refs_4_ = f32[4,192,128]{2,1,0:T(8,128)S(1)} all-to-all(f32[4,192,128]{2,1,0:T(8,128)S(1)} %hand_out.3), channel_id=1, replica_groups=mesh['tm'=8,'block'=8,'chip'=4,'core'=2] {'chip'}, dimensions={0} | all-to-all | bytes 786432 | tf_op jit(solution)/shard_map/all_to_all | solution.py:466
  158.6 3.3 %collective-permute-start.10 = (f32[4,192,128]{2,1,0:T(8,128)S(1)}, f32[4,192,128]{2,1,0:T(8,128)S(1)}, u32[]{:S(2)}, u32[]{:S(2)}) collective-permute-start(f32[4,192,128]{2,1,0:T(8,128)S(1)} %all_to_all.23.refs_4_), channel_id=1, source_target_pairs={{0,1},{1,0},{2,3},{3,2},{4,5},{5,4},{6,7},{7,6},{8,9},{9,8},{10,11... | collective-permute-start | bytes 1179656 | tf_op jit(solution)/shard_map/ppermute | solution.py:448
  161.9 1.3 collective-permute-done.10.refs_5_
  163.2 2.0 %finish_second.1 = (f32[2,2,64,128]{3,2,1,0:T(8,128)}, f32[32,64]{1,0:T(8,128)}) custom-call(f32[48,128]{1,0:T(8,128)S(1)} %get-tuple-element.48.refs_0_, f32[48,128]{1,0:T(8,128)S(1)} %collective-permute-done.8.refs_1_, f32[48,128]{1,0:T(8,128)S(1)} %collective-permute-done.9.refs_2_, f32[8,48,128]{2,1,0:T(8,128)S(1)} %all_to_all.22.refs_3_, ...), custom_call_target="tpu_custom_call" | custom-call | tf_op jit(solution)/shard_map/finish_second/pallas_call | solution.py:426
  (10 shorter events, 0.1 us)
Async XLA Ops:
  0.6 10.1 %copy-start = (f32[1,2,64,128]{3,2,1,0:T(8,128)S(1)}, f32[1,2,64,128]{3,2,1,0:T(8,128)}, u32[]{:S(2)}) copy-start(f32[1,2,64,128]{3,2,1,0:T(8,128)} %param.5) | copy-start | bytes 196612
  1.9 30.6 %collective-permute-start = (f32[208,128]{1,0:T(8,128)S(1)}, f32[208,128]{1,0:T(8,128)S(1)}, u32[]{:S(2)}, u32[]{:S(2)}) collective-permute-start(f32[208,128]{1,0:T(8,128)S(1)} %get-tuple-element.30), channel_id=1, source_target_pairs={{0,1},{1,0},{2,3},{3,2},{4,5},{5,4},{6,7},{7,6},{8,9},{9,8},{10,11... | collective-permute-start | bytes 319496 | tf_op jit(solution)/shard_map/ppermute | solution.py:448
  10.7 21.8 %collective-permute-start.4 = (f32[2,64,128]{2,1,0:T(8,128)S(1)}, f32[2,64,128]{2,1,0:T(8,128)S(1)}, u32[]{:S(2)}, u32[]{:S(2)}) collective-permute-start(f32[2,64,128]{2,1,0:T(8,128)S(1)} %bitcast.4), channel_id=1, source_target_pairs={{0,128},{64,192},{128,256},{192,320},{256,384},{320,448},{1,129},{... | collective-permute-start | bytes 196616 | tf_op jit(solution)/shard_map/ppermute | solution.py:458
  12.0 20.5 %collective-permute-start.3 = (f32[2,64,128]{2,1,0:T(8,128)S(1)}, f32[2,64,128]{2,1,0:T(8,128)S(1)}, u32[]{:S(2)}, u32[]{:S(2)}) collective-permute-start(f32[2,64,128]{2,1,0:T(8,128)S(1)} %bitcast.5), channel_id=1, source_target_pairs={{0,64},{64,128},{128,192},{192,256},{256,320},{320,384},{384,448},... | collective-permute-start | bytes 196616 | tf_op jit(solution)/shard_map/ppermute | solution.py:458
  23.9 7.9 %collective-permute-start.1 = (f32[104,128]{1,0:T(8,128)S(1)}, f32[104,128]{1,0:T(8,128)S(1)}, u32[]{:S(2)}, u32[]{:S(2)}) collective-permute-start(f32[104,128]{1,0:T(8,128)S(1)} %get-tuple-element.31), channel_id=1, source_target_pairs={{0,63},{1,2},{2,1},{3,4},{4,3},{5,6},{6,5},{7,8},{8,7},{9,10},{10,... | collective-permute-start | bytes 159752 | tf_op jit(solution)/shard_map/ppermute | solution.py:453
  27.0 5.5 %collective-permute-start.2 = (f32[104,128]{1,0:T(8,128)S(1)}, f32[104,128]{1,0:T(8,128)S(1)}, u32[]{:S(2)}, u32[]{:S(2)}) collective-permute-start(f32[104,128]{1,0:T(8,128)S(1)} %get-tuple-element.32), channel_id=1, source_target_pairs={{0,63},{1,2},{2,1},{3,4},{4,3},{5,6},{6,5},{7,8},{8,7},{9,10},{10,... | collective-permute-start | bytes 159752 | tf_op jit(solution)/shard_map/ppermute | solution.py:453
  32.7 13.5 %collective-permute-start.5 = (f32[144,128]{1,0:T(8,128)S(1)}, f32[144,128]{1,0:T(8,128)S(1)}, u32[]{:S(2)}, u32[]{:S(2)}) collective-permute-start(f32[144,128]{1,0:T(8,128)S(1)} %get-tuple-element.40), channel_id=1, source_target_pairs={{0,8},{8,0},{16,24},{24,16},{32,40},{40,32},{48,56},{56,48},{1,9},... | collective-permute-start | bytes 221192 | tf_op jit(solution)/shard_map/ppermute | solution.py:444
  37.1 16.4 %collective-permute-start.6 = (f32[144,128]{1,0:T(8,128)S(1)}, f32[144,128]{1,0:T(8,128)S(1)}, u32[]{:S(2)}, u32[]{:S(2)}) collective-permute-start(f32[144,128]{1,0:T(8,128)S(1)} %get-tuple-element.41), channel_id=1, source_target_pairs={{0,56},{8,16},{16,8},{24,32},{32,24},{40,48},{48,40},{56,0},{1,57}... | collective-permute-start | bytes 221192 | tf_op jit(solution)/shard_map/ppermute | solution.py:444
  99.3 6.2 %collective-permute-start.7 = (f32[4,320,128]{2,1,0:T(8,128)S(1)}, f32[4,320,128]{2,1,0:T(8,128)S(1)}, u32[]{:S(2)}, u32[]{:S(2)}) collective-permute-start(f32[4,320,128]{2,1,0:T(8,128)S(1)} %all_to_all.21.refs_4_), channel_id=1, source_target_pairs={{0,1},{1,0},{2,3},{3,2},{4,5},{5,4},{6,7},{7,6},{8,9},{9,8},{10,11... | collective-permute-start | bytes 1966088 | tf_op jit(solution)/shard_map/ppermute | solution.py:448
  107.7 10.8 %collective-permute-start.9 = (f32[48,128]{1,0:T(8,128)S(1)}, f32[48,128]{1,0:T(8,128)S(1)}, u32[]{:S(2)}, u32[]{:S(2)}) collective-permute-start(f32[48,128]{1,0:T(8,128)S(1)} %get-tuple-element.48.refs_0_), channel_id=1, source_target_pairs={{0,56},{8,16},{16,8},{24,32},{32,24},{40,48},{48,40},{56,0},{1,57}... | collective-permute-start | bytes 73736 | tf_op jit(solution)/shard_map/ppermute | solution.py:444
  112.3 8.7 %collective-permute-start.8 = (f32[48,128]{1,0:T(8,128)S(1)}, f32[48,128]{1,0:T(8,128)S(1)}, u32[]{:S(2)}, u32[]{:S(2)}) collective-permute-start(f32[48,128]{1,0:T(8,128)S(1)} %get-tuple-element.48.refs_0_), channel_id=1, source_target_pairs={{0,8},{8,0},{16,24},{24,16},{32,40},{40,32},{48,56},{56,48},{1,9},... | collective-permute-start | bytes 73736 | tf_op jit(solution)/shard_map/ppermute | solution.py:444
  158.6 4.7 %collective-permute-start.10 = (f32[4,192,128]{2,1,0:T(8,128)S(1)}, f32[4,192,128]{2,1,0:T(8,128)S(1)}, u32[]{:S(2)}, u32[]{:S(2)}) collective-permute-start(f32[4,192,128]{2,1,0:T(8,128)S(1)} %all_to_all.23.refs_4_), channel_id=1, source_target_pairs={{0,1},{1,0},{2,3},{3,2},{4,5},{5,4},{6,7},{7,6},{8,9},{9,8},{10,11... | collective-permute-start | bytes 1179656 | tf_op jit(solution)/shard_map/ppermute | solution.py:448

commit v9 on v8

--- a/solution.py
+++ b/solution.py
@@ -105,13 +105,13 @@
     return QUAD[row][0] * nodes[0] + QUAD[row][1] * nodes[1] + QUAD[row][2] * nodes[2]
 
 
-def packets(spot, up, down, inner, outers):
+def packets(spot, up, down, inners, outers):
     def put(to_inner, to_outer):
-        whole = jnp.concatenate(to_outer, axis=0)
-        half = whole.shape[0] // 2
-        inner[...] = jnp.concatenate(to_inner, axis=0)
-        outers[0][...] = whole[:half]
-        outers[1][...] = whole[half:]
+        for parts, outs in ((to_inner, inners), (to_outer, outers)):
+            whole = jnp.concatenate(parts, axis=0)
+            half = whole.shape[0] // 2
+            outs[0][...] = whole[:half]
+            outs[1][...] = whole[half:]
 
     @pl.when(spot[2] == 0)
     def _():
@@ -122,14 +122,15 @@
         put(down, up)
 
 
-def sides(spot, inner, outer, outer_rest):
-    low = jnp.full(inner.shape, spot[2], jnp.int32) == 0
-    a, b = inner[...], jnp.concatenate([outer[...], outer_rest[...]], axis=0)
+def sides(spot, inner, inner_rest, outer, outer_rest):
+    a = jnp.concatenate([inner[...], inner_rest[...]], axis=0)
+    b = jnp.concatenate([outer[...], outer_rest[...]], axis=0)
+    low = jnp.full(a.shape, spot[2], jnp.int32) == 0
     return jnp.where(low, b, a), jnp.where(low, a, b)
 
 
 def first_kernel(
-    spot, initial, coeff, guess, inner, outer, outer_rest, keep, initial_out, coeff_out, guess_out, scratch
+    spot, initial, coeff, guess, inner, inner_rest, outer, outer_rest, keep, initial_out, coeff_out, guess_out, scratch
 ):
     for out, given in ((initial_out, initial), (coeff_out, coeff), (guess_out, guess)):
         out[...] = given[...]
@@ -139,7 +140,7 @@
     total = around(both) - 5.0 * both + c[0] * cubic(u[0]) + c[1] * cubic(u[1])
     own, value, coef, start = squash([total, both, c[0] + c[1], initial[0] + initial[1]], scratch)
     value, coef, start = 0.125 * value, 0.125 * coef, 0.125 * start
-    packets(spot, u + [c[1], pack(start)], u + [c[0], pack(start)], inner, [outer, outer_rest])
+    packets(spot, u + [c[1], pack(start)], u + [c[0], pack(start)], [inner, inner_rest], [outer, outer_rest])
     keep[0] = own
     keep[1] = value
     keep[2] = coef
@@ -152,9 +153,10 @@
 
 
 def complete_first(
-    spot, inner, outer, outer_rest, kept, initial, received, owned, beside, beyond, mine, keep, begin_out, scratch
+    spot, inner, inner_rest, outer, outer_rest, kept, initial, received, owned, beside, beyond, mine, keep, begin_out,
+    scratch,
 ):
-    below, above = sides(spot, inner, outer, outer_rest)
+    below, above = sides(spot, inner, inner_rest, outer, outer_rest)
     begin = starting(spot, initial, received)
     own, value, coef, start = (kept[i] for i in range(4))
     low, high, value_low, value_high, value_begin = squash(
@@ -331,13 +333,13 @@
 
 
 def finish_first(
-    spot, owned, beside, beyond, sections, windows, swapped, started, kept, inner, outer, outer_rest, initial, coeff,
-    guess, begin, earlier, middle_out, end_out, ends, begin_out, keep, owned_out, mine, coefs, line, history, scratch,
+    spot, owned, beside, beyond, sections, windows, swapped, started, kept, inner, inner_rest, outer, outer_rest,
+    initial, coeff, guess, begin, earlier, middle_out, end_out, ends, begin_out, keep, owned_out, mine, coefs, line, history, scratch,
 ):
     fetch = sweep(
         spot, ITEMS[0], ROWS[0], owned, beside, beyond, sections, windows, swapped, coefs, started, line, history
     )
-    below, above = sides(spot, inner, outer, outer_rest)
+    below, above = sides(spot, inner, inner_rest, outer, outer_rest)
     section = spot[0]
     later = jnp.full((32, 128), section, jnp.int32) > 0
     s = [history[5 * section + i] for i in range(5)]
@@ -488,23 +490,25 @@
         return owned, beside, beyond, sections, parcels, links.swap_inner(parcels)
 
     sent = guess
-    inner, outer, outer_rest, kept, initial, coeff, guess = links.call(
+    inner, inner_rest, outer, outer_rest, kept, initial, coeff, guess = links.call(
         first_kernel, (initial, coeff, guess),
-        [(208, 128), (104, 128), (104, 128), (4,) + coarse, slab, slab, slab], [(256, 128)], name="first", first=True,
-    )
-    inner, outer, outer_rest, received, earlier = links.together(
-        links.swap_inner(inner), links.swap_outer(outer), links.swap_outer(outer_rest), links.onward(sent, 1),
-        links.onward(sent, 2),
+        [(104, 128)] * 4 + [(4,) + coarse, slab, slab, slab], [(256, 128)], name="first", first=True,
+    )
+    outer, outer_rest, inner, inner_rest, received = links.together(
+        links.swap_outer(outer), links.swap_outer(outer_rest), links.swap_inner(inner), links.swap_inner(inner_rest),
+        links.onward(sent, 1),
     )
     owned, beside, beyond, mine, started, begin = links.call(
-        complete_first, (inner, outer, outer_rest, kept, initial, received),
+        complete_first, (inner, inner_rest, outer, outer_rest, kept, initial, received),
         [(208, 128), (144, 128), (144, 128), (16, 128), (8,) + coarse, slab], [(320, 128)], name="complete_first",
     )
-    beside, beyond = links.swap_block(beside, True), links.swap_block(beyond, False)
+    beside, beyond, earlier = links.together(
+        links.swap_block(beside, True), links.swap_block(beyond, False), links.onward(sent, 2)
+    )
     middle, end, ends, begin_next, kept, owned, mine, coefs = links.call(
         finish_first,
-        (*windows(owned, beside, beyond, mine, 0), started, kept, inner, outer, outer_rest, initial, coeff, guess, begin,
-         earlier),
+        (*windows(owned, beside, beyond, mine, 0), started, kept, inner, inner_rest, outer, outer_rest, initial,
+         coeff, guess, begin, earlier),
         [slab, slab, (4, 64, 128), slab, (5,) + coarse, (48, 128), (16, 128), (15,) + coarse],
         work + [(576, 128)],
         name="finish_first",

time: 166 us -> 161 us (0.970)
  starting transfers between devices: 54.1 us -> 70.7 us
  waiting for transfers between devices: 21.2 us -> 9.56 us
  blocking collectives: 83.2 us -> 73 us
    ppermute x4, waiting for transfers between devices: 15.2 us -> 4.04 us  [swap_block(): return lax.ppermute(x, 'block', pairs)]
    ppermute x3 -> x4, starting transfers between devices: 16.6 us -> 24.5 us  [swap_inner(): return lax.ppermute(x, 'core', [(0, 1), (1, 0)])]
    ppermute x2, starting transfers between devices: 13.2 us -> 19.4 us  [onward(): return lax.ppermute(x, 'tm', [(i, i + by) for i in range(n - by)])]
    all_to_all x2, blocking collectives: 41.9 us -> 36.2 us  [block(): return lax.all_to_all(x, 'chip', 0, 0)]
    all_to_all x2, blocking collectives: 41.3 us -> 36.8 us  [sections(): lax.all_to_all(jnp.broadcast_to(x, (SECTIONS,) + x.shape), 'tm', 0, 0)]
    ppermute x2, waiting for transfers between devices: 2.98 us -> 0.01 us  [swap_outer(): lax.ppermute(x, ('block', 'chip', 'core'), [(i, (i + 2 * (i % 2) - 1) % n...]
    ppermute x4, starting transfers between devices: 18.7 us -> 21.2 us  [swap_block(): return lax.ppermute(x, 'block', pairs)]
    ppermute x3 -> x4, waiting for transfers between devices: 3.03 us -> 4.2 us  [swap_inner(): return lax.ppermute(x, 'core', [(0, 1), (1, 0)])]
  transfers between devices with their start and end apart: 11 -> 12, of which waited for: 8 -> 5; matrix products, arithmetic and copies ran while one was open for 0% -> 0% of each run, Pallas kernels for 0% -> 1%
where the time goes in v9:
time: 161 us; the launch traced here: 160 us
  blocking collectives  73 us (45%)
  starting transfers between devices  70.7 us (44%)
  waiting for transfers between devices  9.56 us (6%)
  Pallas kernels  5.84 us (4%)
    all_to_all x2, blocking collectives, sections(): lax.all_to_all(jnp.broadcast_to(x, (SECTIONS,) + x.shape), 'tm', 0, 0)  36.8 us
    all_to_all x2, blocking collectives, block(): return lax.all_to_all(x, 'chip', 0, 0)  36.2 us
    ppermute x4, starting transfers between devices, swap_inner(): return lax.ppermute(x, 'core', [(0, 1), (1, 0)])  24.5 us
    ppermute x4, starting transfers between devices, swap_block(): return lax.ppermute(x, 'block', pairs)  21.2 us
    ppermute x2, starting transfers between devices, onward(): return lax.ppermute(x, 'tm', [(i, i + by) for i in range(n - by)])  19.4 us
    pallas_call x6, Pallas kernels, run(): pl.pallas_call(placed, out_shape=[jax.ShapeDtypeStruct(shape, F32) if las...  5.84 us
    ppermute x2, starting transfers between devices, swap_outer(): lax.ppermute(x, ('block', 'chip', 'core'), [(i, (i + 2 * (i % 2) - 1) % n...  5.56 us
    ppermute x4, waiting for transfers between devices, swap_inner(): return lax.ppermute(x, 'core', [(0, 1), (1, 0)])  4.2 us
  transfers between devices with their start and end apart: 12, of which 5 were waited for; matrix products, arithmetic and copies ran while one was open for 0% of the time, Pallas kernels for 1%

profile of v9, /device:TPU:1, one launch (start us, length us, event | category | flops | bytes accessed | tf_op | source)
XLA Modules:
  0.0 160.0 jit_solution(5228222620831647201)
XLA Ops:
  0.6 16.3 %collective-permute-start.4 = (f32[2,64,128]{2,1,0:T(8,128)}, f32[2,64,128]{2,1,0:T(8,128)S(1)}, u32[]{:S(2)}, u32[]{:S(2)}) collective-permute-start(f32[2,64,128]{2,1,0:T(8,128)} %bitcast.3), channel_id=1, source_target_pairs={{0,64},{64,128},{128,192},{192,256},{256,320},{320,384},{384,448},... | collective-permute-start | bytes 196616 | tf_op jit(solution)/shard_map/ppermute | solution.py:460
  16.9 1.2 first.1
  18.1 3.5 %collective-permute-start = (f32[104,128]{1,0:T(8,128)S(1)}, f32[104,128]{1,0:T(8,128)S(1)}, u32[]{:S(2)}, u32[]{:S(2)}) collective-permute-start(f32[104,128]{1,0:T(8,128)S(1)} %get-tuple-element.34), channel_id=1, source_target_pairs={{0,63},{1,2},{2,1},{3,4},{4,3},{5,6},{6,5},{7,8},{8,7},{9,10},{10,... | collective-permute-start | bytes 159752 | tf_op jit(solution)/shard_map/ppermute | solution.py:455
  21.6 2.1 %collective-permute-start.1 = (f32[104,128]{1,0:T(8,128)S(1)}, f32[104,128]{1,0:T(8,128)S(1)}, u32[]{:S(2)}, u32[]{:S(2)}) collective-permute-start(f32[104,128]{1,0:T(8,128)S(1)} %get-tuple-element.35), channel_id=1, source_target_pairs={{0,63},{1,2},{2,1},{3,4},{4,3},{5,6},{6,5},{7,8},{8,7},{9,10},{10,... | collective-permute-start | bytes 159752 | tf_op jit(solution)/shard_map/ppermute | solution.py:455
  23.7 11.6 %collective-permute-start.2 = (f32[104,128]{1,0:T(8,128)S(1)}, f32[104,128]{1,0:T(8,128)S(1)}, u32[]{:S(2)}, u32[]{:S(2)}) collective-permute-start(f32[104,128]{1,0:T(8,128)S(1)} %get-tuple-element.36), channel_id=1, source_target_pairs={{0,1},{1,0},{2,3},{3,2},{4,5},{5,4},{6,7},{7,6},{8,9},{9,8},{10,11... | collective-permute-start | bytes 159752 | tf_op jit(solution)/shard_map/ppermute | solution.py:450
  35.3 1.9 %collective-permute-start.3 = (f32[104,128]{1,0:T(8,128)S(1)}, f32[104,128]{1,0:T(8,128)S(1)}, u32[]{:S(2)}, u32[]{:S(2)}) collective-permute-start(f32[104,128]{1,0:T(8,128)S(1)} %get-tuple-element.37), channel_id=1, source_target_pairs={{0,1},{1,0},{2,3},{3,2},{4,5},{5,4},{6,7},{7,6},{8,9},{9,8},{10,11... | collective-permute-start | bytes 159752 | tf_op jit(solution)/shard_map/ppermute | solution.py:450
  37.2 0.0 collective-permute-done.refs_2_.refs_10_
  37.2 0.0 collective-permute-done.1.refs_3_.refs_11_
  37.2 0.0 collective-permute-done.2.refs_0_.refs_8_
  37.2 1.2 collective-permute-done.3.refs_1_.refs_9_
  38.4 0.0 collective-permute-done.4.refs_6_
  38.4 0.0 copy-start
  38.4 0.3 complete_first.1
  38.7 1.9 %collective-permute-start.5 = (f32[144,128]{1,0:T(8,128)S(1)}, f32[144,128]{1,0:T(8,128)S(1)}, u32[]{:S(2)}, u32[]{:S(2)}) collective-permute-start(f32[144,128]{1,0:T(8,128)S(1)} %get-tuple-element.46), channel_id=1, source_target_pairs={{0,8},{8,0},{16,24},{24,16},{32,40},{40,32},{48,56},{56,48},{1,9},... | collective-permute-start | bytes 221192 | tf_op jit(solution)/shard_map/ppermute | solution.py:446
  40.6 8.5 %collective-permute-start.6 = (f32[144,128]{1,0:T(8,128)S(1)}, f32[144,128]{1,0:T(8,128)S(1)}, u32[]{:S(2)}, u32[]{:S(2)}) collective-permute-start(f32[144,128]{1,0:T(8,128)S(1)} %get-tuple-element.47), channel_id=1, source_target_pairs={{0,56},{8,16},{16,8},{24,32},{32,24},{40,48},{48,40},{56,0},{1,57}... | collective-permute-start | bytes 221192 | tf_op jit(solution)/shard_map/ppermute | solution.py:446
  49.1 0.0 copy-done
  49.1 3.1 %collective-permute-start.7 = (f32[2,64,128]{2,1,0:T(8,128)S(1)}, f32[2,64,128]{2,1,0:T(8,128)S(1)}, u32[]{:S(2)}, u32[]{:S(2)}) collective-permute-start(f32[2,64,128]{2,1,0:T(8,128)S(1)} %bitcast.5), channel_id=1, source_target_pairs={{0,128},{64,192},{128,256},{192,320},{256,384},{320,448},{1,129},{... | collective-permute-start | bytes 196616 | tf_op jit(solution)/shard_map/ppermute | solution.py:460
  52.3 1.3 collective-permute-done.7.refs_16_
  53.6 0.0 collective-permute-done.5.refs_1_
  53.6 0.0 collective-permute-done.6.refs_2_
  53.6 19.2 %all_to_all.20.refs_3_ = f32[8,48,128]{2,1,0:T(8,128)S(1)} all-to-all(f32[8,48,128]{2,1,0:T(8,128)S(1)} %broadcast_in_dim.12), channel_id=1, replica_groups=mesh['tm'=8,'block'=8,'chip'=4,'core'=2] {'tm'}, dimensions={0} | all-to-all | bytes 393216 | tf_op jit(solution)/shard_map/all_to_all | solution.py:464
  72.9 17.8 %all_to_all.21.refs_4_ = f32[4,320,128]{2,1,0:T(8,128)S(1)} all-to-all(f32[4,320,128]{2,1,0:T(8,128)S(1)} %hand_out.2), channel_id=1, replica_groups=mesh['tm'=8,'block'=8,'chip'=4,'core'=2] {'chip'}, dimensions={0} | all-to-all | bytes 1310720 | tf_op jit(solution)/shard_map/all_to_all | solution.py:468
  90.7 6.9 %collective-permute-start.8 = (f32[4,320,128]{2,1,0:T(8,128)S(1)}, f32[4,320,128]{2,1,0:T(8,128)S(1)}, u32[]{:S(2)}, u32[]{:S(2)}) collective-permute-start(f32[4,320,128]{2,1,0:T(8,128)S(1)} %all_to_all.21.refs_4_), channel_id=1, source_target_pairs={{0,1},{1,0},{2,3},{3,2},{4,5},{5,4},{6,7},{7,6},{8,9},{9,8},{10,11... | collective-permute-start | bytes 1966088 | tf_op jit(solution)/shard_map/ppermute | solution.py:450
  97.6 1.7 %collective-permute-done.8.refs_5_ = f32[4,320,128]{2,1,0:T(8,128)S(1)} collective-permute-done((f32[4,320,128]{2,1,0:T(8,128)S(1)}, f32[4,320,128]{2,1,0:T(8,128)S(1)}, u32[]{:S(2)}, u32[]{:S(2)}) %collective-permute-start.8) | collective-permute-done | bytes 655392 | tf_op jit(solution)/shard_map/ppermute | solution.py:450
  99.4 2.2 %finish_first.1 = (f32[2,64,128]{2,1,0:T(8,128)S(1)}, f32[2,64,128]{2,1,0:T(8,128)S(1)}, f32[4,64,128]{2,1,0:T(8,128)S(1)}, f32[2,64,128]{2,1,0:T(8,128)S(1)}, f...) custom-call(f32[208,128]{1,0:T(8,128)S(1)} %get-tuple-element.45.refs_0_, ...), custom_call_target="tpu_custom_call" | custom-call | tf_op jit(solution)/shard_map/finish_first/pallas_call | solution.py:428
  101.6 6.2 %collective-permute-start.10 = (f32[48,128]{1,0:T(8,128)S(1)}, f32[48,128]{1,0:T(8,128)S(1)}, u32[]{:S(2)}, u32[]{:S(2)}) collective-permute-start(f32[48,128]{1,0:T(8,128)S(1)} %get-tuple-element.56.refs_0_), channel_id=1, source_target_pairs={{0,56},{8,16},{16,8},{24,32},{32,24},{40,48},{48,40},{56,0},{1,57}... | collective-permute-start | bytes 73736 | tf_op jit(solution)/shard_map/ppermute | solution.py:446
  107.8 4.6 %collective-permute-start.9 = (f32[48,128]{1,0:T(8,128)S(1)}, f32[48,128]{1,0:T(8,128)S(1)}, u32[]{:S(2)}, u32[]{:S(2)}) collective-permute-start(f32[48,128]{1,0:T(8,128)S(1)} %get-tuple-element.56.refs_0_), channel_id=1, source_target_pairs={{0,8},{8,0},{16,24},{24,16},{32,40},{40,32},{48,56},{56,48},{1,9},... | collective-permute-start | bytes 73736 | tf_op jit(solution)/shard_map/ppermute | solution.py:446
  112.4 0.0 collective-permute-done.10.refs_2_
  112.4 4.0 %collective-permute-done.9.refs_1_ = f32[48,128]{1,0:T(8,128)S(1)} collective-permute-done((f32[48,128]{1,0:T(8,128)S(1)}, f32[48,128]{1,0:T(8,128)S(1)}, u32[]{:S(2)}, u32[]{:S(2)}) %collective-permute-start.9) | collective-permute-done | bytes 24608 | tf_op jit(solution)/shard_map/ppermute | solution.py:446
  116.5 17.6 %all_to_all.22.refs_3_ = f32[8,48,128]{2,1,0:T(8,128)S(1)} all-to-all(f32[8,48,128]{2,1,0:T(8,128)S(1)} %broadcast_in_dim.13), channel_id=1, replica_groups=mesh['tm'=8,'block'=8,'chip'=4,'core'=2] {'tm'}, dimensions={0} | all-to-all | bytes 393216 | tf_op jit(solution)/shard_map/all_to_all | solution.py:464
  134.1 18.4 %all_to_all.23.refs_4_ = f32[4,192,128]{2,1,0:T(8,128)S(1)} all-to-all(f32[4,192,128]{2,1,0:T(8,128)S(1)} %hand_out.3), channel_id=1, replica_groups=mesh['tm'=8,'block'=8,'chip'=4,'core'=2] {'chip'}, dimensions={0} | all-to-all | bytes 786432 | tf_op jit(solution)/shard_map/all_to_all | solution.py:468
  152.6 4.1 %collective-permute-start.11 = (f32[4,192,128]{2,1,0:T(8,128)S(1)}, f32[4,192,128]{2,1,0:T(8,128)S(1)}, u32[]{:S(2)}, u32[]{:S(2)}) collective-permute-start(f32[4,192,128]{2,1,0:T(8,128)S(1)} %all_to_all.23.refs_4_), channel_id=1, source_target_pairs={{0,1},{1,0},{2,3},{3,2},{4,5},{5,4},{6,7},{7,6},{8,9},{9,8},{10,11... | collective-permute-start | bytes 1179656 | tf_op jit(solution)/shard_map/ppermute | solution.py:450
  156.7 1.3 collective-permute-done.11.refs_5_
  158.0 2.0 %finish_second.1 = (f32[2,2,64,128]{3,2,1,0:T(8,128)}, f32[32,64]{1,0:T(8,128)}) custom-call(f32[48,128]{1,0:T(8,128)S(1)} %get-tuple-element.56.refs_0_, f32[48,128]{1,0:T(8,128)S(1)} %collective-permute-done.9.refs_1_, f32[48,128]{1,0:T(8,128)S(1)} %collective-permute-done.10.refs_2_, f32[8,48,128]{2,1,0:T(8,128)S(1)} %all_to_all.22.refs_3_, ...), custom_call_target="tpu_custom_call" | custom-call | tf_op jit(solution)/shard_map/finish_second/pallas_call | solution.py:428
  (10 shorter events, 0.1 us)
Async XLA Ops:
  0.6 37.8 %collective-permute-start.4 = (f32[2,64,128]{2,1,0:T(8,128)}, f32[2,64,128]{2,1,0:T(8,128)S(1)}, u32[]{:S(2)}, u32[]{:S(2)}) collective-permute-start(f32[2,64,128]{2,1,0:T(8,128)} %bitcast.3), channel_id=1, source_target_pairs={{0,64},{64,128},{128,192},{192,256},{256,320},{320,384},{384,448},... | collective-permute-start | bytes 196616 | tf_op jit(solution)/shard_map/ppermute | solution.py:460
  18.1 19.1 %collective-permute-start = (f32[104,128]{1,0:T(8,128)S(1)}, f32[104,128]{1,0:T(8,128)S(1)}, u32[]{:S(2)}, u32[]{:S(2)}) collective-permute-start(f32[104,128]{1,0:T(8,128)S(1)} %get-tuple-element.34), channel_id=1, source_target_pairs={{0,63},{1,2},{2,1},{3,4},{4,3},{5,6},{6,5},{7,8},{8,7},{9,10},{10,... | collective-permute-start | bytes 159752 | tf_op jit(solution)/shard_map/ppermute | solution.py:455
  21.6 15.6 %collective-permute-start.1 = (f32[104,128]{1,0:T(8,128)S(1)}, f32[104,128]{1,0:T(8,128)S(1)}, u32[]{:S(2)}, u32[]{:S(2)}) collective-permute-start(f32[104,128]{1,0:T(8,128)S(1)} %get-tuple-element.35), channel_id=1, source_target_pairs={{0,63},{1,2},{2,1},{3,4},{4,3},{5,6},{6,5},{7,8},{8,7},{9,10},{10,... | collective-permute-start | bytes 159752 | tf_op jit(solution)/shard_map/ppermute | solution.py:455
  23.7 13.5 %collective-permute-start.2 = (f32[104,128]{1,0:T(8,128)S(1)}, f32[104,128]{1,0:T(8,128)S(1)}, u32[]{:S(2)}, u32[]{:S(2)}) collective-permute-start(f32[104,128]{1,0:T(8,128)S(1)} %get-tuple-element.36), channel_id=1, source_target_pairs={{0,1},{1,0},{2,3},{3,2},{4,5},{5,4},{6,7},{7,6},{8,9},{9,8},{10,11... | collective-permute-start | bytes 159752 | tf_op jit(solution)/shard_map/ppermute | solution.py:450
  35.3 3.1 %collective-permute-start.3 = (f32[104,128]{1,0:T(8,128)S(1)}, f32[104,128]{1,0:T(8,128)S(1)}, u32[]{:S(2)}, u32[]{:S(2)}) collective-permute-start(f32[104,128]{1,0:T(8,128)S(1)} %get-tuple-element.37), channel_id=1, source_target_pairs={{0,1},{1,0},{2,3},{3,2},{4,5},{5,4},{6,7},{7,6},{8,9},{9,8},{10,11... | collective-permute-start | bytes 159752 | tf_op jit(solution)/shard_map/ppermute | solution.py:450
  38.4 10.7 %copy-start = (f32[1,2,64,128]{3,2,1,0:T(8,128)S(1)}, f32[1,2,64,128]{3,2,1,0:T(8,128)}, u32[]{:S(2)}) copy-start(f32[1,2,64,128]{3,2,1,0:T(8,128)} %param.5) | copy-start | bytes 196612
  38.7 14.9 %collective-permute-start.5 = (f32[144,128]{1,0:T(8,128)S(1)}, f32[144,128]{1,0:T(8,128)S(1)}, u32[]{:S(2)}, u32[]{:S(2)}) collective-permute-start(f32[144,128]{1,0:T(8,128)S(1)} %get-tuple-element.46), channel_id=1, source_target_pairs={{0,8},{8,0},{16,24},{24,16},{32,40},{40,32},{48,56},{56,48},{1,9},... | collective-permute-start | bytes 221192 | tf_op jit(solution)/shard_map/ppermute | solution.py:446
  40.6 13.0 %collective-permute-start.6 = (f32[144,128]{1,0:T(8,128)S(1)}, f32[144,128]{1,0:T(8,128)S(1)}, u32[]{:S(2)}, u32[]{:S(2)}) collective-permute-start(f32[144,128]{1,0:T(8,128)S(1)} %get-tuple-element.47), channel_id=1, source_target_pairs={{0,56},{8,16},{16,8},{24,32},{32,24},{40,48},{48,40},{56,0},{1,57}... | collective-permute-start | bytes 221192 | tf_op jit(solution)/shard_map/ppermute | solution.py:446
  49.1 4.4 %collective-permute-start.7 = (f32[2,64,128]{2,1,0:T(8,128)S(1)}, f32[2,64,128]{2,1,0:T(8,128)S(1)}, u32[]{:S(2)}, u32[]{:S(2)}) collective-permute-start(f32[2,64,128]{2,1,0:T(8,128)S(1)} %bitcast.5), channel_id=1, source_target_pairs={{0,128},{64,192},{128,256},{192,320},{256,384},{320,448},{1,129},{... | collective-permute-start | bytes 196616 | tf_op jit(solution)/shard_map/ppermute | solution.py:460
  90.7 8.7 %collective-permute-start.8 = (f32[4,320,128]{2,1,0:T(8,128)S(1)}, f32[4,320,128]{2,1,0:T(8,128)S(1)}, u32[]{:S(2)}, u32[]{:S(2)}) collective-permute-start(f32[4,320,128]{2,1,0:T(8,128)S(1)} %all_to_all.21.refs_4_), channel_id=1, source_target_pairs={{0,1},{1,0},{2,3},{3,2},{4,5},{5,4},{6,7},{7,6},{8,9},{9,8},{10,11... | collective-permute-start | bytes 1966088 | tf_op jit(solution)/shard_map/ppermute | solution.py:450
  101.6 10.8 %collective-permute-start.10 = (f32[48,128]{1,0:T(8,128)S(1)}, f32[48,128]{1,0:T(8,128)S(1)}, u32[]{:S(2)}, u32[]{:S(2)}) collective-permute-start(f32[48,128]{1,0:T(8,128)S(1)} %get-tuple-element.56.refs_0_), channel_id=1, source_target_pairs={{0,56},{8,16},{16,8},{24,32},{32,24},{40,48},{48,40},{56,0},{1,57}... | collective-permute-start | bytes 73736 | tf_op jit(solution)/shard_map/ppermute | solution.py:446
  107.8 8.7 %collective-permute-start.9 = (f32[48,128]{1,0:T(8,128)S(1)}, f32[48,128]{1,0:T(8,128)S(1)}, u32[]{:S(2)}, u32[]{:S(2)}) collective-permute-start(f32[48,128]{1,0:T(8,128)S(1)} %get-tuple-element.56.refs_0_), channel_id=1, source_target_pairs={{0,8},{8,0},{16,24},{24,16},{32,40},{40,32},{48,56},{56,48},{1,9},... | collective-permute-start | bytes 73736 | tf_op jit(solution)/shard_map/ppermute | solution.py:446
  152.6 5.4 %collective-permute-start.11 = (f32[4,192,128]{2,1,0:T(8,128)S(1)}, f32[4,192,128]{2,1,0:T(8,128)S(1)}, u32[]{:S(2)}, u32[]{:S(2)}) collective-permute-start(f32[4,192,128]{2,1,0:T(8,128)S(1)} %all_to_all.23.refs_4_), channel_id=1, source_target_pairs={{0,1},{1,0},{2,3},{3,2},{4,5},{5,4},{6,7},{7,6},{8,9},{9,8},{10,11... | collective-permute-start | bytes 1179656 | tf_op jit(solution)/shard_map/ppermute | solution.py:450

commit v10 on v9

--- a/solution.py
+++ b/solution.py
@@ -502,9 +502,7 @@
         complete_first, (inner, inner_rest, outer, outer_rest, kept, initial, received),
         [(208, 128), (144, 128), (144, 128), (16, 128), (8,) + coarse, slab], [(320, 128)], name="complete_first",
     )
-    beside, beyond, earlier = links.together(
-        links.swap_block(beside, True), links.swap_block(beyond, False), links.onward(sent, 2)
-    )
+    beside, beyond, earlier = links.swap_block(beside, True), links.swap_block(beyond, False), links.onward(sent, 2)
     middle, end, ends, begin_next, kept, owned, mine, coefs = links.call(
         finish_first,
         (*windows(owned, beside, beyond, mine, 0), started, kept, inner, inner_rest, outer, outer_rest, initial,

time: 161 us -> 165 us (1.025)
  blocking collectives: 73 us -> 78.5 us
  starting transfers between devices: 70.7 us -> 67 us
  waiting for transfers between devices: 9.56 us -> 12.3 us
    all_to_all x2, blocking collectives: 36.8 us -> 41.2 us  [sections(): lax.all_to_all(jnp.broadcast_to(x, (SECTIONS,) + x.shape), 'tm', 0, 0)]
    ppermute x4, waiting for transfers between devices: 4.04 us -> 8.26 us  [swap_block(): return lax.ppermute(x, 'block', pairs)]
    ppermute x4, starting transfers between devices: 21.2 us -> 19.5 us  [swap_block(): return lax.ppermute(x, 'block', pairs)]
    ppermute x4, waiting for transfers between devices: 4.2 us -> 2.5 us  [swap_inner(): return lax.ppermute(x, 'core', [(0, 1), (1, 0)])]
  transfers between devices with their start and end apart: 12 -> 12, of which waited for: 5 -> 6; matrix products, arithmetic and copies ran while one was open for 0% -> 0% of each run, Pallas kernels for 1% -> 1%
where the time goes in v10:
time: 165 us; the launch traced here: 164 us
  blocking collectives  78.5 us (48%)
  starting transfers between devices  67 us (41%)
  waiting for transfers between devices  12.3 us (7%)
  Pallas kernels  5.84 us (4%)
    all_to_all x2, blocking collectives, sections(): lax.all_to_all(jnp.broadcast_to(x, (SECTIONS,) + x.shape), 'tm', 0, 0)  41.2 us
    all_to_all x2, blocking collectives, block(): return lax.all_to_all(x, 'chip', 0, 0)  37.3 us
    ppermute x4, starting transfers between devices, swap_inner(): return lax.ppermute(x, 'core', [(0, 1), (1, 0)])  23.8 us
    ppermute x4, starting transfers between devices, swap_block(): return lax.ppermute(x, 'block', pairs)  19.5 us
    ppermute x2, starting transfers between devices, onward(): return lax.ppermute(x, 'tm', [(i, i + by) for i in range(n - by)])  18.2 us
    ppermute x4, waiting for transfers between devices, swap_block(): return lax.ppermute(x, 'block', pairs)  8.26 us
    pallas_call x6, Pallas kernels, run(): pl.pallas_call(placed, out_shape=[jax.ShapeDtypeStruct(shape, F32) if las...  5.84 us
    ppermute x2, starting transfers between devices, swap_outer(): lax.ppermute(x, ('block', 'chip', 'core'), [(i, (i + 2 * (i % 2) - 1) % n...  5.56 us
  transfers between devices with their start and end apart: 12, of which 6 were waited for; matrix products, arithmetic and copies ran while one was open for 0% of the time, Pallas kernels for 1%

profile of v10, /device:TPU:1, one launch (start us, length us, event | category | flops | bytes accessed | tf_op | source)
XLA Modules:
  0.0 164.5 jit_solution(17649571736003337762)
XLA Ops:
  0.6 16.3 %collective-permute-start.4 = (f32[2,64,128]{2,1,0:T(8,128)}, f32[2,64,128]{2,1,0:T(8,128)S(1)}, u32[]{:S(2)}, u32[]{:S(2)}) collective-permute-start(f32[2,64,128]{2,1,0:T(8,128)} %bitcast.3), channel_id=1, source_target_pairs={{0,64},{64,128},{128,192},{192,256},{256,320},{320,384},{384,448},... | collective-permute-start | bytes 196616 | tf_op jit(solution)/shard_map/ppermute | solution.py:460
  16.9 1.2 first.1
  18.1 3.5 %collective-permute-start = (f32[104,128]{1,0:T(8,128)S(1)}, f32[104,128]{1,0:T(8,128)S(1)}, u32[]{:S(2)}, u32[]{:S(2)}) collective-permute-start(f32[104,128]{1,0:T(8,128)S(1)} %get-tuple-element.31), channel_id=1, source_target_pairs={{0,63},{1,2},{2,1},{3,4},{4,3},{5,6},{6,5},{7,8},{8,7},{9,10},{10,... | collective-permute-start | bytes 159752 | tf_op jit(solution)/shard_map/ppermute | solution.py:455
  21.6 2.1 %collective-permute-start.1 = (f32[104,128]{1,0:T(8,128)S(1)}, f32[104,128]{1,0:T(8,128)S(1)}, u32[]{:S(2)}, u32[]{:S(2)}) collective-permute-start(f32[104,128]{1,0:T(8,128)S(1)} %get-tuple-element.32), channel_id=1, source_target_pairs={{0,63},{1,2},{2,1},{3,4},{4,3},{5,6},{6,5},{7,8},{8,7},{9,10},{10,... | collective-permute-start | bytes 159752 | tf_op jit(solution)/shard_map/ppermute | solution.py:455
  23.7 11.6 %collective-permute-start.2 = (f32[104,128]{1,0:T(8,128)S(1)}, f32[104,128]{1,0:T(8,128)S(1)}, u32[]{:S(2)}, u32[]{:S(2)}) collective-permute-start(f32[104,128]{1,0:T(8,128)S(1)} %get-tuple-element.33), channel_id=1, source_target_pairs={{0,1},{1,0},{2,3},{3,2},{4,5},{5,4},{6,7},{7,6},{8,9},{9,8},{10,11... | collective-permute-start | bytes 159752 | tf_op jit(solution)/shard_map/ppermute | solution.py:450
  35.3 1.9 %collective-permute-start.3 = (f32[104,128]{1,0:T(8,128)S(1)}, f32[104,128]{1,0:T(8,128)S(1)}, u32[]{:S(2)}, u32[]{:S(2)}) collective-permute-start(f32[104,128]{1,0:T(8,128)S(1)} %get-tuple-element.34), channel_id=1, source_target_pairs={{0,1},{1,0},{2,3},{3,2},{4,5},{5,4},{6,7},{7,6},{8,9},{9,8},{10,11... | collective-permute-start | bytes 159752 | tf_op jit(solution)/shard_map/ppermute | solution.py:450
  37.2 0.0 collective-permute-done.refs_2_.refs_10_
  37.2 0.0 collective-permute-done.1.refs_3_.refs_11_
  37.2 0.0 collective-permute-done.2.refs_0_.refs_8_
  37.2 1.2 collective-permute-done.3.refs_1_.refs_9_
  38.4 0.0 collective-permute-done.4.refs_6_
  38.4 0.3 complete_first.1
  38.7 1.9 %collective-permute-start.5 = (f32[144,128]{1,0:T(8,128)S(1)}, f32[144,128]{1,0:T(8,128)S(1)}, u32[]{:S(2)}, u32[]{:S(2)}) collective-permute-start(f32[144,128]{1,0:T(8,128)S(1)} %get-tuple-element.43), channel_id=1, source_target_pairs={{0,8},{8,0},{16,24},{24,16},{32,40},{40,32},{48,56},{56,48},{1,9},... | collective-permute-start | bytes 221192 | tf_op jit(solution)/shard_map/ppermute | solution.py:446
  40.6 8.5 %collective-permute-start.6 = (f32[144,128]{1,0:T(8,128)S(1)}, f32[144,128]{1,0:T(8,128)S(1)}, u32[]{:S(2)}, u32[]{:S(2)}) collective-permute-start(f32[144,128]{1,0:T(8,128)S(1)} %get-tuple-element.44), channel_id=1, source_target_pairs={{0,56},{8,16},{16,8},{24,32},{32,24},{40,48},{48,40},{56,0},{1,57}... | collective-permute-start | bytes 221192 | tf_op jit(solution)/shard_map/ppermute | solution.py:446
  49.1 0.0 collective-permute-done.5.refs_1_
  49.2 2.7 %collective-permute-done.6.refs_2_ = f32[144,128]{1,0:T(8,128)S(1)} collective-permute-done((f32[144,128]{1,0:T(8,128)S(1)}, f32[144,128]{1,0:T(8,128)S(1)}, u32[]{:S(2)}, u32[]{:S(2)}) %collective-permute-start.6) | collective-permute-done | bytes 73760 | tf_op jit(solution)/shard_map/ppermute | solution.py:446
  51.9 20.9 %all_to_all.20.refs_3_ = f32[8,48,128]{2,1,0:T(8,128)S(1)} all-to-all(f32[8,48,128]{2,1,0:T(8,128)S(1)} %broadcast_in_dim.12), channel_id=1, replica_groups=mesh['tm'=8,'block'=8,'chip'=4,'core'=2] {'tm'}, dimensions={0} | all-to-all | bytes 393216 | tf_op jit(solution)/shard_map/all_to_all | solution.py:464
  72.9 0.0 copy-start
  72.9 18.7 %all_to_all.21.refs_4_ = f32[4,320,128]{2,1,0:T(8,128)S(1)} all-to-all(f32[4,320,128]{2,1,0:T(8,128)S(1)} %hand_out.2), channel_id=1, replica_groups=mesh['tm'=8,'block'=8,'chip'=4,'core'=2] {'chip'}, dimensions={0} | all-to-all | bytes 1310720 | tf_op jit(solution)/shard_map/all_to_all | solution.py:468
  91.6 6.1 %collective-permute-start.7 = (f32[4,320,128]{2,1,0:T(8,128)S(1)}, f32[4,320,128]{2,1,0:T(8,128)S(1)}, u32[]{:S(2)}, u32[]{:S(2)}) collective-permute-start(f32[4,320,128]{2,1,0:T(8,128)S(1)} %all_to_all.21.refs_4_), channel_id=1, source_target_pairs={{0,1},{1,0},{2,3},{3,2},{4,5},{5,4},{6,7},{7,6},{8,9},{9,8},{10,11... | collective-permute-start | bytes 1966088 | tf_op jit(solution)/shard_map/ppermute | solution.py:450
  97.8 0.0 copy-done
  97.8 1.9 %collective-permute-start.8 = (f32[2,64,128]{2,1,0:T(8,128)S(1)}, f32[2,64,128]{2,1,0:T(8,128)S(1)}, u32[]{:S(2)}, u32[]{:S(2)}) collective-permute-start(f32[2,64,128]{2,1,0:T(8,128)S(1)} %bitcast.5), channel_id=1, source_target_pairs={{0,128},{64,192},{128,256},{192,320},{256,384},{320,448},{1,129},{... | collective-permute-start | bytes 196616 | tf_op jit(solution)/shard_map/ppermute | solution.py:460
  99.7 1.5 collective-permute-done.8.refs_16_
  101.2 0.0 collective-permute-done.7.refs_5_
  101.2 2.2 %finish_first.1 = (f32[2,64,128]{2,1,0:T(8,128)S(1)}, f32[2,64,128]{2,1,0:T(8,128)S(1)}, f32[4,64,128]{2,1,0:T(8,128)S(1)}, f32[2,64,128]{2,1,0:T(8,128)S(1)}, f...) custom-call(f32[208,128]{1,0:T(8,128)S(1)} %get-tuple-element.42.refs_0_, ...), custom_call_target="tpu_custom_call" | custom-call | tf_op jit(solution)/shard_map/finish_first/pallas_call | solution.py:428
  103.5 5.9 %collective-permute-start.10 = (f32[48,128]{1,0:T(8,128)S(1)}, f32[48,128]{1,0:T(8,128)S(1)}, u32[]{:S(2)}, u32[]{:S(2)}) collective-permute-start(f32[48,128]{1,0:T(8,128)S(1)} %get-tuple-element.50.refs_0_), channel_id=1, source_target_pairs={{0,56},{8,16},{16,8},{24,32},{32,24},{40,48},{48,40},{56,0},{1,57}... | collective-permute-start | bytes 73736 | tf_op jit(solution)/shard_map/ppermute | solution.py:446
  109.4 3.1 %collective-permute-start.9 = (f32[48,128]{1,0:T(8,128)S(1)}, f32[48,128]{1,0:T(8,128)S(1)}, u32[]{:S(2)}, u32[]{:S(2)}) collective-permute-start(f32[48,128]{1,0:T(8,128)S(1)} %get-tuple-element.50.refs_0_), channel_id=1, source_target_pairs={{0,8},{8,0},{16,24},{24,16},{32,40},{40,32},{48,56},{56,48},{1,9},... | collective-permute-start | bytes 73736 | tf_op jit(solution)/shard_map/ppermute | solution.py:446
  112.6 1.7 %collective-permute-done.10.refs_2_ = f32[48,128]{1,0:T(8,128)S(1)} collective-permute-done((f32[48,128]{1,0:T(8,128)S(1)}, f32[48,128]{1,0:T(8,128)S(1)}, u32[]{:S(2)}, u32[]{:S(2)}) %collective-permute-start.10) | collective-permute-done | bytes 24608 | tf_op jit(solution)/shard_map/ppermute | solution.py:446
  114.2 3.8 %collective-permute-done.9.refs_1_ = f32[48,128]{1,0:T(8,128)S(1)} collective-permute-done((f32[48,128]{1,0:T(8,128)S(1)}, f32[48,128]{1,0:T(8,128)S(1)}, u32[]{:S(2)}, u32[]{:S(2)}) %collective-permute-start.9) | collective-permute-done | bytes 24608 | tf_op jit(solution)/shard_map/ppermute | solution.py:446
  118.1 20.3 %all_to_all.22.refs_3_ = f32[8,48,128]{2,1,0:T(8,128)S(1)} all-to-all(f32[8,48,128]{2,1,0:T(8,128)S(1)} %broadcast_in_dim.13), channel_id=1, replica_groups=mesh['tm'=8,'block'=8,'chip'=4,'core'=2] {'tm'}, dimensions={0} | all-to-all | bytes 393216 | tf_op jit(solution)/shard_map/all_to_all | solution.py:464
  138.4 18.5 %all_to_all.23.refs_4_ = f32[4,192,128]{2,1,0:T(8,128)S(1)} all-to-all(f32[4,192,128]{2,1,0:T(8,128)S(1)} %hand_out.3), channel_id=1, replica_groups=mesh['tm'=8,'block'=8,'chip'=4,'core'=2] {'chip'}, dimensions={0} | all-to-all | bytes 786432 | tf_op jit(solution)/shard_map/all_to_all | solution.py:468
  157.0 4.1 %collective-permute-start.11 = (f32[4,192,128]{2,1,0:T(8,128)S(1)}, f32[4,192,128]{2,1,0:T(8,128)S(1)}, u32[]{:S(2)}, u32[]{:S(2)}) collective-permute-start(f32[4,192,128]{2,1,0:T(8,128)S(1)} %all_to_all.23.refs_4_), channel_id=1, source_target_pairs={{0,1},{1,0},{2,3},{3,2},{4,5},{5,4},{6,7},{7,6},{8,9},{9,8},{10,11... | collective-permute-start | bytes 1179656 | tf_op jit(solution)/shard_map/ppermute | solution.py:450
  161.1 1.3 collective-permute-done.11.refs_5_
  162.4 2.0 %finish_second.1 = (f32[2,2,64,128]{3,2,1,0:T(8,128)}, f32[32,64]{1,0:T(8,128)}) custom-call(f32[48,128]{1,0:T(8,128)S(1)} %get-tuple-element.50.refs_0_, f32[48,128]{1,0:T(8,128)S(1)} %collective-permute-done.9.refs_1_, f32[48,128]{1,0:T(8,128)S(1)} %collective-permute-done.10.refs_2_, f32[8,48,128]{2,1,0:T(8,128)S(1)} %all_to_all.22.refs_3_, ...), custom_call_target="tpu_custom_call" | custom-call | tf_op jit(solution)/shard_map/finish_second/pallas_call | solution.py:428
  (10 shorter events, 0.1 us)
Async XLA Ops:
  0.6 37.8 %collective-permute-start.4 = (f32[2,64,128]{2,1,0:T(8,128)}, f32[2,64,128]{2,1,0:T(8,128)S(1)}, u32[]{:S(2)}, u32[]{:S(2)}) collective-permute-start(f32[2,64,128]{2,1,0:T(8,128)} %bitcast.3), channel_id=1, source_target_pairs={{0,64},{64,128},{128,192},{192,256},{256,320},{320,384},{384,448},... | collective-permute-start | bytes 196616 | tf_op jit(solution)/shard_map/ppermute | solution.py:460
  18.1 19.1 %collective-permute-start = (f32[104,128]{1,0:T(8,128)S(1)}, f32[104,128]{1,0:T(8,128)S(1)}, u32[]{:S(2)}, u32[]{:S(2)}) collective-permute-start(f32[104,128]{1,0:T(8,128)S(1)} %get-tuple-element.31), channel_id=1, source_target_pairs={{0,63},{1,2},{2,1},{3,4},{4,3},{5,6},{6,5},{7,8},{8,7},{9,10},{10,... | collective-permute-start | bytes 159752 | tf_op jit(solution)/shard_map/ppermute | solution.py:455
  21.6 15.6 %collective-permute-start.1 = (f32[104,128]{1,0:T(8,128)S(1)}, f32[104,128]{1,0:T(8,128)S(1)}, u32[]{:S(2)}, u32[]{:S(2)}) collective-permute-start(f32[104,128]{1,0:T(8,128)S(1)} %get-tuple-element.32), channel_id=1, source_target_pairs={{0,63},{1,2},{2,1},{3,4},{4,3},{5,6},{6,5},{7,8},{8,7},{9,10},{10,... | collective-permute-start | bytes 159752 | tf_op jit(solution)/shard_map/ppermute | solution.py:455
  23.7 13.5 %collective-permute-start.2 = (f32[104,128]{1,0:T(8,128)S(1)}, f32[104,128]{1,0:T(8,128)S(1)}, u32[]{:S(2)}, u32[]{:S(2)}) collective-permute-start(f32[104,128]{1,0:T(8,128)S(1)} %get-tuple-element.33), channel_id=1, source_target_pairs={{0,1},{1,0},{2,3},{3,2},{4,5},{5,4},{6,7},{7,6},{8,9},{9,8},{10,11... | collective-permute-start | bytes 159752 | tf_op jit(solution)/shard_map/ppermute | solution.py:450
  35.3 3.1 %collective-permute-start.3 = (f32[104,128]{1,0:T(8,128)S(1)}, f32[104,128]{1,0:T(8,128)S(1)}, u32[]{:S(2)}, u32[]{:S(2)}) collective-permute-start(f32[104,128]{1,0:T(8,128)S(1)} %get-tuple-element.34), channel_id=1, source_target_pairs={{0,1},{1,0},{2,3},{3,2},{4,5},{5,4},{6,7},{7,6},{8,9},{9,8},{10,11... | collective-permute-start | bytes 159752 | tf_op jit(solution)/shard_map/ppermute | solution.py:450
  38.7 10.4 %collective-permute-start.5 = (f32[144,128]{1,0:T(8,128)S(1)}, f32[144,128]{1,0:T(8,128)S(1)}, u32[]{:S(2)}, u32[]{:S(2)}) collective-permute-start(f32[144,128]{1,0:T(8,128)S(1)} %get-tuple-element.43), channel_id=1, source_target_pairs={{0,8},{8,0},{16,24},{24,16},{32,40},{40,32},{48,56},{56,48},{1,9},... | collective-permute-start | bytes 221192 | tf_op jit(solution)/shard_map/ppermute | solution.py:446
  40.6 11.3 %collective-permute-start.6 = (f32[144,128]{1,0:T(8,128)S(1)}, f32[144,128]{1,0:T(8,128)S(1)}, u32[]{:S(2)}, u32[]{:S(2)}) collective-permute-start(f32[144,128]{1,0:T(8,128)S(1)} %get-tuple-element.44), channel_id=1, source_target_pairs={{0,56},{8,16},{16,8},{24,32},{32,24},{40,48},{48,40},{56,0},{1,57}... | collective-permute-start | bytes 221192 | tf_op jit(solution)/shard_map/ppermute | solution.py:446
  72.9 24.9 %copy-start = (f32[1,2,64,128]{3,2,1,0:T(8,128)S(1)}, f32[1,2,64,128]{3,2,1,0:T(8,128)}, u32[]{:S(2)}) copy-start(f32[1,2,64,128]{3,2,1,0:T(8,128)} %param.5) | copy-start | bytes 196612
  91.6 9.6 %collective-permute-start.7 = (f32[4,320,128]{2,1,0:T(8,128)S(1)}, f32[4,320,128]{2,1,0:T(8,128)S(1)}, u32[]{:S(2)}, u32[]{:S(2)}) collective-permute-start(f32[4,320,128]{2,1,0:T(8,128)S(1)} %all_to_all.21.refs_4_), channel_id=1, source_target_pairs={{0,1},{1,0},{2,3},{3,2},{4,5},{5,4},{6,7},{7,6},{8,9},{9,8},{10,11... | collective-permute-start | bytes 1966088 | tf_op jit(solution)/shard_map/ppermute | solution.py:450
  97.8 3.4 %collective-permute-start.8 = (f32[2,64,128]{2,1,0:T(8,128)S(1)}, f32[2,64,128]{2,1,0:T(8,128)S(1)}, u32[]{:S(2)}, u32[]{:S(2)}) collective-permute-start(f32[2,64,128]{2,1,0:T(8,128)S(1)} %bitcast.5), channel_id=1, source_target_pairs={{0,128},{64,192},{128,256},{192,320},{256,384},{320,448},{1,129},{... | collective-permute-start | bytes 196616 | tf_op jit(solution)/shard_map/ppermute | solution.py:460
  103.5 10.8 %collective-permute-start.10 = (f32[48,128]{1,0:T(8,128)S(1)}, f32[48,128]{1,0:T(8,128)S(1)}, u32[]{:S(2)}, u32[]{:S(2)}) collective-permute-start(f32[48,128]{1,0:T(8,128)S(1)} %get-tuple-element.50.refs_0_), channel_id=1, source_target_pairs={{0,56},{8,16},{16,8},{24,32},{32,24},{40,48},{48,40},{56,0},{1,57}... | collective-permute-start | bytes 73736 | tf_op jit(solution)/shard_map/ppermute | solution.py:446
  109.4 8.7 %collective-permute-start.9 = (f32[48,128]{1,0:T(8,128)S(1)}, f32[48,128]{1,0:T(8,128)S(1)}, u32[]{:S(2)}, u32[]{:S(2)}) collective-permute-start(f32[48,128]{1,0:T(8,128)S(1)} %get-tuple-element.50.refs_0_), channel_id=1, source_target_pairs={{0,8},{8,0},{16,24},{24,16},{32,40},{40,32},{48,56},{56,48},{1,9},... | collective-permute-start | bytes 73736 | tf_op jit(solution)/shard_map/ppermute | solution.py:446
  157.0 5.5 %collective-permute-start.11 = (f32[4,192,128]{2,1,0:T(8,128)S(1)}, f32[4,192,128]{2,1,0:T(8,128)S(1)}, u32[]{:S(2)}, u32[]{:S(2)}) collective-permute-start(f32[4,192,128]{2,1,0:T(8,128)S(1)} %all_to_all.23.refs_4_), channel_id=1, source_target_pairs={{0,1},{1,0},{2,3},{3,2},{4,5},{5,4},{6,7},{7,6},{8,9},{9,8},{10,11... | collective-permute-start | bytes 1179656 | tf_op jit(solution)/shard_map/ppermute | solution.py:450

commit v11 on v10

--- a/solution.py
+++ b/solution.py
@@ -122,9 +122,9 @@
         put(down, up)
 
 
-def sides(spot, inner, inner_rest, outer, outer_rest):
-    a = jnp.concatenate([inner[...], inner_rest[...]], axis=0)
-    b = jnp.concatenate([outer[...], outer_rest[...]], axis=0)
+def sides(spot, inners, outers):
+    a = jnp.concatenate([part[...] for part in inners], axis=0)
+    b = jnp.concatenate([part[...] for part in outers], axis=0)
     low = jnp.full(a.shape, spot[2], jnp.int32) == 0
     return jnp.where(low, b, a), jnp.where(low, a, b)
 
@@ -140,7 +140,10 @@
     total = around(both) - 5.0 * both + c[0] * cubic(u[0]) + c[1] * cubic(u[1])
     own, value, coef, start = squash([total, both, c[0] + c[1], initial[0] + initial[1]], scratch)
     value, coef, start = 0.125 * value, 0.125 * coef, 0.125 * start
-    packets(spot, u + [c[1], pack(start)], u + [c[0], pack(start)], [inner, inner_rest], [outer, outer_rest])
+    small = [pack(value), pack(start)]
+    packets(
+        spot, [u[1]] + small + [u[0], c[1]], [u[0]] + small + [u[1], c[0]], [inner, inner_rest], [outer, outer_rest]
+    )
     keep[0] = own
     keep[1] = value
     keep[2] = coef
@@ -153,19 +156,14 @@
 
 
 def complete_first(
-    spot, inner, inner_rest, outer, outer_rest, kept, initial, received, owned, beside, beyond, mine, keep, begin_out,
-    scratch,
+    spot, inner, outer, kept, initial, earlier, received, owned, beside, beyond, mine, keep, begin_out, earlier_out, scratch
 ):
-    below, above = sides(spot, inner, inner_rest, outer, outer_rest)
+    below, above = sides(spot, [inner], [outer])
     begin = starting(spot, initial, received)
     own, value, coef, start = (kept[i] for i in range(4))
-    low, high, value_low, value_high, value_begin = squash(
-        [below[64:128, :], above[0:64, :], below[0:64, :] + below[64:128, :], above[0:64, :] + above[64:128, :],
-         begin[0] + begin[1]],
-        scratch,
-    )
-    value_low, value_high = 0.125 * value_low, 0.125 * value_high
-    start_low, start_high = unpack(below[192:208, :]), unpack(above[192:208, :])
+    low, high, value_begin = squash([below[0:64, :], above[0:64, :], begin[0] + begin[1]], scratch)
+    value_low, value_high = unpack(below[64:80, :]), unpack(above[64:80, :])
+    start_low, start_high = unpack(below[80:96, :]), unpack(above[80:96, :])
     start_slope = coarse_slope(start_low, start, start_high, coef)
     whole = own + low + high
     k = own_k([ROWSUM[1] * whole, ROWSUM[2] * whole], value, [value_low, value_high], coef)
@@ -182,6 +180,7 @@
     for x in (0, 1):
         owned[80 + 64 * x : 144 + 64 * x, :] = begin[x]
         begin_out[x] = begin[x]
+        earlier_out[x] = jnp.where(jnp.full((64, 128), spot[0], jnp.int32) == 1, initial[x], earlier[x])
     for i, part in enumerate([k[0], k[1], start, start_slope, start_low, start_high, value_low, value_high]):
         keep[i] = part
 
@@ -322,13 +321,12 @@
     wide = spread([mix(2, shift[0])] + shift[1] + [mix(2, shift[2])], scratch)
     fixed = [[starts[x] + wide[1 + j] for j in range(3)] for x in (1, 2)]
     sums = [ROWSUM[2] * starts[0] + wide[0], mix(2, fixed[0]), mix(2, fixed[1]), ROWSUM[2] * starts[3] + wide[4]]
-    number = jnp.full((64, 128), section, jnp.int32)
+    first = jnp.full((64, 128), section, jnp.int32) == 0
     out = []
     for x in (0, 1):
         change = around(sums[x + 1]) - 6.0 * sums[x + 1] + sums[x] + sums[x + 2]
         change = change + coeff[x] * mix(2, [cubic(part) for part in fixed[x]])
-        end = jnp.where(number == 1, initial[x], earlier[x]) + STEP * change
-        out.append(jnp.where(number == 0, initial[x], end))
+        out.append(jnp.where(first, initial[x], earlier[x] + STEP * change))
     return out
 
 
@@ -339,7 +337,7 @@
     fetch = sweep(
         spot, ITEMS[0], ROWS[0], owned, beside, beyond, sections, windows, swapped, coefs, started, line, history
     )
-    below, above = sides(spot, inner, inner_rest, outer, outer_rest)
+    below, above = sides(spot, [inner, inner_rest], [outer, outer_rest])
     section = spot[0]
     later = jnp.full((32, 128), section, jnp.int32) > 0
     s = [history[5 * section + i] for i in range(5)]
@@ -355,8 +353,8 @@
             two = history[5 * section + 6 + i]
         coarse += [s[i + 1] - value[i], one - value[i], two - value[i]]
     wide = spread(coarse, scratch)
-    u = [below[0:64, :], below[64:128, :], guess[0], guess[1], above[0:64, :], above[64:128, :]]
-    c = [None, below[128:192, :], coeff[0], coeff[1], above[128:192, :], None]
+    u = [below[96:160, :], below[0:64, :], guess[0], guess[1], above[0:64, :], above[96:160, :]]
+    c = [None, below[160:224, :], coeff[0], coeff[1], above[160:224, :], None]
     b = [None] + [None] * 4 + [None]
     b[2], b[3] = begin[0], begin[1]
     for x, w in ((1, -1), (4, 1)):
@@ -492,17 +490,18 @@
     sent = guess
     inner, inner_rest, outer, outer_rest, kept, initial, coeff, guess = links.call(
         first_kernel, (initial, coeff, guess),
-        [(104, 128)] * 4 + [(4,) + coarse, slab, slab, slab], [(256, 128)], name="first", first=True,
-    )
-    outer, outer_rest, inner, inner_rest, received = links.together(
-        links.swap_outer(outer), links.swap_outer(outer_rest), links.swap_inner(inner), links.swap_inner(inner_rest),
-        links.onward(sent, 1),
-    )
-    owned, beside, beyond, mine, started, begin = links.call(
-        complete_first, (inner, inner_rest, outer, outer_rest, kept, initial, received),
-        [(208, 128), (144, 128), (144, 128), (16, 128), (8,) + coarse, slab], [(320, 128)], name="complete_first",
-    )
-    beside, beyond, earlier = links.swap_block(beside, True), links.swap_block(beyond, False), links.onward(sent, 2)
+        [(112, 128)] * 4 + [(4,) + coarse, slab, slab, slab], [(256, 128)], name="first", first=True,
+    )
+    earlier, received, outer, outer_rest, inner = links.together(
+        links.onward(sent, 2), links.onward(sent, 1), links.swap_outer(outer), links.swap_outer(outer_rest),
+        links.swap_inner(inner),
+    )
+    inner_rest = links.swap_inner(inner_rest)
+    owned, beside, beyond, mine, started, begin, earlier = links.call(
+        complete_first, (inner, outer, kept, initial, earlier, received),
+        [(208, 128), (144, 128), (144, 128), (16, 128), (8,) + coarse, slab, slab], [(192, 128)], name="complete_first",
+    )
+    beside, beyond = links.swap_block(beside, True), links.swap_block(beyond, False)
     middle, end, ends, begin_next, kept, owned, mine, coefs = links.call(
         finish_first,
         (*windows(owned, beside, beyond, mine, 0), started, kept, inner, inner_rest, outer, outer_rest, initial,

time: 165 us -> 165 us (level)
  starting transfers between devices: 67 us -> 62.8 us
  blocking collectives: 78.5 us -> 81.7 us
    all_to_all x2, blocking collectives: 37.3 us -> 44.7 us  [block(): return lax.all_to_all(x, 'chip', 0, 0)]
    all_to_all x2, blocking collectives: 41.2 us -> 37 us  [sections(): lax.all_to_all(jnp.broadcast_to(x, (SECTIONS,) + x.shape), 'tm', 0, 0)]
    ppermute x4, starting transfers between devices: 19.5 us -> 16.2 us  [swap_block(): return lax.ppermute(x, 'block', pairs)]
    ppermute x4, starting transfers between devices: 23.8 us -> 21.6 us  [swap_inner(): return lax.ppermute(x, 'core', [(0, 1), (1, 0)])]
    ppermute x4, waiting for transfers between devices: 8.26 us -> 9.94 us  [swap_block(): return lax.ppermute(x, 'block', pairs)]
  transfers between devices with their start and end apart: 12 -> 12, of which waited for: 6 -> 5; matrix products, arithmetic and copies ran while one was open for 0% -> 0% of each run, Pallas kernels for 1% -> 1%
where the time goes in v11:
time: 165 us
  blocking collectives  81.7 us (50%)
  starting transfers between devices  62.8 us (38%)
  waiting for transfers between devices  13.3 us (8%)
  Pallas kernels  5.81 us (4%)
    all_to_all x2, blocking collectives, block(): return lax.all_to_all(x, 'chip', 0, 0)  44.7 us
    all_to_all x2, blocking collectives, sections(): lax.all_to_all(jnp.broadcast_to(x, (SECTIONS,) + x.shape), 'tm', 0, 0)  37 us
    ppermute x4, starting transfers between devices, swap_inner(): return lax.ppermute(x, 'core', [(0, 1), (1, 0)])  21.6 us
    ppermute x2, starting transfers between devices, onward(): return lax.ppermute(x, 'tm', [(i, i + by) for i in range(n - by)])  19.4 us
    ppermute x4, starting transfers between devices, swap_block(): return lax.ppermute(x, 'block', pairs)  16.2 us
    ppermute x4, waiting for transfers between devices, swap_block(): return lax.ppermute(x, 'block', pairs)  9.94 us
    pallas_call x6, Pallas kernels, run(): pl.pallas_call(placed, out_shape=[jax.ShapeDtypeStruct(shape, F32) if las...  5.81 us
    ppermute x2, starting transfers between devices, swap_outer(): lax.ppermute(x, ('block', 'chip', 'core'), [(i, (i + 2 * (i % 2) - 1) % n...  5.68 us
  transfers between devices with their start and end apart: 12, of which 5 were waited for; matrix products, arithmetic and copies ran while one was open for 0% of the time, Pallas kernels for 1%

profile of v11, /device:TPU:1, one launch (start us, length us, event | category | flops | bytes accessed | tf_op | source)
XLA Modules:
  0.0 164.5 jit_solution(9985721831173573015)
XLA Ops:
  0.6 16.3 %collective-permute-start.1 = (f32[2,64,128]{2,1,0:T(8,128)}, f32[2,64,128]{2,1,0:T(8,128)S(1)}, u32[]{:S(2)}, u32[]{:S(2)}) collective-permute-start(f32[2,64,128]{2,1,0:T(8,128)} %bitcast.3), channel_id=1, source_target_pairs={{0,64},{64,128},{128,192},{192,256},{256,320},{320,384},{384,448},... | collective-permute-start | bytes 196616 | tf_op jit(solution)/shard_map/ppermute | solution.py:458
  16.9 3.1 %collective-permute-start = (f32[2,64,128]{2,1,0:T(8,128)}, f32[2,64,128]{2,1,0:T(8,128)S(1)}, u32[]{:S(2)}, u32[]{:S(2)}) collective-permute-start(f32[2,64,128]{2,1,0:T(8,128)} %bitcast.4), channel_id=1, source_target_pairs={{0,128},{64,192},{128,256},{192,320},{256,384},{320,448},{1,129},{... | collective-permute-start | bytes 196616 | tf_op jit(solution)/shard_map/ppermute | solution.py:458
  20.0 1.2 first.1
  21.3 3.8 %collective-permute-start.2 = (f32[112,128]{1,0:T(8,128)S(1)}, f32[112,128]{1,0:T(8,128)S(1)}, u32[]{:S(2)}, u32[]{:S(2)}) collective-permute-start(f32[112,128]{1,0:T(8,128)S(1)} %get-tuple-element.32), channel_id=1, source_target_pairs={{0,63},{1,2},{2,1},{3,4},{4,3},{5,6},{6,5},{7,8},{8,7},{9,10},{10,... | collective-permute-start | bytes 172040 | tf_op jit(solution)/shard_map/ppermute | solution.py:453
  25.0 1.9 %collective-permute-start.3 = (f32[112,128]{1,0:T(8,128)S(1)}, f32[112,128]{1,0:T(8,128)S(1)}, u32[]{:S(2)}, u32[]{:S(2)}) collective-permute-start(f32[112,128]{1,0:T(8,128)S(1)} %get-tuple-element.33), channel_id=1, source_target_pairs={{0,63},{1,2},{2,1},{3,4},{4,3},{5,6},{6,5},{7,8},{8,7},{9,10},{10,... | collective-permute-start | bytes 172040 | tf_op jit(solution)/shard_map/ppermute | solution.py:453
  27.0 11.7 %collective-permute-start.4 = (f32[112,128]{1,0:T(8,128)S(1)}, f32[112,128]{1,0:T(8,128)S(1)}, u32[]{:S(2)}, u32[]{:S(2)}) collective-permute-start(f32[112,128]{1,0:T(8,128)S(1)} %get-tuple-element.34), channel_id=1, source_target_pairs={{0,1},{1,0},{2,3},{3,2},{4,5},{5,4},{6,7},{7,6},{8,9},{9,8},{10,11... | collective-permute-start | bytes 172040 | tf_op jit(solution)/shard_map/ppermute | solution.py:448
  38.7 0.0 collective-permute-done.2.refs_1_.refs_10_
  38.7 0.0 collective-permute-done.3.refs_11_
  38.7 0.8 collective-permute-done.4.refs_0_.refs_8_
  39.6 0.0 collective-permute-done.1.refs_5_
  39.6 0.0 collective-permute-done.refs_4_
  39.6 0.2 complete_first.1
  39.8 1.9 %collective-permute-start.5 = (f32[144,128]{1,0:T(8,128)S(1)}, f32[144,128]{1,0:T(8,128)S(1)}, u32[]{:S(2)}, u32[]{:S(2)}) collective-permute-start(f32[144,128]{1,0:T(8,128)S(1)} %get-tuple-element.42), channel_id=1, source_target_pairs={{0,8},{8,0},{16,24},{24,16},{32,40},{40,32},{48,56},{56,48},{1,9},... | collective-permute-start | bytes 221192 | tf_op jit(solution)/shard_map/ppermute | solution.py:444
  41.7 8.5 %collective-permute-start.6 = (f32[144,128]{1,0:T(8,128)S(1)}, f32[144,128]{1,0:T(8,128)S(1)}, u32[]{:S(2)}, u32[]{:S(2)}) collective-permute-start(f32[144,128]{1,0:T(8,128)S(1)} %get-tuple-element.43), channel_id=1, source_target_pairs={{0,56},{8,16},{16,8},{24,32},{32,24},{40,48},{48,40},{56,0},{1,57}... | collective-permute-start | bytes 221192 | tf_op jit(solution)/shard_map/ppermute | solution.py:444
  50.2 0.0 collective-permute-done.5.refs_1_
  50.3 3.7 %collective-permute-done.6.refs_2_ = f32[144,128]{1,0:T(8,128)S(1)} collective-permute-done((f32[144,128]{1,0:T(8,128)S(1)}, f32[144,128]{1,0:T(8,128)S(1)}, u32[]{:S(2)}, u32[]{:S(2)}) %collective-permute-start.6) | collective-permute-done | bytes 73760 | tf_op jit(solution)/shard_map/ppermute | solution.py:444
  54.0 18.5 %all_to_all.20.refs_3_ = f32[8,48,128]{2,1,0:T(8,128)S(1)} all-to-all(f32[8,48,128]{2,1,0:T(8,128)S(1)} %broadcast_in_dim.12), channel_id=1, replica_groups=mesh['tm'=8,'block'=8,'chip'=4,'core'=2] {'tm'}, dimensions={0} | all-to-all | bytes 393216 | tf_op jit(solution)/shard_map/all_to_all | solution.py:462
  72.5 26.4 %all_to_all.21.refs_4_ = f32[4,320,128]{2,1,0:T(8,128)S(1)} all-to-all(f32[4,320,128]{2,1,0:T(8,128)S(1)} %hand_out.2), channel_id=1, replica_groups=mesh['tm'=8,'block'=8,'chip'=4,'core'=2] {'chip'}, dimensions={0} | all-to-all | bytes 1310720 | tf_op jit(solution)/shard_map/all_to_all | solution.py:466
  99.0 3.8 %collective-permute-start.7 = (f32[4,320,128]{2,1,0:T(8,128)S(1)}, f32[4,320,128]{2,1,0:T(8,128)S(1)}, u32[]{:S(2)}, u32[]{:S(2)}) collective-permute-start(f32[4,320,128]{2,1,0:T(8,128)S(1)} %all_to_all.21.refs_4_), channel_id=1, source_target_pairs={{0,1},{1,0},{2,3},{3,2},{4,5},{5,4},{6,7},{7,6},{8,9},{9,8},{10,11... | collective-permute-start | bytes 1966088 | tf_op jit(solution)/shard_map/ppermute | solution.py:448
  102.8 1.9 %collective-permute-start.8 = (f32[112,128]{1,0:T(8,128)S(1)}, f32[112,128]{1,0:T(8,128)S(1)}, u32[]{:S(2)}, u32[]{:S(2)}) collective-permute-start(f32[112,128]{1,0:T(8,128)S(1)} %get-tuple-element.46), channel_id=1, source_target_pairs={{0,1},{1,0},{2,3},{3,2},{4,5},{5,4},{6,7},{7,6},{8,9},{9,8},{10,11... | collective-permute-start | bytes 172040 | tf_op jit(solution)/shard_map/ppermute | solution.py:448
  104.7 1.2 collective-permute-done.8.refs_9_
  105.9 0.0 collective-permute-done.7.refs_5_
  105.9 2.3 %finish_first.1 = (f32[2,64,128]{2,1,0:T(8,128)S(1)}, f32[2,64,128]{2,1,0:T(8,128)S(1)}, f32[4,64,128]{2,1,0:T(8,128)S(1)}, f32[2,64,128]{2,1,0:T(8,128)S(1)}, f...) custom-call(f32[208,128]{1,0:T(8,128)S(1)} %get-tuple-element.41.refs_0_, ...), custom_call_target="tpu_custom_call" | custom-call | tf_op jit(solution)/shard_map/finish_first/pallas_call | solution.py:426
  108.1 2.5 %collective-permute-start.10 = (f32[48,128]{1,0:T(8,128)S(1)}, f32[48,128]{1,0:T(8,128)S(1)}, u32[]{:S(2)}, u32[]{:S(2)}) collective-permute-start(f32[48,128]{1,0:T(8,128)S(1)} %get-tuple-element.52.refs_0_), channel_id=1, source_target_pairs={{0,56},{8,16},{16,8},{24,32},{32,24},{40,48},{48,40},{56,0},{1,57}... | collective-permute-start | bytes 73736 | tf_op jit(solution)/shard_map/ppermute | solution.py:444
  110.6 3.3 %collective-permute-start.9 = (f32[48,128]{1,0:T(8,128)S(1)}, f32[48,128]{1,0:T(8,128)S(1)}, u32[]{:S(2)}, u32[]{:S(2)}) collective-permute-start(f32[48,128]{1,0:T(8,128)S(1)} %get-tuple-element.52.refs_0_), channel_id=1, source_target_pairs={{0,8},{8,0},{16,24},{24,16},{32,40},{40,32},{48,56},{56,48},{1,9},... | collective-permute-start | bytes 73736 | tf_op jit(solution)/shard_map/ppermute | solution.py:444
  113.9 6.2 %collective-permute-done.10.refs_2_ = f32[48,128]{1,0:T(8,128)S(1)} collective-permute-done((f32[48,128]{1,0:T(8,128)S(1)}, f32[48,128]{1,0:T(8,128)S(1)}, u32[]{:S(2)}, u32[]{:S(2)}) %collective-permute-start.10) | collective-permute-done | bytes 24608 | tf_op jit(solution)/shard_map/ppermute | solution.py:444
  120.2 0.0 collective-permute-done.9.refs_1_
  120.2 18.5 %all_to_all.22.refs_3_ = f32[8,48,128]{2,1,0:T(8,128)S(1)} all-to-all(f32[8,48,128]{2,1,0:T(8,128)S(1)} %broadcast_in_dim.13), channel_id=1, replica_groups=mesh['tm'=8,'block'=8,'chip'=4,'core'=2] {'tm'}, dimensions={0} | all-to-all | bytes 393216 | tf_op jit(solution)/shard_map/all_to_all | solution.py:462
  138.8 18.2 %all_to_all.23.refs_4_ = f32[4,192,128]{2,1,0:T(8,128)S(1)} all-to-all(f32[4,192,128]{2,1,0:T(8,128)S(1)} %hand_out.3), channel_id=1, replica_groups=mesh['tm'=8,'block'=8,'chip'=4,'core'=2] {'chip'}, dimensions={0} | all-to-all | bytes 786432 | tf_op jit(solution)/shard_map/all_to_all | solution.py:466
  157.0 4.1 %collective-permute-start.11 = (f32[4,192,128]{2,1,0:T(8,128)S(1)}, f32[4,192,128]{2,1,0:T(8,128)S(1)}, u32[]{:S(2)}, u32[]{:S(2)}) collective-permute-start(f32[4,192,128]{2,1,0:T(8,128)S(1)} %all_to_all.23.refs_4_), channel_id=1, source_target_pairs={{0,1},{1,0},{2,3},{3,2},{4,5},{5,4},{6,7},{7,6},{8,9},{9,8},{10,11... | collective-permute-start | bytes 1179656 | tf_op jit(solution)/shard_map/ppermute | solution.py:448
  161.2 1.3 collective-permute-done.11.refs_5_
  162.5 2.0 %finish_second.1 = (f32[2,2,64,128]{3,2,1,0:T(8,128)}, f32[32,64]{1,0:T(8,128)}) custom-call(f32[48,128]{1,0:T(8,128)S(1)} %get-tuple-element.52.refs_0_, f32[48,128]{1,0:T(8,128)S(1)} %collective-permute-done.9.refs_1_, f32[48,128]{1,0:T(8,128)S(1)} %collective-permute-done.10.refs_2_, f32[8,48,128]{2,1,0:T(8,128)S(1)} %all_to_all.22.refs_3_, ...), custom_call_target="tpu_custom_call" | custom-call | tf_op jit(solution)/shard_map/finish_second/pallas_call | solution.py:426
  (10 shorter events, 0.1 us)
Async XLA Ops:
  0.6 38.9 %collective-permute-start.1 = (f32[2,64,128]{2,1,0:T(8,128)}, f32[2,64,128]{2,1,0:T(8,128)S(1)}, u32[]{:S(2)}, u32[]{:S(2)}) collective-permute-start(f32[2,64,128]{2,1,0:T(8,128)} %bitcast.3), channel_id=1, source_target_pairs={{0,64},{64,128},{128,192},{192,256},{256,320},{320,384},{384,448},... | collective-permute-start | bytes 196616 | tf_op jit(solution)/shard_map/ppermute | solution.py:458
  16.9 22.7 %collective-permute-start = (f32[2,64,128]{2,1,0:T(8,128)}, f32[2,64,128]{2,1,0:T(8,128)S(1)}, u32[]{:S(2)}, u32[]{:S(2)}) collective-permute-start(f32[2,64,128]{2,1,0:T(8,128)} %bitcast.4), channel_id=1, source_target_pairs={{0,128},{64,192},{128,256},{192,320},{256,384},{320,448},{1,129},{... | collective-permute-start | bytes 196616 | tf_op jit(solution)/shard_map/ppermute | solution.py:458
  21.3 17.4 %collective-permute-start.2 = (f32[112,128]{1,0:T(8,128)S(1)}, f32[112,128]{1,0:T(8,128)S(1)}, u32[]{:S(2)}, u32[]{:S(2)}) collective-permute-start(f32[112,128]{1,0:T(8,128)S(1)} %get-tuple-element.32), channel_id=1, source_target_pairs={{0,63},{1,2},{2,1},{3,4},{4,3},{5,6},{6,5},{7,8},{8,7},{9,10},{10,... | collective-permute-start | bytes 172040 | tf_op jit(solution)/shard_map/ppermute | solution.py:453
  25.0 13.7 %collective-permute-start.3 = (f32[112,128]{1,0:T(8,128)S(1)}, f32[112,128]{1,0:T(8,128)S(1)}, u32[]{:S(2)}, u32[]{:S(2)}) collective-permute-start(f32[112,128]{1,0:T(8,128)S(1)} %get-tuple-element.33), channel_id=1, source_target_pairs={{0,63},{1,2},{2,1},{3,4},{4,3},{5,6},{6,5},{7,8},{8,7},{9,10},{10,... | collective-permute-start | bytes 172040 | tf_op jit(solution)/shard_map/ppermute | solution.py:453
  27.0 12.6 %collective-permute-start.4 = (f32[112,128]{1,0:T(8,128)S(1)}, f32[112,128]{1,0:T(8,128)S(1)}, u32[]{:S(2)}, u32[]{:S(2)}) collective-permute-start(f32[112,128]{1,0:T(8,128)S(1)} %get-tuple-element.34), channel_id=1, source_target_pairs={{0,1},{1,0},{2,3},{3,2},{4,5},{5,4},{6,7},{7,6},{8,9},{9,8},{10,11... | collective-permute-start | bytes 172040 | tf_op jit(solution)/shard_map/ppermute | solution.py:448
  39.8 10.4 %collective-permute-start.5 = (f32[144,128]{1,0:T(8,128)S(1)}, f32[144,128]{1,0:T(8,128)S(1)}, u32[]{:S(2)}, u32[]{:S(2)}) collective-permute-start(f32[144,128]{1,0:T(8,128)S(1)} %get-tuple-element.42), channel_id=1, source_target_pairs={{0,8},{8,0},{16,24},{24,16},{32,40},{40,32},{48,56},{56,48},{1,9},... | collective-permute-start | bytes 221192 | tf_op jit(solution)/shard_map/ppermute | solution.py:444
  41.7 12.2 %collective-permute-start.6 = (f32[144,128]{1,0:T(8,128)S(1)}, f32[144,128]{1,0:T(8,128)S(1)}, u32[]{:S(2)}, u32[]{:S(2)}) collective-permute-start(f32[144,128]{1,0:T(8,128)S(1)} %get-tuple-element.43), channel_id=1, source_target_pairs={{0,56},{8,16},{16,8},{24,32},{32,24},{40,48},{48,40},{56,0},{1,57}... | collective-permute-start | bytes 221192 | tf_op jit(solution)/shard_map/ppermute | solution.py:444
  99.0 6.9 %collective-permute-start.7 = (f32[4,320,128]{2,1,0:T(8,128)S(1)}, f32[4,320,128]{2,1,0:T(8,128)S(1)}, u32[]{:S(2)}, u32[]{:S(2)}) collective-permute-start(f32[4,320,128]{2,1,0:T(8,128)S(1)} %all_to_all.21.refs_4_), channel_id=1, source_target_pairs={{0,1},{1,0},{2,3},{3,2},{4,5},{5,4},{6,7},{7,6},{8,9},{9,8},{10,11... | collective-permute-start | bytes 1966088 | tf_op jit(solution)/shard_map/ppermute | solution.py:448
  102.8 3.1 %collective-permute-start.8 = (f32[112,128]{1,0:T(8,128)S(1)}, f32[112,128]{1,0:T(8,128)S(1)}, u32[]{:S(2)}, u32[]{:S(2)}) collective-permute-start(f32[112,128]{1,0:T(8,128)S(1)} %get-tuple-element.46), channel_id=1, source_target_pairs={{0,1},{1,0},{2,3},{3,2},{4,5},{5,4},{6,7},{7,6},{8,9},{9,8},{10,11... | collective-permute-start | bytes 172040 | tf_op jit(solution)/shard_map/ppermute | solution.py:448
  108.1 12.0 %collective-permute-start.10 = (f32[48,128]{1,0:T(8,128)S(1)}, f32[48,128]{1,0:T(8,128)S(1)}, u32[]{:S(2)}, u32[]{:S(2)}) collective-permute-start(f32[48,128]{1,0:T(8,128)S(1)} %get-tuple-element.52.refs_0_), channel_id=1, source_target_pairs={{0,56},{8,16},{16,8},{24,32},{32,24},{40,48},{48,40},{56,0},{1,57}... | collective-permute-start | bytes 73736 | tf_op jit(solution)/shard_map/ppermute | solution.py:444
  110.6 9.5 %collective-permute-start.9 = (f32[48,128]{1,0:T(8,128)S(1)}, f32[48,128]{1,0:T(8,128)S(1)}, u32[]{:S(2)}, u32[]{:S(2)}) collective-permute-start(f32[48,128]{1,0:T(8,128)S(1)} %get-tuple-element.52.refs_0_), channel_id=1, source_target_pairs={{0,8},{8,0},{16,24},{24,16},{32,40},{40,32},{48,56},{56,48},{1,9},... | collective-permute-start | bytes 73736 | tf_op jit(solution)/shard_map/ppermute | solution.py:444
  157.0 5.5 %collective-permute-start.11 = (f32[4,192,128]{2,1,0:T(8,128)S(1)}, f32[4,192,128]{2,1,0:T(8,128)S(1)}, u32[]{:S(2)}, u32[]{:S(2)}) collective-permute-start(f32[4,192,128]{2,1,0:T(8,128)S(1)} %all_to_all.23.refs_4_), channel_id=1, source_target_pairs={{0,1},{1,0},{2,3},{3,2},{4,5},{5,4},{6,7},{7,6},{8,9},{9,8},{10,11... | collective-permute-start | bytes 1179656 | tf_op jit(solution)/shard_map/ppermute | solution.py:448

commit v12 on v10

--- a/solution.py
+++ b/solution.py
@@ -502,7 +502,9 @@
         complete_first, (inner, inner_rest, outer, outer_rest, kept, initial, received),
         [(208, 128), (144, 128), (144, 128), (16, 128), (8,) + coarse, slab], [(320, 128)], name="complete_first",
     )
-    beside, beyond, earlier = links.swap_block(beside, True), links.swap_block(beyond, False), links.onward(sent, 2)
+    beyond, beside, earlier = links.together(
+        links.swap_block(beyond, False), links.swap_block(beside, True), links.onward(sent, 2)
+    )
     middle, end, ends, begin_next, kept, owned, mine, coefs = links.call(
         finish_first,
         (*windows(owned, beside, beyond, mine, 0), started, kept, inner, inner_rest, outer, outer_rest, initial,

time: 165 us -> 164 us (level)
  the two profiles are of different devices: /device:TPU:1 before, /device:TPU:9 now
where the time goes in v12:
time: 164 us; the launch traced here: 163 us
  blocking collectives  73.7 us (45%)
  starting transfers between devices  70.4 us (43%)
  waiting for transfers between devices  12.2 us (7%)
  Pallas kernels  5.83 us (4%)
    all_to_all x2, blocking collectives, sections(): lax.all_to_all(jnp.broadcast_to(x, (SECTIONS,) + x.shape), 'tm', 0, 0)  39.9 us
    all_to_all x2, blocking collectives, block(): return lax.all_to_all(x, 'chip', 0, 0)  33.8 us
    ppermute x4, starting transfers between devices, swap_inner(): return lax.ppermute(x, 'core', [(0, 1), (1, 0)])  24.9 us
    ppermute x4, starting transfers between devices, swap_block(): return lax.ppermute(x, 'block', pairs)  21.4 us
    ppermute x2, starting transfers between devices, onward(): return lax.ppermute(x, 'tm', [(i, i + by) for i in range(n - by)])  18.6 us
    ppermute x4, waiting for transfers between devices, swap_block(): return lax.ppermute(x, 'block', pairs)  6.73 us
    pallas_call x6, Pallas kernels, run(): pl.pallas_call(placed, out_shape=[jax.ShapeDtypeStruct(shape, F32) if las...  5.83 us
    ppermute x2, starting transfers between devices, swap_outer(): lax.ppermute(x, ('block', 'chip', 'core'), [(i, (i + 2 * (i % 2) - 1) % n...  5.56 us
  transfers between devices with their start and end apart: 12, of which 6 were waited for; matrix products, arithmetic and copies ran while one was open for 0% of the time, Pallas kernels for 1%

profile of v12, /device:TPU:9, one launch (start us, length us, event | category | flops | bytes accessed | tf_op | source)
XLA Modules:
  0.0 163.0 jit_solution(17226578795243025844)
XLA Ops:
  0.6 15.4 %collective-permute-start.4 = (f32[2,64,128]{2,1,0:T(8,128)}, f32[2,64,128]{2,1,0:T(8,128)S(1)}, u32[]{:S(2)}, u32[]{:S(2)}) collective-permute-start(f32[2,64,128]{2,1,0:T(8,128)} %bitcast.3), channel_id=1, source_target_pairs={{0,64},{64,128},{128,192},{192,256},{256,320},{320,384},{384,448},... | collective-permute-start | bytes 196616 | tf_op jit(solution)/shard_map/ppermute | solution.py:460
  16.1 1.2 first.1
  17.3 3.5 %collective-permute-start = (f32[104,128]{1,0:T(8,128)S(1)}, f32[104,128]{1,0:T(8,128)S(1)}, u32[]{:S(2)}, u32[]{:S(2)}) collective-permute-start(f32[104,128]{1,0:T(8,128)S(1)} %get-tuple-element.34), channel_id=1, source_target_pairs={{0,63},{1,2},{2,1},{3,4},{4,3},{5,6},{6,5},{7,8},{8,7},{9,10},{10,... | collective-permute-start | bytes 159752 | tf_op jit(solution)/shard_map/ppermute | solution.py:455
  20.8 2.1 %collective-permute-start.1 = (f32[104,128]{1,0:T(8,128)S(1)}, f32[104,128]{1,0:T(8,128)S(1)}, u32[]{:S(2)}, u32[]{:S(2)}) collective-permute-start(f32[104,128]{1,0:T(8,128)S(1)} %get-tuple-element.35), channel_id=1, source_target_pairs={{0,63},{1,2},{2,1},{3,4},{4,3},{5,6},{6,5},{7,8},{8,7},{9,10},{10,... | collective-permute-start | bytes 159752 | tf_op jit(solution)/shard_map/ppermute | solution.py:455
  22.9 10.4 %collective-permute-start.2 = (f32[104,128]{1,0:T(8,128)S(1)}, f32[104,128]{1,0:T(8,128)S(1)}, u32[]{:S(2)}, u32[]{:S(2)}) collective-permute-start(f32[104,128]{1,0:T(8,128)S(1)} %get-tuple-element.36), channel_id=1, source_target_pairs={{0,1},{1,0},{2,3},{3,2},{4,5},{5,4},{6,7},{7,6},{8,9},{9,8},{10,11... | collective-permute-start | bytes 159752 | tf_op jit(solution)/shard_map/ppermute | solution.py:450
  33.2 1.9 %collective-permute-start.3 = (f32[104,128]{1,0:T(8,128)S(1)}, f32[104,128]{1,0:T(8,128)S(1)}, u32[]{:S(2)}, u32[]{:S(2)}) collective-permute-start(f32[104,128]{1,0:T(8,128)S(1)} %get-tuple-element.37), channel_id=1, source_target_pairs={{0,1},{1,0},{2,3},{3,2},{4,5},{5,4},{6,7},{7,6},{8,9},{9,8},{10,11... | collective-permute-start | bytes 159752 | tf_op jit(solution)/shard_map/ppermute | solution.py:450
  35.2 0.0 collective-permute-done.refs_2_.refs_10_
  35.2 0.0 collective-permute-done.1.refs_3_.refs_11_
  35.2 0.0 collective-permute-done.2.refs_0_.refs_8_
  35.2 1.2 collective-permute-done.3.refs_1_.refs_9_
  36.4 0.0 collective-permute-done.4.refs_6_
  36.4 0.0 copy-start
  36.4 0.3 complete_first.1
  36.7 1.9 %collective-permute-start.5 = (f32[144,128]{1,0:T(8,128)S(1)}, f32[144,128]{1,0:T(8,128)S(1)}, u32[]{:S(2)}, u32[]{:S(2)}) collective-permute-start(f32[144,128]{1,0:T(8,128)S(1)} %get-tuple-element.46), channel_id=1, source_target_pairs={{0,56},{8,16},{16,8},{24,32},{32,24},{40,48},{48,40},{56,0},{1,57}... | collective-permute-start | bytes 221192 | tf_op jit(solution)/shard_map/ppermute | solution.py:446
  38.6 8.3 %collective-permute-start.6 = (f32[144,128]{1,0:T(8,128)S(1)}, f32[144,128]{1,0:T(8,128)S(1)}, u32[]{:S(2)}, u32[]{:S(2)}) collective-permute-start(f32[144,128]{1,0:T(8,128)S(1)} %get-tuple-element.47), channel_id=1, source_target_pairs={{0,8},{8,0},{16,24},{24,16},{32,40},{40,32},{48,56},{56,48},{1,9},... | collective-permute-start | bytes 221192 | tf_op jit(solution)/shard_map/ppermute | solution.py:446
  46.9 0.0 copy-done
  46.9 3.1 %collective-permute-start.7 = (f32[2,64,128]{2,1,0:T(8,128)S(1)}, f32[2,64,128]{2,1,0:T(8,128)S(1)}, u32[]{:S(2)}, u32[]{:S(2)}) collective-permute-start(f32[2,64,128]{2,1,0:T(8,128)S(1)} %bitcast.5), channel_id=1, source_target_pairs={{0,128},{64,192},{128,256},{192,320},{256,384},{320,448},{1,129},{... | collective-permute-start | bytes 196616 | tf_op jit(solution)/shard_map/ppermute | solution.py:460
  50.0 1.3 collective-permute-done.7.refs_16_
  51.3 0.0 collective-permute-done.5.refs_2_
  51.3 0.0 collective-permute-done.6.refs_1_
  51.4 19.3 %all_to_all.20.refs_3_ = f32[8,48,128]{2,1,0:T(8,128)S(1)} all-to-all(f32[8,48,128]{2,1,0:T(8,128)S(1)} %broadcast_in_dim.12), channel_id=1, replica_groups=mesh['tm'=8,'block'=8,'chip'=4,'core'=2] {'tm'}, dimensions={0} | all-to-all | bytes 393216 | tf_op jit(solution)/shard_map/all_to_all | solution.py:464
  70.7 15.4 %all_to_all.21.refs_4_ = f32[4,320,128]{2,1,0:T(8,128)S(1)} all-to-all(f32[4,320,128]{2,1,0:T(8,128)S(1)} %hand_out.2), channel_id=1, replica_groups=mesh['tm'=8,'block'=8,'chip'=4,'core'=2] {'chip'}, dimensions={0} | all-to-all | bytes 1310720 | tf_op jit(solution)/shard_map/all_to_all | solution.py:468
  86.1 8.5 %collective-permute-start.8 = (f32[4,320,128]{2,1,0:T(8,128)S(1)}, f32[4,320,128]{2,1,0:T(8,128)S(1)}, u32[]{:S(2)}, u32[]{:S(2)}) collective-permute-start(f32[4,320,128]{2,1,0:T(8,128)S(1)} %all_to_all.21.refs_4_), channel_id=1, source_target_pairs={{0,1},{1,0},{2,3},{3,2},{4,5},{5,4},{6,7},{7,6},{8,9},{9,8},{10,11... | collective-permute-start | bytes 1966088 | tf_op jit(solution)/shard_map/ppermute | solution.py:450
  94.6 1.7 %collective-permute-done.8.refs_5_ = f32[4,320,128]{2,1,0:T(8,128)S(1)} collective-permute-done((f32[4,320,128]{2,1,0:T(8,128)S(1)}, f32[4,320,128]{2,1,0:T(8,128)S(1)}, u32[]{:S(2)}, u32[]{:S(2)}) %collective-permute-start.8) | collective-permute-done | bytes 655392 | tf_op jit(solution)/shard_map/ppermute | solution.py:450
  96.3 2.2 %finish_first.1 = (f32[2,64,128]{2,1,0:T(8,128)S(1)}, f32[2,64,128]{2,1,0:T(8,128)S(1)}, f32[4,64,128]{2,1,0:T(8,128)S(1)}, f32[2,64,128]{2,1,0:T(8,128)S(1)}, f...) custom-call(f32[208,128]{1,0:T(8,128)S(1)} %get-tuple-element.45.refs_0_, ...), custom_call_target="tpu_custom_call" | custom-call | tf_op jit(solution)/shard_map/finish_first/pallas_call | solution.py:428
  98.6 9.2 %collective-permute-start.10 = (f32[48,128]{1,0:T(8,128)S(1)}, f32[48,128]{1,0:T(8,128)S(1)}, u32[]{:S(2)}, u32[]{:S(2)}) collective-permute-start(f32[48,128]{1,0:T(8,128)S(1)} %get-tuple-element.56.refs_0_), channel_id=1, source_target_pairs={{0,56},{8,16},{16,8},{24,32},{32,24},{40,48},{48,40},{56,0},{1,57}... | collective-permute-start | bytes 73736 | tf_op jit(solution)/shard_map/ppermute | solution.py:446
  107.8 1.9 %collective-permute-start.9 = (f32[48,128]{1,0:T(8,128)S(1)}, f32[48,128]{1,0:T(8,128)S(1)}, u32[]{:S(2)}, u32[]{:S(2)}) collective-permute-start(f32[48,128]{1,0:T(8,128)S(1)} %get-tuple-element.56.refs_0_), channel_id=1, source_target_pairs={{0,8},{8,0},{16,24},{24,16},{32,40},{40,32},{48,56},{56,48},{1,9},... | collective-permute-start | bytes 73736 | tf_op jit(solution)/shard_map/ppermute | solution.py:446
  109.7 0.7 collective-permute-done.10.refs_2_
  110.5 6.0 %collective-permute-done.9.refs_1_ = f32[48,128]{1,0:T(8,128)S(1)} collective-permute-done((f32[48,128]{1,0:T(8,128)S(1)}, f32[48,128]{1,0:T(8,128)S(1)}, u32[]{:S(2)}, u32[]{:S(2)}) %collective-permute-start.9) | collective-permute-done | bytes 24608 | tf_op jit(solution)/shard_map/ppermute | solution.py:446
  116.5 20.6 %all_to_all.22.refs_3_ = f32[8,48,128]{2,1,0:T(8,128)S(1)} all-to-all(f32[8,48,128]{2,1,0:T(8,128)S(1)} %broadcast_in_dim.13), channel_id=1, replica_groups=mesh['tm'=8,'block'=8,'chip'=4,'core'=2] {'tm'}, dimensions={0} | all-to-all | bytes 393216 | tf_op jit(solution)/shard_map/all_to_all | solution.py:464
  137.2 18.4 %all_to_all.23.refs_4_ = f32[4,192,128]{2,1,0:T(8,128)S(1)} all-to-all(f32[4,192,128]{2,1,0:T(8,128)S(1)} %hand_out.3), channel_id=1, replica_groups=mesh['tm'=8,'block'=8,'chip'=4,'core'=2] {'chip'}, dimensions={0} | all-to-all | bytes 786432 | tf_op jit(solution)/shard_map/all_to_all | solution.py:468
  155.5 4.1 %collective-permute-start.11 = (f32[4,192,128]{2,1,0:T(8,128)S(1)}, f32[4,192,128]{2,1,0:T(8,128)S(1)}, u32[]{:S(2)}, u32[]{:S(2)}) collective-permute-start(f32[4,192,128]{2,1,0:T(8,128)S(1)} %all_to_all.23.refs_4_), channel_id=1, source_target_pairs={{0,1},{1,0},{2,3},{3,2},{4,5},{5,4},{6,7},{7,6},{8,9},{9,8},{10,11... | collective-permute-start | bytes 1179656 | tf_op jit(solution)/shard_map/ppermute | solution.py:450
  159.7 1.3 collective-permute-done.11.refs_5_
  161.0 2.0 %finish_second.1 = (f32[2,2,64,128]{3,2,1,0:T(8,128)}, f32[32,64]{1,0:T(8,128)}) custom-call(f32[48,128]{1,0:T(8,128)S(1)} %get-tuple-element.56.refs_0_, f32[48,128]{1,0:T(8,128)S(1)} %collective-permute-done.9.refs_1_, f32[48,128]{1,0:T(8,128)S(1)} %collective-permute-done.10.refs_2_, f32[8,48,128]{2,1,0:T(8,128)S(1)} %all_to_all.22.refs_3_, ...), custom_call_target="tpu_custom_call" | custom-call | tf_op jit(solution)/shard_map/finish_second/pallas_call | solution.py:428
  (10 shorter events, 0.1 us)
Async XLA Ops:
  0.6 35.8 %collective-permute-start.4 = (f32[2,64,128]{2,1,0:T(8,128)}, f32[2,64,128]{2,1,0:T(8,128)S(1)}, u32[]{:S(2)}, u32[]{:S(2)}) collective-permute-start(f32[2,64,128]{2,1,0:T(8,128)} %bitcast.3), channel_id=1, source_target_pairs={{0,64},{64,128},{128,192},{192,256},{256,320},{320,384},{384,448},... | collective-permute-start | bytes 196616 | tf_op jit(solution)/shard_map/ppermute | solution.py:460
  17.3 17.9 %collective-permute-start = (f32[104,128]{1,0:T(8,128)S(1)}, f32[104,128]{1,0:T(8,128)S(1)}, u32[]{:S(2)}, u32[]{:S(2)}) collective-permute-start(f32[104,128]{1,0:T(8,128)S(1)} %get-tuple-element.34), channel_id=1, source_target_pairs={{0,63},{1,2},{2,1},{3,4},{4,3},{5,6},{6,5},{7,8},{8,7},{9,10},{10,... | collective-permute-start | bytes 159752 | tf_op jit(solution)/shard_map/ppermute | solution.py:455
  20.8 14.4 %collective-permute-start.1 = (f32[104,128]{1,0:T(8,128)S(1)}, f32[104,128]{1,0:T(8,128)S(1)}, u32[]{:S(2)}, u32[]{:S(2)}) collective-permute-start(f32[104,128]{1,0:T(8,128)S(1)} %get-tuple-element.35), channel_id=1, source_target_pairs={{0,63},{1,2},{2,1},{3,4},{4,3},{5,6},{6,5},{7,8},{8,7},{9,10},{10,... | collective-permute-start | bytes 159752 | tf_op jit(solution)/shard_map/ppermute | solution.py:455
  22.9 12.3 %collective-permute-start.2 = (f32[104,128]{1,0:T(8,128)S(1)}, f32[104,128]{1,0:T(8,128)S(1)}, u32[]{:S(2)}, u32[]{:S(2)}) collective-permute-start(f32[104,128]{1,0:T(8,128)S(1)} %get-tuple-element.36), channel_id=1, source_target_pairs={{0,1},{1,0},{2,3},{3,2},{4,5},{5,4},{6,7},{7,6},{8,9},{9,8},{10,11... | collective-permute-start | bytes 159752 | tf_op jit(solution)/shard_map/ppermute | solution.py:450
  33.2 3.1 %collective-permute-start.3 = (f32[104,128]{1,0:T(8,128)S(1)}, f32[104,128]{1,0:T(8,128)S(1)}, u32[]{:S(2)}, u32[]{:S(2)}) collective-permute-start(f32[104,128]{1,0:T(8,128)S(1)} %get-tuple-element.37), channel_id=1, source_target_pairs={{0,1},{1,0},{2,3},{3,2},{4,5},{5,4},{6,7},{7,6},{8,9},{9,8},{10,11... | collective-permute-start | bytes 159752 | tf_op jit(solution)/shard_map/ppermute | solution.py:450
  36.4 10.5 %copy-start = (f32[1,2,64,128]{3,2,1,0:T(8,128)S(1)}, f32[1,2,64,128]{3,2,1,0:T(8,128)}, u32[]{:S(2)}) copy-start(f32[1,2,64,128]{3,2,1,0:T(8,128)} %param.5) | copy-start | bytes 196612
  36.7 14.7 %collective-permute-start.5 = (f32[144,128]{1,0:T(8,128)S(1)}, f32[144,128]{1,0:T(8,128)S(1)}, u32[]{:S(2)}, u32[]{:S(2)}) collective-permute-start(f32[144,128]{1,0:T(8,128)S(1)} %get-tuple-element.46), channel_id=1, source_target_pairs={{0,56},{8,16},{16,8},{24,32},{32,24},{40,48},{48,40},{56,0},{1,57}... | collective-permute-start | bytes 221192 | tf_op jit(solution)/shard_map/ppermute | solution.py:446
  38.6 12.7 %collective-permute-start.6 = (f32[144,128]{1,0:T(8,128)S(1)}, f32[144,128]{1,0:T(8,128)S(1)}, u32[]{:S(2)}, u32[]{:S(2)}) collective-permute-start(f32[144,128]{1,0:T(8,128)S(1)} %get-tuple-element.47), channel_id=1, source_target_pairs={{0,8},{8,0},{16,24},{24,16},{32,40},{40,32},{48,56},{56,48},{1,9},... | collective-permute-start | bytes 221192 | tf_op jit(solution)/shard_map/ppermute | solution.py:446
  46.9 4.4 %collective-permute-start.7 = (f32[2,64,128]{2,1,0:T(8,128)S(1)}, f32[2,64,128]{2,1,0:T(8,128)S(1)}, u32[]{:S(2)}, u32[]{:S(2)}) collective-permute-start(f32[2,64,128]{2,1,0:T(8,128)S(1)} %bitcast.5), channel_id=1, source_target_pairs={{0,128},{64,192},{128,256},{192,320},{256,384},{320,448},{1,129},{... | collective-permute-start | bytes 196616 | tf_op jit(solution)/shard_map/ppermute | solution.py:460
  86.1 10.2 %collective-permute-start.8 = (f32[4,320,128]{2,1,0:T(8,128)S(1)}, f32[4,320,128]{2,1,0:T(8,128)S(1)}, u32[]{:S(2)}, u32[]{:S(2)}) collective-permute-start(f32[4,320,128]{2,1,0:T(8,128)S(1)} %all_to_all.21.refs_4_), channel_id=1, source_target_pairs={{0,1},{1,0},{2,3},{3,2},{4,5},{5,4},{6,7},{7,6},{8,9},{9,8},{10,11... | collective-permute-start | bytes 1966088 | tf_op jit(solution)/shard_map/ppermute | solution.py:450
  98.6 11.9 %collective-permute-start.10 = (f32[48,128]{1,0:T(8,128)S(1)}, f32[48,128]{1,0:T(8,128)S(1)}, u32[]{:S(2)}, u32[]{:S(2)}) collective-permute-start(f32[48,128]{1,0:T(8,128)S(1)} %get-tuple-element.56.refs_0_), channel_id=1, source_target_pairs={{0,56},{8,16},{16,8},{24,32},{32,24},{40,48},{48,40},{56,0},{1,57}... | collective-permute-start | bytes 73736 | tf_op jit(solution)/shard_map/ppermute | solution.py:446
  107.8 8.7 %collective-permute-start.9 = (f32[48,128]{1,0:T(8,128)S(1)}, f32[48,128]{1,0:T(8,128)S(1)}, u32[]{:S(2)}, u32[]{:S(2)}) collective-permute-start(f32[48,128]{1,0:T(8,128)S(1)} %get-tuple-element.56.refs_0_), channel_id=1, source_target_pairs={{0,8},{8,0},{16,24},{24,16},{32,40},{40,32},{48,56},{56,48},{1,9},... | collective-permute-start | bytes 73736 | tf_op jit(solution)/shard_map/ppermute | solution.py:446
  155.5 5.5 %collective-permute-start.11 = (f32[4,192,128]{2,1,0:T(8,128)S(1)}, f32[4,192,128]{2,1,0:T(8,128)S(1)}, u32[]{:S(2)}, u32[]{:S(2)}) collective-permute-start(f32[4,192,128]{2,1,0:T(8,128)S(1)} %all_to_all.23.refs_4_), channel_id=1, source_target_pairs={{0,1},{1,0},{2,3},{3,2},{4,5},{5,4},{6,7},{7,6},{8,9},{9,8},{10,11... | collective-permute-start | bytes 1179656 | tf_op jit(solution)/shard_map/ppermute | solution.py:450

commit v13 on v9

--- a/solution.py
+++ b/solution.py
@@ -513,7 +513,7 @@
         work + [(576, 128)],
         name="finish_first",
     )
-    beside, beyond = links.swap_block(owned, True), links.swap_block(owned, False)
+    beyond, beside = links.together(links.swap_block(owned, False), links.swap_block(owned, True))
     fine, coarse_end = links.call(
         finish_second,
         (*windows(owned, beside, beyond, mine, 1), started, kept, ends, coeff, begin, middle, end, begin_next, coefs),

time: 161 us -> 160 us (level)
  blocking collectives: 73 us -> 70.3 us
  starting transfers between devices: 70.7 us -> 73 us
    all_to_all x2, blocking collectives: 36.2 us -> 33.9 us  [block(): return lax.all_to_all(x, 'chip', 0, 0)]
where the time goes in v13:
time: 160 us; the launch traced here: 159 us
  starting transfers between devices  73 us (46%)
  blocking collectives  70.3 us (44%)
  waiting for transfers between devices  9.23 us (6%)
  Pallas kernels  5.84 us (4%)
    all_to_all x2, blocking collectives, sections(): lax.all_to_all(jnp.broadcast_to(x, (SECTIONS,) + x.shape), 'tm', 0, 0)  36.4 us
    all_to_all x2, blocking collectives, block(): return lax.all_to_all(x, 'chip', 0, 0)  33.9 us
    ppermute x4, starting transfers between devices, swap_inner(): return lax.ppermute(x, 'core', [(0, 1), (1, 0)])  25.5 us
    ppermute x4, starting transfers between devices, swap_block(): return lax.ppermute(x, 'block', pairs)  22.6 us
    ppermute x2, starting transfers between devices, onward(): return lax.ppermute(x, 'tm', [(i, i + by) for i in range(n - by)])  19.4 us
    pallas_call x6, Pallas kernels, run(): pl.pallas_call(placed, out_shape=[jax.ShapeDtypeStruct(shape, F32) if las...  5.84 us
    ppermute x2, starting transfers between devices, swap_outer(): lax.ppermute(x, ('block', 'chip', 'core'), [(i, (i + 2 * (i % 2) - 1) % n...  5.56 us
    ppermute x4, waiting for transfers between devices, swap_inner(): return lax.ppermute(x, 'core', [(0, 1), (1, 0)])  4.2 us
  transfers between devices with their start and end apart: 12, of which 5 were waited for; matrix products, arithmetic and copies ran while one was open for 0% of the time, Pallas kernels for 1%

profile of v13, /device:TPU:1, one launch (start us, length us, event | category | flops | bytes accessed | tf_op | source)
XLA Modules:
  0.0 159.2 jit_solution(16476063895931613343)
XLA Ops:
  0.6 16.3 %collective-permute-start.4 = (f32[2,64,128]{2,1,0:T(8,128)}, f32[2,64,128]{2,1,0:T(8,128)S(1)}, u32[]{:S(2)}, u32[]{:S(2)}) collective-permute-start(f32[2,64,128]{2,1,0:T(8,128)} %bitcast.3), channel_id=1, source_target_pairs={{0,64},{64,128},{128,192},{192,256},{256,320},{320,384},{384,448},... | collective-permute-start | bytes 196616 | tf_op jit(solution)/shard_map/ppermute | solution.py:460
  16.9 1.2 first.1
  18.1 3.5 %collective-permute-start = (f32[104,128]{1,0:T(8,128)S(1)}, f32[104,128]{1,0:T(8,128)S(1)}, u32[]{:S(2)}, u32[]{:S(2)}) collective-permute-start(f32[104,128]{1,0:T(8,128)S(1)} %get-tuple-element.36), channel_id=1, source_target_pairs={{0,63},{1,2},{2,1},{3,4},{4,3},{5,6},{6,5},{7,8},{8,7},{9,10},{10,... | collective-permute-start | bytes 159752 | tf_op jit(solution)/shard_map/ppermute | solution.py:455
  21.6 2.1 %collective-permute-start.1 = (f32[104,128]{1,0:T(8,128)S(1)}, f32[104,128]{1,0:T(8,128)S(1)}, u32[]{:S(2)}, u32[]{:S(2)}) collective-permute-start(f32[104,128]{1,0:T(8,128)S(1)} %get-tuple-element.37), channel_id=1, source_target_pairs={{0,63},{1,2},{2,1},{3,4},{4,3},{5,6},{6,5},{7,8},{8,7},{9,10},{10,... | collective-permute-start | bytes 159752 | tf_op jit(solution)/shard_map/ppermute | solution.py:455
  23.7 11.6 %collective-permute-start.2 = (f32[104,128]{1,0:T(8,128)S(1)}, f32[104,128]{1,0:T(8,128)S(1)}, u32[]{:S(2)}, u32[]{:S(2)}) collective-permute-start(f32[104,128]{1,0:T(8,128)S(1)} %get-tuple-element.38), channel_id=1, source_target_pairs={{0,1},{1,0},{2,3},{3,2},{4,5},{5,4},{6,7},{7,6},{8,9},{9,8},{10,11... | collective-permute-start | bytes 159752 | tf_op jit(solution)/shard_map/ppermute | solution.py:450
  35.3 1.9 %collective-permute-start.3 = (f32[104,128]{1,0:T(8,128)S(1)}, f32[104,128]{1,0:T(8,128)S(1)}, u32[]{:S(2)}, u32[]{:S(2)}) collective-permute-start(f32[104,128]{1,0:T(8,128)S(1)} %get-tuple-element.39), channel_id=1, source_target_pairs={{0,1},{1,0},{2,3},{3,2},{4,5},{5,4},{6,7},{7,6},{8,9},{9,8},{10,11... | collective-permute-start | bytes 159752 | tf_op jit(solution)/shard_map/ppermute | solution.py:450
  37.2 0.0 collective-permute-done.refs_2_.refs_10_
  37.2 0.0 collective-permute-done.1.refs_3_.refs_11_
  37.2 0.0 collective-permute-done.2.refs_0_.refs_8_
  37.2 1.2 collective-permute-done.3.refs_1_.refs_9_
  38.4 0.0 collective-permute-done.4.refs_6_
  38.4 0.0 copy-start
  38.4 0.3 complete_first.1
  38.7 1.9 %collective-permute-start.5 = (f32[144,128]{1,0:T(8,128)S(1)}, f32[144,128]{1,0:T(8,128)S(1)}, u32[]{:S(2)}, u32[]{:S(2)}) collective-permute-start(f32[144,128]{1,0:T(8,128)S(1)} %get-tuple-element.48), channel_id=1, source_target_pairs={{0,8},{8,0},{16,24},{24,16},{32,40},{40,32},{48,56},{56,48},{1,9},... | collective-permute-start | bytes 221192 | tf_op jit(solution)/shard_map/ppermute | solution.py:446
  40.6 8.5 %collective-permute-start.6 = (f32[144,128]{1,0:T(8,128)S(1)}, f32[144,128]{1,0:T(8,128)S(1)}, u32[]{:S(2)}, u32[]{:S(2)}) collective-permute-start(f32[144,128]{1,0:T(8,128)S(1)} %get-tuple-element.49), channel_id=1, source_target_pairs={{0,56},{8,16},{16,8},{24,32},{32,24},{40,48},{48,40},{56,0},{1,57}... | collective-permute-start | bytes 221192 | tf_op jit(solution)/shard_map/ppermute | solution.py:446
  49.1 0.0 copy-done
  49.1 3.1 %collective-permute-start.7 = (f32[2,64,128]{2,1,0:T(8,128)S(1)}, f32[2,64,128]{2,1,0:T(8,128)S(1)}, u32[]{:S(2)}, u32[]{:S(2)}) collective-permute-start(f32[2,64,128]{2,1,0:T(8,128)S(1)} %bitcast.5), channel_id=1, source_target_pairs={{0,128},{64,192},{128,256},{192,320},{256,384},{320,448},{1,129},{... | collective-permute-start | bytes 196616 | tf_op jit(solution)/shard_map/ppermute | solution.py:460
  52.3 1.3 collective-permute-done.7.refs_16_
  53.6 0.0 collective-permute-done.5.refs_1_
  53.6 0.0 collective-permute-done.6.refs_2_
  53.6 19.2 %all_to_all.20.refs_3_ = f32[8,48,128]{2,1,0:T(8,128)S(1)} all-to-all(f32[8,48,128]{2,1,0:T(8,128)S(1)} %broadcast_in_dim.12), channel_id=1, replica_groups=mesh['tm'=8,'block'=8,'chip'=4,'core'=2] {'tm'}, dimensions={0} | all-to-all | bytes 393216 | tf_op jit(solution)/shard_map/all_to_all | solution.py:464
  72.9 17.8 %all_to_all.21.refs_4_ = f32[4,320,128]{2,1,0:T(8,128)S(1)} all-to-all(f32[4,320,128]{2,1,0:T(8,128)S(1)} %hand_out.2), channel_id=1, replica_groups=mesh['tm'=8,'block'=8,'chip'=4,'core'=2] {'chip'}, dimensions={0} | all-to-all | bytes 1310720 | tf_op jit(solution)/shard_map/all_to_all | solution.py:468
  90.7 6.9 %collective-permute-start.8 = (f32[4,320,128]{2,1,0:T(8,128)S(1)}, f32[4,320,128]{2,1,0:T(8,128)S(1)}, u32[]{:S(2)}, u32[]{:S(2)}) collective-permute-start(f32[4,320,128]{2,1,0:T(8,128)S(1)} %all_to_all.21.refs_4_), channel_id=1, source_target_pairs={{0,1},{1,0},{2,3},{3,2},{4,5},{5,4},{6,7},{7,6},{8,9},{9,8},{10,11... | collective-permute-start | bytes 1966088 | tf_op jit(solution)/shard_map/ppermute | solution.py:450
  97.6 1.7 %collective-permute-done.8.refs_5_ = f32[4,320,128]{2,1,0:T(8,128)S(1)} collective-permute-done((f32[4,320,128]{2,1,0:T(8,128)S(1)}, f32[4,320,128]{2,1,0:T(8,128)S(1)}, u32[]{:S(2)}, u32[]{:S(2)}) %collective-permute-start.8) | collective-permute-done | bytes 655392 | tf_op jit(solution)/shard_map/ppermute | solution.py:450
  99.4 2.2 %finish_first.1 = (f32[2,64,128]{2,1,0:T(8,128)S(1)}, f32[2,64,128]{2,1,0:T(8,128)S(1)}, f32[4,64,128]{2,1,0:T(8,128)S(1)}, f32[2,64,128]{2,1,0:T(8,128)S(1)}, f...) custom-call(f32[208,128]{1,0:T(8,128)S(1)} %get-tuple-element.47.refs_0_, ...), custom_call_target="tpu_custom_call" | custom-call | tf_op jit(solution)/shard_map/finish_first/pallas_call | solution.py:428
  101.6 5.1 %collective-permute-start.10 = (f32[48,128]{1,0:T(8,128)S(1)}, f32[48,128]{1,0:T(8,128)S(1)}, u32[]{:S(2)}, u32[]{:S(2)}) collective-permute-start(f32[48,128]{1,0:T(8,128)S(1)} %get-tuple-element.58.refs_0_), channel_id=1, source_target_pairs={{0,8},{8,0},{16,24},{24,16},{32,40},{40,32},{48,56},{56,48},{1,9},... | collective-permute-start | bytes 73736 | tf_op jit(solution)/shard_map/ppermute | solution.py:446
  106.7 7.0 %collective-permute-start.9 = (f32[48,128]{1,0:T(8,128)S(1)}, f32[48,128]{1,0:T(8,128)S(1)}, u32[]{:S(2)}, u32[]{:S(2)}) collective-permute-start(f32[48,128]{1,0:T(8,128)S(1)} %get-tuple-element.58.refs_0_), channel_id=1, source_target_pairs={{0,56},{8,16},{16,8},{24,32},{32,24},{40,48},{48,40},{56,0},{1,57}... | collective-permute-start | bytes 73736 | tf_op jit(solution)/shard_map/ppermute | solution.py:446
  113.8 0.0 collective-permute-done.10.refs_1_
  113.8 3.7 %collective-permute-done.9.refs_2_ = f32[48,128]{1,0:T(8,128)S(1)} collective-permute-done((f32[48,128]{1,0:T(8,128)S(1)}, f32[48,128]{1,0:T(8,128)S(1)}, u32[]{:S(2)}, u32[]{:S(2)}) %collective-permute-start.9) | collective-permute-done | bytes 24608 | tf_op jit(solution)/shard_map/ppermute | solution.py:446
  117.5 17.2 %all_to_all.22.refs_3_ = f32[8,48,128]{2,1,0:T(8,128)S(1)} all-to-all(f32[8,48,128]{2,1,0:T(8,128)S(1)} %broadcast_in_dim.13), channel_id=1, replica_groups=mesh['tm'=8,'block'=8,'chip'=4,'core'=2] {'tm'}, dimensions={0} | all-to-all | bytes 393216 | tf_op jit(solution)/shard_map/all_to_all | solution.py:464
  134.7 16.1 %all_to_all.23.refs_4_ = f32[4,192,128]{2,1,0:T(8,128)S(1)} all-to-all(f32[4,192,128]{2,1,0:T(8,128)S(1)} %hand_out.3), channel_id=1, replica_groups=mesh['tm'=8,'block'=8,'chip'=4,'core'=2] {'chip'}, dimensions={0} | all-to-all | bytes 786432 | tf_op jit(solution)/shard_map/all_to_all | solution.py:468
  150.8 5.1 %collective-permute-start.11 = (f32[4,192,128]{2,1,0:T(8,128)S(1)}, f32[4,192,128]{2,1,0:T(8,128)S(1)}, u32[]{:S(2)}, u32[]{:S(2)}) collective-permute-start(f32[4,192,128]{2,1,0:T(8,128)S(1)} %all_to_all.23.refs_4_), channel_id=1, source_target_pairs={{0,1},{1,0},{2,3},{3,2},{4,5},{5,4},{6,7},{7,6},{8,9},{9,8},{10,11... | collective-permute-start | bytes 1179656 | tf_op jit(solution)/shard_map/ppermute | solution.py:450
  155.9 1.3 collective-permute-done.11.refs_5_
  157.2 2.0 %finish_second.1 = (f32[2,2,64,128]{3,2,1,0:T(8,128)}, f32[32,64]{1,0:T(8,128)}) custom-call(f32[48,128]{1,0:T(8,128)S(1)} %get-tuple-element.58.refs_0_, f32[48,128]{1,0:T(8,128)S(1)} %collective-permute-done.10.refs_1_, f32[48,128]{1,0:T(8,128)S(1)} %collective-permute-done.9.refs_2_, f32[8,48,128]{2,1,0:T(8,128)S(1)} %all_to_all.22.refs_3_, ...), custom_call_target="tpu_custom_call" | custom-call | tf_op jit(solution)/shard_map/finish_second/pallas_call | solution.py:428
  (10 shorter events, 0.1 us)
Async XLA Ops:
  0.6 37.8 %collective-permute-start.4 = (f32[2,64,128]{2,1,0:T(8,128)}, f32[2,64,128]{2,1,0:T(8,128)S(1)}, u32[]{:S(2)}, u32[]{:S(2)}) collective-permute-start(f32[2,64,128]{2,1,0:T(8,128)} %bitcast.3), channel_id=1, source_target_pairs={{0,64},{64,128},{128,192},{192,256},{256,320},{320,384},{384,448},... | collective-permute-start | bytes 196616 | tf_op jit(solution)/shard_map/ppermute | solution.py:460
  18.1 19.1 %collective-permute-start = (f32[104,128]{1,0:T(8,128)S(1)}, f32[104,128]{1,0:T(8,128)S(1)}, u32[]{:S(2)}, u32[]{:S(2)}) collective-permute-start(f32[104,128]{1,0:T(8,128)S(1)} %get-tuple-element.36), channel_id=1, source_target_pairs={{0,63},{1,2},{2,1},{3,4},{4,3},{5,6},{6,5},{7,8},{8,7},{9,10},{10,... | collective-permute-start | bytes 159752 | tf_op jit(solution)/shard_map/ppermute | solution.py:455
  21.6 15.6 %collective-permute-start.1 = (f32[104,128]{1,0:T(8,128)S(1)}, f32[104,128]{1,0:T(8,128)S(1)}, u32[]{:S(2)}, u32[]{:S(2)}) collective-permute-start(f32[104,128]{1,0:T(8,128)S(1)} %get-tuple-element.37), channel_id=1, source_target_pairs={{0,63},{1,2},{2,1},{3,4},{4,3},{5,6},{6,5},{7,8},{8,7},{9,10},{10,... | collective-permute-start | bytes 159752 | tf_op jit(solution)/shard_map/ppermute | solution.py:455
  23.7 13.5 %collective-permute-start.2 = (f32[104,128]{1,0:T(8,128)S(1)}, f32[104,128]{1,0:T(8,128)S(1)}, u32[]{:S(2)}, u32[]{:S(2)}) collective-permute-start(f32[104,128]{1,0:T(8,128)S(1)} %get-tuple-element.38), channel_id=1, source_target_pairs={{0,1},{1,0},{2,3},{3,2},{4,5},{5,4},{6,7},{7,6},{8,9},{9,8},{10,11... | collective-permute-start | bytes 159752 | tf_op jit(solution)/shard_map/ppermute | solution.py:450
  35.3 3.1 %collective-permute-start.3 = (f32[104,128]{1,0:T(8,128)S(1)}, f32[104,128]{1,0:T(8,128)S(1)}, u32[]{:S(2)}, u32[]{:S(2)}) collective-permute-start(f32[104,128]{1,0:T(8,128)S(1)} %get-tuple-element.39), channel_id=1, source_target_pairs={{0,1},{1,0},{2,3},{3,2},{4,5},{5,4},{6,7},{7,6},{8,9},{9,8},{10,11... | collective-permute-start | bytes 159752 | tf_op jit(solution)/shard_map/ppermute | solution.py:450
  38.4 10.7 %copy-start = (f32[1,2,64,128]{3,2,1,0:T(8,128)S(1)}, f32[1,2,64,128]{3,2,1,0:T(8,128)}, u32[]{:S(2)}) copy-start(f32[1,2,64,128]{3,2,1,0:T(8,128)} %param.5) | copy-start | bytes 196612
  38.7 14.9 %collective-permute-start.5 = (f32[144,128]{1,0:T(8,128)S(1)}, f32[144,128]{1,0:T(8,128)S(1)}, u32[]{:S(2)}, u32[]{:S(2)}) collective-permute-start(f32[144,128]{1,0:T(8,128)S(1)} %get-tuple-element.48), channel_id=1, source_target_pairs={{0,8},{8,0},{16,24},{24,16},{32,40},{40,32},{48,56},{56,48},{1,9},... | collective-permute-start | bytes 221192 | tf_op jit(solution)/shard_map/ppermute | solution.py:446
  40.6 13.0 %collective-permute-start.6 = (f32[144,128]{1,0:T(8,128)S(1)}, f32[144,128]{1,0:T(8,128)S(1)}, u32[]{:S(2)}, u32[]{:S(2)}) collective-permute-start(f32[144,128]{1,0:T(8,128)S(1)} %get-tuple-element.49), channel_id=1, source_target_pairs={{0,56},{8,16},{16,8},{24,32},{32,24},{40,48},{48,40},{56,0},{1,57}... | collective-permute-start | bytes 221192 | tf_op jit(solution)/shard_map/ppermute | solution.py:446
  49.1 4.4 %collective-permute-start.7 = (f32[2,64,128]{2,1,0:T(8,128)S(1)}, f32[2,64,128]{2,1,0:T(8,128)S(1)}, u32[]{:S(2)}, u32[]{:S(2)}) collective-permute-start(f32[2,64,128]{2,1,0:T(8,128)S(1)} %bitcast.5), channel_id=1, source_target_pairs={{0,128},{64,192},{128,256},{192,320},{256,384},{320,448},{1,129},{... | collective-permute-start | bytes 196616 | tf_op jit(solution)/shard_map/ppermute | solution.py:460
  90.7 8.7 %collective-permute-start.8 = (f32[4,320,128]{2,1,0:T(8,128)S(1)}, f32[4,320,128]{2,1,0:T(8,128)S(1)}, u32[]{:S(2)}, u32[]{:S(2)}) collective-permute-start(f32[4,320,128]{2,1,0:T(8,128)S(1)} %all_to_all.21.refs_4_), channel_id=1, source_target_pairs={{0,1},{1,0},{2,3},{3,2},{4,5},{5,4},{6,7},{7,6},{8,9},{9,8},{10,11... | collective-permute-start | bytes 1966088 | tf_op jit(solution)/shard_map/ppermute | solution.py:450
  101.6 12.2 %collective-permute-start.10 = (f32[48,128]{1,0:T(8,128)S(1)}, f32[48,128]{1,0:T(8,128)S(1)}, u32[]{:S(2)}, u32[]{:S(2)}) collective-permute-start(f32[48,128]{1,0:T(8,128)S(1)} %get-tuple-element.58.refs_0_), channel_id=1, source_target_pairs={{0,8},{8,0},{16,24},{24,16},{32,40},{40,32},{48,56},{56,48},{1,9},... | collective-permute-start | bytes 73736 | tf_op jit(solution)/shard_map/ppermute | solution.py:446
  106.7 10.8 %collective-permute-start.9 = (f32[48,128]{1,0:T(8,128)S(1)}, f32[48,128]{1,0:T(8,128)S(1)}, u32[]{:S(2)}, u32[]{:S(2)}) collective-permute-start(f32[48,128]{1,0:T(8,128)S(1)} %get-tuple-element.58.refs_0_), channel_id=1, source_target_pairs={{0,56},{8,16},{16,8},{24,32},{32,24},{40,48},{48,40},{56,0},{1,57}... | collective-permute-start | bytes 73736 | tf_op jit(solution)/shard_map/ppermute | solution.py:446
  150.8 6.4 %collective-permute-start.11 = (f32[4,192,128]{2,1,0:T(8,128)S(1)}, f32[4,192,128]{2,1,0:T(8,128)S(1)}, u32[]{:S(2)}, u32[]{:S(2)}) collective-permute-start(f32[4,192,128]{2,1,0:T(8,128)S(1)} %all_to_all.23.refs_4_), channel_id=1, source_target_pairs={{0,1},{1,0},{2,3},{3,2},{4,5},{5,4},{6,7},{7,6},{8,9},{9,8},{10,11... | collective-permute-start | bytes 1179656 | tf_op jit(solution)/shard_map/ppermute | solution.py:450

commit v14 on v11

--- a/solution.py
+++ b/solution.py
@@ -492,11 +492,10 @@
         first_kernel, (initial, coeff, guess),
         [(112, 128)] * 4 + [(4,) + coarse, slab, slab, slab], [(256, 128)], name="first", first=True,
     )
-    earlier, received, outer, outer_rest, inner = links.together(
+    earlier, received, outer, outer_rest, inner, inner_rest = links.together(
         links.onward(sent, 2), links.onward(sent, 1), links.swap_outer(outer), links.swap_outer(outer_rest),
-        links.swap_inner(inner),
-    )
-    inner_rest = links.swap_inner(inner_rest)
+        links.swap_inner(inner), links.swap_inner(inner_rest),
+    )
     owned, beside, beyond, mine, started, begin, earlier = links.call(
         complete_first, (inner, outer, kept, initial, earlier, received),
         [(208, 128), (144, 128), (144, 128), (16, 128), (8,) + coarse, slab, slab], [(192, 128)], name="complete_first",
@@ -510,7 +509,7 @@
         work + [(576, 128)],
         name="finish_first",
     )
-    beside, beyond = links.swap_block(owned, True), links.swap_block(owned, False)
+    beyond, beside = links.together(links.swap_block(owned, False), links.swap_block(owned, True))
     fine, coarse_end = links.call(
         finish_second,
         (*windows(owned, beside, beyond, mine, 1), started, kept, ends, coeff, begin, middle, end, begin_next, coefs),

time: 165 us -> 164 us (level)
  starting transfers between devices: 62.8 us -> 72.2 us
  blocking collectives: 81.7 us -> 74.5 us
  waiting for transfers between devices: 13.3 us -> 10.1 us
    all_to_all x2, blocking collectives: 44.7 us -> 34.2 us  [block(): return lax.all_to_all(x, 'chip', 0, 0)]
    ppermute x4, starting transfers between devices: 16.2 us -> 22.9 us  [swap_block(): return lax.ppermute(x, 'block', pairs)]
    ppermute x4, waiting for transfers between devices: 9.94 us -> 5.84 us  [swap_block(): return lax.ppermute(x, 'block', pairs)]
    all_to_all x2, blocking collectives: 37 us -> 40.4 us  [sections(): lax.all_to_all(jnp.broadcast_to(x, (SECTIONS,) + x.shape), 'tm', 0, 0)]
    ppermute x2, starting transfers between devices: 5.68 us -> 7.86 us  [swap_outer(): lax.ppermute(x, ('block', 'chip', 'core'), [(i, (i + 2 * (i % 2) - 1) % n...]
    ppermute x4, starting transfers between devices: 21.6 us -> 23.7 us  [swap_inner(): return lax.ppermute(x, 'core', [(0, 1), (1, 0)])]
    ppermute x2, starting transfers between devices: 19.4 us -> 17.7 us  [onward(): return lax.ppermute(x, 'tm', [(i, i + by) for i in range(n - by)])]
  transfers between devices with their start and end apart: 12 -> 12, of which waited for: 5 -> 6; matrix products, arithmetic and copies ran while one was open for 0% -> 0% of each run, Pallas kernels for 1% -> 0%
where the time goes in v14:
time: 164 us; the launch traced here: 163 us
  blocking collectives  74.5 us (45%)
  starting transfers between devices  72.2 us (44%)
  waiting for transfers between devices  10.1 us (6%)
  Pallas kernels  5.83 us (4%)
    all_to_all x2, blocking collectives, sections(): lax.all_to_all(jnp.broadcast_to(x, (SECTIONS,) + x.shape), 'tm', 0, 0)  40.4 us
    all_to_all x2, blocking collectives, block(): return lax.all_to_all(x, 'chip', 0, 0)  34.2 us
    ppermute x4, starting transfers between devices, swap_inner(): return lax.ppermute(x, 'core', [(0, 1), (1, 0)])  23.7 us
    ppermute x4, starting transfers between devices, swap_block(): return lax.ppermute(x, 'block', pairs)  22.9 us
    ppermute x2, starting transfers between devices, onward(): return lax.ppermute(x, 'tm', [(i, i + by) for i in range(n - by)])  17.7 us
    ppermute x2, starting transfers between devices, swap_outer(): lax.ppermute(x, ('block', 'chip', 'core'), [(i, (i + 2 * (i % 2) - 1) % n...  7.86 us
    ppermute x4, waiting for transfers between devices, swap_block(): return lax.ppermute(x, 'block', pairs)  5.84 us
    pallas_call x6, Pallas kernels, run(): pl.pallas_call(placed, out_shape=[jax.ShapeDtypeStruct(shape, F32) if las...  5.83 us
  transfers between devices with their start and end apart: 12, of which 6 were waited for; matrix products, arithmetic and copies ran while one was open for 0% of the time, Pallas kernels for 0%

profile of v14, /device:TPU:1, one launch (start us, length us, event | category | flops | bytes accessed | tf_op | source)
XLA Modules:
  0.0 163.5 jit_solution(9522317686737350921)
XLA Ops:
  0.6 0.0 copy-start
  0.6 1.2 first.1
  1.9 4.9 %collective-permute-start.2 = (f32[112,128]{1,0:T(8,128)S(1)}, f32[112,128]{1,0:T(8,128)S(1)}, u32[]{:S(2)}, u32[]{:S(2)}) collective-permute-start(f32[112,128]{1,0:T(8,128)S(1)} %get-tuple-element.35), channel_id=1, source_target_pairs={{0,63},{1,2},{2,1},{3,4},{4,3},{5,6},{6,5},{7,8},{8,7},{9,10},{10,... | collective-permute-start | bytes 172040 | tf_op jit(solution)/shard_map/ppermute | solution.py:453
  6.8 0.0 copy-done
  6.8 14.5 %collective-permute-start.1 = (f32[2,64,128]{2,1,0:T(8,128)S(1)}, f32[2,64,128]{2,1,0:T(8,128)S(1)}, u32[]{:S(2)}, u32[]{:S(2)}) collective-permute-start(f32[2,64,128]{2,1,0:T(8,128)S(1)} %bitcast.4), channel_id=1, source_target_pairs={{0,64},{64,128},{128,192},{192,256},{256,320},{320,384},{384,448},... | collective-permute-start | bytes 196616 | tf_op jit(solution)/shard_map/ppermute | solution.py:458
  21.4 3.1 %collective-permute-start = (f32[2,64,128]{2,1,0:T(8,128)S(1)}, f32[2,64,128]{2,1,0:T(8,128)S(1)}, u32[]{:S(2)}, u32[]{:S(2)}) collective-permute-start(f32[2,64,128]{2,1,0:T(8,128)S(1)} %bitcast.5), channel_id=1, source_target_pairs={{0,128},{64,192},{128,256},{192,320},{256,384},{320,448},{1,129},{... | collective-permute-start | bytes 196616 | tf_op jit(solution)/shard_map/ppermute | solution.py:458
  24.5 2.9 %collective-permute-start.3 = (f32[112,128]{1,0:T(8,128)S(1)}, f32[112,128]{1,0:T(8,128)S(1)}, u32[]{:S(2)}, u32[]{:S(2)}) collective-permute-start(f32[112,128]{1,0:T(8,128)S(1)} %get-tuple-element.36), channel_id=1, source_target_pairs={{0,63},{1,2},{2,1},{3,4},{4,3},{5,6},{6,5},{7,8},{8,7},{9,10},{10,... | collective-permute-start | bytes 172040 | tf_op jit(solution)/shard_map/ppermute | solution.py:453
  27.4 10.7 %collective-permute-start.4 = (f32[112,128]{1,0:T(8,128)S(1)}, f32[112,128]{1,0:T(8,128)S(1)}, u32[]{:S(2)}, u32[]{:S(2)}) collective-permute-start(f32[112,128]{1,0:T(8,128)S(1)} %get-tuple-element.37), channel_id=1, source_target_pairs={{0,1},{1,0},{2,3},{3,2},{4,5},{5,4},{6,7},{7,6},{8,9},{9,8},{10,11... | collective-permute-start | bytes 172040 | tf_op jit(solution)/shard_map/ppermute | solution.py:448
  38.2 0.0 collective-permute-done.2.refs_1_.refs_10_
  38.2 1.9 %collective-permute-start.5 = (f32[112,128]{1,0:T(8,128)S(1)}, f32[112,128]{1,0:T(8,128)S(1)}, u32[]{:S(2)}, u32[]{:S(2)}) collective-permute-start(f32[112,128]{1,0:T(8,128)S(1)} %get-tuple-element.38), channel_id=1, source_target_pairs={{0,1},{1,0},{2,3},{3,2},{4,5},{5,4},{6,7},{7,6},{8,9},{9,8},{10,11... | collective-permute-start | bytes 172040 | tf_op jit(solution)/shard_map/ppermute | solution.py:448
  40.1 0.0 collective-permute-done.3.refs_11_
  40.1 0.0 collective-permute-done.4.refs_0_.refs_8_
  40.1 1.2 collective-permute-done.5.refs_9_
  41.3 0.0 collective-permute-done.1.refs_5_
  41.3 0.0 collective-permute-done.refs_4_
  41.3 0.2 complete_first.1
  41.6 1.9 %collective-permute-start.6 = (f32[144,128]{1,0:T(8,128)S(1)}, f32[144,128]{1,0:T(8,128)S(1)}, u32[]{:S(2)}, u32[]{:S(2)}) collective-permute-start(f32[144,128]{1,0:T(8,128)S(1)} %get-tuple-element.46), channel_id=1, source_target_pairs={{0,8},{8,0},{16,24},{24,16},{32,40},{40,32},{48,56},{56,48},{1,9},... | collective-permute-start | bytes 221192 | tf_op jit(solution)/shard_map/ppermute | solution.py:444
  43.5 8.5 %collective-permute-start.7 = (f32[144,128]{1,0:T(8,128)S(1)}, f32[144,128]{1,0:T(8,128)S(1)}, u32[]{:S(2)}, u32[]{:S(2)}) collective-permute-start(f32[144,128]{1,0:T(8,128)S(1)} %get-tuple-element.47), channel_id=1, source_target_pairs={{0,56},{8,16},{16,8},{24,32},{32,24},{40,48},{48,40},{56,0},{1,57}... | collective-permute-start | bytes 221192 | tf_op jit(solution)/shard_map/ppermute | solution.py:444
  52.0 0.1 collective-permute-done.6.refs_1_
  52.1 2.7 %collective-permute-done.7.refs_2_ = f32[144,128]{1,0:T(8,128)S(1)} collective-permute-done((f32[144,128]{1,0:T(8,128)S(1)}, f32[144,128]{1,0:T(8,128)S(1)}, u32[]{:S(2)}, u32[]{:S(2)}) %collective-permute-start.7) | collective-permute-done | bytes 73760 | tf_op jit(solution)/shard_map/ppermute | solution.py:444
  54.9 22.6 %all_to_all.20.refs_3_ = f32[8,48,128]{2,1,0:T(8,128)S(1)} all-to-all(f32[8,48,128]{2,1,0:T(8,128)S(1)} %broadcast_in_dim.12), channel_id=1, replica_groups=mesh['tm'=8,'block'=8,'chip'=4,'core'=2] {'tm'}, dimensions={0} | all-to-all | bytes 393216 | tf_op jit(solution)/shard_map/all_to_all | solution.py:462
  77.5 15.6 %all_to_all.21.refs_4_ = f32[4,320,128]{2,1,0:T(8,128)S(1)} all-to-all(f32[4,320,128]{2,1,0:T(8,128)S(1)} %hand_out.2), channel_id=1, replica_groups=mesh['tm'=8,'block'=8,'chip'=4,'core'=2] {'chip'}, dimensions={0} | all-to-all | bytes 1310720 | tf_op jit(solution)/shard_map/all_to_all | solution.py:466
  93.2 6.9 %collective-permute-start.8 = (f32[4,320,128]{2,1,0:T(8,128)S(1)}, f32[4,320,128]{2,1,0:T(8,128)S(1)}, u32[]{:S(2)}, u32[]{:S(2)}) collective-permute-start(f32[4,320,128]{2,1,0:T(8,128)S(1)} %all_to_all.21.refs_4_), channel_id=1, source_target_pairs={{0,1},{1,0},{2,3},{3,2},{4,5},{5,4},{6,7},{7,6},{8,9},{9,8},{10,11... | collective-permute-start | bytes 1966088 | tf_op jit(solution)/shard_map/ppermute | solution.py:448
  100.1 1.7 %collective-permute-done.8.refs_5_ = f32[4,320,128]{2,1,0:T(8,128)S(1)} collective-permute-done((f32[4,320,128]{2,1,0:T(8,128)S(1)}, f32[4,320,128]{2,1,0:T(8,128)S(1)}, u32[]{:S(2)}, u32[]{:S(2)}) %collective-permute-start.8) | collective-permute-done | bytes 655392 | tf_op jit(solution)/shard_map/ppermute | solution.py:448
  101.8 2.2 %finish_first.1 = (f32[2,64,128]{2,1,0:T(8,128)S(1)}, f32[2,64,128]{2,1,0:T(8,128)S(1)}, f32[4,64,128]{2,1,0:T(8,128)S(1)}, f32[2,64,128]{2,1,0:T(8,128)S(1)}, f...) custom-call(f32[208,128]{1,0:T(8,128)S(1)} %get-tuple-element.45.refs_0_, ...), custom_call_target="tpu_custom_call" | custom-call | tf_op jit(solution)/shard_map/finish_first/pallas_call | solution.py:426
  104.1 4.9 %collective-permute-start.10 = (f32[48,128]{1,0:T(8,128)S(1)}, f32[48,128]{1,0:T(8,128)S(1)}, u32[]{:S(2)}, u32[]{:S(2)}) collective-permute-start(f32[48,128]{1,0:T(8,128)S(1)} %get-tuple-element.56.refs_0_), channel_id=1, source_target_pairs={{0,8},{8,0},{16,24},{24,16},{32,40},{40,32},{48,56},{56,48},{1,9},... | collective-permute-start | bytes 73736 | tf_op jit(solution)/shard_map/ppermute | solution.py:444
  109.0 7.6 %collective-permute-start.9 = (f32[48,128]{1,0:T(8,128)S(1)}, f32[48,128]{1,0:T(8,128)S(1)}, u32[]{:S(2)}, u32[]{:S(2)}) collective-permute-start(f32[48,128]{1,0:T(8,128)S(1)} %get-tuple-element.56.refs_0_), channel_id=1, source_target_pairs={{0,56},{8,16},{16,8},{24,32},{32,24},{40,48},{48,40},{56,0},{1,57}... | collective-permute-start | bytes 73736 | tf_op jit(solution)/shard_map/ppermute | solution.py:444
  116.6 0.0 collective-permute-done.10.refs_1_
  116.6 3.0 %collective-permute-done.9.refs_2_ = f32[48,128]{1,0:T(8,128)S(1)} collective-permute-done((f32[48,128]{1,0:T(8,128)S(1)}, f32[48,128]{1,0:T(8,128)S(1)}, u32[]{:S(2)}, u32[]{:S(2)}) %collective-permute-start.9) | collective-permute-done | bytes 24608 | tf_op jit(solution)/shard_map/ppermute | solution.py:444
  119.6 17.8 %all_to_all.22.refs_3_ = f32[8,48,128]{2,1,0:T(8,128)S(1)} all-to-all(f32[8,48,128]{2,1,0:T(8,128)S(1)} %broadcast_in_dim.13), channel_id=1, replica_groups=mesh['tm'=8,'block'=8,'chip'=4,'core'=2] {'tm'}, dimensions={0} | all-to-all | bytes 393216 | tf_op jit(solution)/shard_map/all_to_all | solution.py:462
  137.4 18.5 %all_to_all.23.refs_4_ = f32[4,192,128]{2,1,0:T(8,128)S(1)} all-to-all(f32[4,192,128]{2,1,0:T(8,128)S(1)} %hand_out.3), channel_id=1, replica_groups=mesh['tm'=8,'block'=8,'chip'=4,'core'=2] {'chip'}, dimensions={0} | all-to-all | bytes 786432 | tf_op jit(solution)/shard_map/all_to_all | solution.py:466
  155.9 4.1 %collective-permute-start.11 = (f32[4,192,128]{2,1,0:T(8,128)S(1)}, f32[4,192,128]{2,1,0:T(8,128)S(1)}, u32[]{:S(2)}, u32[]{:S(2)}) collective-permute-start(f32[4,192,128]{2,1,0:T(8,128)S(1)} %all_to_all.23.refs_4_), channel_id=1, source_target_pairs={{0,1},{1,0},{2,3},{3,2},{4,5},{5,4},{6,7},{7,6},{8,9},{9,8},{10,11... | collective-permute-start | bytes 1179656 | tf_op jit(solution)/shard_map/ppermute | solution.py:448
  160.1 1.3 collective-permute-done.11.refs_5_
  161.4 2.0 %finish_second.1 = (f32[2,2,64,128]{3,2,1,0:T(8,128)}, f32[32,64]{1,0:T(8,128)}) custom-call(f32[48,128]{1,0:T(8,128)S(1)} %get-tuple-element.56.refs_0_, f32[48,128]{1,0:T(8,128)S(1)} %collective-permute-done.10.refs_1_, f32[48,128]{1,0:T(8,128)S(1)} %collective-permute-done.9.refs_2_, f32[8,48,128]{2,1,0:T(8,128)S(1)} %all_to_all.22.refs_3_, ...), custom_call_target="tpu_custom_call" | custom-call | tf_op jit(solution)/shard_map/finish_second/pallas_call | solution.py:426
  (10 shorter events, 0.1 us)
Async XLA Ops:
  0.6 6.2 %copy-start = (f32[1,2,64,128]{3,2,1,0:T(8,128)S(1)}, f32[1,2,64,128]{3,2,1,0:T(8,128)}, u32[]{:S(2)}) copy-start(f32[1,2,64,128]{3,2,1,0:T(8,128)} %param.5) | copy-start | bytes 196612
  1.9 36.3 %collective-permute-start.2 = (f32[112,128]{1,0:T(8,128)S(1)}, f32[112,128]{1,0:T(8,128)S(1)}, u32[]{:S(2)}, u32[]{:S(2)}) collective-permute-start(f32[112,128]{1,0:T(8,128)S(1)} %get-tuple-element.35), channel_id=1, source_target_pairs={{0,63},{1,2},{2,1},{3,4},{4,3},{5,6},{6,5},{7,8},{8,7},{9,10},{10,... | collective-permute-start | bytes 172040 | tf_op jit(solution)/shard_map/ppermute | solution.py:453
  6.8 34.5 %collective-permute-start.1 = (f32[2,64,128]{2,1,0:T(8,128)S(1)}, f32[2,64,128]{2,1,0:T(8,128)S(1)}, u32[]{:S(2)}, u32[]{:S(2)}) collective-permute-start(f32[2,64,128]{2,1,0:T(8,128)S(1)} %bitcast.4), channel_id=1, source_target_pairs={{0,64},{64,128},{128,192},{192,256},{256,320},{320,384},{384,448},... | collective-permute-start | bytes 196616 | tf_op jit(solution)/shard_map/ppermute | solution.py:458
  21.4 19.9 %collective-permute-start = (f32[2,64,128]{2,1,0:T(8,128)S(1)}, f32[2,64,128]{2,1,0:T(8,128)S(1)}, u32[]{:S(2)}, u32[]{:S(2)}) collective-permute-start(f32[2,64,128]{2,1,0:T(8,128)S(1)} %bitcast.5), channel_id=1, source_target_pairs={{0,128},{64,192},{128,256},{192,320},{256,384},{320,448},{1,129},{... | collective-permute-start | bytes 196616 | tf_op jit(solution)/shard_map/ppermute | solution.py:458
  24.5 15.6 %collective-permute-start.3 = (f32[112,128]{1,0:T(8,128)S(1)}, f32[112,128]{1,0:T(8,128)S(1)}, u32[]{:S(2)}, u32[]{:S(2)}) collective-permute-start(f32[112,128]{1,0:T(8,128)S(1)} %get-tuple-element.36), channel_id=1, source_target_pairs={{0,63},{1,2},{2,1},{3,4},{4,3},{5,6},{6,5},{7,8},{8,7},{9,10},{10,... | collective-permute-start | bytes 172040 | tf_op jit(solution)/shard_map/ppermute | solution.py:453
  27.4 12.7 %collective-permute-start.4 = (f32[112,128]{1,0:T(8,128)S(1)}, f32[112,128]{1,0:T(8,128)S(1)}, u32[]{:S(2)}, u32[]{:S(2)}) collective-permute-start(f32[112,128]{1,0:T(8,128)S(1)} %get-tuple-element.37), channel_id=1, source_target_pairs={{0,1},{1,0},{2,3},{3,2},{4,5},{5,4},{6,7},{7,6},{8,9},{9,8},{10,11... | collective-permute-start | bytes 172040 | tf_op jit(solution)/shard_map/ppermute | solution.py:448
  38.2 3.1 %collective-permute-start.5 = (f32[112,128]{1,0:T(8,128)S(1)}, f32[112,128]{1,0:T(8,128)S(1)}, u32[]{:S(2)}, u32[]{:S(2)}) collective-permute-start(f32[112,128]{1,0:T(8,128)S(1)} %get-tuple-element.38), channel_id=1, source_target_pairs={{0,1},{1,0},{2,3},{3,2},{4,5},{5,4},{6,7},{7,6},{8,9},{9,8},{10,11... | collective-permute-start | bytes 172040 | tf_op jit(solution)/shard_map/ppermute | solution.py:448
  41.6 10.6 %collective-permute-start.6 = (f32[144,128]{1,0:T(8,128)S(1)}, f32[144,128]{1,0:T(8,128)S(1)}, u32[]{:S(2)}, u32[]{:S(2)}) collective-permute-start(f32[144,128]{1,0:T(8,128)S(1)} %get-tuple-element.46), channel_id=1, source_target_pairs={{0,8},{8,0},{16,24},{24,16},{32,40},{40,32},{48,56},{56,48},{1,9},... | collective-permute-start | bytes 221192 | tf_op jit(solution)/shard_map/ppermute | solution.py:444
  43.5 11.4 %collective-permute-start.7 = (f32[144,128]{1,0:T(8,128)S(1)}, f32[144,128]{1,0:T(8,128)S(1)}, u32[]{:S(2)}, u32[]{:S(2)}) collective-permute-start(f32[144,128]{1,0:T(8,128)S(1)} %get-tuple-element.47), channel_id=1, source_target_pairs={{0,56},{8,16},{16,8},{24,32},{32,24},{40,48},{48,40},{56,0},{1,57}... | collective-permute-start | bytes 221192 | tf_op jit(solution)/shard_map/ppermute | solution.py:444
  93.2 8.7 %collective-permute-start.8 = (f32[4,320,128]{2,1,0:T(8,128)S(1)}, f32[4,320,128]{2,1,0:T(8,128)S(1)}, u32[]{:S(2)}, u32[]{:S(2)}) collective-permute-start(f32[4,320,128]{2,1,0:T(8,128)S(1)} %all_to_all.21.refs_4_), channel_id=1, source_target_pairs={{0,1},{1,0},{2,3},{3,2},{4,5},{5,4},{6,7},{7,6},{8,9},{9,8},{10,11... | collective-permute-start | bytes 1966088 | tf_op jit(solution)/shard_map/ppermute | solution.py:448
  104.1 12.5 %collective-permute-start.10 = (f32[48,128]{1,0:T(8,128)S(1)}, f32[48,128]{1,0:T(8,128)S(1)}, u32[]{:S(2)}, u32[]{:S(2)}) collective-permute-start(f32[48,128]{1,0:T(8,128)S(1)} %get-tuple-element.56.refs_0_), channel_id=1, source_target_pairs={{0,8},{8,0},{16,24},{24,16},{32,40},{40,32},{48,56},{56,48},{1,9},... | collective-permute-start | bytes 73736 | tf_op jit(solution)/shard_map/ppermute | solution.py:444
  109.0 10.6 %collective-permute-start.9 = (f32[48,128]{1,0:T(8,128)S(1)}, f32[48,128]{1,0:T(8,128)S(1)}, u32[]{:S(2)}, u32[]{:S(2)}) collective-permute-start(f32[48,128]{1,0:T(8,128)S(1)} %get-tuple-element.56.refs_0_), channel_id=1, source_target_pairs={{0,56},{8,16},{16,8},{24,32},{32,24},{40,48},{48,40},{56,0},{1,57}... | collective-permute-start | bytes 73736 | tf_op jit(solution)/shard_map/ppermute | solution.py:444
  155.9 5.5 %collective-permute-start.11 = (f32[4,192,128]{2,1,0:T(8,128)S(1)}, f32[4,192,128]{2,1,0:T(8,128)S(1)}, u32[]{:S(2)}, u32[]{:S(2)}) collective-permute-start(f32[4,192,128]{2,1,0:T(8,128)S(1)} %all_to_all.23.refs_4_), channel_id=1, source_target_pairs={{0,1},{1,0},{2,3},{3,2},{4,5},{5,4},{6,7},{7,6},{8,9},{9,8},{10,11... | collective-permute-start | bytes 1179656 | tf_op jit(solution)/shard_map/ppermute | solution.py:448

commit v15 on v13

--- a/solution.py
+++ b/solution.py
@@ -53,7 +53,14 @@
 
 
 def dot(a, b):
-    return jnp.dot(a, b, precision=lax.Precision.HIGHEST, preferred_element_type=F32)
+    b = b.astype(jnp.bfloat16)
+    total, rest = None, a
+    for _ in range(3):
+        part = rest.astype(jnp.bfloat16)
+        rest = rest - part.astype(F32)
+        product = jnp.dot(part, b, preferred_element_type=F32)
+        total = product if total is None else total + product
+    return total
 
 
 def pair_lanes():

time: 160 us -> 160 us (level)
  no operation moved by 1% of the time
where the time goes in v15:
time: 160 us; the launch traced here: 159 us
  starting transfers between devices  73.9 us (46%)
  blocking collectives  69.2 us (43%)
  waiting for transfers between devices  9.24 us (6%)
  Pallas kernels  5.62 us (4%)
    all_to_all x2, blocking collectives, sections(): lax.all_to_all(jnp.broadcast_to(x, (SECTIONS,) + x.shape), 'tm', 0, 0)  36.5 us
    all_to_all x2, blocking collectives, block(): return lax.all_to_all(x, 'chip', 0, 0)  32.8 us
    ppermute x4, starting transfers between devices, swap_inner(): return lax.ppermute(x, 'core', [(0, 1), (1, 0)])  26.4 us
    ppermute x4, starting transfers between devices, swap_block(): return lax.ppermute(x, 'block', pairs)  22.6 us
    ppermute x2, starting transfers between devices, onward(): return lax.ppermute(x, 'tm', [(i, i + by) for i in range(n - by)])  19.4 us
    pallas_call x6, Pallas kernels, run(): pl.pallas_call(placed, out_shape=[jax.ShapeDtypeStruct(shape, F32) if las...  5.62 us
    ppermute x2, starting transfers between devices, swap_outer(): lax.ppermute(x, ('block', 'chip', 'core'), [(i, (i + 2 * (i % 2) - 1) % n...  5.56 us
    ppermute x4, waiting for transfers between devices, swap_inner(): return lax.ppermute(x, 'core', [(0, 1), (1, 0)])  4.2 us
  transfers between devices with their start and end apart: 12, of which 5 were waited for; matrix products, arithmetic and copies ran while one was open for 0% of the time, Pallas kernels for 1%

profile of v15, /device:TPU:1, one launch (start us, length us, event | category | flops | bytes accessed | tf_op | source)
XLA Modules:
  0.0 158.9 jit_solution(12096738054144951184)
XLA Ops:
  0.6 16.3 %collective-permute-start.4 = (f32[2,64,128]{2,1,0:T(8,128)}, f32[2,64,128]{2,1,0:T(8,128)S(1)}, u32[]{:S(2)}, u32[]{:S(2)}) collective-permute-start(f32[2,64,128]{2,1,0:T(8,128)} %bitcast.3), channel_id=1, source_target_pairs={{0,64},{64,128},{128,192},{192,256},{256,320},{320,384},{384,448},... | collective-permute-start | bytes 196616 | tf_op jit(solution)/shard_map/ppermute | solution.py:467
  16.9 1.2 first.1
  18.1 3.5 %collective-permute-start = (f32[104,128]{1,0:T(8,128)S(1)}, f32[104,128]{1,0:T(8,128)S(1)}, u32[]{:S(2)}, u32[]{:S(2)}) collective-permute-start(f32[104,128]{1,0:T(8,128)S(1)} %get-tuple-element.36), channel_id=1, source_target_pairs={{0,63},{1,2},{2,1},{3,4},{4,3},{5,6},{6,5},{7,8},{8,7},{9,10},{10,... | collective-permute-start | bytes 159752 | tf_op jit(solution)/shard_map/ppermute | solution.py:462
  21.6 2.1 %collective-permute-start.1 = (f32[104,128]{1,0:T(8,128)S(1)}, f32[104,128]{1,0:T(8,128)S(1)}, u32[]{:S(2)}, u32[]{:S(2)}) collective-permute-start(f32[104,128]{1,0:T(8,128)S(1)} %get-tuple-element.37), channel_id=1, source_target_pairs={{0,63},{1,2},{2,1},{3,4},{4,3},{5,6},{6,5},{7,8},{8,7},{9,10},{10,... | collective-permute-start | bytes 159752 | tf_op jit(solution)/shard_map/ppermute | solution.py:462
  23.7 11.6 %collective-permute-start.2 = (f32[104,128]{1,0:T(8,128)S(1)}, f32[104,128]{1,0:T(8,128)S(1)}, u32[]{:S(2)}, u32[]{:S(2)}) collective-permute-start(f32[104,128]{1,0:T(8,128)S(1)} %get-tuple-element.38), channel_id=1, source_target_pairs={{0,1},{1,0},{2,3},{3,2},{4,5},{5,4},{6,7},{7,6},{8,9},{9,8},{10,11... | collective-permute-start | bytes 159752 | tf_op jit(solution)/shard_map/ppermute | solution.py:457
  35.3 1.9 %collective-permute-start.3 = (f32[104,128]{1,0:T(8,128)S(1)}, f32[104,128]{1,0:T(8,128)S(1)}, u32[]{:S(2)}, u32[]{:S(2)}) collective-permute-start(f32[104,128]{1,0:T(8,128)S(1)} %get-tuple-element.39), channel_id=1, source_target_pairs={{0,1},{1,0},{2,3},{3,2},{4,5},{5,4},{6,7},{7,6},{8,9},{9,8},{10,11... | collective-permute-start | bytes 159752 | tf_op jit(solution)/shard_map/ppermute | solution.py:457
  37.2 0.0 collective-permute-done.refs_2_.refs_10_
  37.2 0.0 collective-permute-done.1.refs_3_.refs_11_
  37.2 0.0 collective-permute-done.2.refs_0_.refs_8_
  37.2 1.2 collective-permute-done.3.refs_1_.refs_9_
  38.4 0.0 collective-permute-done.4.refs_6_
  38.4 0.0 copy-start
  38.4 0.2 complete_first.1
  38.6 1.9 %collective-permute-start.5 = (f32[144,128]{1,0:T(8,128)S(1)}, f32[144,128]{1,0:T(8,128)S(1)}, u32[]{:S(2)}, u32[]{:S(2)}) collective-permute-start(f32[144,128]{1,0:T(8,128)S(1)} %get-tuple-element.48), channel_id=1, source_target_pairs={{0,8},{8,0},{16,24},{24,16},{32,40},{40,32},{48,56},{56,48},{1,9},... | collective-permute-start | bytes 221192 | tf_op jit(solution)/shard_map/ppermute | solution.py:453
  40.5 8.5 %collective-permute-start.6 = (f32[144,128]{1,0:T(8,128)S(1)}, f32[144,128]{1,0:T(8,128)S(1)}, u32[]{:S(2)}, u32[]{:S(2)}) collective-permute-start(f32[144,128]{1,0:T(8,128)S(1)} %get-tuple-element.49), channel_id=1, source_target_pairs={{0,56},{8,16},{16,8},{24,32},{32,24},{40,48},{48,40},{56,0},{1,57}... | collective-permute-start | bytes 221192 | tf_op jit(solution)/shard_map/ppermute | solution.py:453
  49.1 0.0 copy-done
  49.1 3.1 %collective-permute-start.7 = (f32[2,64,128]{2,1,0:T(8,128)S(1)}, f32[2,64,128]{2,1,0:T(8,128)S(1)}, u32[]{:S(2)}, u32[]{:S(2)}) collective-permute-start(f32[2,64,128]{2,1,0:T(8,128)S(1)} %bitcast.5), channel_id=1, source_target_pairs={{0,128},{64,192},{128,256},{192,320},{256,384},{320,448},{1,129},{... | collective-permute-start | bytes 196616 | tf_op jit(solution)/shard_map/ppermute | solution.py:467
  52.2 1.3 collective-permute-done.7.refs_16_
  53.5 0.0 collective-permute-done.5.refs_1_
  53.5 0.0 collective-permute-done.6.refs_2_
  53.6 19.2 %all_to_all.20.refs_3_ = f32[8,48,128]{2,1,0:T(8,128)S(1)} all-to-all(f32[8,48,128]{2,1,0:T(8,128)S(1)} %broadcast_in_dim.12), channel_id=1, replica_groups=mesh['tm'=8,'block'=8,'chip'=4,'core'=2] {'tm'}, dimensions={0} | all-to-all | bytes 393216 | tf_op jit(solution)/shard_map/all_to_all | solution.py:471
  72.8 17.8 %all_to_all.21.refs_4_ = f32[4,320,128]{2,1,0:T(8,128)S(1)} all-to-all(f32[4,320,128]{2,1,0:T(8,128)S(1)} %hand_out.2), channel_id=1, replica_groups=mesh['tm'=8,'block'=8,'chip'=4,'core'=2] {'chip'}, dimensions={0} | all-to-all | bytes 1310720 | tf_op jit(solution)/shard_map/all_to_all | solution.py:475
  90.6 6.9 %collective-permute-start.8 = (f32[4,320,128]{2,1,0:T(8,128)S(1)}, f32[4,320,128]{2,1,0:T(8,128)S(1)}, u32[]{:S(2)}, u32[]{:S(2)}) collective-permute-start(f32[4,320,128]{2,1,0:T(8,128)S(1)} %all_to_all.21.refs_4_), channel_id=1, source_target_pairs={{0,1},{1,0},{2,3},{3,2},{4,5},{5,4},{6,7},{7,6},{8,9},{9,8},{10,11... | collective-permute-start | bytes 1966088 | tf_op jit(solution)/shard_map/ppermute | solution.py:457
  97.6 1.7 %collective-permute-done.8.refs_5_ = f32[4,320,128]{2,1,0:T(8,128)S(1)} collective-permute-done((f32[4,320,128]{2,1,0:T(8,128)S(1)}, f32[4,320,128]{2,1,0:T(8,128)S(1)}, u32[]{:S(2)}, u32[]{:S(2)}) %collective-permute-start.8) | collective-permute-done | bytes 655392 | tf_op jit(solution)/shard_map/ppermute | solution.py:457
  99.3 2.1 %finish_first.1 = (f32[2,64,128]{2,1,0:T(8,128)S(1)}, f32[2,64,128]{2,1,0:T(8,128)S(1)}, f32[4,64,128]{2,1,0:T(8,128)S(1)}, f32[2,64,128]{2,1,0:T(8,128)S(1)}, f...) custom-call(f32[208,128]{1,0:T(8,128)S(1)} %get-tuple-element.47.refs_0_, ...), custom_call_target="tpu_custom_call" | custom-call | tf_op jit(solution)/shard_map/finish_first/pallas_call | solution.py:435
  101.4 5.1 %collective-permute-start.10 = (f32[48,128]{1,0:T(8,128)S(1)}, f32[48,128]{1,0:T(8,128)S(1)}, u32[]{:S(2)}, u32[]{:S(2)}) collective-permute-start(f32[48,128]{1,0:T(8,128)S(1)} %get-tuple-element.58.refs_0_), channel_id=1, source_target_pairs={{0,8},{8,0},{16,24},{24,16},{32,40},{40,32},{48,56},{56,48},{1,9},... | collective-permute-start | bytes 73736 | tf_op jit(solution)/shard_map/ppermute | solution.py:453
  106.5 7.0 %collective-permute-start.9 = (f32[48,128]{1,0:T(8,128)S(1)}, f32[48,128]{1,0:T(8,128)S(1)}, u32[]{:S(2)}, u32[]{:S(2)}) collective-permute-start(f32[48,128]{1,0:T(8,128)S(1)} %get-tuple-element.58.refs_0_), channel_id=1, source_target_pairs={{0,56},{8,16},{16,8},{24,32},{32,24},{40,48},{48,40},{56,0},{1,57}... | collective-permute-start | bytes 73736 | tf_op jit(solution)/shard_map/ppermute | solution.py:453
  113.6 0.0 collective-permute-done.10.refs_1_
  113.6 3.7 %collective-permute-done.9.refs_2_ = f32[48,128]{1,0:T(8,128)S(1)} collective-permute-done((f32[48,128]{1,0:T(8,128)S(1)}, f32[48,128]{1,0:T(8,128)S(1)}, u32[]{:S(2)}, u32[]{:S(2)}) %collective-permute-start.9) | collective-permute-done | bytes 24608 | tf_op jit(solution)/shard_map/ppermute | solution.py:453
  117.3 17.2 %all_to_all.22.refs_3_ = f32[8,48,128]{2,1,0:T(8,128)S(1)} all-to-all(f32[8,48,128]{2,1,0:T(8,128)S(1)} %broadcast_in_dim.13), channel_id=1, replica_groups=mesh['tm'=8,'block'=8,'chip'=4,'core'=2] {'tm'}, dimensions={0} | all-to-all | bytes 393216 | tf_op jit(solution)/shard_map/all_to_all | solution.py:471
  134.6 15.0 %all_to_all.23.refs_4_ = f32[4,192,128]{2,1,0:T(8,128)S(1)} all-to-all(f32[4,192,128]{2,1,0:T(8,128)S(1)} %hand_out.3), channel_id=1, replica_groups=mesh['tm'=8,'block'=8,'chip'=4,'core'=2] {'chip'}, dimensions={0} | all-to-all | bytes 786432 | tf_op jit(solution)/shard_map/all_to_all | solution.py:475
  149.6 6.0 %collective-permute-start.11 = (f32[4,192,128]{2,1,0:T(8,128)S(1)}, f32[4,192,128]{2,1,0:T(8,128)S(1)}, u32[]{:S(2)}, u32[]{:S(2)}) collective-permute-start(f32[4,192,128]{2,1,0:T(8,128)S(1)} %all_to_all.23.refs_4_), channel_id=1, source_target_pairs={{0,1},{1,0},{2,3},{3,2},{4,5},{5,4},{6,7},{7,6},{8,9},{9,8},{10,11... | collective-permute-start | bytes 1179656 | tf_op jit(solution)/shard_map/ppermute | solution.py:457
  155.6 1.3 collective-permute-done.11.refs_5_
  156.9 2.0 %finish_second.1 = (f32[2,2,64,128]{3,2,1,0:T(8,128)}, f32[32,64]{1,0:T(8,128)}) custom-call(f32[48,128]{1,0:T(8,128)S(1)} %get-tuple-element.58.refs_0_, f32[48,128]{1,0:T(8,128)S(1)} %collective-permute-done.10.refs_1_, f32[48,128]{1,0:T(8,128)S(1)} %collective-permute-done.9.refs_2_, f32[8,48,128]{2,1,0:T(8,128)S(1)} %all_to_all.22.refs_3_, ...), custom_call_target="tpu_custom_call" | custom-call | tf_op jit(solution)/shard_map/finish_second/pallas_call | solution.py:435
  (10 shorter events, 0.1 us)
Async XLA Ops:
  0.6 37.8 %collective-permute-start.4 = (f32[2,64,128]{2,1,0:T(8,128)}, f32[2,64,128]{2,1,0:T(8,128)S(1)}, u32[]{:S(2)}, u32[]{:S(2)}) collective-permute-start(f32[2,64,128]{2,1,0:T(8,128)} %bitcast.3), channel_id=1, source_target_pairs={{0,64},{64,128},{128,192},{192,256},{256,320},{320,384},{384,448},... | collective-permute-start | bytes 196616 | tf_op jit(solution)/shard_map/ppermute | solution.py:467
  18.1 19.1 %collective-permute-start = (f32[104,128]{1,0:T(8,128)S(1)}, f32[104,128]{1,0:T(8,128)S(1)}, u32[]{:S(2)}, u32[]{:S(2)}) collective-permute-start(f32[104,128]{1,0:T(8,128)S(1)} %get-tuple-element.36), channel_id=1, source_target_pairs={{0,63},{1,2},{2,1},{3,4},{4,3},{5,6},{6,5},{7,8},{8,7},{9,10},{10,... | collective-permute-start | bytes 159752 | tf_op jit(solution)/shard_map/ppermute | solution.py:462
  21.6 15.6 %collective-permute-start.1 = (f32[104,128]{1,0:T(8,128)S(1)}, f32[104,128]{1,0:T(8,128)S(1)}, u32[]{:S(2)}, u32[]{:S(2)}) collective-permute-start(f32[104,128]{1,0:T(8,128)S(1)} %get-tuple-element.37), channel_id=1, source_target_pairs={{0,63},{1,2},{2,1},{3,4},{4,3},{5,6},{6,5},{7,8},{8,7},{9,10},{10,... | collective-permute-start | bytes 159752 | tf_op jit(solution)/shard_map/ppermute | solution.py:462
  23.7 13.5 %collective-permute-start.2 = (f32[104,128]{1,0:T(8,128)S(1)}, f32[104,128]{1,0:T(8,128)S(1)}, u32[]{:S(2)}, u32[]{:S(2)}) collective-permute-start(f32[104,128]{1,0:T(8,128)S(1)} %get-tuple-element.38), channel_id=1, source_target_pairs={{0,1},{1,0},{2,3},{3,2},{4,5},{5,4},{6,7},{7,6},{8,9},{9,8},{10,11... | collective-permute-start | bytes 159752 | tf_op jit(solution)/shard_map/ppermute | solution.py:457
  35.3 3.1 %collective-permute-start.3 = (f32[104,128]{1,0:T(8,128)S(1)}, f32[104,128]{1,0:T(8,128)S(1)}, u32[]{:S(2)}, u32[]{:S(2)}) collective-permute-start(f32[104,128]{1,0:T(8,128)S(1)} %get-tuple-element.39), channel_id=1, source_target_pairs={{0,1},{1,0},{2,3},{3,2},{4,5},{5,4},{6,7},{7,6},{8,9},{9,8},{10,11... | collective-permute-start | bytes 159752 | tf_op jit(solution)/shard_map/ppermute | solution.py:457
  38.4 10.7 %copy-start = (f32[1,2,64,128]{3,2,1,0:T(8,128)S(1)}, f32[1,2,64,128]{3,2,1,0:T(8,128)}, u32[]{:S(2)}) copy-start(f32[1,2,64,128]{3,2,1,0:T(8,128)} %param.5) | copy-start | bytes 196612
  38.6 14.9 %collective-permute-start.5 = (f32[144,128]{1,0:T(8,128)S(1)}, f32[144,128]{1,0:T(8,128)S(1)}, u32[]{:S(2)}, u32[]{:S(2)}) collective-permute-start(f32[144,128]{1,0:T(8,128)S(1)} %get-tuple-element.48), channel_id=1, source_target_pairs={{0,8},{8,0},{16,24},{24,16},{32,40},{40,32},{48,56},{56,48},{1,9},... | collective-permute-start | bytes 221192 | tf_op jit(solution)/shard_map/ppermute | solution.py:453
  40.5 13.0 %collective-permute-start.6 = (f32[144,128]{1,0:T(8,128)S(1)}, f32[144,128]{1,0:T(8,128)S(1)}, u32[]{:S(2)}, u32[]{:S(2)}) collective-permute-start(f32[144,128]{1,0:T(8,128)S(1)} %get-tuple-element.49), channel_id=1, source_target_pairs={{0,56},{8,16},{16,8},{24,32},{32,24},{40,48},{48,40},{56,0},{1,57}... | collective-permute-start | bytes 221192 | tf_op jit(solution)/shard_map/ppermute | solution.py:453
  49.1 4.4 %collective-permute-start.7 = (f32[2,64,128]{2,1,0:T(8,128)S(1)}, f32[2,64,128]{2,1,0:T(8,128)S(1)}, u32[]{:S(2)}, u32[]{:S(2)}) collective-permute-start(f32[2,64,128]{2,1,0:T(8,128)S(1)} %bitcast.5), channel_id=1, source_target_pairs={{0,128},{64,192},{128,256},{192,320},{256,384},{320,448},{1,129},{... | collective-permute-start | bytes 196616 | tf_op jit(solution)/shard_map/ppermute | solution.py:467
  90.6 8.7 %collective-permute-start.8 = (f32[4,320,128]{2,1,0:T(8,128)S(1)}, f32[4,320,128]{2,1,0:T(8,128)S(1)}, u32[]{:S(2)}, u32[]{:S(2)}) collective-permute-start(f32[4,320,128]{2,1,0:T(8,128)S(1)} %all_to_all.21.refs_4_), channel_id=1, source_target_pairs={{0,1},{1,0},{2,3},{3,2},{4,5},{5,4},{6,7},{7,6},{8,9},{9,8},{10,11... | collective-permute-start | bytes 1966088 | tf_op jit(solution)/shard_map/ppermute | solution.py:457
  101.4 12.2 %collective-permute-start.10 = (f32[48,128]{1,0:T(8,128)S(1)}, f32[48,128]{1,0:T(8,128)S(1)}, u32[]{:S(2)}, u32[]{:S(2)}) collective-permute-start(f32[48,128]{1,0:T(8,128)S(1)} %get-tuple-element.58.refs_0_), channel_id=1, source_target_pairs={{0,8},{8,0},{16,24},{24,16},{32,40},{40,32},{48,56},{56,48},{1,9},... | collective-permute-start | bytes 73736 | tf_op jit(solution)/shard_map/ppermute | solution.py:453
  106.5 10.8 %collective-permute-start.9 = (f32[48,128]{1,0:T(8,128)S(1)}, f32[48,128]{1,0:T(8,128)S(1)}, u32[]{:S(2)}, u32[]{:S(2)}) collective-permute-start(f32[48,128]{1,0:T(8,128)S(1)} %get-tuple-element.58.refs_0_), channel_id=1, source_target_pairs={{0,56},{8,16},{16,8},{24,32},{32,24},{40,48},{48,40},{56,0},{1,57}... | collective-permute-start | bytes 73736 | tf_op jit(solution)/shard_map/ppermute | solution.py:453
  149.6 7.3 %collective-permute-start.11 = (f32[4,192,128]{2,1,0:T(8,128)S(1)}, f32[4,192,128]{2,1,0:T(8,128)S(1)}, u32[]{:S(2)}, u32[]{:S(2)}) collective-permute-start(f32[4,192,128]{2,1,0:T(8,128)S(1)} %all_to_all.23.refs_4_), channel_id=1, source_target_pairs={{0,1},{1,0},{2,3},{3,2},{4,5},{5,4},{6,7},{7,6},{8,9},{9,8},{10,11... | collective-permute-start | bytes 1179656 | tf_op jit(solution)/shard_map/ppermute | solution.py:457

commit v16 on v15

--- a/solution.py
+++ b/solution.py
@@ -501,8 +501,8 @@
         first_kernel, (initial, coeff, guess),
         [(104, 128)] * 4 + [(4,) + coarse, slab, slab, slab], [(256, 128)], name="first", first=True,
     )
-    outer, outer_rest, inner, inner_rest, received = links.together(
-        links.swap_outer(outer), links.swap_outer(outer_rest), links.swap_inner(inner), links.swap_inner(inner_rest),
+    inner, inner_rest, outer, outer_rest, received = links.together(
+        links.swap_inner(inner), links.swap_inner(inner_rest), links.swap_outer(outer), links.swap_outer(outer_rest),
         links.onward(sent, 1),
     )
     owned, beside, beyond, mine, started, begin = links.call(

time: 160 us -> 166 us (1.038)
  waiting for transfers between devices: 9.24 us -> 19.4 us
  starting transfers between devices: 73.9 us -> 65.3 us
  blocking collectives: 69.2 us -> 74.2 us
    ppermute x4, waiting for transfers between devices: 3.72 us -> 12.1 us  [swap_block(): return lax.ppermute(x, 'block', pairs)]
    ppermute x4, starting transfers between devices: 26.4 us -> 20.4 us  [swap_inner(): return lax.ppermute(x, 'core', [(0, 1), (1, 0)])]
    all_to_all x2, blocking collectives: 36.5 us -> 39.7 us  [sections(): lax.all_to_all(jnp.broadcast_to(x, (SECTIONS,) + x.shape), 'tm', 0, 0)]
    ppermute x2, waiting for transfers between devices: 0.01 us -> 2.88 us  [swap_outer(): lax.ppermute(x, ('block', 'chip', 'core'), [(i, (i + 2 * (i % 2) - 1) % n...]
    ppermute x4, starting transfers between devices: 22.6 us -> 19.9 us  [swap_block(): return lax.ppermute(x, 'block', pairs)]
    all_to_all x2, blocking collectives: 32.8 us -> 34.5 us  [block(): return lax.all_to_all(x, 'chip', 0, 0)]
  transfers between devices with their start and end apart: 12 -> 12, of which waited for: 5 -> 7; matrix products, arithmetic and copies ran while one was open for 0% -> 0% of each run, Pallas kernels for 1% -> 1%
where the time goes in v16:
time: 166 us; the launch traced here: 165 us
  blocking collectives  74.2 us (45%)
  starting transfers between devices  65.3 us (39%)
  waiting for transfers between devices  19.4 us (12%)
  Pallas kernels  5.61 us (3%)
    all_to_all x2, blocking collectives, sections(): lax.all_to_all(jnp.broadcast_to(x, (SECTIONS,) + x.shape), 'tm', 0, 0)  39.7 us
    all_to_all x2, blocking collectives, block(): return lax.all_to_all(x, 'chip', 0, 0)  34.5 us
    ppermute x4, starting transfers between devices, swap_inner(): return lax.ppermute(x, 'core', [(0, 1), (1, 0)])  20.4 us
    ppermute x4, starting transfers between devices, swap_block(): return lax.ppermute(x, 'block', pairs)  19.9 us
    ppermute x2, starting transfers between devices, onward(): return lax.ppermute(x, 'tm', [(i, i + by) for i in range(n - by)])  19.4 us
    ppermute x4, waiting for transfers between devices, swap_block(): return lax.ppermute(x, 'block', pairs)  12.1 us
    pallas_call x6, Pallas kernels, run(): pl.pallas_call(placed, out_shape=[jax.ShapeDtypeStruct(shape, F32) if las...  5.61 us
    ppermute x2, starting transfers between devices, swap_outer(): lax.ppermute(x, ('block', 'chip', 'core'), [(i, (i + 2 * (i % 2) - 1) % n...  5.56 us
  transfers between devices with their start and end apart: 12, of which 7 were waited for; matrix products, arithmetic and copies ran while one was open for 0% of the time, Pallas kernels for 1%

profile of v16, /device:TPU:1, one launch (start us, length us, event | category | flops | bytes accessed | tf_op | source)
XLA Modules:
  0.0 165.4 jit_solution(14171551206587299121)
XLA Ops:
  0.6 16.3 %collective-permute-start.4 = (f32[2,64,128]{2,1,0:T(8,128)}, f32[2,64,128]{2,1,0:T(8,128)S(1)}, u32[]{:S(2)}, u32[]{:S(2)}) collective-permute-start(f32[2,64,128]{2,1,0:T(8,128)} %bitcast.3), channel_id=1, source_target_pairs={{0,64},{64,128},{128,192},{192,256},{256,320},{320,384},{384,448},... | collective-permute-start | bytes 196616 | tf_op jit(solution)/shard_map/ppermute | solution.py:467
  16.9 1.2 first.1
  18.1 2.9 %collective-permute-start = (f32[104,128]{1,0:T(8,128)S(1)}, f32[104,128]{1,0:T(8,128)S(1)}, u32[]{:S(2)}, u32[]{:S(2)}) collective-permute-start(f32[104,128]{1,0:T(8,128)S(1)} %get-tuple-element.36), channel_id=1, source_target_pairs={{0,1},{1,0},{2,3},{3,2},{4,5},{5,4},{6,7},{7,6},{8,9},{9,8},{10,11... | collective-permute-start | bytes 159752 | tf_op jit(solution)/shard_map/ppermute | solution.py:457
  21.0 1.9 %collective-permute-start.1 = (f32[104,128]{1,0:T(8,128)S(1)}, f32[104,128]{1,0:T(8,128)S(1)}, u32[]{:S(2)}, u32[]{:S(2)}) collective-permute-start(f32[104,128]{1,0:T(8,128)S(1)} %get-tuple-element.37), channel_id=1, source_target_pairs={{0,1},{1,0},{2,3},{3,2},{4,5},{5,4},{6,7},{7,6},{8,9},{9,8},{10,11... | collective-permute-start | bytes 159752 | tf_op jit(solution)/shard_map/ppermute | solution.py:457
  22.9 3.0 %collective-permute-start.2 = (f32[104,128]{1,0:T(8,128)S(1)}, f32[104,128]{1,0:T(8,128)S(1)}, u32[]{:S(2)}, u32[]{:S(2)}) collective-permute-start(f32[104,128]{1,0:T(8,128)S(1)} %get-tuple-element.38), channel_id=1, source_target_pairs={{0,63},{1,2},{2,1},{3,4},{4,3},{5,6},{6,5},{7,8},{8,7},{9,10},{10,... | collective-permute-start | bytes 159752 | tf_op jit(solution)/shard_map/ppermute | solution.py:462
  25.9 2.5 %collective-permute-start.3 = (f32[104,128]{1,0:T(8,128)S(1)}, f32[104,128]{1,0:T(8,128)S(1)}, u32[]{:S(2)}, u32[]{:S(2)}) collective-permute-start(f32[104,128]{1,0:T(8,128)S(1)} %get-tuple-element.39), channel_id=1, source_target_pairs={{0,63},{1,2},{2,1},{3,4},{4,3},{5,6},{6,5},{7,8},{8,7},{9,10},{10,... | collective-permute-start | bytes 159752 | tf_op jit(solution)/shard_map/ppermute | solution.py:462
  28.5 0.0 collective-permute-done.refs_0_.refs_8_
  28.5 0.0 collective-permute-done.1.refs_1_.refs_9_
  28.5 0.0 collective-permute-done.2.refs_2_.refs_10_
  28.5 2.9 %collective-permute-done.3.refs_3_.refs_11_ = f32[104,128]{1,0:T(8,128)S(1)} collective-permute-done((f32[104,128]{1,0:T(8,128)S(1)}, f32[104,128]{1,0:T(8,128)S(1)}, u32[]{:S(2)}, u32[]{:S(2)}) %collective-permute-start.3) | collective-permute-done | bytes 53280 | tf_op jit(solution)/shard_map/ppermute | solution.py:462
  31.4 0.0 collective-permute-done.4.refs_6_
  31.4 0.0 copy-start
  31.4 0.2 complete_first.1
  31.6 4.0 %collective-permute-start.5 = (f32[144,128]{1,0:T(8,128)S(1)}, f32[144,128]{1,0:T(8,128)S(1)}, u32[]{:S(2)}, u32[]{:S(2)}) collective-permute-start(f32[144,128]{1,0:T(8,128)S(1)} %get-tuple-element.48), channel_id=1, source_target_pairs={{0,8},{8,0},{16,24},{24,16},{32,40},{40,32},{48,56},{56,48},{1,9},... | collective-permute-start | bytes 221192 | tf_op jit(solution)/shard_map/ppermute | solution.py:453
  35.6 7.6 %collective-permute-start.6 = (f32[144,128]{1,0:T(8,128)S(1)}, f32[144,128]{1,0:T(8,128)S(1)}, u32[]{:S(2)}, u32[]{:S(2)}) collective-permute-start(f32[144,128]{1,0:T(8,128)S(1)} %get-tuple-element.49), channel_id=1, source_target_pairs={{0,56},{8,16},{16,8},{24,32},{32,24},{40,48},{48,40},{56,0},{1,57}... | collective-permute-start | bytes 221192 | tf_op jit(solution)/shard_map/ppermute | solution.py:453
  43.3 0.0 copy-done
  43.3 3.1 %collective-permute-start.7 = (f32[2,64,128]{2,1,0:T(8,128)S(1)}, f32[2,64,128]{2,1,0:T(8,128)S(1)}, u32[]{:S(2)}, u32[]{:S(2)}) collective-permute-start(f32[2,64,128]{2,1,0:T(8,128)S(1)} %bitcast.5), channel_id=1, source_target_pairs={{0,128},{64,192},{128,256},{192,320},{256,384},{320,448},{1,129},{... | collective-permute-start | bytes 196616 | tf_op jit(solution)/shard_map/ppermute | solution.py:467
  46.4 1.3 collective-permute-done.7.refs_16_
  47.7 0.0 collective-permute-done.5.refs_1_
  47.7 4.6 %collective-permute-done.6.refs_2_ = f32[144,128]{1,0:T(8,128)S(1)} collective-permute-done((f32[144,128]{1,0:T(8,128)S(1)}, f32[144,128]{1,0:T(8,128)S(1)}, u32[]{:S(2)}, u32[]{:S(2)}) %collective-permute-start.6) | collective-permute-done | bytes 73760 | tf_op jit(solution)/shard_map/ppermute | solution.py:453
  52.4 20.6 %all_to_all.20.refs_3_ = f32[8,48,128]{2,1,0:T(8,128)S(1)} all-to-all(f32[8,48,128]{2,1,0:T(8,128)S(1)} %broadcast_in_dim.12), channel_id=1, replica_groups=mesh['tm'=8,'block'=8,'chip'=4,'core'=2] {'tm'}, dimensions={0} | all-to-all | bytes 393216 | tf_op jit(solution)/shard_map/all_to_all | solution.py:471
  73.1 18.0 %all_to_all.21.refs_4_ = f32[4,320,128]{2,1,0:T(8,128)S(1)} all-to-all(f32[4,320,128]{2,1,0:T(8,128)S(1)} %hand_out.2), channel_id=1, replica_groups=mesh['tm'=8,'block'=8,'chip'=4,'core'=2] {'chip'}, dimensions={0} | all-to-all | bytes 1310720 | tf_op jit(solution)/shard_map/all_to_all | solution.py:475
  91.1 11.6 %collective-permute-start.8 = (f32[4,320,128]{2,1,0:T(8,128)S(1)}, f32[4,320,128]{2,1,0:T(8,128)S(1)}, u32[]{:S(2)}, u32[]{:S(2)}) collective-permute-start(f32[4,320,128]{2,1,0:T(8,128)S(1)} %all_to_all.21.refs_4_), channel_id=1, source_target_pairs={{0,1},{1,0},{2,3},{3,2},{4,5},{5,4},{6,7},{7,6},{8,9},{9,8},{10,11... | collective-permute-start | bytes 1966088 | tf_op jit(solution)/shard_map/ppermute | solution.py:457
  102.7 1.7 %collective-permute-done.8.refs_5_ = f32[4,320,128]{2,1,0:T(8,128)S(1)} collective-permute-done((f32[4,320,128]{2,1,0:T(8,128)S(1)}, f32[4,320,128]{2,1,0:T(8,128)S(1)}, u32[]{:S(2)}, u32[]{:S(2)}) %collective-permute-start.8) | collective-permute-done | bytes 655392 | tf_op jit(solution)/shard_map/ppermute | solution.py:457
  104.4 2.1 %finish_first.1 = (f32[2,64,128]{2,1,0:T(8,128)S(1)}, f32[2,64,128]{2,1,0:T(8,128)S(1)}, f32[4,64,128]{2,1,0:T(8,128)S(1)}, f32[2,64,128]{2,1,0:T(8,128)S(1)}, f...) custom-call(f32[208,128]{1,0:T(8,128)S(1)} %get-tuple-element.47.refs_0_, ...), custom_call_target="tpu_custom_call" | custom-call | tf_op jit(solution)/shard_map/finish_first/pallas_call | solution.py:435
  106.5 5.3 %collective-permute-start.10 = (f32[48,128]{1,0:T(8,128)S(1)}, f32[48,128]{1,0:T(8,128)S(1)}, u32[]{:S(2)}, u32[]{:S(2)}) collective-permute-start(f32[48,128]{1,0:T(8,128)S(1)} %get-tuple-element.58.refs_0_), channel_id=1, source_target_pairs={{0,8},{8,0},{16,24},{24,16},{32,40},{40,32},{48,56},{56,48},{1,9},... | collective-permute-start | bytes 73736 | tf_op jit(solution)/shard_map/ppermute | solution.py:453
  111.8 3.0 %collective-permute-start.9 = (f32[48,128]{1,0:T(8,128)S(1)}, f32[48,128]{1,0:T(8,128)S(1)}, u32[]{:S(2)}, u32[]{:S(2)}) collective-permute-start(f32[48,128]{1,0:T(8,128)S(1)} %get-tuple-element.58.refs_0_), channel_id=1, source_target_pairs={{0,56},{8,16},{16,8},{24,32},{32,24},{40,48},{48,40},{56,0},{1,57}... | collective-permute-start | bytes 73736 | tf_op jit(solution)/shard_map/ppermute | solution.py:453
  114.8 0.2 collective-permute-done.10.refs_1_
  115.0 7.4 %collective-permute-done.9.refs_2_ = f32[48,128]{1,0:T(8,128)S(1)} collective-permute-done((f32[48,128]{1,0:T(8,128)S(1)}, f32[48,128]{1,0:T(8,128)S(1)}, u32[]{:S(2)}, u32[]{:S(2)}) %collective-permute-start.9) | collective-permute-done | bytes 24608 | tf_op jit(solution)/shard_map/ppermute | solution.py:453
  122.4 19.1 %all_to_all.22.refs_3_ = f32[8,48,128]{2,1,0:T(8,128)S(1)} all-to-all(f32[8,48,128]{2,1,0:T(8,128)S(1)} %broadcast_in_dim.13), channel_id=1, replica_groups=mesh['tm'=8,'block'=8,'chip'=4,'core'=2] {'tm'}, dimensions={0} | all-to-all | bytes 393216 | tf_op jit(solution)/shard_map/all_to_all | solution.py:471
  141.5 16.4 %all_to_all.23.refs_4_ = f32[4,192,128]{2,1,0:T(8,128)S(1)} all-to-all(f32[4,192,128]{2,1,0:T(8,128)S(1)} %hand_out.3), channel_id=1, replica_groups=mesh['tm'=8,'block'=8,'chip'=4,'core'=2] {'chip'}, dimensions={0} | all-to-all | bytes 786432 | tf_op jit(solution)/shard_map/all_to_all | solution.py:475
  158.0 4.1 %collective-permute-start.11 = (f32[4,192,128]{2,1,0:T(8,128)S(1)}, f32[4,192,128]{2,1,0:T(8,128)S(1)}, u32[]{:S(2)}, u32[]{:S(2)}) collective-permute-start(f32[4,192,128]{2,1,0:T(8,128)S(1)} %all_to_all.23.refs_4_), channel_id=1, source_target_pairs={{0,1},{1,0},{2,3},{3,2},{4,5},{5,4},{6,7},{7,6},{8,9},{9,8},{10,11... | collective-permute-start | bytes 1179656 | tf_op jit(solution)/shard_map/ppermute | solution.py:457
  162.0 1.3 collective-permute-done.11.refs_5_
  163.4 2.0 %finish_second.1 = (f32[2,2,64,128]{3,2,1,0:T(8,128)}, f32[32,64]{1,0:T(8,128)}) custom-call(f32[48,128]{1,0:T(8,128)S(1)} %get-tuple-element.58.refs_0_, f32[48,128]{1,0:T(8,128)S(1)} %collective-permute-done.10.refs_1_, f32[48,128]{1,0:T(8,128)S(1)} %collective-permute-done.9.refs_2_, f32[8,48,128]{2,1,0:T(8,128)S(1)} %all_to_all.22.refs_3_, ...), custom_call_target="tpu_custom_call" | custom-call | tf_op jit(solution)/shard_map/finish_second/pallas_call | solution.py:435
  (10 shorter events, 0.1 us)
Async XLA Ops:
  0.6 30.8 %collective-permute-start.4 = (f32[2,64,128]{2,1,0:T(8,128)}, f32[2,64,128]{2,1,0:T(8,128)S(1)}, u32[]{:S(2)}, u32[]{:S(2)}) collective-permute-start(f32[2,64,128]{2,1,0:T(8,128)} %bitcast.3), channel_id=1, source_target_pairs={{0,64},{64,128},{128,192},{192,256},{256,320},{320,384},{384,448},... | collective-permute-start | bytes 196616 | tf_op jit(solution)/shard_map/ppermute | solution.py:467
  18.1 10.4 %collective-permute-start = (f32[104,128]{1,0:T(8,128)S(1)}, f32[104,128]{1,0:T(8,128)S(1)}, u32[]{:S(2)}, u32[]{:S(2)}) collective-permute-start(f32[104,128]{1,0:T(8,128)S(1)} %get-tuple-element.36), channel_id=1, source_target_pairs={{0,1},{1,0},{2,3},{3,2},{4,5},{5,4},{6,7},{7,6},{8,9},{9,8},{10,11... | collective-permute-start | bytes 159752 | tf_op jit(solution)/shard_map/ppermute | solution.py:457
  21.0 7.5 %collective-permute-start.1 = (f32[104,128]{1,0:T(8,128)S(1)}, f32[104,128]{1,0:T(8,128)S(1)}, u32[]{:S(2)}, u32[]{:S(2)}) collective-permute-start(f32[104,128]{1,0:T(8,128)S(1)} %get-tuple-element.37), channel_id=1, source_target_pairs={{0,1},{1,0},{2,3},{3,2},{4,5},{5,4},{6,7},{7,6},{8,9},{9,8},{10,11... | collective-permute-start | bytes 159752 | tf_op jit(solution)/shard_map/ppermute | solution.py:457
  22.9 5.6 %collective-permute-start.2 = (f32[104,128]{1,0:T(8,128)S(1)}, f32[104,128]{1,0:T(8,128)S(1)}, u32[]{:S(2)}, u32[]{:S(2)}) collective-permute-start(f32[104,128]{1,0:T(8,128)S(1)} %get-tuple-element.38), channel_id=1, source_target_pairs={{0,63},{1,2},{2,1},{3,4},{4,3},{5,6},{6,5},{7,8},{8,7},{9,10},{10,... | collective-permute-start | bytes 159752 | tf_op jit(solution)/shard_map/ppermute | solution.py:462
  25.9 5.5 %collective-permute-start.3 = (f32[104,128]{1,0:T(8,128)S(1)}, f32[104,128]{1,0:T(8,128)S(1)}, u32[]{:S(2)}, u32[]{:S(2)}) collective-permute-start(f32[104,128]{1,0:T(8,128)S(1)} %get-tuple-element.39), channel_id=1, source_target_pairs={{0,63},{1,2},{2,1},{3,4},{4,3},{5,6},{6,5},{7,8},{8,7},{9,10},{10,... | collective-permute-start | bytes 159752 | tf_op jit(solution)/shard_map/ppermute | solution.py:462
  31.4 11.9 %copy-start = (f32[1,2,64,128]{3,2,1,0:T(8,128)S(1)}, f32[1,2,64,128]{3,2,1,0:T(8,128)}, u32[]{:S(2)}) copy-start(f32[1,2,64,128]{3,2,1,0:T(8,128)} %param.5) | copy-start | bytes 196612
  31.6 16.1 %collective-permute-start.5 = (f32[144,128]{1,0:T(8,128)S(1)}, f32[144,128]{1,0:T(8,128)S(1)}, u32[]{:S(2)}, u32[]{:S(2)}) collective-permute-start(f32[144,128]{1,0:T(8,128)S(1)} %get-tuple-element.48), channel_id=1, source_target_pairs={{0,8},{8,0},{16,24},{24,16},{32,40},{40,32},{48,56},{56,48},{1,9},... | collective-permute-start | bytes 221192 | tf_op jit(solution)/shard_map/ppermute | solution.py:453
  35.6 16.7 %collective-permute-start.6 = (f32[144,128]{1,0:T(8,128)S(1)}, f32[144,128]{1,0:T(8,128)S(1)}, u32[]{:S(2)}, u32[]{:S(2)}) collective-permute-start(f32[144,128]{1,0:T(8,128)S(1)} %get-tuple-element.49), channel_id=1, source_target_pairs={{0,56},{8,16},{16,8},{24,32},{32,24},{40,48},{48,40},{56,0},{1,57}... | collective-permute-start | bytes 221192 | tf_op jit(solution)/shard_map/ppermute | solution.py:453
  43.3 4.4 %collective-permute-start.7 = (f32[2,64,128]{2,1,0:T(8,128)S(1)}, f32[2,64,128]{2,1,0:T(8,128)S(1)}, u32[]{:S(2)}, u32[]{:S(2)}) collective-permute-start(f32[2,64,128]{2,1,0:T(8,128)S(1)} %bitcast.5), channel_id=1, source_target_pairs={{0,128},{64,192},{128,256},{192,320},{256,384},{320,448},{1,129},{... | collective-permute-start | bytes 196616 | tf_op jit(solution)/shard_map/ppermute | solution.py:467
  91.1 13.3 %collective-permute-start.8 = (f32[4,320,128]{2,1,0:T(8,128)S(1)}, f32[4,320,128]{2,1,0:T(8,128)S(1)}, u32[]{:S(2)}, u32[]{:S(2)}) collective-permute-start(f32[4,320,128]{2,1,0:T(8,128)S(1)} %all_to_all.21.refs_4_), channel_id=1, source_target_pairs={{0,1},{1,0},{2,3},{3,2},{4,5},{5,4},{6,7},{7,6},{8,9},{9,8},{10,11... | collective-permute-start | bytes 1966088 | tf_op jit(solution)/shard_map/ppermute | solution.py:457
  106.5 8.5 %collective-permute-start.10 = (f32[48,128]{1,0:T(8,128)S(1)}, f32[48,128]{1,0:T(8,128)S(1)}, u32[]{:S(2)}, u32[]{:S(2)}) collective-permute-start(f32[48,128]{1,0:T(8,128)S(1)} %get-tuple-element.58.refs_0_), channel_id=1, source_target_pairs={{0,8},{8,0},{16,24},{24,16},{32,40},{40,32},{48,56},{56,48},{1,9},... | collective-permute-start | bytes 73736 | tf_op jit(solution)/shard_map/ppermute | solution.py:453
  111.8 10.6 %collective-permute-start.9 = (f32[48,128]{1,0:T(8,128)S(1)}, f32[48,128]{1,0:T(8,128)S(1)}, u32[]{:S(2)}, u32[]{:S(2)}) collective-permute-start(f32[48,128]{1,0:T(8,128)S(1)} %get-tuple-element.58.refs_0_), channel_id=1, source_target_pairs={{0,56},{8,16},{16,8},{24,32},{32,24},{40,48},{48,40},{56,0},{1,57}... | collective-permute-start | bytes 73736 | tf_op jit(solution)/shard_map/ppermute | solution.py:453
  158.0 5.4 %collective-permute-start.11 = (f32[4,192,128]{2,1,0:T(8,128)S(1)}, f32[4,192,128]{2,1,0:T(8,128)S(1)}, u32[]{:S(2)}, u32[]{:S(2)}) collective-permute-start(f32[4,192,128]{2,1,0:T(8,128)S(1)} %all_to_all.23.refs_4_), channel_id=1, source_target_pairs={{0,1},{1,0},{2,3},{3,2},{4,5},{5,4},{6,7},{7,6},{8,9},{9,8},{10,11... | collective-permute-start | bytes 1179656 | tf_op jit(solution)/shard_map/ppermute | solution.py:457

commit v17 on v16

--- a/solution.py
+++ b/solution.py
@@ -501,8 +501,8 @@
         first_kernel, (initial, coeff, guess),
         [(104, 128)] * 4 + [(4,) + coarse, slab, slab, slab], [(256, 128)], name="first", first=True,
     )
-    inner, inner_rest, outer, outer_rest, received = links.together(
-        links.swap_inner(inner), links.swap_inner(inner_rest), links.swap_outer(outer), links.swap_outer(outer_rest),
+    outer, inner, outer_rest, inner_rest, received = links.together(
+        links.swap_outer(outer), links.swap_inner(inner), links.swap_outer(outer_rest), links.swap_inner(inner_rest),
         links.onward(sent, 1),
     )
     owned, beside, beyond, mine, started, begin = links.call(

time: 166 us -> 163 us (0.982)
  starting transfers between devices: 65.3 us -> 73.3 us
  waiting for transfers between devices: 19.4 us -> 12 us
  blocking collectives: 74.2 us -> 71 us
    ppermute x4, starting transfers between devices: 20.4 us -> 29.6 us  [swap_inner(): return lax.ppermute(x, 'core', [(0, 1), (1, 0)])]
    ppermute x4, waiting for transfers between devices: 12.1 us -> 6.82 us  [swap_block(): return lax.ppermute(x, 'block', pairs)]
    all_to_all x2, blocking collectives: 39.7 us -> 35.9 us  [sections(): lax.all_to_all(jnp.broadcast_to(x, (SECTIONS,) + x.shape), 'tm', 0, 0)]
    ppermute x2, waiting for transfers between devices: 2.88 us -> 0.01 us  [swap_outer(): lax.ppermute(x, ('block', 'chip', 'core'), [(i, (i + 2 * (i % 2) - 1) % n...]
where the time goes in v17:
time: 163 us
  starting transfers between devices  73.3 us (45%)
  blocking collectives  71 us (44%)
  waiting for transfers between devices  12 us (7%)
  Pallas kernels  5.61 us (3%)
    all_to_all x2, blocking collectives, sections(): lax.all_to_all(jnp.broadcast_to(x, (SECTIONS,) + x.shape), 'tm', 0, 0)  35.9 us
    all_to_all x2, blocking collectives, block(): return lax.all_to_all(x, 'chip', 0, 0)  35 us
    ppermute x4, starting transfers between devices, swap_inner(): return lax.ppermute(x, 'core', [(0, 1), (1, 0)])  29.6 us
    ppermute x2, starting transfers between devices, onward(): return lax.ppermute(x, 'tm', [(i, i + by) for i in range(n - by)])  19.4 us
    ppermute x4, starting transfers between devices, swap_block(): return lax.ppermute(x, 'block', pairs)  18.9 us
    ppermute x4, waiting for transfers between devices, swap_block(): return lax.ppermute(x, 'block', pairs)  6.82 us
    pallas_call x6, Pallas kernels, run(): pl.pallas_call(placed, out_shape=[jax.ShapeDtypeStruct(shape, F32) if las...  5.61 us
    ppermute x2, starting transfers between devices, swap_outer(): lax.ppermute(x, ('block', 'chip', 'core'), [(i, (i + 2 * (i % 2) - 1) % n...  5.4 us
  transfers between devices with their start and end apart: 12, of which 7 were waited for; matrix products, arithmetic and copies ran while one was open for 0% of the time, Pallas kernels for 1%

profile of v17, /device:TPU:1, one launch (start us, length us, event | category | flops | bytes accessed | tf_op | source)
XLA Modules:
  0.0 162.7 jit_solution(15186913430668231577)
XLA Ops:
  0.6 16.3 %collective-permute-start.4 = (f32[2,64,128]{2,1,0:T(8,128)}, f32[2,64,128]{2,1,0:T(8,128)S(1)}, u32[]{:S(2)}, u32[]{:S(2)}) collective-permute-start(f32[2,64,128]{2,1,0:T(8,128)} %bitcast.3), channel_id=1, source_target_pairs={{0,64},{64,128},{128,192},{192,256},{256,320},{320,384},{384,448},... | collective-permute-start | bytes 196616 | tf_op jit(solution)/shard_map/ppermute | solution.py:467
  16.9 1.2 first.1
  18.1 3.5 %collective-permute-start = (f32[104,128]{1,0:T(8,128)S(1)}, f32[104,128]{1,0:T(8,128)S(1)}, u32[]{:S(2)}, u32[]{:S(2)}) collective-permute-start(f32[104,128]{1,0:T(8,128)S(1)} %get-tuple-element.36), channel_id=1, source_target_pairs={{0,63},{1,2},{2,1},{3,4},{4,3},{5,6},{6,5},{7,8},{8,7},{9,10},{10,... | collective-permute-start | bytes 159752 | tf_op jit(solution)/shard_map/ppermute | solution.py:462
  21.6 6.7 %collective-permute-start.1 = (f32[104,128]{1,0:T(8,128)S(1)}, f32[104,128]{1,0:T(8,128)S(1)}, u32[]{:S(2)}, u32[]{:S(2)}) collective-permute-start(f32[104,128]{1,0:T(8,128)S(1)} %get-tuple-element.37), channel_id=1, source_target_pairs={{0,1},{1,0},{2,3},{3,2},{4,5},{5,4},{6,7},{7,6},{8,9},{9,8},{10,11... | collective-permute-start | bytes 159752 | tf_op jit(solution)/shard_map/ppermute | solution.py:457
  28.2 1.9 %collective-permute-start.2 = (f32[104,128]{1,0:T(8,128)S(1)}, f32[104,128]{1,0:T(8,128)S(1)}, u32[]{:S(2)}, u32[]{:S(2)}) collective-permute-start(f32[104,128]{1,0:T(8,128)S(1)} %get-tuple-element.38), channel_id=1, source_target_pairs={{0,63},{1,2},{2,1},{3,4},{4,3},{5,6},{6,5},{7,8},{8,7},{9,10},{10,... | collective-permute-start | bytes 159752 | tf_op jit(solution)/shard_map/ppermute | solution.py:462
  30.2 7.0 %collective-permute-start.3 = (f32[104,128]{1,0:T(8,128)S(1)}, f32[104,128]{1,0:T(8,128)S(1)}, u32[]{:S(2)}, u32[]{:S(2)}) collective-permute-start(f32[104,128]{1,0:T(8,128)S(1)} %get-tuple-element.39), channel_id=1, source_target_pairs={{0,1},{1,0},{2,3},{3,2},{4,5},{5,4},{6,7},{7,6},{8,9},{9,8},{10,11... | collective-permute-start | bytes 159752 | tf_op jit(solution)/shard_map/ppermute | solution.py:457
  37.2 0.0 collective-permute-done.refs_2_.refs_10_
  37.2 0.0 collective-permute-done.1.refs_0_.refs_8_
  37.2 0.0 collective-permute-done.2.refs_3_.refs_11_
  37.2 0.8 collective-permute-done.3.refs_1_.refs_9_
  38.0 0.0 collective-permute-done.4.refs_6_
  38.1 0.0 copy-start
  38.1 0.2 complete_first.1
  38.3 1.9 %collective-permute-start.5 = (f32[144,128]{1,0:T(8,128)S(1)}, f32[144,128]{1,0:T(8,128)S(1)}, u32[]{:S(2)}, u32[]{:S(2)}) collective-permute-start(f32[144,128]{1,0:T(8,128)S(1)} %get-tuple-element.48), channel_id=1, source_target_pairs={{0,8},{8,0},{16,24},{24,16},{32,40},{40,32},{48,56},{56,48},{1,9},... | collective-permute-start | bytes 221192 | tf_op jit(solution)/shard_map/ppermute | solution.py:453
  40.2 8.5 %collective-permute-start.6 = (f32[144,128]{1,0:T(8,128)S(1)}, f32[144,128]{1,0:T(8,128)S(1)}, u32[]{:S(2)}, u32[]{:S(2)}) collective-permute-start(f32[144,128]{1,0:T(8,128)S(1)} %get-tuple-element.49), channel_id=1, source_target_pairs={{0,56},{8,16},{16,8},{24,32},{32,24},{40,48},{48,40},{56,0},{1,57}... | collective-permute-start | bytes 221192 | tf_op jit(solution)/shard_map/ppermute | solution.py:453
  48.7 0.0 copy-done
  48.7 3.1 %collective-permute-start.7 = (f32[2,64,128]{2,1,0:T(8,128)S(1)}, f32[2,64,128]{2,1,0:T(8,128)S(1)}, u32[]{:S(2)}, u32[]{:S(2)}) collective-permute-start(f32[2,64,128]{2,1,0:T(8,128)S(1)} %bitcast.5), channel_id=1, source_target_pairs={{0,128},{64,192},{128,256},{192,320},{256,384},{320,448},{1,129},{... | collective-permute-start | bytes 196616 | tf_op jit(solution)/shard_map/ppermute | solution.py:467
  51.9 1.3 collective-permute-done.7.refs_16_
  53.2 0.0 collective-permute-done.5.refs_1_
  53.2 1.6 collective-permute-done.6.refs_2_
  54.8 18.8 %all_to_all.20.refs_3_ = f32[8,48,128]{2,1,0:T(8,128)S(1)} all-to-all(f32[8,48,128]{2,1,0:T(8,128)S(1)} %broadcast_in_dim.12), channel_id=1, replica_groups=mesh['tm'=8,'block'=8,'chip'=4,'core'=2] {'tm'}, dimensions={0} | all-to-all | bytes 393216 | tf_op jit(solution)/shard_map/all_to_all | solution.py:471
  73.7 24.9 %all_to_all.21.refs_4_ = f32[4,320,128]{2,1,0:T(8,128)S(1)} all-to-all(f32[4,320,128]{2,1,0:T(8,128)S(1)} %hand_out.2), channel_id=1, replica_groups=mesh['tm'=8,'block'=8,'chip'=4,'core'=2] {'chip'}, dimensions={0} | all-to-all | bytes 1310720 | tf_op jit(solution)/shard_map/all_to_all | solution.py:475
  98.6 4.0 %collective-permute-start.8 = (f32[4,320,128]{2,1,0:T(8,128)S(1)}, f32[4,320,128]{2,1,0:T(8,128)S(1)}, u32[]{:S(2)}, u32[]{:S(2)}) collective-permute-start(f32[4,320,128]{2,1,0:T(8,128)S(1)} %all_to_all.21.refs_4_), channel_id=1, source_target_pairs={{0,1},{1,0},{2,3},{3,2},{4,5},{5,4},{6,7},{7,6},{8,9},{9,8},{10,11... | collective-permute-start | bytes 1966088 | tf_op jit(solution)/shard_map/ppermute | solution.py:457
  102.6 1.7 %collective-permute-done.8.refs_5_ = f32[4,320,128]{2,1,0:T(8,128)S(1)} collective-permute-done((f32[4,320,128]{2,1,0:T(8,128)S(1)}, f32[4,320,128]{2,1,0:T(8,128)S(1)}, u32[]{:S(2)}, u32[]{:S(2)}) %collective-permute-start.8) | collective-permute-done | bytes 655392 | tf_op jit(solution)/shard_map/ppermute | solution.py:457
  104.3 2.1 %finish_first.1 = (f32[2,64,128]{2,1,0:T(8,128)S(1)}, f32[2,64,128]{2,1,0:T(8,128)S(1)}, f32[4,64,128]{2,1,0:T(8,128)S(1)}, f32[2,64,128]{2,1,0:T(8,128)S(1)}, f...) custom-call(f32[208,128]{1,0:T(8,128)S(1)} %get-tuple-element.47.refs_0_, ...), custom_call_target="tpu_custom_call" | custom-call | tf_op jit(solution)/shard_map/finish_first/pallas_call | solution.py:435
  106.4 3.1 %collective-permute-start.10 = (f32[48,128]{1,0:T(8,128)S(1)}, f32[48,128]{1,0:T(8,128)S(1)}, u32[]{:S(2)}, u32[]{:S(2)}) collective-permute-start(f32[48,128]{1,0:T(8,128)S(1)} %get-tuple-element.58.refs_0_), channel_id=1, source_target_pairs={{0,8},{8,0},{16,24},{24,16},{32,40},{40,32},{48,56},{56,48},{1,9},... | collective-permute-start | bytes 73736 | tf_op jit(solution)/shard_map/ppermute | solution.py:453
  109.5 5.4 %collective-permute-start.9 = (f32[48,128]{1,0:T(8,128)S(1)}, f32[48,128]{1,0:T(8,128)S(1)}, u32[]{:S(2)}, u32[]{:S(2)}) collective-permute-start(f32[48,128]{1,0:T(8,128)S(1)} %get-tuple-element.58.refs_0_), channel_id=1, source_target_pairs={{0,56},{8,16},{16,8},{24,32},{32,24},{40,48},{48,40},{56,0},{1,57}... | collective-permute-start | bytes 73736 | tf_op jit(solution)/shard_map/ppermute | solution.py:453
  114.9 0.2 collective-permute-done.10.refs_1_
  115.1 5.0 %collective-permute-done.9.refs_2_ = f32[48,128]{1,0:T(8,128)S(1)} collective-permute-done((f32[48,128]{1,0:T(8,128)S(1)}, f32[48,128]{1,0:T(8,128)S(1)}, u32[]{:S(2)}, u32[]{:S(2)}) %collective-permute-start.9) | collective-permute-done | bytes 24608 | tf_op jit(solution)/shard_map/ppermute | solution.py:453
  120.1 17.1 %all_to_all.22.refs_3_ = f32[8,48,128]{2,1,0:T(8,128)S(1)} all-to-all(f32[8,48,128]{2,1,0:T(8,128)S(1)} %broadcast_in_dim.13), channel_id=1, replica_groups=mesh['tm'=8,'block'=8,'chip'=4,'core'=2] {'tm'}, dimensions={0} | all-to-all | bytes 393216 | tf_op jit(solution)/shard_map/all_to_all | solution.py:471
  137.3 10.1 %all_to_all.23.refs_4_ = f32[4,192,128]{2,1,0:T(8,128)S(1)} all-to-all(f32[4,192,128]{2,1,0:T(8,128)S(1)} %hand_out.3), channel_id=1, replica_groups=mesh['tm'=8,'block'=8,'chip'=4,'core'=2] {'chip'}, dimensions={0} | all-to-all | bytes 786432 | tf_op jit(solution)/shard_map/all_to_all | solution.py:475
  147.4 12.0 %collective-permute-start.11 = (f32[4,192,128]{2,1,0:T(8,128)S(1)}, f32[4,192,128]{2,1,0:T(8,128)S(1)}, u32[]{:S(2)}, u32[]{:S(2)}) collective-permute-start(f32[4,192,128]{2,1,0:T(8,128)S(1)} %all_to_all.23.refs_4_), channel_id=1, source_target_pairs={{0,1},{1,0},{2,3},{3,2},{4,5},{5,4},{6,7},{7,6},{8,9},{9,8},{10,11... | collective-permute-start | bytes 1179656 | tf_op jit(solution)/shard_map/ppermute | solution.py:457
  159.4 1.3 collective-permute-done.11.refs_5_
  160.7 2.0 %finish_second.1 = (f32[2,2,64,128]{3,2,1,0:T(8,128)}, f32[32,64]{1,0:T(8,128)}) custom-call(f32[48,128]{1,0:T(8,128)S(1)} %get-tuple-element.58.refs_0_, f32[48,128]{1,0:T(8,128)S(1)} %collective-permute-done.10.refs_1_, f32[48,128]{1,0:T(8,128)S(1)} %collective-permute-done.9.refs_2_, f32[8,48,128]{2,1,0:T(8,128)S(1)} %all_to_all.22.refs_3_, ...), custom_call_target="tpu_custom_call" | custom-call | tf_op jit(solution)/shard_map/finish_second/pallas_call | solution.py:435
  (10 shorter events, 0.1 us)
Async XLA Ops:
  0.6 37.4 %collective-permute-start.4 = (f32[2,64,128]{2,1,0:T(8,128)}, f32[2,64,128]{2,1,0:T(8,128)S(1)}, u32[]{:S(2)}, u32[]{:S(2)}) collective-permute-start(f32[2,64,128]{2,1,0:T(8,128)} %bitcast.3), channel_id=1, source_target_pairs={{0,64},{64,128},{128,192},{192,256},{256,320},{320,384},{384,448},... | collective-permute-start | bytes 196616 | tf_op jit(solution)/shard_map/ppermute | solution.py:467
  18.1 19.1 %collective-permute-start = (f32[104,128]{1,0:T(8,128)S(1)}, f32[104,128]{1,0:T(8,128)S(1)}, u32[]{:S(2)}, u32[]{:S(2)}) collective-permute-start(f32[104,128]{1,0:T(8,128)S(1)} %get-tuple-element.36), channel_id=1, source_target_pairs={{0,63},{1,2},{2,1},{3,4},{4,3},{5,6},{6,5},{7,8},{8,7},{9,10},{10,... | collective-permute-start | bytes 159752 | tf_op jit(solution)/shard_map/ppermute | solution.py:462
  21.6 15.6 %collective-permute-start.1 = (f32[104,128]{1,0:T(8,128)S(1)}, f32[104,128]{1,0:T(8,128)S(1)}, u32[]{:S(2)}, u32[]{:S(2)}) collective-permute-start(f32[104,128]{1,0:T(8,128)S(1)} %get-tuple-element.37), channel_id=1, source_target_pairs={{0,1},{1,0},{2,3},{3,2},{4,5},{5,4},{6,7},{7,6},{8,9},{9,8},{10,11... | collective-permute-start | bytes 159752 | tf_op jit(solution)/shard_map/ppermute | solution.py:457
  28.2 9.0 %collective-permute-start.2 = (f32[104,128]{1,0:T(8,128)S(1)}, f32[104,128]{1,0:T(8,128)S(1)}, u32[]{:S(2)}, u32[]{:S(2)}) collective-permute-start(f32[104,128]{1,0:T(8,128)S(1)} %get-tuple-element.38), channel_id=1, source_target_pairs={{0,63},{1,2},{2,1},{3,4},{4,3},{5,6},{6,5},{7,8},{8,7},{9,10},{10,... | collective-permute-start | bytes 159752 | tf_op jit(solution)/shard_map/ppermute | solution.py:462
  30.2 7.9 %collective-permute-start.3 = (f32[104,128]{1,0:T(8,128)S(1)}, f32[104,128]{1,0:T(8,128)S(1)}, u32[]{:S(2)}, u32[]{:S(2)}) collective-permute-start(f32[104,128]{1,0:T(8,128)S(1)} %get-tuple-element.39), channel_id=1, source_target_pairs={{0,1},{1,0},{2,3},{3,2},{4,5},{5,4},{6,7},{7,6},{8,9},{9,8},{10,11... | collective-permute-start | bytes 159752 | tf_op jit(solution)/shard_map/ppermute | solution.py:457
  38.1 10.7 %copy-start = (f32[1,2,64,128]{3,2,1,0:T(8,128)S(1)}, f32[1,2,64,128]{3,2,1,0:T(8,128)}, u32[]{:S(2)}) copy-start(f32[1,2,64,128]{3,2,1,0:T(8,128)} %param.5) | copy-start | bytes 196612
  38.3 14.9 %collective-permute-start.5 = (f32[144,128]{1,0:T(8,128)S(1)}, f32[144,128]{1,0:T(8,128)S(1)}, u32[]{:S(2)}, u32[]{:S(2)}) collective-permute-start(f32[144,128]{1,0:T(8,128)S(1)} %get-tuple-element.48), channel_id=1, source_target_pairs={{0,8},{8,0},{16,24},{24,16},{32,40},{40,32},{48,56},{56,48},{1,9},... | collective-permute-start | bytes 221192 | tf_op jit(solution)/shard_map/ppermute | solution.py:453
  40.2 14.6 %collective-permute-start.6 = (f32[144,128]{1,0:T(8,128)S(1)}, f32[144,128]{1,0:T(8,128)S(1)}, u32[]{:S(2)}, u32[]{:S(2)}) collective-permute-start(f32[144,128]{1,0:T(8,128)S(1)} %get-tuple-element.49), channel_id=1, source_target_pairs={{0,56},{8,16},{16,8},{24,32},{32,24},{40,48},{48,40},{56,0},{1,57}... | collective-permute-start | bytes 221192 | tf_op jit(solution)/shard_map/ppermute | solution.py:453
  48.7 4.4 %collective-permute-start.7 = (f32[2,64,128]{2,1,0:T(8,128)S(1)}, f32[2,64,128]{2,1,0:T(8,128)S(1)}, u32[]{:S(2)}, u32[]{:S(2)}) collective-permute-start(f32[2,64,128]{2,1,0:T(8,128)S(1)} %bitcast.5), channel_id=1, source_target_pairs={{0,128},{64,192},{128,256},{192,320},{256,384},{320,448},{1,129},{... | collective-permute-start | bytes 196616 | tf_op jit(solution)/shard_map/ppermute | solution.py:467
  98.6 5.7 %collective-permute-start.8 = (f32[4,320,128]{2,1,0:T(8,128)S(1)}, f32[4,320,128]{2,1,0:T(8,128)S(1)}, u32[]{:S(2)}, u32[]{:S(2)}) collective-permute-start(f32[4,320,128]{2,1,0:T(8,128)S(1)} %all_to_all.21.refs_4_), channel_id=1, source_target_pairs={{0,1},{1,0},{2,3},{3,2},{4,5},{5,4},{6,7},{7,6},{8,9},{9,8},{10,11... | collective-permute-start | bytes 1966088 | tf_op jit(solution)/shard_map/ppermute | solution.py:457
  106.4 8.7 %collective-permute-start.10 = (f32[48,128]{1,0:T(8,128)S(1)}, f32[48,128]{1,0:T(8,128)S(1)}, u32[]{:S(2)}, u32[]{:S(2)}) collective-permute-start(f32[48,128]{1,0:T(8,128)S(1)} %get-tuple-element.58.refs_0_), channel_id=1, source_target_pairs={{0,8},{8,0},{16,24},{24,16},{32,40},{40,32},{48,56},{56,48},{1,9},... | collective-permute-start | bytes 73736 | tf_op jit(solution)/shard_map/ppermute | solution.py:453
  109.5 10.6 %collective-permute-start.9 = (f32[48,128]{1,0:T(8,128)S(1)}, f32[48,128]{1,0:T(8,128)S(1)}, u32[]{:S(2)}, u32[]{:S(2)}) collective-permute-start(f32[48,128]{1,0:T(8,128)S(1)} %get-tuple-element.58.refs_0_), channel_id=1, source_target_pairs={{0,56},{8,16},{16,8},{24,32},{32,24},{40,48},{48,40},{56,0},{1,57}... | collective-permute-start | bytes 73736 | tf_op jit(solution)/shard_map/ppermute | solution.py:453
  147.4 13.3 %collective-permute-start.11 = (f32[4,192,128]{2,1,0:T(8,128)S(1)}, f32[4,192,128]{2,1,0:T(8,128)S(1)}, u32[]{:S(2)}, u32[]{:S(2)}) collective-permute-start(f32[4,192,128]{2,1,0:T(8,128)S(1)} %all_to_all.23.refs_4_), channel_id=1, source_target_pairs={{0,1},{1,0},{2,3},{3,2},{4,5},{5,4},{6,7},{7,6},{8,9},{9,8},{10,11... | collective-permute-start | bytes 1179656 | tf_op jit(solution)/shard_map/ppermute | solution.py:457
